TPU v7x, 256 devices: a whole 4x4x8 slice. The times are simulated.
256 devices in a mesh: elem: 16 (over z, y_hi), orb: 16 (over x, y_lo, core).
Axes of the slice: x: 4, y: 4 (y_hi: 2, y_lo: 2; y = y_hi * 2 + y_lo), z: 8, core: 2. Of those that a mesh axis runs over, the one named last changes fastest.
Arguments:
- hamiltonian: bfloat16 [512, 7, 128, 128], P('elem'), may hold values from -1 to 1, as said below
- start: bfloat16 [512, 128, 1024], P('elem', None, 'orb'), may hold values from -6 to 6
- ritz: bfloat16 [1024, 1024], P(None, 'orb'), may hold values from -0.1875 to 0.1875
Outputs:
- margin: float32 [1024, 1024], P('orb', 'elem')
- rotated: float32 [512, 128, 1024], P('elem', None, 'orb')
Inputs may be any that keep to these rules, and one draw needn't show every extreme that they name: hamiltonian[e, 1 + 2 k] is the transpose of hamiltonian[n(e, 1 + 2 k), 2 + 2 k], and each diagonal block hamiltonian[e, 0] is symmetric, so the operator is symmetric.
All inputs are finite; a program needn't handle non-finite values.
Results may differ from a plain program's by a relative error of at most 0.0095.
Values may be sent and summed in bfloat16 or wider, within the bound.
No kernel may reach another device: no remote copies, remote signals or barrier semaphores. Data moves between devices by JAX's collectives and lax.ppermute only.
A program may use at most 64 MiB of HBM per device.

v0:
```python
import functools

import jax
import jax.numpy as jnp
from jax import lax
from jax.experimental import pallas as pl
from jax.experimental.pallas import tpu as pltpu
from jax.sharding import Mesh, PartitionSpec as P


GY = 4
GZ = 4
NB = 128
DEG = 6
PLANE = GY * GZ

center_shift = 0.1
half_width = 1.25

ELEM = ("z", "yh")
ORB = ("x", "yl", "c")
CHIP = ("x", "yl")
VMEM = pl.BlockSpec(memory_space=pltpu.VMEM)


def weighted(ham, e, pair):
    return jnp.concatenate([ham[e, d] for d in pair], axis=1)


def interior_kernel(base, inside, scale, shift, has_previous, ham, own, inner, current, *rest):
    previous, out = rest if has_previous else (None, rest[0])
    contract = (((1,), (1,)), ((), ()))

    def plane(gy, carry):
        above = lax.rem(gy + GY - 1, GY) * GZ
        below = lax.rem(gy + 1, GY) * GZ
        for gz in range(GZ):
            e = gy * GZ + gz
            values = {
                0: own[e],
                inside: inner[e],
                3: own[above + gz],
                4: own[below + gz],
                5: own[gy * GZ + (gz - 1) % GZ],
                6: own[gy * GZ + (gz + 1) % GZ],
            }
            total = None
            for pair in ((0, inside), (3, 4), (5, 6)):
                left = jnp.concatenate([values[d] for d in pair], axis=1)
                term = lax.dot_general(left, weighted(ham, base + e, pair), contract, preferred_element_type=jnp.float32)
                total = term if total is None else total + term
            total = scale * total - shift * current[e].astype(jnp.float32)
            if has_previous:
                total = total - previous[e].astype(jnp.float32)
            out[e] = total
        return carry

    lax.fori_loop(0, GY, plane, 0)


def boundary_kernel(base, direction, scale, ham, halo, partial, full, rounded):
    contract = (((1,), (1,)), ((), ()))

    def plane(gy, carry):
        for gz in range(GZ):
            e = gy * GZ + gz
            term = lax.dot_general(halo[e], ham[base + e, direction], contract, preferred_element_type=jnp.float32)
            value = partial[e] + scale * term
            full[e] = value
            rounded[e] = value.astype(jnp.bfloat16)
        return carry

    lax.fori_loop(0, GY, plane, 0)


def cost(elements, cols, directions):
    size = elements * cols * NB
    return pl.CostEstimate(flops=2 * size * NB * directions, bytes_accessed=elements * NB * NB * 2 * directions, transcendentals=0)


def interior(ham, base, own, inner, inside, current, previous):
    first = previous is None
    scale = (1.0 if first else 2.0) / half_width
    operands = [ham, own, inner, current] + ([] if first else [previous])
    return pl.pallas_call(
        functools.partial(interior_kernel, base, inside, scale, scale * center_shift, not first),
        out_shape=jax.ShapeDtypeStruct(own.shape, jnp.float32),
        in_specs=[VMEM] * len(operands),
        out_specs=VMEM,
        cost_estimate=cost(own.shape[0], own.shape[1], 6),
        compiler_params=pltpu.CompilerParams(vmem_limit_bytes=12 << 20),
    )(*operands)


def boundary(ham, base, outside, halo, partial, first):
    scale = (1.0 if first else 2.0) / half_width
    return pl.pallas_call(
        functools.partial(boundary_kernel, base, outside, scale),
        out_shape=(
            jax.ShapeDtypeStruct(partial.shape, jnp.float32),
            jax.ShapeDtypeStruct(partial.shape, jnp.bfloat16),
        ),
        in_specs=[VMEM] * 3,
        out_specs=(VMEM, VMEM),
        cost_estimate=cost(halo.shape[0], halo.shape[1], 1),
        compiler_params=pltpu.CompilerParams(vmem_limit_bytes=12 << 20),
    )(ham, halo, partial)


def message_kernel(chips, core_ref, mine0, mine1, other0, other1, ritz, out, rows, own):
    cols = mine0.shape[2]
    held = mine0.shape[1]

    def fill(parity, source0, source1):
        for t in range(chips):
            for layer, source in enumerate((source0, source1)):
                for el in range(held):
                    at = (layer * held + el) * NB
                    rows[pl.ds((2 * t + parity) * cols, cols), pl.ds(at, NB)] = source[t, el]

    for t in range(chips):
        for layer, source in enumerate((mine0, mine1)):
            for el in range(held):
                own[pl.ds(t * cols, cols), pl.ds((layer * held + el) * NB, NB)] = source[t, el]

    @pl.when(core_ref[0] == 0)
    def _():
        fill(0, mine0, mine1)
        fill(1, other0, other1)

    @pl.when(core_ref[0] != 0)
    def _():
        fill(1, mine0, mine1)
        fill(0, other0, other1)

    contract = (((1,), (1,)), ((), ()))
    plain = (((1,), (0,)), ((), ()))
    base = chips * cols
    for s in range(0, chips, 2):
        left = own[pl.ds(s * cols, 2 * cols), :]
        part = lax.dot_general(left, rows[...], contract, preferred_element_type=jnp.float32)
        part = part.astype(jnp.bfloat16)
        for q in range(2):
            for t in range(chips):
                out[s + q, pl.ds(t * cols, cols), :] = part[q * cols : (q + 1) * cols, t * NB : (t + 1) * NB]
    for d in range(0, chips, 2):
        left = ritz[pl.ds(d * cols, 2 * cols), :]
        turned = lax.dot_general(left, rows[...], plain, preferred_element_type=jnp.float32)
        turned = turned.astype(jnp.bfloat16)
        for q in range(2):
            for el in range(2 * held):
                out[d + q, pl.ds(base + el * cols, cols), :] = turned[q * cols : (q + 1) * cols, el * NB : (el + 1) * NB]


def message(core, mine0, mine1, other0, other1, ritz):
    chips, held, cols, _ = mine0.shape
    depth = 2 * held * NB
    flops = 2 * (chips * cols) * (2 * chips * cols) * depth * 2
    return pl.pallas_call(
        functools.partial(message_kernel, chips),
        out_shape=jax.ShapeDtypeStruct((chips, (chips + 2 * held) * cols, NB), jnp.bfloat16),
        in_specs=[pl.BlockSpec(memory_space=pltpu.SMEM)] + [VMEM] * 5,
        out_specs=VMEM,
        scratch_shapes=[
            pltpu.VMEM((2 * chips * cols, depth), jnp.bfloat16),
            pltpu.VMEM((chips * cols, depth), jnp.bfloat16),
        ],
        cost_estimate=pl.CostEstimate(flops=flops, bytes_accessed=4 << 20, transcendentals=0),
        compiler_params=pltpu.CompilerParams(vmem_limit_bytes=24 << 20),
        name="message",
    )(core, mine0, mine1, other0, other1, ritz)


def step(hamiltonian, start, ritz):
    slabs = lax.axis_size("z") * lax.axis_size("yh")
    chips = lax.axis_size("x") * lax.axis_size("yl")
    rows_total = float(slabs * hamiltonian.shape[0] * NB)
    orb_cols = start.shape[2]
    up = [(i, (i + 1) % slabs) for i in range(slabs)]
    down = [((i + 1) % slabs, i) for i in range(slabs)]
    begin = jnp.swapaxes(start, 1, 2)
    base = {"a": 0, "b": PLANE}
    val = {("a", 0): begin[:PLANE], ("b", 0): begin[PLANE:]}
    full = dict(val)
    halo = {}

    def send(name, k):
        if name == "a":
            halo["b", k] = lax.ppermute(val["a", k], ELEM, down)
        else:
            halo["a", k] = lax.ppermute(val["b", k], ELEM, up)

    send("b", 0)
    send("a", 0)
    ritz_rows = jnp.swapaxes(ritz, 0, 1)
    ritz_chip = lax.all_to_all(
        jnp.broadcast_to(ritz_rows, (chips,) + ritz_rows.shape), CHIP, 0, 0, tiled=False
    )

    order = []
    for k in range(1, DEG + 1):
        order += [("a", k), ("b", k)] if k % 2 else [("b", k), ("a", k)]
    token = None
    rows = {}
    for count, (name, k) in enumerate(order):
        other = "b" if name == "a" else "a"
        inside, outside = (2, 1) if name == "a" else (1, 2)
        own, inner = val[name, k - 1], val[other, k - 1]
        if token is not None:
            own, inner, _ = lax.optimization_barrier((own, inner, token))
        part = interior(hamiltonian, base[name], own, inner, inside, full[name, k - 1], full.get((name, k - 2)))
        if count == 2 * DEG - 1:
            done, part, ritz_chip = lax.optimization_barrier((val[other, k], part, ritz_chip))
            rows[other] = lax.all_to_all(done, CHIP, 0, 0, tiled=True)
            edge = hamiltonian[base[name] : base[name] + PLANE, outside : outside + 1]
            full[name, k], token = boundary(edge, 0, 0, halo[name, k - 1], part, k == 1)
            rows[name] = lax.all_to_all(token, CHIP, 0, 0, tiled=True)
        else:
            full[name, k], token = boundary(hamiltonian, base[name], outside, halo[name, k - 1], part, k == 1)
        val[name, k] = token
        if k < DEG:
            send(name, k)
    rows = {n: r.reshape(chips, PLANE // chips, orb_cols, NB) for n, r in rows.items()}
    swap = {n: lax.ppermute(r, "c", [(0, 1), (1, 0)]) for n, r in rows.items()}

    core = lax.axis_index("c").astype(jnp.int32).reshape(1)
    sent = message(core, rows["a"], rows["b"], swap["a"], swap["b"], ritz_chip.reshape(chips * orb_cols, -1))
    got = lax.all_to_all(sent, CHIP, 0, 0, tiled=True)
    part, turned = got[:, : chips * orb_cols], got[:, chips * orb_cols :]
    total = jnp.sum(part.astype(jnp.float32), axis=0).astype(jnp.bfloat16)
    half = orb_cols // 2
    total = total.reshape(chips, 2, half, 2, orb_cols).transpose(0, 3, 2, 1, 4)
    total = lax.all_to_all(total.reshape(slabs, half, 2 * orb_cols), ELEM, 0, 0, tiled=True)
    margin = jnp.sum(total.astype(jnp.float32), axis=0) / rows_total
    margin = margin.reshape(half, 2, orb_cols).transpose(1, 0, 2).reshape(orb_cols, orb_cols)
    turned = turned.reshape(chips, 2, PLANE // chips, orb_cols, NB).transpose(1, 0, 2, 3, 4)
    rotated = turned.reshape(2 * PLANE, orb_cols, NB).astype(jnp.float32)
    return margin, jnp.swapaxes(rotated, 1, 2)


def solution(mesh):
    fine = Mesh(mesh.devices.reshape(8, 2, 4, 2, 2), ("z", "yh", "x", "yl", "c"))
    in_specs = (P(ELEM, None, None, None), P(ELEM, None, ORB), P(None, ORB))
    out_specs = (P(ORB, ELEM), P(ELEM, None, ORB))
    return jax.shard_map(step, mesh=fine, in_specs=in_specs, out_specs=out_specs, check_vma=False)
```

profile of v0, /device:TPU:4, one launch (start us, length us, event | category | flops | bytes accessed | tf_op | source)
XLA Modules:
  0.0 172.4 jit_solution(8050771337082395599)
XLA Ops:
  1.7 3.3 %collective-permute-start.1 = (bf16[16,64,128]{2,1,0:T(8,128)(2,1)S(1)}, bf16[16,64,128]{2,1,0:T(8,128)(2,1)S(1)}, u32[]{:S(2)}, u32[]{:S(2)}) collective-permute-start(bf16[16,64,128]{2,1,0:T(8,128)(2,1)S(1)} %get-tuple-element.50.inner.own.current.rest_0_), channel_id=1, source_target_pairs={{0,16},{16,32},{32,48},{48,64},{64,80},{80,96},{96,112},{112,128},... | collective-permute-start | bytes 786440 | tf_op jit(solution)/shard_map/ppermute | solution.py:191
  5.0 5.4 %collective-permute-start = (bf16[16,64,128]{2,1,0:T(8,128)(2,1)S(1)}, bf16[16,64,128]{2,1,0:T(8,128)(2,1)S(1)}, u32[]{:S(2)}, u32[]{:S(2)}) collective-permute-start(bf16[16,64,128]{2,1,0:T(8,128)(2,1)S(1)} %get-tuple-element.51.own.current.inner.rest_0_), channel_id=1, source_target_pairs={{16,0},{32,16},{48,32},{64,48},{80,64},{96,80},{112,96},{128,112},... | collective-permute-start | bytes 786440 | tf_op jit(solution)/shard_map/ppermute | solution.py:189
  10.4 3.1 %copy-done = bf16[32,7,128,128]{3,2,1,0:T(8,128)(2,1)S(1)} copy-done((bf16[32,7,128,128]{3,2,1,0:T(8,128)(2,1)S(1)}, bf16[32,7,128,128]{3,2,1,0:T(8,128)(2,1)}, u32[]{:S(2)}) %copy-start) | copy-done | bytes 7340056
  15.0 1.7 collective-permute-done.1.halo
  17.5 8.8 %collective-permute-start.3 = (bf16[16,64,128]{2,1,0:T(8,128)(2,1)S(1)}, bf16[16,64,128]{2,1,0:T(8,128)(2,1)S(1)}, u32[]{:S(2)}, u32[]{:S(2)}) collective-permute-start(bf16[16,64,128]{2,1,0:T(8,128)(2,1)S(1)} %get-tuple-element.57.inner.own), channel_id=1, source_target_pairs={{16,0},{32,16},{48,32},{64,48},{80,64},{96,80},{112,96},{128,112},... | collective-permute-start | bytes 786440 | tf_op jit(solution)/shard_map/ppermute | solution.py:189
  33.5 8.0 %collective-permute-done.2.halo = bf16[16,64,128]{2,1,0:T(8,128)(2,1)S(1)} collective-permute-done((bf16[16,64,128]{2,1,0:T(8,128)(2,1)S(1)}, bf16[16,64,128]{2,1,0:T(8,128)(2,1)S(1)}, u32[]{:S(2)}, u32[]{:S(2)}) %collective-permute-start.2) | collective-permute-done | bytes 262176 | tf_op jit(solution)/shard_map/ppermute | solution.py:191
  44.8 4.9 %all-to-all-start = ((bf16[8,64,1024]{2,1,0:T(8,128)(2,1)}), bf16[8,64,1024]{2,1,0:T(8,128)(2,1)}, u32[]{:S(2)}, u32[]{:S(2)}) async-start(bf16[8,64,1024]{2,1,0:T(8,128)(2,1)} %broadcast_in_dim.3), calls=%async_computation | async-start | bytes 2097152 | tf_op jit(solution)/shard_map/all_to_all | solution.py:196
  49.7 3.1 %copy-done.1 = bf16[32,7,128,128]{3,2,1,0:T(8,128)(2,1)S(1)} copy-done((bf16[32,7,128,128]{3,2,1,0:T(8,128)(2,1)S(1)}, bf16[32,7,128,128]{3,2,1,0:T(8,128)(2,1)}, u32[]{:S(2)}) %copy-start.1) | copy-done | bytes 7340056
  55.2 2.2 %collective-permute-start.7 = (bf16[16,64,128]{2,1,0:T(8,128)(2,1)S(1)}, bf16[16,64,128]{2,1,0:T(8,128)(2,1)S(1)}, u32[]{:S(2)}, u32[]{:S(2)}) collective-permute-start(bf16[16,64,128]{2,1,0:T(8,128)(2,1)S(1)} %get-tuple-element.73.inner.own), channel_id=1, source_target_pairs={{16,0},{32,16},{48,32},{64,48},{80,64},{96,80},{112,96},{128,112},... | collective-permute-start | bytes 786440 | tf_op jit(solution)/shard_map/ppermute | solution.py:189
  59.0 2.2 %collective-permute-done.4.halo = bf16[16,64,128]{2,1,0:T(8,128)(2,1)S(1)} collective-permute-done((bf16[16,64,128]{2,1,0:T(8,128)(2,1)S(1)}, bf16[16,64,128]{2,1,0:T(8,128)(2,1)S(1)}, u32[]{:S(2)}, u32[]{:S(2)}) %collective-permute-start.4) | collective-permute-done | bytes 262176 | tf_op jit(solution)/shard_map/ppermute | solution.py:189
  63.6 9.4 %collective-permute-done.7.halo = bf16[16,64,128]{2,1,0:T(8,128)(2,1)S(1)} collective-permute-done((bf16[16,64,128]{2,1,0:T(8,128)(2,1)S(1)}, bf16[16,64,128]{2,1,0:T(8,128)(2,1)S(1)}, u32[]{:S(2)}, u32[]{:S(2)}) %collective-permute-start.7) | collective-permute-done | bytes 262176 | tf_op jit(solution)/shard_map/ppermute | solution.py:189
  76.3 5.7 %collective-permute-start.8 = (bf16[16,64,128]{2,1,0:T(8,128)(2,1)S(1)}, bf16[16,64,128]{2,1,0:T(8,128)(2,1)S(1)}, u32[]{:S(2)}, u32[]{:S(2)}) collective-permute-start(bf16[16,64,128]{2,1,0:T(8,128)(2,1)S(1)} %get-tuple-element.82.own.inner), channel_id=1, source_target_pairs={{16,0},{32,16},{48,32},{64,48},{80,64},{96,80},{112,96},{128,112},... | collective-permute-start | bytes 786440 | tf_op jit(solution)/shard_map/ppermute | solution.py:189
  86.6 1.7 collective-permute-done.8.halo
  89.1 2.0 %collective-permute-start.10 = (bf16[16,64,128]{2,1,0:T(8,128)(2,1)S(1)}, bf16[16,64,128]{2,1,0:T(8,128)(2,1)S(1)}, u32[]{:S(2)}, u32[]{:S(2)}) collective-permute-start(bf16[16,64,128]{2,1,0:T(8,128)(2,1)S(1)} %get-tuple-element.90.own.inner), channel_id=1, source_target_pairs={{0,16},{16,32},{32,48},{48,64},{64,80},{80,96},{96,112},{112,128},... | collective-permute-start | bytes 786440 | tf_op jit(solution)/shard_map/ppermute | solution.py:191
  92.8 1.7 shard_map.71
  96.0 3.3 %collective-permute-done.10.halo = bf16[16,64,128]{2,1,0:T(8,128)(2,1)S(1)} collective-permute-done((bf16[16,64,128]{2,1,0:T(8,128)(2,1)S(1)}, bf16[16,64,128]{2,1,0:T(8,128)(2,1)S(1)}, u32[]{:S(2)}, u32[]{:S(2)}) %collective-permute-start.10) | collective-permute-done | bytes 262176 | tf_op jit(solution)/shard_map/ppermute | solution.py:191
  99.3 1.6 shard_map.73
  100.9 14.2 %all_to_all.25 = bf16[16,64,128]{2,1,0:T(8,128)(2,1)S(1)} all-to-all(bf16[16,64,128]{2,1,0:T(8,128)(2,1)S(1)} %get-tuple-element.93), channel_id=1, replica_groups=mesh['z'=8,'yh'=2,'x'=4,'yl'=2,'c'=2] {'x','yl'}, dimensions={0} | all-to-all | bytes 524288 | tf_op jit(solution)/shard_map/all_to_all | solution.py:217
  115.1 5.4 %all-to-all-start.2 = ((bf16[16,64,128]{2,1,0:T(8,128)(2,1)}), bf16[16,64,128]{2,1,0:T(8,128)(2,1)S(1)}, u32[]{:S(2)}, u32[]{:S(2)}) async-start(bf16[16,64,128]{2,1,0:T(8,128)(2,1)} %get-tuple-element.94), calls=%async_computation.2 | async-start | bytes 524288 | tf_op jit(solution)/shard_map/all_to_all | solution.py:214
  120.5 4.9 %all-to-all-done.2 = bf16[16,64,128]{2,1,0:T(8,128)(2,1)S(1)} async-done(((bf16[16,64,128]{2,1,0:T(8,128)(2,1)}), bf16[16,64,128]{2,1,0:T(8,128)(2,1)S(1)}, u32[]{:S(2)}, u32[]{:S(2)}) %all-to-all-start.2) | async-done | bytes 262176 | tf_op jit(solution)/shard_map/all_to_all | solution.py:214
  127.0 3.5 %message.1 = bf16[8,768,128]{2,1,0:T(8,128)(2,1)S(1)} custom-call(s32[1]{0:T(128)} %bitcast.core_ref, bf16[8,2,64,128]{3,2,1,0:T(8,128)(2,1)S(1)} %bitcast.19, bf16[8,2,64,128]{3,2,1,0:T(8,128)(2,1)S(1)} %bitcast.21, bf16[8,2,64,128]{3,2,1,0:T(8,128)(2,1)S(1)} %collective-permute-done.12.other0, bf16[8,2,64,128]{3,2,1,0:T(8,128)(2,1)S(1)} %collective-permute-done.13.other1, ...), custom_call_target="tpu_custom_call" | custom-call | flops 1073741824 | bytes 4194304 | tf_op jit(solution)/shard_map/message/pallas_call | solution.py:159
  130.5 24.1 %all_to_all.26 = bf16[8,768,128]{2,1,0:T(8,128)(2,1)S(1)} all-to-all(bf16[8,768,128]{2,1,0:T(8,128)(2,1)S(1)} %message.1), channel_id=1, replica_groups=mesh['z'=8,'yh'=2,'x'=4,'yl'=2,'c'=2] {'x','yl'}, dimensions={0} | all-to-all | bytes 3145728 | tf_op jit(solution)/shard_map/all_to_all | solution.py:228
  156.0 4.6 %all-to-all-start.4 = ((bf16[16,32,128]{2,1,0:T(8,128)(2,1)}), bf16[16,32,128]{2,1,0:T(8,128)(2,1)S(1)}, u32[]{:S(2)}, u32[]{:S(2)}) async-start(bf16[16,32,128]{2,1,0:T(8,128)(2,1)} %reshape.40), calls=%async_computation.4 | async-start | bytes 262144 | tf_op jit(solution)/shard_map/all_to_all | solution.py:233
  161.8 9.9 %all-to-all-done.4 = bf16[16,32,128]{2,1,0:T(8,128)(2,1)S(1)} async-done(((bf16[16,32,128]{2,1,0:T(8,128)(2,1)}), bf16[16,32,128]{2,1,0:T(8,128)(2,1)S(1)}, u32[]{:S(2)}, u32[]{:S(2)}) %all-to-all-start.4) | async-done | bytes 131104 | tf_op jit(solution)/shard_map/all_to_all | solution.py:233
  (62 shorter events, 36.9 us)
Async XLA Ops:
  1.7 15.0 %collective-permute-start.1 = (bf16[16,64,128]{2,1,0:T(8,128)(2,1)S(1)}, bf16[16,64,128]{2,1,0:T(8,128)(2,1)S(1)}, u32[]{:S(2)}, u32[]{:S(2)}) collective-permute-start(bf16[16,64,128]{2,1,0:T(8,128)(2,1)S(1)} %get-tuple-element.50.inner.own.current.rest_0_), channel_id=1, source_target_pairs={{0,16},{16,32},{32,48},{48,64},{64,80},{80,96},{96,112},{112,128},... | collective-permute-start | bytes 786440 | tf_op jit(solution)/shard_map/ppermute | solution.py:191
  5.0 22.9 %collective-permute-start = (bf16[16,64,128]{2,1,0:T(8,128)(2,1)S(1)}, bf16[16,64,128]{2,1,0:T(8,128)(2,1)S(1)}, u32[]{:S(2)}, u32[]{:S(2)}) collective-permute-start(bf16[16,64,128]{2,1,0:T(8,128)(2,1)S(1)} %get-tuple-element.51.own.current.inner.rest_0_), channel_id=1, source_target_pairs={{16,0},{32,16},{48,32},{64,48},{80,64},{96,80},{112,96},{128,112},... | collective-permute-start | bytes 786440 | tf_op jit(solution)/shard_map/ppermute | solution.py:189
  10.4 3.1 %copy-start = (bf16[32,7,128,128]{3,2,1,0:T(8,128)(2,1)S(1)}, bf16[32,7,128,128]{3,2,1,0:T(8,128)(2,1)}, u32[]{:S(2)}) copy-start(bf16[32,7,128,128]{3,2,1,0:T(8,128)(2,1)} %ham.45) | copy-start | bytes 22020100
  17.5 13.6 %collective-permute-start.3 = (bf16[16,64,128]{2,1,0:T(8,128)(2,1)S(1)}, bf16[16,64,128]{2,1,0:T(8,128)(2,1)S(1)}, u32[]{:S(2)}, u32[]{:S(2)}) collective-permute-start(bf16[16,64,128]{2,1,0:T(8,128)(2,1)S(1)} %get-tuple-element.57.inner.own), channel_id=1, source_target_pairs={{16,0},{32,16},{48,32},{64,48},{80,64},{96,80},{112,96},{128,112},... | collective-permute-start | bytes 786440 | tf_op jit(solution)/shard_map/ppermute | solution.py:189
  28.7 12.9 %collective-permute-start.2 = (bf16[16,64,128]{2,1,0:T(8,128)(2,1)S(1)}, bf16[16,64,128]{2,1,0:T(8,128)(2,1)S(1)}, u32[]{:S(2)}, u32[]{:S(2)}) collective-permute-start(bf16[16,64,128]{2,1,0:T(8,128)(2,1)S(1)} %get-tuple-element.58.own.inner), channel_id=1, source_target_pairs={{0,16},{16,32},{32,48},{48,64},{64,80},{80,96},{96,112},{112,128},... | collective-permute-start | bytes 786440 | tf_op jit(solution)/shard_map/ppermute | solution.py:191
  31.9 22.5 %collective-permute-start.5 = (bf16[16,64,128]{2,1,0:T(8,128)(2,1)S(1)}, bf16[16,64,128]{2,1,0:T(8,128)(2,1)S(1)}, u32[]{:S(2)}, u32[]{:S(2)}) collective-permute-start(bf16[16,64,128]{2,1,0:T(8,128)(2,1)S(1)} %get-tuple-element.65.inner.own), channel_id=1, source_target_pairs={{0,16},{16,32},{32,48},{48,64},{64,80},{80,96},{96,112},{112,128},... | collective-permute-start | bytes 786440 | tf_op jit(solution)/shard_map/ppermute | solution.py:191
  33.5 10.2 %copy-start.2 = (bf16[1024,64]{0,1:T(8,128)(2,1)S(1)}, bf16[1024,64]{0,1:T(8,128)(2,1)}, u32[]{:S(2)}) copy-start(bf16[1024,64]{0,1:T(8,128)(2,1)} %param.5) | copy-start | bytes 393220
  42.4 18.7 %collective-permute-start.4 = (bf16[16,64,128]{2,1,0:T(8,128)(2,1)S(1)}, bf16[16,64,128]{2,1,0:T(8,128)(2,1)S(1)}, u32[]{:S(2)}, u32[]{:S(2)}) collective-permute-start(bf16[16,64,128]{2,1,0:T(8,128)(2,1)S(1)} %get-tuple-element.66.own.inner), channel_id=1, source_target_pairs={{16,0},{32,16},{48,32},{64,48},{80,64},{96,80},{112,96},{128,112},... | collective-permute-start | bytes 786440 | tf_op jit(solution)/shard_map/ppermute | solution.py:189
  44.8 51.2 %all-to-all-start = ((bf16[8,64,1024]{2,1,0:T(8,128)(2,1)}), bf16[8,64,1024]{2,1,0:T(8,128)(2,1)}, u32[]{:S(2)}, u32[]{:S(2)}) async-start(bf16[8,64,1024]{2,1,0:T(8,128)(2,1)} %broadcast_in_dim.3), calls=%async_computation | async-start | bytes 2097152 | tf_op jit(solution)/shard_map/all_to_all | solution.py:196
  49.7 3.1 %copy-start.1 = (bf16[32,7,128,128]{3,2,1,0:T(8,128)(2,1)S(1)}, bf16[32,7,128,128]{3,2,1,0:T(8,128)(2,1)}, u32[]{:S(2)}) copy-start(bf16[32,7,128,128]{3,2,1,0:T(8,128)(2,1)} %ham.45) | copy-start | bytes 22020100
  55.2 17.8 %collective-permute-start.7 = (bf16[16,64,128]{2,1,0:T(8,128)(2,1)S(1)}, bf16[16,64,128]{2,1,0:T(8,128)(2,1)S(1)}, u32[]{:S(2)}, u32[]{:S(2)}) collective-permute-start(bf16[16,64,128]{2,1,0:T(8,128)(2,1)S(1)} %get-tuple-element.73.inner.own), channel_id=1, source_target_pairs={{16,0},{32,16},{48,32},{64,48},{80,64},{96,80},{112,96},{128,112},... | collective-permute-start | bytes 786440 | tf_op jit(solution)/shard_map/ppermute | solution.py:189
  61.9 13.5 %collective-permute-start.6 = (bf16[16,64,128]{2,1,0:T(8,128)(2,1)S(1)}, bf16[16,64,128]{2,1,0:T(8,128)(2,1)S(1)}, u32[]{:S(2)}, u32[]{:S(2)}) collective-permute-start(bf16[16,64,128]{2,1,0:T(8,128)(2,1)S(1)} %get-tuple-element.74.own.inner), channel_id=1, source_target_pairs={{0,16},{16,32},{32,48},{48,64},{64,80},{80,96},{96,112},{112,128},... | collective-permute-start | bytes 786440 | tf_op jit(solution)/shard_map/ppermute | solution.py:191
  73.8 10.2 %collective-permute-start.9 = (bf16[16,64,128]{2,1,0:T(8,128)(2,1)S(1)}, bf16[16,64,128]{2,1,0:T(8,128)(2,1)S(1)}, u32[]{:S(2)}, u32[]{:S(2)}) collective-permute-start(bf16[16,64,128]{2,1,0:T(8,128)(2,1)S(1)} %get-tuple-element.81.inner.own), channel_id=1, source_target_pairs={{0,16},{16,32},{32,48},{48,64},{64,80},{80,96},{96,112},{112,128},... | collective-permute-start | bytes 786440 | tf_op jit(solution)/shard_map/ppermute | solution.py:191
  76.3 12.0 %collective-permute-start.8 = (bf16[16,64,128]{2,1,0:T(8,128)(2,1)S(1)}, bf16[16,64,128]{2,1,0:T(8,128)(2,1)S(1)}, u32[]{:S(2)}, u32[]{:S(2)}) collective-permute-start(bf16[16,64,128]{2,1,0:T(8,128)(2,1)S(1)} %get-tuple-element.82.own.inner), channel_id=1, source_target_pairs={{16,0},{32,16},{48,32},{64,48},{80,64},{96,80},{112,96},{128,112},... | collective-permute-start | bytes 786440 | tf_op jit(solution)/shard_map/ppermute | solution.py:189
  84.0 7.1 %slice-start = ((s8[7340032]{0:T(1024)(128)(4,1)}), s8[4194304]{0:T(1024)(128)(4,1)S(1)}, s32[]{:S(2)}) async-start(s8[7340032]{0:T(1024)(128)(4,1)} %bitcast.16), calls=%async_computation.5 | async-start | bytes 8388608
  84.8 8.0 %collective-permute-start.11 = (bf16[16,64,128]{2,1,0:T(8,128)(2,1)S(1)}, bf16[16,64,128]{2,1,0:T(8,128)(2,1)S(1)}, u32[]{:S(2)}, u32[]{:S(2)}) collective-permute-start(bf16[16,64,128]{2,1,0:T(8,128)(2,1)S(1)} %get-tuple-element.89.inner.own), channel_id=1, source_target_pairs={{16,0},{32,16},{48,32},{64,48},{80,64},{96,80},{112,96},{128,112},... | collective-permute-start | bytes 786440 | tf_op jit(solution)/shard_map/ppermute | solution.py:189
  85.1 6.0 %slice-start.1 = ((s8[7340032]{0:T(1024)(128)(4,1)}), s8[3145728]{0:T(1024)(128)(4,1)S(1)}, s32[]{:S(2)}) async-start(s8[7340032]{0:T(1024)(128)(4,1)} %bitcast.16), calls=%async_computation.6 | async-start | bytes 6291456
  89.1 10.2 %collective-permute-start.10 = (bf16[16,64,128]{2,1,0:T(8,128)(2,1)S(1)}, bf16[16,64,128]{2,1,0:T(8,128)(2,1)S(1)}, u32[]{:S(2)}, u32[]{:S(2)}) collective-permute-start(bf16[16,64,128]{2,1,0:T(8,128)(2,1)S(1)} %get-tuple-element.90.own.inner), channel_id=1, source_target_pairs={{0,16},{16,32},{32,48},{48,64},{64,80},{80,96},{96,112},{112,128},... | collective-permute-start | bytes 786440 | tf_op jit(solution)/shard_map/ppermute | solution.py:191
  115.1 10.3 %all-to-all-start.2 = ((bf16[16,64,128]{2,1,0:T(8,128)(2,1)}), bf16[16,64,128]{2,1,0:T(8,128)(2,1)S(1)}, u32[]{:S(2)}, u32[]{:S(2)}) async-start(bf16[16,64,128]{2,1,0:T(8,128)(2,1)} %get-tuple-element.94), calls=%async_computation.2 | async-start | bytes 524288 | tf_op jit(solution)/shard_map/all_to_all | solution.py:214
  120.5 4.9 %collective-permute-start.12 = (bf16[8,2,64,128]{3,2,1,0:T(8,128)(2,1)S(1)}, bf16[8,2,64,128]{3,2,1,0:T(8,128)(2,1)S(1)}, u32[]{:S(2)}, u32[]{:S(2)}) collective-permute-start(bf16[8,2,64,128]{3,2,1,0:T(8,128)(2,1)S(1)} %bitcast.18), channel_id=1, source_target_pairs={{0,1},{1,0},{2,3},{3,2},{4,5},{5,4},{6,7},{7,6},{8,9},{9,8},{10,11... | collective-permute-start | bytes 786440 | tf_op jit(solution)/shard_map/ppermute | solution.py:224
  125.4 1.5 collective-permute-start.13
  156.0 15.7 %all-to-all-start.4 = ((bf16[16,32,128]{2,1,0:T(8,128)(2,1)}), bf16[16,32,128]{2,1,0:T(8,128)(2,1)S(1)}, u32[]{:S(2)}, u32[]{:S(2)}) async-start(bf16[16,32,128]{2,1,0:T(8,128)(2,1)} %reshape.40), calls=%async_computation.4 | async-start | bytes 262144 | tf_op jit(solution)/shard_map/all_to_all | solution.py:233
where the time goes:
time: 174 us; the launch traced here: 172 us
  starting transfers between devices  44.1 us (25%)
  waiting for transfers between devices  43.8 us (25%)
  blocking collectives  38.3 us (22%)
  Pallas kernels  33.5 us (19%)
  local copies, waits for them, and re-layouts  11.4 us (7%)
    all_to_all x1, blocking collectives, step(): got = lax.all_to_all(sent, CHIP, 0, 0, tiled=True)  24.1 us
    ppermute x6, starting transfers between devices, send(): halo['b', k] = lax.ppermute(val['a', k], ELEM, down)  23.7 us
    pallas_call x12, Pallas kernels, interior(): pl.pallas_call(functools.partial(interior_kernel, base, inside, scale, sc...  18.7 us
    all_to_all x1, blocking collectives, step(): rows[name] = lax.all_to_all(token, CHIP, 0, 0, tiled=True)  14.2 us
    ppermute x6, waiting for transfers between devices, send(): halo['b', k] = lax.ppermute(val['a', k], ELEM, down)  14 us
    ppermute x6, waiting for transfers between devices, send(): halo['a', k] = lax.ppermute(val['b', k], ELEM, up)  13.4 us
    pallas_call x12, Pallas kernels, boundary(): pl.pallas_call(functools.partial(boundary_kernel, base, outside, scale),...  11.4 us
    all_to_all x1, waiting for transfers between devices, step(): lax.all_to_all(total.reshape(slabs, half, 2 * orb_cols), ELEM, 0, 0, tile...  9.87 us
  transfers between devices with their start and end apart: 17, of which 12 were waited for; matrix products, arithmetic and copies ran while one was open for 1% of the time, Pallas kernels for 16%

commit v1 on v0

v1 whole, which is shorter than its diff:
```python
import functools

import jax
import jax.numpy as jnp
from jax import lax
from jax.experimental import pallas as pl
from jax.experimental.pallas import tpu as pltpu
from jax.sharding import Mesh, PartitionSpec as P


GY = 4
GZ = 4
NB = 128
DEG = 6
PLANE = GY * GZ

center_shift = 0.1
half_width = 1.25

ELEM = ("z", "yh")
ORB = ("x", "yl", "c")
CHIP = ("x", "yl")
VMEM = pl.BlockSpec(memory_space=pltpu.VMEM)
SMEM = pl.BlockSpec(memory_space=pltpu.SMEM)
ROWS = (((1,), (1,)), ((), ()))
PLAIN = (((1,), (0,)), ((), ()))


def product(left, right, contract):
    return lax.dot_general(left, right, contract, preferred_element_type=jnp.float32)


def inside_kernel(base, inside, scale, shift, has_previous, ham, own, inner, current, *rest):
    previous, out = rest if has_previous else (None, rest[0])

    def line(gy, carry):
        above = lax.rem(gy + GY - 1, GY) * GZ
        below = lax.rem(gy + 1, GY) * GZ
        for gz in range(GZ):
            e = gy * GZ + gz
            values = {
                0: own[e],
                inside: inner[e],
                3: own[above + gz],
                4: own[below + gz],
                5: own[gy * GZ + (gz - 1) % GZ],
                6: own[gy * GZ + (gz + 1) % GZ],
            }
            total = None
            for pair in ((0, inside), (3, 4), (5, 6)):
                left = jnp.concatenate([values[d] for d in pair], axis=1)
                right = jnp.concatenate([ham[base + e, d] for d in pair], axis=1)
                term = product(left, right, ROWS)
                total = term if total is None else total + term
            total = scale * total - shift * current[e].astype(jnp.float32)
            if has_previous:
                total = total - previous[e].astype(jnp.float32)
            out[e] = total
        return carry

    lax.fori_loop(0, GY, line, 0)


def outside_kernel(base, direction, scale, ham, halo, partial, rounded, *full):
    def line(gy, carry):
        for gz in range(GZ):
            e = gy * GZ + gz
            value = partial[e] + scale * product(halo[e], ham[base + e, direction], ROWS)
            rounded[e] = value.astype(jnp.bfloat16)
            if full:
                full[0][e] = value
        return carry

    lax.fori_loop(0, GY, line, 0)


def last_kernel(base, direction, scale, ham, halo, partial, other, filtered):
    def line(gy, carry):
        for gz in range(GZ):
            e = gy * GZ + gz
            value = partial[e] + scale * product(halo[e], ham[base + e, direction], ROWS)
            filtered[base + e] = value.astype(jnp.bfloat16)
            filtered[PLANE - base + e] = other[e]
        return carry

    lax.fori_loop(0, GY, line, 0)


def cost(elements, cols, directions):
    size = elements * cols * NB
    read = elements * NB * NB * 2 * directions
    return pl.CostEstimate(flops=2 * size * NB * directions, bytes_accessed=read, transcendentals=0)


def call(kernel, operands, out_shape, estimate, limit, scratch=(), in_specs=None):
    many = isinstance(out_shape, tuple)
    return pl.pallas_call(
        kernel,
        out_shape=out_shape,
        in_specs=in_specs or [VMEM] * len(operands),
        out_specs=(VMEM,) * len(out_shape) if many else VMEM,
        scratch_shapes=scratch,
        cost_estimate=estimate,
        compiler_params=pltpu.CompilerParams(vmem_limit_bytes=limit << 20),
    )(*operands)


def message_kernel(chips, place, mine, other, ritz, ritz_back, ritz_next, ritz_far, out, rows, own):
    held, cols = mine.shape[1], mine.shape[2]

    def fill(parity, source):
        for t in range(chips):
            for el in range(held):
                rows[pl.ds((2 * t + parity) * cols, cols), pl.ds(el * NB, NB)] = source[t, el]

    for t in range(chips):
        for el in range(held):
            own[pl.ds(t * cols, cols), pl.ds(el * NB, NB)] = mine[t, el]

    @pl.when(place[2] == 0)
    def _():
        fill(0, mine)
        fill(1, other)

    @pl.when(place[2] != 0)
    def _():
        fill(1, mine)
        fill(0, other)

    base = chips * cols
    for s in range(0, chips, 2):
        part = product(own[pl.ds(s * cols, 2 * cols), :], rows[...], ROWS).astype(jnp.bfloat16)
        for q in range(2):
            for t in range(chips):
                out[s + q, pl.ds(t * cols, cols), :] = part[q * cols : (q + 1) * cols, t * NB : (t + 1) * NB]
    around = chips // 2
    for away, source in ((0, ritz), (around - 1, ritz_back), (1, ritz_next), (2, ritz_far)):
        turned = product(source[...].reshape(2 * cols, -1), rows[...], PLAIN).astype(jnp.bfloat16)
        for q in range(2):
            to = lax.rem(place[0] + away, around) * 2 + (place[1] if q == 0 else 1 - place[1])
            for el in range(held):
                piece = turned[q * cols : (q + 1) * cols, el * NB : (el + 1) * NB]
                out[to, pl.ds(base + el * cols, cols), :] = piece


def margin_rows_kernel(chips, got, out):
    cols = out.shape[2] // 2
    half = cols // 2
    for t in range(chips):
        total = got[0, pl.ds(t * cols, cols), :].astype(jnp.float32)
        for s in range(1, chips):
            total = total + got[s, pl.ds(t * cols, cols), :].astype(jnp.float32)
        for core in range(2):
            block = total[:, core * cols : (core + 1) * cols]
            out[2 * t + core] = jnp.concatenate([block[:half], block[half:]], axis=1).astype(jnp.bfloat16)


def margin_kernel(scale, got, out):
    total = got[0].astype(jnp.float32)
    for s in range(1, got.shape[0]):
        total = total + got[s].astype(jnp.float32)
    total = total * scale
    half, cols = got.shape[1], out.shape[1]
    out[0:half, :] = total[:, :cols]
    out[half : 2 * half, :] = total[:, cols:]


def whole(hamiltonian, start, ritz):
    slabs = lax.axis_size("z") * lax.axis_size("yh")
    chips = lax.axis_size("x") * lax.axis_size("yl")
    around = lax.axis_size("x")
    rows_total = float(slabs * hamiltonian.shape[0] * NB)
    cols = start.shape[2]
    layer = jax.ShapeDtypeStruct((PLANE, cols, NB), jnp.float32)
    up = [(i, (i + 1) % slabs) for i in range(slabs)]
    down = [((i + 1) % slabs, i) for i in range(slabs)]
    begin = jnp.swapaxes(start, 1, 2)
    base = {"a": 0, "b": PLANE}
    val = {("a", 0): begin[:PLANE], ("b", 0): begin[PLANE:]}
    full = dict(val)
    halo = {}

    def send(name, k):
        if name == "a":
            halo["b", k] = lax.ppermute(val["a", k], ELEM, down)
        else:
            halo["a", k] = lax.ppermute(val["b", k], ELEM, up)

    send("b", 0)
    send("a", 0)

    order = []
    for k in range(1, DEG + 1):
        order += [("a", k), ("b", k)] if k % 2 else [("b", k), ("a", k)]
    token = None
    shared = {"own": jnp.swapaxes(ritz, 0, 1)}
    for count, (name, k) in enumerate(order):
        other = "b" if name == "a" else "a"
        inside, outside = (2, 1) if name == "a" else (1, 2)
        own, inner = val[name, k - 1], val[other, k - 1]
        if token is not None:
            own, inner, _ = lax.optimization_barrier((own, inner, token))
        scale = (1.0 if k == 1 else 2.0) / half_width
        operands = [hamiltonian, own, inner, full[name, k - 1]]
        if k > 1:
            operands.append(full[name, k - 2])
        part = call(
            functools.partial(inside_kernel, base[name], inside, scale, scale * center_shift, k > 1),
            operands, layer, cost(PLANE, cols, 6), 12,
        )
        edge = [hamiltonian, halo[name, k - 1], part]
        if count == 2 * DEG - 1:
            filtered = call(
                functools.partial(last_kernel, base[name], outside, scale),
                edge + [val[other, k]],
                jax.ShapeDtypeStruct((2 * PLANE, cols, NB), jnp.bfloat16), cost(PLANE, cols, 1), 12,
            )
            break
        kept = (layer,) if k < DEG else ()
        token, *kept = call(
            functools.partial(outside_kernel, base[name], outside, scale),
            edge, (layer.update(dtype=jnp.bfloat16), *kept), cost(PLANE, cols, 1), 12,
        )
        val[name, k] = token
        if kept:
            full[name, k] = kept[0]
        if k < DEG:
            send(name, k)
        if count == 1:
            source, _ = lax.optimization_barrier((shared["own"], token))
            shared["pair"] = jnp.stack([source, lax.ppermute(source, "yl", [(0, 1), (1, 0)])])
        elif count in (4, 6, 8):
            shift = {4: 1, 6: around - 1, 8: 2}[count]
            source, _ = lax.optimization_barrier((shared["pair"], token))
            shared[shift] = lax.ppermute(source, "x", [(i, (i + shift) % around) for i in range(around)])

    mine = lax.all_to_all(filtered, CHIP, 0, 0, tiled=True)
    mine = mine.reshape(chips, 2 * PLANE // chips, cols, NB)
    theirs = lax.ppermute(mine, "c", [(0, 1), (1, 0)])
    place = jnp.stack([lax.axis_index("x"), lax.axis_index("yl"), lax.axis_index("c")]).astype(jnp.int32)
    held = mine.shape[1]
    depth = held * NB
    sent = call(
        functools.partial(message_kernel, chips),
        (place, mine, theirs, shared["pair"], shared[1], shared[around - 1], shared[2]),
        jax.ShapeDtypeStruct((chips, (chips + held) * cols, NB), jnp.bfloat16),
        pl.CostEstimate(flops=8 * (chips * cols) ** 2 * depth, bytes_accessed=4 << 20, transcendentals=0),
        24,
        (pltpu.VMEM((2 * chips * cols, depth), jnp.bfloat16), pltpu.VMEM((chips * cols, depth), jnp.bfloat16)),
        [SMEM] + [VMEM] * 6,
    )
    got = lax.all_to_all(sent, CHIP, 0, 0, tiled=True)
    small = pl.CostEstimate(flops=1 << 20, bytes_accessed=1 << 20, transcendentals=0)
    rows = call(
        functools.partial(margin_rows_kernel, chips), (got,),
        jax.ShapeDtypeStruct((slabs, cols // 2, 2 * cols), jnp.bfloat16), small, 12,
    )
    rows = lax.all_to_all(rows, ELEM, 0, 0, tiled=True)
    margin = call(
        functools.partial(margin_kernel, 1.0 / rows_total), (rows,),
        jax.ShapeDtypeStruct((cols, cols), jnp.float32), small, 12,
    )
    turned = got[:, chips * cols :].reshape(2 * PLANE, cols, NB).astype(jnp.float32)
    return margin, jnp.swapaxes(turned, 1, 2)


def solution(mesh):
    fine = Mesh(mesh.devices.reshape(8, 2, 4, 2, 2), ("z", "yh", "x", "yl", "c"))
    in_specs = (P(ELEM, None, None, None), P(ELEM, None, ORB), P(None, ORB))
    out_specs = (P(ORB, ELEM), P(ELEM, None, ORB))
    return jax.shard_map(whole, mesh=fine, in_specs=in_specs, out_specs=out_specs, check_vma=False)
```

time: 174 us -> 170 us (0.977)
  local copies, waits for them, and re-layouts: 11.4 us -> 4.19 us
  starting transfers between devices: 44.1 us -> 48.3 us
  blocking collectives: 38.3 us -> 34.7 us
  waiting for transfers between devices: 43.8 us -> 46.8 us
    ppermute x2 -> x5, waiting for transfers between devices: 1.53 us -> 14.2 us  [the longest x3 8.61 us: whole(): lax.ppermute(source, 'x', [(i, (i + shift) % around) for i in range(aroun...]
    ppermute x6, waiting for transfers between devices: 14 us -> 4.8 us  [send(): halo['b', k] = lax.ppermute(val['a', k], ELEM, down)]
    ppermute x2 -> x5, starting transfers between devices: 0.01 us -> 5.83 us  [the longest x3 5.52 us: whole(): lax.ppermute(source, 'x', [(i, (i + shift) % around) for i in range(aroun...]
    all_to_all x3 -> x1, waiting for transfers between devices: 14.8 us -> 9.99 us  [whole(): rows = lax.all_to_all(rows, ELEM, 0, 0, tiled=True)]
    ppermute x6, waiting for transfers between devices: 13.4 us -> 17.8 us  [send(): halo['a', k] = lax.ppermute(val['b', k], ELEM, up)]
    all_to_all x3 -> x1, starting transfers between devices: 14.9 us -> 10.7 us  [whole(): rows = lax.all_to_all(rows, ELEM, 0, 0, tiled=True)]
    all_to_all x2, blocking collectives: 38.3 us -> 34.7 us  [the longest x1 23.7 us: whole(): got = lax.all_to_all(sent, CHIP, 0, 0, tiled=True)]
    unnamed x10 -> x4, local copies, waits for them, and re-layouts: 6.18 us -> 3.09 us
  transfers between devices with their start and end apart: 17 -> 18, of which waited for: 12 -> 13; matrix products, arithmetic and copies ran while one was open for 1% -> 1% of each run, Pallas kernels for 16% -> 16%
where the time goes in v1:
time: 170 us; the launch traced here: 169 us
  starting transfers between devices  48.3 us (28%)
  waiting for transfers between devices  46.8 us (28%)
  blocking collectives  34.7 us (20%)
  Pallas kernels  32.7 us (19%)
  local copies, waits for them, and re-layouts  4.19 us (2%)
    pallas_call x27, Pallas kernels, call(): pl.pallas_call(kernel, out_shape=out_shape, in_specs=in_specs or [VMEM] *...  32.7 us
    ppermute x6, starting transfers between devices, send(): halo['b', k] = lax.ppermute(val['a', k], ELEM, down)  25.5 us
    all_to_all x1, blocking collectives, whole(): got = lax.all_to_all(sent, CHIP, 0, 0, tiled=True)  23.7 us
    ppermute x6, waiting for transfers between devices, send(): halo['a', k] = lax.ppermute(val['b', k], ELEM, up)  17.8 us
    all_to_all x1, blocking collectives, whole(): mine = lax.all_to_all(filtered, CHIP, 0, 0, tiled=True)  11 us
    all_to_all x1, starting transfers between devices, whole(): rows = lax.all_to_all(rows, ELEM, 0, 0, tiled=True)  10.7 us
    all_to_all x1, waiting for transfers between devices, whole(): rows = lax.all_to_all(rows, ELEM, 0, 0, tiled=True)  9.99 us
    ppermute x3, waiting for transfers between devices, whole(): lax.ppermute(source, 'x', [(i, (i + shift) % around) for i in range(aroun...  8.61 us
  transfers between devices with their start and end apart: 18, of which 13 were waited for; matrix products, arithmetic and copies ran while one was open for 1% of the time, Pallas kernels for 16%

profile of v1, /device:TPU:4, one launch (start us, length us, event | category | flops | bytes accessed | tf_op | source)
XLA Modules:
  0.0 168.8 jit_solution(16791324210133493072)
XLA Ops:
  1.7 3.3 %collective-permute-start.1 = (bf16[16,64,128]{2,1,0:T(8,128)(2,1)S(1)}, bf16[16,64,128]{2,1,0:T(8,128)(2,1)S(1)}, u32[]{:S(2)}, u32[]{:S(2)}) collective-permute-start(bf16[16,64,128]{2,1,0:T(8,128)(2,1)S(1)} %get-tuple-element.49.inner.own.current.rest_0_), channel_id=1, source_target_pairs={{0,16},{16,32},{32,48},{48,64},{64,80},{80,96},{96,112},{112,128},... | collective-permute-start | bytes 786440 | tf_op jit(solution)/shard_map/ppermute | solution.py:187
  5.0 5.4 %collective-permute-start = (bf16[16,64,128]{2,1,0:T(8,128)(2,1)S(1)}, bf16[16,64,128]{2,1,0:T(8,128)(2,1)S(1)}, u32[]{:S(2)}, u32[]{:S(2)}) collective-permute-start(bf16[16,64,128]{2,1,0:T(8,128)(2,1)S(1)} %get-tuple-element.50.own.current.inner.rest_0_), channel_id=1, source_target_pairs={{16,0},{32,16},{48,32},{64,48},{80,64},{96,80},{112,96},{128,112},... | collective-permute-start | bytes 786440 | tf_op jit(solution)/shard_map/ppermute | solution.py:185
  10.4 3.1 %copy-done = bf16[32,7,128,128]{3,2,1,0:T(8,128)(2,1)S(1)} copy-done((bf16[32,7,128,128]{3,2,1,0:T(8,128)(2,1)S(1)}, bf16[32,7,128,128]{3,2,1,0:T(8,128)(2,1)}, u32[]{:S(2)}) %copy-start) | copy-done | bytes 7340056
  13.4 1.6 shard_map.50.partial
  15.0 1.7 collective-permute-done.1.halo
  17.5 8.8 %collective-permute-start.3 = (bf16[16,64,128]{2,1,0:T(8,128)(2,1)S(1)}, bf16[16,64,128]{2,1,0:T(8,128)(2,1)S(1)}, u32[]{:S(2)}, u32[]{:S(2)}) collective-permute-start(bf16[16,64,128]{2,1,0:T(8,128)(2,1)S(1)} %get-tuple-element.56.inner.own), channel_id=1, source_target_pairs={{16,0},{32,16},{48,32},{64,48},{80,64},{96,80},{112,96},{128,112},... | collective-permute-start | bytes 786440 | tf_op jit(solution)/shard_map/ppermute | solution.py:185
  26.3 1.6 shard_map.52.partial
  33.5 8.1 %collective-permute-done.2.halo = bf16[16,64,128]{2,1,0:T(8,128)(2,1)S(1)} collective-permute-done((bf16[16,64,128]{2,1,0:T(8,128)(2,1)S(1)}, bf16[16,64,128]{2,1,0:T(8,128)(2,1)S(1)}, u32[]{:S(2)}, u32[]{:S(2)}) %collective-permute-start.2) | collective-permute-done | bytes 262176 | tf_op jit(solution)/shard_map/ppermute | solution.py:187
  46.1 3.1 %collective-permute-start.7 = (bf16[16,64,128]{2,1,0:T(8,128)(2,1)S(1)}, bf16[16,64,128]{2,1,0:T(8,128)(2,1)S(1)}, u32[]{:S(2)}, u32[]{:S(2)}) collective-permute-start(bf16[16,64,128]{2,1,0:T(8,128)(2,1)S(1)} %get-tuple-element.72.inner.own), channel_id=1, source_target_pairs={{16,0},{32,16},{48,32},{64,48},{80,64},{96,80},{112,96},{128,112},... | collective-permute-start | bytes 786440 | tf_op jit(solution)/shard_map/ppermute | solution.py:185
  53.8 2.4 %collective-permute-done.7.halo = bf16[16,64,128]{2,1,0:T(8,128)(2,1)S(1)} collective-permute-done((bf16[16,64,128]{2,1,0:T(8,128)(2,1)S(1)}, bf16[16,64,128]{2,1,0:T(8,128)(2,1)S(1)}, u32[]{:S(2)}, u32[]{:S(2)}) %collective-permute-start.7) | collective-permute-done | bytes 262176 | tf_op jit(solution)/shard_map/ppermute | solution.py:185
  59.8 3.4 %collective-permute-done.6.halo = bf16[16,64,128]{2,1,0:T(8,128)(2,1)S(1)} collective-permute-done((bf16[16,64,128]{2,1,0:T(8,128)(2,1)S(1)}, bf16[16,64,128]{2,1,0:T(8,128)(2,1)S(1)}, u32[]{:S(2)}, u32[]{:S(2)}) %collective-permute-start.6) | collective-permute-done | bytes 262176 | tf_op jit(solution)/shard_map/ppermute | solution.py:187
  64.0 4.2 %collective-permute-start.8 = (bf16[16,64,128]{2,1,0:T(8,128)(2,1)S(1)}, bf16[16,64,128]{2,1,0:T(8,128)(2,1)S(1)}, u32[]{:S(2)}, u32[]{:S(2)}) collective-permute-start(bf16[16,64,128]{2,1,0:T(8,128)(2,1)S(1)} %get-tuple-element.81.own.inner), channel_id=1, source_target_pairs={{16,0},{32,16},{48,32},{64,48},{80,64},{96,80},{112,96},{128,112},... | collective-permute-start | bytes 786440 | tf_op jit(solution)/shard_map/ppermute | solution.py:185
  70.7 2.6 %collective-permute-start.11 = (bf16[16,64,128]{2,1,0:T(8,128)(2,1)S(1)}, bf16[16,64,128]{2,1,0:T(8,128)(2,1)S(1)}, u32[]{:S(2)}, u32[]{:S(2)}) collective-permute-start(bf16[16,64,128]{2,1,0:T(8,128)(2,1)S(1)} %get-tuple-element.87.inner.own), channel_id=1, source_target_pairs={{16,0},{32,16},{48,32},{64,48},{80,64},{96,80},{112,96},{128,112},... | collective-permute-start | bytes 786440 | tf_op jit(solution)/shard_map/ppermute | solution.py:185
  82.2 4.7 %collective-permute-done.10.halo = bf16[16,64,128]{2,1,0:T(8,128)(2,1)S(1)} collective-permute-done((bf16[16,64,128]{2,1,0:T(8,128)(2,1)S(1)}, bf16[16,64,128]{2,1,0:T(8,128)(2,1)S(1)}, u32[]{:S(2)}, u32[]{:S(2)}) %collective-permute-start.10) | collective-permute-done | bytes 262176 | tf_op jit(solution)/shard_map/ppermute | solution.py:187
  87.6 11.0 %all_to_all.15 = bf16[32,64,128]{2,1,0:T(8,128)(2,1)S(1)} all-to-all(bf16[32,64,128]{2,1,0:T(8,128)(2,1)S(1)} %shard_map.73), channel_id=1, replica_groups=mesh['z'=8,'yh'=2,'x'=4,'yl'=2,'c'=2] {'x','yl'}, dimensions={0} | all-to-all | bytes 1048576 | tf_op jit(solution)/shard_map/all_to_all | solution.py:237
  98.9 5.6 %collective-permute-done.13 = bf16[64,1024]{1,0:T(8,128)(2,1)S(1)} collective-permute-done((bf16[64,1024]{1,0:T(8,128)(2,1)S(1)}, bf16[64,1024]{1,0:T(8,128)(2,1)S(1)}, u32[]{:S(2)}, u32[]{:S(2)}) %collective-permute-start.13) | collective-permute-done | bytes 131104 | tf_op jit(solution)/shard_map/ppermute | solution.py:231
  106.7 3.4 %collective-permute-start.16 = (bf16[2,64,1024]{2,1,0:T(8,128)(2,1)S(1)}, bf16[2,64,1024]{2,1,0:T(8,128)(2,1)S(1)}, u32[]{:S(2)}, u32[]{:S(2)}) collective-permute-start(bf16[2,64,1024]{2,1,0:T(8,128)(2,1)S(1)} %pad_maximum_fusion.ritz), channel_id=1, source_target_pairs={{0,8},{4,12},{8,0},{12,4},{1,9},{5,13},{9,1},{13,5},{2,10},{6,14},... | collective-permute-start | bytes 786440 | tf_op jit(solution)/shard_map/ppermute | solution.py:235
  110.2 3.0 %collective-permute-done.14.ritz_back = bf16[2,64,1024]{2,1,0:T(8,128)(2,1)S(1)} collective-permute-done((bf16[2,64,1024]{2,1,0:T(8,128)(2,1)S(1)}, bf16[2,64,1024]{2,1,0:T(8,128)(2,1)S(1)}, u32[]{:S(2)}, u32[]{:S(2)}) %collective-permute-start.14) | collective-permute-done | bytes 262176 | tf_op jit(solution)/shard_map/ppermute | solution.py:235
  113.2 2.0 %collective-permute-done.15.ritz_next = bf16[2,64,1024]{2,1,0:T(8,128)(2,1)S(1)} collective-permute-done((bf16[2,64,1024]{2,1,0:T(8,128)(2,1)S(1)}, bf16[2,64,1024]{2,1,0:T(8,128)(2,1)S(1)}, u32[]{:S(2)}, u32[]{:S(2)}) %collective-permute-start.15) | collective-permute-done | bytes 262176 | tf_op jit(solution)/shard_map/ppermute | solution.py:235
  115.2 3.6 %collective-permute-done.16.ritz_far = bf16[2,64,1024]{2,1,0:T(8,128)(2,1)S(1)} collective-permute-done((bf16[2,64,1024]{2,1,0:T(8,128)(2,1)S(1)}, bf16[2,64,1024]{2,1,0:T(8,128)(2,1)S(1)}, u32[]{:S(2)}, u32[]{:S(2)}) %collective-permute-start.16) | collective-permute-done | bytes 262176 | tf_op jit(solution)/shard_map/ppermute | solution.py:235
  118.8 2.9 %shard_map.74 = bf16[8,768,128]{2,1,0:T(8,128)(2,1)S(1)} custom-call(s32[3]{0:T(128)S(1)} %pad_add_fusion.place, bf16[8,4,64,128]{3,2,1,0:T(8,128)(2,1)S(1)} %bitcast.13, bf16[8,4,64,128]{3,2,1,0:T(8,128)(2,1)S(1)} %collective-permute-done.12.other, bf16[2,64,1024]{2,1,0:T(8,128)(2,1)S(1)} %pad_maximum_fusion.ritz, ...), custom_call_target="tpu_custom_call" | custom-call | flops 1073741824 | bytes 4194304 | tf_op jit(solution)/shard_map/pallas_call | solution.py:97
  121.6 23.7 %all_to_all.16.got = bf16[8,768,128]{2,1,0:T(8,128)(2,1)S(1)} all-to-all(bf16[8,768,128]{2,1,0:T(8,128)(2,1)S(1)} %shard_map.74), channel_id=1, replica_groups=mesh['z'=8,'yh'=2,'x'=4,'yl'=2,'c'=2] {'x','yl'}, dimensions={0} | all-to-all | bytes 3145728 | tf_op jit(solution)/shard_map/all_to_all | solution.py:252
  146.2 10.7 %all-to-all-start.2 = ((bf16[16,32,128]{2,1,0:T(8,128)(2,1)}), bf16[16,32,128]{2,1,0:T(8,128)(2,1)S(1)}, u32[]{:S(2)}, u32[]{:S(2)}) async-start(bf16[16,32,128]{2,1,0:T(8,128)(2,1)} %shard_map.75), calls=%async_computation.2 | async-start | bytes 262144 | tf_op jit(solution)/shard_map/all_to_all | solution.py:258
  158.1 10.0 %all-to-all-done.2.got = bf16[16,32,128]{2,1,0:T(8,128)(2,1)S(1)} async-done(((bf16[16,32,128]{2,1,0:T(8,128)(2,1)}), bf16[16,32,128]{2,1,0:T(8,128)(2,1)S(1)}, u32[]{:S(2)}, u32[]{:S(2)}) %all-to-all-start.2) | async-done | bytes 131104 | tf_op jit(solution)/shard_map/all_to_all | solution.py:258
  (50 shorter events, 38.1 us)
Async XLA Ops:
  1.7 15.0 %collective-permute-start.1 = (bf16[16,64,128]{2,1,0:T(8,128)(2,1)S(1)}, bf16[16,64,128]{2,1,0:T(8,128)(2,1)S(1)}, u32[]{:S(2)}, u32[]{:S(2)}) collective-permute-start(bf16[16,64,128]{2,1,0:T(8,128)(2,1)S(1)} %get-tuple-element.49.inner.own.current.rest_0_), channel_id=1, source_target_pairs={{0,16},{16,32},{32,48},{48,64},{64,80},{80,96},{96,112},{112,128},... | collective-permute-start | bytes 786440 | tf_op jit(solution)/shard_map/ppermute | solution.py:187
  5.0 22.9 %collective-permute-start = (bf16[16,64,128]{2,1,0:T(8,128)(2,1)S(1)}, bf16[16,64,128]{2,1,0:T(8,128)(2,1)S(1)}, u32[]{:S(2)}, u32[]{:S(2)}) collective-permute-start(bf16[16,64,128]{2,1,0:T(8,128)(2,1)S(1)} %get-tuple-element.50.own.current.inner.rest_0_), channel_id=1, source_target_pairs={{16,0},{32,16},{48,32},{64,48},{80,64},{96,80},{112,96},{128,112},... | collective-permute-start | bytes 786440 | tf_op jit(solution)/shard_map/ppermute | solution.py:185
  10.4 3.1 %copy-start = (bf16[32,7,128,128]{3,2,1,0:T(8,128)(2,1)S(1)}, bf16[32,7,128,128]{3,2,1,0:T(8,128)(2,1)}, u32[]{:S(2)}) copy-start(bf16[32,7,128,128]{3,2,1,0:T(8,128)(2,1)} %ham.47) | copy-start | bytes 22020100
  17.5 13.6 %collective-permute-start.3 = (bf16[16,64,128]{2,1,0:T(8,128)(2,1)S(1)}, bf16[16,64,128]{2,1,0:T(8,128)(2,1)S(1)}, u32[]{:S(2)}, u32[]{:S(2)}) collective-permute-start(bf16[16,64,128]{2,1,0:T(8,128)(2,1)S(1)} %get-tuple-element.56.inner.own), channel_id=1, source_target_pairs={{16,0},{32,16},{48,32},{64,48},{80,64},{96,80},{112,96},{128,112},... | collective-permute-start | bytes 786440 | tf_op jit(solution)/shard_map/ppermute | solution.py:185
  28.7 12.9 %collective-permute-start.2 = (bf16[16,64,128]{2,1,0:T(8,128)(2,1)S(1)}, bf16[16,64,128]{2,1,0:T(8,128)(2,1)S(1)}, u32[]{:S(2)}, u32[]{:S(2)}) collective-permute-start(bf16[16,64,128]{2,1,0:T(8,128)(2,1)S(1)} %get-tuple-element.57.own.inner), channel_id=1, source_target_pairs={{0,16},{16,32},{32,48},{48,64},{64,80},{80,96},{96,112},{112,128},... | collective-permute-start | bytes 786440 | tf_op jit(solution)/shard_map/ppermute | solution.py:187
  31.9 13.4 %collective-permute-start.5 = (bf16[16,64,128]{2,1,0:T(8,128)(2,1)S(1)}, bf16[16,64,128]{2,1,0:T(8,128)(2,1)S(1)}, u32[]{:S(2)}, u32[]{:S(2)}) collective-permute-start(bf16[16,64,128]{2,1,0:T(8,128)(2,1)S(1)} %get-tuple-element.64.inner.own), channel_id=1, source_target_pairs={{0,16},{16,32},{32,48},{48,64},{64,80},{80,96},{96,112},{112,128},... | collective-permute-start | bytes 786440 | tf_op jit(solution)/shard_map/ppermute | solution.py:187
  42.4 8.8 %collective-permute-start.4 = (bf16[16,64,128]{2,1,0:T(8,128)(2,1)S(1)}, bf16[16,64,128]{2,1,0:T(8,128)(2,1)S(1)}, u32[]{:S(2)}, u32[]{:S(2)}) collective-permute-start(bf16[16,64,128]{2,1,0:T(8,128)(2,1)S(1)} %get-tuple-element.65.own.inner), channel_id=1, source_target_pairs={{16,0},{32,16},{48,32},{64,48},{80,64},{96,80},{112,96},{128,112},... | collective-permute-start | bytes 786440 | tf_op jit(solution)/shard_map/ppermute | solution.py:185
  46.1 10.0 %collective-permute-start.7 = (bf16[16,64,128]{2,1,0:T(8,128)(2,1)S(1)}, bf16[16,64,128]{2,1,0:T(8,128)(2,1)S(1)}, u32[]{:S(2)}, u32[]{:S(2)}) collective-permute-start(bf16[16,64,128]{2,1,0:T(8,128)(2,1)S(1)} %get-tuple-element.72.inner.own), channel_id=1, source_target_pairs={{16,0},{32,16},{48,32},{64,48},{80,64},{96,80},{112,96},{128,112},... | collective-permute-start | bytes 786440 | tf_op jit(solution)/shard_map/ppermute | solution.py:185
  52.0 11.2 %collective-permute-start.6 = (bf16[16,64,128]{2,1,0:T(8,128)(2,1)S(1)}, bf16[16,64,128]{2,1,0:T(8,128)(2,1)S(1)}, u32[]{:S(2)}, u32[]{:S(2)}) collective-permute-start(bf16[16,64,128]{2,1,0:T(8,128)(2,1)S(1)} %get-tuple-element.73.own.inner), channel_id=1, source_target_pairs={{0,16},{16,32},{32,48},{48,64},{64,80},{80,96},{96,112},{112,128},... | collective-permute-start | bytes 786440 | tf_op jit(solution)/shard_map/ppermute | solution.py:187
  57.0 12.9 %collective-permute-start.9 = (bf16[16,64,128]{2,1,0:T(8,128)(2,1)S(1)}, bf16[16,64,128]{2,1,0:T(8,128)(2,1)S(1)}, u32[]{:S(2)}, u32[]{:S(2)}) collective-permute-start(bf16[16,64,128]{2,1,0:T(8,128)(2,1)S(1)} %get-tuple-element.80.inner.own), channel_id=1, source_target_pairs={{0,16},{16,32},{32,48},{48,64},{64,80},{80,96},{96,112},{112,128},... | collective-permute-start | bytes 786440 | tf_op jit(solution)/shard_map/ppermute | solution.py:187
  64.0 10.8 %collective-permute-start.8 = (bf16[16,64,128]{2,1,0:T(8,128)(2,1)S(1)}, bf16[16,64,128]{2,1,0:T(8,128)(2,1)S(1)}, u32[]{:S(2)}, u32[]{:S(2)}) collective-permute-start(bf16[16,64,128]{2,1,0:T(8,128)(2,1)S(1)} %get-tuple-element.81.own.inner), channel_id=1, source_target_pairs={{16,0},{32,16},{48,32},{64,48},{80,64},{96,80},{112,96},{128,112},... | collective-permute-start | bytes 786440 | tf_op jit(solution)/shard_map/ppermute | solution.py:185
  70.7 9.1 %collective-permute-start.11 = (bf16[16,64,128]{2,1,0:T(8,128)(2,1)S(1)}, bf16[16,64,128]{2,1,0:T(8,128)(2,1)S(1)}, u32[]{:S(2)}, u32[]{:S(2)}) collective-permute-start(bf16[16,64,128]{2,1,0:T(8,128)(2,1)S(1)} %get-tuple-element.87.inner.own), channel_id=1, source_target_pairs={{16,0},{32,16},{48,32},{64,48},{80,64},{96,80},{112,96},{128,112},... | collective-permute-start | bytes 786440 | tf_op jit(solution)/shard_map/ppermute | solution.py:185
  75.6 11.2 %collective-permute-start.10 = (bf16[16,64,128]{2,1,0:T(8,128)(2,1)S(1)}, bf16[16,64,128]{2,1,0:T(8,128)(2,1)S(1)}, u32[]{:S(2)}, u32[]{:S(2)}) collective-permute-start(bf16[16,64,128]{2,1,0:T(8,128)(2,1)S(1)} %get-tuple-element.88.own.inner), channel_id=1, source_target_pairs={{0,16},{16,32},{32,48},{48,64},{64,80},{80,96},{96,112},{112,128},... | collective-permute-start | bytes 786440 | tf_op jit(solution)/shard_map/ppermute | solution.py:187
  82.2 16.5 %copy-start.1 = (bf16[1024,64]{0,1:T(8,128)(2,1)S(1)}, bf16[1024,64]{0,1:T(8,128)(2,1)}, u32[]{:S(2)}) copy-start(bf16[1024,64]{0,1:T(8,128)(2,1)} %param.5) | copy-start | bytes 393220
  98.6 20.1 %collective-permute-start.12 = (bf16[8,4,64,128]{3,2,1,0:T(8,128)(2,1)S(1)}, bf16[8,4,64,128]{3,2,1,0:T(8,128)(2,1)S(1)}, u32[]{:S(2)}, u32[]{:S(2)}) collective-permute-start(bf16[8,4,64,128]{3,2,1,0:T(8,128)(2,1)S(1)} %bitcast.12), channel_id=1, source_target_pairs={{0,1},{1,0},{2,3},{3,2},{4,5},{5,4},{6,7},{7,6},{8,9},{9,8},{10,11... | collective-permute-start | bytes 1572872 | tf_op jit(solution)/shard_map/ppermute | solution.py:239
  98.6 5.9 %collective-permute-start.13 = (bf16[64,1024]{1,0:T(8,128)(2,1)S(1)}, bf16[64,1024]{1,0:T(8,128)(2,1)S(1)}, u32[]{:S(2)}, u32[]{:S(2)}) collective-permute-start(bf16[64,1024]{1,0:T(8,128)(2,1)S(1)} %bitcast.16), channel_id=1, source_target_pairs={{0,2},{2,0},{1,3},{3,1},{4,6},{6,4},{5,7},{7,5},{8,10},{10,8},{9,1... | collective-permute-start | bytes 393224 | tf_op jit(solution)/shard_map/ppermute | solution.py:231
  104.6 8.6 %collective-permute-start.14 = (bf16[2,64,1024]{2,1,0:T(8,128)(2,1)S(1)}, bf16[2,64,1024]{2,1,0:T(8,128)(2,1)S(1)}, u32[]{:S(2)}, u32[]{:S(2)}) collective-permute-start(bf16[2,64,1024]{2,1,0:T(8,128)(2,1)S(1)} %pad_maximum_fusion.ritz), channel_id=1, source_target_pairs={{0,4},{4,8},{8,12},{12,0},{1,5},{5,9},{9,13},{13,1},{2,6},{6,10},{... | collective-permute-start | bytes 786440 | tf_op jit(solution)/shard_map/ppermute | solution.py:235
  105.9 9.3 %collective-permute-start.15 = (bf16[2,64,1024]{2,1,0:T(8,128)(2,1)S(1)}, bf16[2,64,1024]{2,1,0:T(8,128)(2,1)S(1)}, u32[]{:S(2)}, u32[]{:S(2)}) collective-permute-start(bf16[2,64,1024]{2,1,0:T(8,128)(2,1)S(1)} %pad_maximum_fusion.ritz), channel_id=1, source_target_pairs={{0,12},{4,0},{8,4},{12,8},{1,13},{5,1},{9,5},{13,9},{2,14},{6,2},{... | collective-permute-start | bytes 786440 | tf_op jit(solution)/shard_map/ppermute | solution.py:235
  106.7 12.1 %collective-permute-start.16 = (bf16[2,64,1024]{2,1,0:T(8,128)(2,1)S(1)}, bf16[2,64,1024]{2,1,0:T(8,128)(2,1)S(1)}, u32[]{:S(2)}, u32[]{:S(2)}) collective-permute-start(bf16[2,64,1024]{2,1,0:T(8,128)(2,1)S(1)} %pad_maximum_fusion.ritz), channel_id=1, source_target_pairs={{0,8},{4,12},{8,0},{12,4},{1,9},{5,13},{9,1},{13,5},{2,10},{6,14},... | collective-permute-start | bytes 786440 | tf_op jit(solution)/shard_map/ppermute | solution.py:235
  146.2 21.9 %all-to-all-start.2 = ((bf16[16,32,128]{2,1,0:T(8,128)(2,1)}), bf16[16,32,128]{2,1,0:T(8,128)(2,1)S(1)}, u32[]{:S(2)}, u32[]{:S(2)}) async-start(bf16[16,32,128]{2,1,0:T(8,128)(2,1)} %shard_map.75), calls=%async_computation.2 | async-start | bytes 262144 | tf_op jit(solution)/shard_map/all_to_all | solution.py:258

commit v2 on v1

--- a/solution.py
+++ b/solution.py
@@ -186,14 +186,19 @@
         else:
             halo["a", k] = lax.ppermute(val["b", k], ELEM, up)
 
+    shared = {}
+    source = jnp.swapaxes(ritz, 0, 1)
+    across = lax.ppermute(source, "yl", [(0, 1), (1, 0)])
     send("b", 0)
     send("a", 0)
+    shared["pair"] = jnp.stack([source, across])
+    for shift in (1, around - 1, 2):
+        shared[shift] = lax.ppermute(shared["pair"], "x", [(i, (i + shift) % around) for i in range(around)])
 
     order = []
     for k in range(1, DEG + 1):
         order += [("a", k), ("b", k)] if k % 2 else [("b", k), ("a", k)]
     token = None
-    shared = {"own": jnp.swapaxes(ritz, 0, 1)}
     for count, (name, k) in enumerate(order):
         other = "b" if name == "a" else "a"
         inside, outside = (2, 1) if name == "a" else (1, 2)
@@ -226,13 +231,6 @@
             full[name, k] = kept[0]
         if k < DEG:
             send(name, k)
-        if count == 1:
-            source, _ = lax.optimization_barrier((shared["own"], token))
-            shared["pair"] = jnp.stack([source, lax.ppermute(source, "yl", [(0, 1), (1, 0)])])
-        elif count in (4, 6, 8):
-            shift = {4: 1, 6: around - 1, 8: 2}[count]
-            source, _ = lax.optimization_barrier((shared["pair"], token))
-            shared[shift] = lax.ppermute(source, "x", [(i, (i + shift) % around) for i in range(around)])
 
     mine = lax.all_to_all(filtered, CHIP, 0, 0, tiled=True)
     mine = mine.reshape(chips, 2 * PLANE // chips, cols, NB)

time: 170 us -> 170 us (level)
  no operation moved by 1% of the time
where the time goes in v2:
time: 170 us; the launch traced here: 169 us
  starting transfers between devices  48.3 us (28%)
  waiting for transfers between devices  46.8 us (28%)
  blocking collectives  34.7 us (20%)
  Pallas kernels  32.7 us (19%)
  local copies, waits for them, and re-layouts  4.19 us (2%)
    pallas_call x27, Pallas kernels, call(): pl.pallas_call(kernel, out_shape=out_shape, in_specs=in_specs or [VMEM] *...  32.7 us
    ppermute x6, starting transfers between devices, send(): halo['b', k] = lax.ppermute(val['a', k], ELEM, down)  25.5 us
    all_to_all x1, blocking collectives, whole(): got = lax.all_to_all(sent, CHIP, 0, 0, tiled=True)  23.7 us
    ppermute x6, waiting for transfers between devices, send(): halo['a', k] = lax.ppermute(val['b', k], ELEM, up)  17.8 us
    all_to_all x1, blocking collectives, whole(): mine = lax.all_to_all(filtered, CHIP, 0, 0, tiled=True)  11 us
    all_to_all x1, starting transfers between devices, whole(): rows = lax.all_to_all(rows, ELEM, 0, 0, tiled=True)  10.7 us
    all_to_all x1, waiting for transfers between devices, whole(): rows = lax.all_to_all(rows, ELEM, 0, 0, tiled=True)  9.99 us
    ppermute x3, waiting for transfers between devices, whole(): lax.ppermute(shared['pair'], 'x', [(i, (i + shift) % around) for i in ran...  8.61 us
  transfers between devices with their start and end apart: 18, of which 13 were waited for; matrix products, arithmetic and copies ran while one was open for 1% of the time, Pallas kernels for 16%

profile of v2, /device:TPU:4, one launch (start us, length us, event | category | flops | bytes accessed | tf_op | source)
XLA Modules:
  0.0 168.8 jit_solution(16791324210133493072)
XLA Ops:
  1.7 3.3 %collective-permute-start.1 = (bf16[16,64,128]{2,1,0:T(8,128)(2,1)S(1)}, bf16[16,64,128]{2,1,0:T(8,128)(2,1)S(1)}, u32[]{:S(2)}, u32[]{:S(2)}) collective-permute-start(bf16[16,64,128]{2,1,0:T(8,128)(2,1)S(1)} %get-tuple-element.45.inner.own.current.rest_0_), channel_id=1, source_target_pairs={{0,16},{16,32},{32,48},{48,64},{64,80},{80,96},{96,112},{112,128},... | collective-permute-start | bytes 786440 | tf_op jit(solution)/shard_map/ppermute | solution.py:187
  5.0 5.4 %collective-permute-start = (bf16[16,64,128]{2,1,0:T(8,128)(2,1)S(1)}, bf16[16,64,128]{2,1,0:T(8,128)(2,1)S(1)}, u32[]{:S(2)}, u32[]{:S(2)}) collective-permute-start(bf16[16,64,128]{2,1,0:T(8,128)(2,1)S(1)} %get-tuple-element.46.own.current.inner.rest_0_), channel_id=1, source_target_pairs={{16,0},{32,16},{48,32},{64,48},{80,64},{96,80},{112,96},{128,112},... | collective-permute-start | bytes 786440 | tf_op jit(solution)/shard_map/ppermute | solution.py:185
  10.4 3.1 %copy-done = bf16[32,7,128,128]{3,2,1,0:T(8,128)(2,1)S(1)} copy-done((bf16[32,7,128,128]{3,2,1,0:T(8,128)(2,1)S(1)}, bf16[32,7,128,128]{3,2,1,0:T(8,128)(2,1)}, u32[]{:S(2)}) %copy-start) | copy-done | bytes 7340056
  13.4 1.6 shard_map.50.partial
  15.0 1.7 collective-permute-done.1.halo
  17.5 8.8 %collective-permute-start.3 = (bf16[16,64,128]{2,1,0:T(8,128)(2,1)S(1)}, bf16[16,64,128]{2,1,0:T(8,128)(2,1)S(1)}, u32[]{:S(2)}, u32[]{:S(2)}) collective-permute-start(bf16[16,64,128]{2,1,0:T(8,128)(2,1)S(1)} %get-tuple-element.52.inner.own), channel_id=1, source_target_pairs={{16,0},{32,16},{48,32},{64,48},{80,64},{96,80},{112,96},{128,112},... | collective-permute-start | bytes 786440 | tf_op jit(solution)/shard_map/ppermute | solution.py:185
  26.3 1.6 shard_map.52.partial
  33.5 8.1 %collective-permute-done.2.halo = bf16[16,64,128]{2,1,0:T(8,128)(2,1)S(1)} collective-permute-done((bf16[16,64,128]{2,1,0:T(8,128)(2,1)S(1)}, bf16[16,64,128]{2,1,0:T(8,128)(2,1)S(1)}, u32[]{:S(2)}, u32[]{:S(2)}) %collective-permute-start.2) | collective-permute-done | bytes 262176 | tf_op jit(solution)/shard_map/ppermute | solution.py:187
  46.1 3.1 %collective-permute-start.7 = (bf16[16,64,128]{2,1,0:T(8,128)(2,1)S(1)}, bf16[16,64,128]{2,1,0:T(8,128)(2,1)S(1)}, u32[]{:S(2)}, u32[]{:S(2)}) collective-permute-start(bf16[16,64,128]{2,1,0:T(8,128)(2,1)S(1)} %get-tuple-element.68.inner.own), channel_id=1, source_target_pairs={{16,0},{32,16},{48,32},{64,48},{80,64},{96,80},{112,96},{128,112},... | collective-permute-start | bytes 786440 | tf_op jit(solution)/shard_map/ppermute | solution.py:185
  53.8 2.4 %collective-permute-done.7.halo = bf16[16,64,128]{2,1,0:T(8,128)(2,1)S(1)} collective-permute-done((bf16[16,64,128]{2,1,0:T(8,128)(2,1)S(1)}, bf16[16,64,128]{2,1,0:T(8,128)(2,1)S(1)}, u32[]{:S(2)}, u32[]{:S(2)}) %collective-permute-start.7) | collective-permute-done | bytes 262176 | tf_op jit(solution)/shard_map/ppermute | solution.py:185
  59.8 3.4 %collective-permute-done.6.halo = bf16[16,64,128]{2,1,0:T(8,128)(2,1)S(1)} collective-permute-done((bf16[16,64,128]{2,1,0:T(8,128)(2,1)S(1)}, bf16[16,64,128]{2,1,0:T(8,128)(2,1)S(1)}, u32[]{:S(2)}, u32[]{:S(2)}) %collective-permute-start.6) | collective-permute-done | bytes 262176 | tf_op jit(solution)/shard_map/ppermute | solution.py:187
  64.0 4.2 %collective-permute-start.8 = (bf16[16,64,128]{2,1,0:T(8,128)(2,1)S(1)}, bf16[16,64,128]{2,1,0:T(8,128)(2,1)S(1)}, u32[]{:S(2)}, u32[]{:S(2)}) collective-permute-start(bf16[16,64,128]{2,1,0:T(8,128)(2,1)S(1)} %get-tuple-element.77.own.inner), channel_id=1, source_target_pairs={{16,0},{32,16},{48,32},{64,48},{80,64},{96,80},{112,96},{128,112},... | collective-permute-start | bytes 786440 | tf_op jit(solution)/shard_map/ppermute | solution.py:185
  70.7 2.6 %collective-permute-start.11 = (bf16[16,64,128]{2,1,0:T(8,128)(2,1)S(1)}, bf16[16,64,128]{2,1,0:T(8,128)(2,1)S(1)}, u32[]{:S(2)}, u32[]{:S(2)}) collective-permute-start(bf16[16,64,128]{2,1,0:T(8,128)(2,1)S(1)} %get-tuple-element.83.inner.own), channel_id=1, source_target_pairs={{16,0},{32,16},{48,32},{64,48},{80,64},{96,80},{112,96},{128,112},... | collective-permute-start | bytes 786440 | tf_op jit(solution)/shard_map/ppermute | solution.py:185
  82.2 4.7 %collective-permute-done.10.halo = bf16[16,64,128]{2,1,0:T(8,128)(2,1)S(1)} collective-permute-done((bf16[16,64,128]{2,1,0:T(8,128)(2,1)S(1)}, bf16[16,64,128]{2,1,0:T(8,128)(2,1)S(1)}, u32[]{:S(2)}, u32[]{:S(2)}) %collective-permute-start.10) | collective-permute-done | bytes 262176 | tf_op jit(solution)/shard_map/ppermute | solution.py:187
  87.6 11.0 %all_to_all.15 = bf16[32,64,128]{2,1,0:T(8,128)(2,1)S(1)} all-to-all(bf16[32,64,128]{2,1,0:T(8,128)(2,1)S(1)} %shard_map.73), channel_id=1, replica_groups=mesh['z'=8,'yh'=2,'x'=4,'yl'=2,'c'=2] {'x','yl'}, dimensions={0} | all-to-all | bytes 1048576 | tf_op jit(solution)/shard_map/all_to_all | solution.py:235
  98.9 5.6 %collective-permute-done.13 = bf16[64,1024]{1,0:T(8,128)(2,1)S(1)} collective-permute-done((bf16[64,1024]{1,0:T(8,128)(2,1)S(1)}, bf16[64,1024]{1,0:T(8,128)(2,1)S(1)}, u32[]{:S(2)}, u32[]{:S(2)}) %collective-permute-start.13) | collective-permute-done | bytes 131104 | tf_op jit(solution)/shard_map/ppermute | solution.py:191
  106.7 3.4 %collective-permute-start.16 = (bf16[2,64,1024]{2,1,0:T(8,128)(2,1)S(1)}, bf16[2,64,1024]{2,1,0:T(8,128)(2,1)S(1)}, u32[]{:S(2)}, u32[]{:S(2)}) collective-permute-start(bf16[2,64,1024]{2,1,0:T(8,128)(2,1)S(1)} %pad_maximum_fusion.ritz), channel_id=1, source_target_pairs={{0,8},{4,12},{8,0},{12,4},{1,9},{5,13},{9,1},{13,5},{2,10},{6,14},... | collective-permute-start | bytes 786440 | tf_op jit(solution)/shard_map/ppermute | solution.py:196
  110.2 3.0 %collective-permute-done.14.ritz_back = bf16[2,64,1024]{2,1,0:T(8,128)(2,1)S(1)} collective-permute-done((bf16[2,64,1024]{2,1,0:T(8,128)(2,1)S(1)}, bf16[2,64,1024]{2,1,0:T(8,128)(2,1)S(1)}, u32[]{:S(2)}, u32[]{:S(2)}) %collective-permute-start.14) | collective-permute-done | bytes 262176 | tf_op jit(solution)/shard_map/ppermute | solution.py:196
  113.2 2.0 %collective-permute-done.15.ritz_next = bf16[2,64,1024]{2,1,0:T(8,128)(2,1)S(1)} collective-permute-done((bf16[2,64,1024]{2,1,0:T(8,128)(2,1)S(1)}, bf16[2,64,1024]{2,1,0:T(8,128)(2,1)S(1)}, u32[]{:S(2)}, u32[]{:S(2)}) %collective-permute-start.15) | collective-permute-done | bytes 262176 | tf_op jit(solution)/shard_map/ppermute | solution.py:196
  115.2 3.6 %collective-permute-done.16.ritz_far = bf16[2,64,1024]{2,1,0:T(8,128)(2,1)S(1)} collective-permute-done((bf16[2,64,1024]{2,1,0:T(8,128)(2,1)S(1)}, bf16[2,64,1024]{2,1,0:T(8,128)(2,1)S(1)}, u32[]{:S(2)}, u32[]{:S(2)}) %collective-permute-start.16) | collective-permute-done | bytes 262176 | tf_op jit(solution)/shard_map/ppermute | solution.py:196
  118.8 2.9 %shard_map.74 = bf16[8,768,128]{2,1,0:T(8,128)(2,1)S(1)} custom-call(s32[3]{0:T(128)S(1)} %pad_add_fusion.place, bf16[8,4,64,128]{3,2,1,0:T(8,128)(2,1)S(1)} %bitcast.14, bf16[8,4,64,128]{3,2,1,0:T(8,128)(2,1)S(1)} %collective-permute-done.12.other, bf16[2,64,1024]{2,1,0:T(8,128)(2,1)S(1)} %pad_maximum_fusion.ritz, ...), custom_call_target="tpu_custom_call" | custom-call | flops 1073741824 | bytes 4194304 | tf_op jit(solution)/shard_map/pallas_call | solution.py:97
  121.6 23.7 %all_to_all.16.got = bf16[8,768,128]{2,1,0:T(8,128)(2,1)S(1)} all-to-all(bf16[8,768,128]{2,1,0:T(8,128)(2,1)S(1)} %shard_map.74), channel_id=1, replica_groups=mesh['z'=8,'yh'=2,'x'=4,'yl'=2,'c'=2] {'x','yl'}, dimensions={0} | all-to-all | bytes 3145728 | tf_op jit(solution)/shard_map/all_to_all | solution.py:250
  146.2 10.7 %all-to-all-start.2 = ((bf16[16,32,128]{2,1,0:T(8,128)(2,1)}), bf16[16,32,128]{2,1,0:T(8,128)(2,1)S(1)}, u32[]{:S(2)}, u32[]{:S(2)}) async-start(bf16[16,32,128]{2,1,0:T(8,128)(2,1)} %shard_map.75), calls=%async_computation.2 | async-start | bytes 262144 | tf_op jit(solution)/shard_map/all_to_all | solution.py:256
  158.1 10.0 %all-to-all-done.2.got = bf16[16,32,128]{2,1,0:T(8,128)(2,1)S(1)} async-done(((bf16[16,32,128]{2,1,0:T(8,128)(2,1)}), bf16[16,32,128]{2,1,0:T(8,128)(2,1)S(1)}, u32[]{:S(2)}, u32[]{:S(2)}) %all-to-all-start.2) | async-done | bytes 131104 | tf_op jit(solution)/shard_map/all_to_all | solution.py:256
  (50 shorter events, 38.1 us)
Async XLA Ops:
  1.7 15.0 %collective-permute-start.1 = (bf16[16,64,128]{2,1,0:T(8,128)(2,1)S(1)}, bf16[16,64,128]{2,1,0:T(8,128)(2,1)S(1)}, u32[]{:S(2)}, u32[]{:S(2)}) collective-permute-start(bf16[16,64,128]{2,1,0:T(8,128)(2,1)S(1)} %get-tuple-element.45.inner.own.current.rest_0_), channel_id=1, source_target_pairs={{0,16},{16,32},{32,48},{48,64},{64,80},{80,96},{96,112},{112,128},... | collective-permute-start | bytes 786440 | tf_op jit(solution)/shard_map/ppermute | solution.py:187
  5.0 22.9 %collective-permute-start = (bf16[16,64,128]{2,1,0:T(8,128)(2,1)S(1)}, bf16[16,64,128]{2,1,0:T(8,128)(2,1)S(1)}, u32[]{:S(2)}, u32[]{:S(2)}) collective-permute-start(bf16[16,64,128]{2,1,0:T(8,128)(2,1)S(1)} %get-tuple-element.46.own.current.inner.rest_0_), channel_id=1, source_target_pairs={{16,0},{32,16},{48,32},{64,48},{80,64},{96,80},{112,96},{128,112},... | collective-permute-start | bytes 786440 | tf_op jit(solution)/shard_map/ppermute | solution.py:185
  10.4 3.1 %copy-start = (bf16[32,7,128,128]{3,2,1,0:T(8,128)(2,1)S(1)}, bf16[32,7,128,128]{3,2,1,0:T(8,128)(2,1)}, u32[]{:S(2)}) copy-start(bf16[32,7,128,128]{3,2,1,0:T(8,128)(2,1)} %ham.47) | copy-start | bytes 22020100
  17.5 13.6 %collective-permute-start.3 = (bf16[16,64,128]{2,1,0:T(8,128)(2,1)S(1)}, bf16[16,64,128]{2,1,0:T(8,128)(2,1)S(1)}, u32[]{:S(2)}, u32[]{:S(2)}) collective-permute-start(bf16[16,64,128]{2,1,0:T(8,128)(2,1)S(1)} %get-tuple-element.52.inner.own), channel_id=1, source_target_pairs={{16,0},{32,16},{48,32},{64,48},{80,64},{96,80},{112,96},{128,112},... | collective-permute-start | bytes 786440 | tf_op jit(solution)/shard_map/ppermute | solution.py:185
  28.7 12.9 %collective-permute-start.2 = (bf16[16,64,128]{2,1,0:T(8,128)(2,1)S(1)}, bf16[16,64,128]{2,1,0:T(8,128)(2,1)S(1)}, u32[]{:S(2)}, u32[]{:S(2)}) collective-permute-start(bf16[16,64,128]{2,1,0:T(8,128)(2,1)S(1)} %get-tuple-element.53.own.inner), channel_id=1, source_target_pairs={{0,16},{16,32},{32,48},{48,64},{64,80},{80,96},{96,112},{112,128},... | collective-permute-start | bytes 786440 | tf_op jit(solution)/shard_map/ppermute | solution.py:187
  31.9 13.4 %collective-permute-start.5 = (bf16[16,64,128]{2,1,0:T(8,128)(2,1)S(1)}, bf16[16,64,128]{2,1,0:T(8,128)(2,1)S(1)}, u32[]{:S(2)}, u32[]{:S(2)}) collective-permute-start(bf16[16,64,128]{2,1,0:T(8,128)(2,1)S(1)} %get-tuple-element.60.inner.own), channel_id=1, source_target_pairs={{0,16},{16,32},{32,48},{48,64},{64,80},{80,96},{96,112},{112,128},... | collective-permute-start | bytes 786440 | tf_op jit(solution)/shard_map/ppermute | solution.py:187
  42.4 8.8 %collective-permute-start.4 = (bf16[16,64,128]{2,1,0:T(8,128)(2,1)S(1)}, bf16[16,64,128]{2,1,0:T(8,128)(2,1)S(1)}, u32[]{:S(2)}, u32[]{:S(2)}) collective-permute-start(bf16[16,64,128]{2,1,0:T(8,128)(2,1)S(1)} %get-tuple-element.61.own.inner), channel_id=1, source_target_pairs={{16,0},{32,16},{48,32},{64,48},{80,64},{96,80},{112,96},{128,112},... | collective-permute-start | bytes 786440 | tf_op jit(solution)/shard_map/ppermute | solution.py:185
  46.1 10.0 %collective-permute-start.7 = (bf16[16,64,128]{2,1,0:T(8,128)(2,1)S(1)}, bf16[16,64,128]{2,1,0:T(8,128)(2,1)S(1)}, u32[]{:S(2)}, u32[]{:S(2)}) collective-permute-start(bf16[16,64,128]{2,1,0:T(8,128)(2,1)S(1)} %get-tuple-element.68.inner.own), channel_id=1, source_target_pairs={{16,0},{32,16},{48,32},{64,48},{80,64},{96,80},{112,96},{128,112},... | collective-permute-start | bytes 786440 | tf_op jit(solution)/shard_map/ppermute | solution.py:185
  52.0 11.2 %collective-permute-start.6 = (bf16[16,64,128]{2,1,0:T(8,128)(2,1)S(1)}, bf16[16,64,128]{2,1,0:T(8,128)(2,1)S(1)}, u32[]{:S(2)}, u32[]{:S(2)}) collective-permute-start(bf16[16,64,128]{2,1,0:T(8,128)(2,1)S(1)} %get-tuple-element.69.own.inner), channel_id=1, source_target_pairs={{0,16},{16,32},{32,48},{48,64},{64,80},{80,96},{96,112},{112,128},... | collective-permute-start | bytes 786440 | tf_op jit(solution)/shard_map/ppermute | solution.py:187
  57.0 12.9 %collective-permute-start.9 = (bf16[16,64,128]{2,1,0:T(8,128)(2,1)S(1)}, bf16[16,64,128]{2,1,0:T(8,128)(2,1)S(1)}, u32[]{:S(2)}, u32[]{:S(2)}) collective-permute-start(bf16[16,64,128]{2,1,0:T(8,128)(2,1)S(1)} %get-tuple-element.76.inner.own), channel_id=1, source_target_pairs={{0,16},{16,32},{32,48},{48,64},{64,80},{80,96},{96,112},{112,128},... | collective-permute-start | bytes 786440 | tf_op jit(solution)/shard_map/ppermute | solution.py:187
  64.0 10.8 %collective-permute-start.8 = (bf16[16,64,128]{2,1,0:T(8,128)(2,1)S(1)}, bf16[16,64,128]{2,1,0:T(8,128)(2,1)S(1)}, u32[]{:S(2)}, u32[]{:S(2)}) collective-permute-start(bf16[16,64,128]{2,1,0:T(8,128)(2,1)S(1)} %get-tuple-element.77.own.inner), channel_id=1, source_target_pairs={{16,0},{32,16},{48,32},{64,48},{80,64},{96,80},{112,96},{128,112},... | collective-permute-start | bytes 786440 | tf_op jit(solution)/shard_map/ppermute | solution.py:185
  70.7 9.1 %collective-permute-start.11 = (bf16[16,64,128]{2,1,0:T(8,128)(2,1)S(1)}, bf16[16,64,128]{2,1,0:T(8,128)(2,1)S(1)}, u32[]{:S(2)}, u32[]{:S(2)}) collective-permute-start(bf16[16,64,128]{2,1,0:T(8,128)(2,1)S(1)} %get-tuple-element.83.inner.own), channel_id=1, source_target_pairs={{16,0},{32,16},{48,32},{64,48},{80,64},{96,80},{112,96},{128,112},... | collective-permute-start | bytes 786440 | tf_op jit(solution)/shard_map/ppermute | solution.py:185
  75.6 11.2 %collective-permute-start.10 = (bf16[16,64,128]{2,1,0:T(8,128)(2,1)S(1)}, bf16[16,64,128]{2,1,0:T(8,128)(2,1)S(1)}, u32[]{:S(2)}, u32[]{:S(2)}) collective-permute-start(bf16[16,64,128]{2,1,0:T(8,128)(2,1)S(1)} %get-tuple-element.84.own.inner), channel_id=1, source_target_pairs={{0,16},{16,32},{32,48},{48,64},{64,80},{80,96},{96,112},{112,128},... | collective-permute-start | bytes 786440 | tf_op jit(solution)/shard_map/ppermute | solution.py:187
  82.2 16.5 %copy-start.1 = (bf16[1024,64]{0,1:T(8,128)(2,1)S(1)}, bf16[1024,64]{0,1:T(8,128)(2,1)}, u32[]{:S(2)}) copy-start(bf16[1024,64]{0,1:T(8,128)(2,1)} %param.5) | copy-start | bytes 393220
  98.6 20.1 %collective-permute-start.12 = (bf16[8,4,64,128]{3,2,1,0:T(8,128)(2,1)S(1)}, bf16[8,4,64,128]{3,2,1,0:T(8,128)(2,1)S(1)}, u32[]{:S(2)}, u32[]{:S(2)}) collective-permute-start(bf16[8,4,64,128]{3,2,1,0:T(8,128)(2,1)S(1)} %bitcast.13), channel_id=1, source_target_pairs={{0,1},{1,0},{2,3},{3,2},{4,5},{5,4},{6,7},{7,6},{8,9},{9,8},{10,11... | collective-permute-start | bytes 1572872 | tf_op jit(solution)/shard_map/ppermute | solution.py:237
  98.6 5.9 %collective-permute-start.13 = (bf16[64,1024]{1,0:T(8,128)(2,1)S(1)}, bf16[64,1024]{1,0:T(8,128)(2,1)S(1)}, u32[]{:S(2)}, u32[]{:S(2)}) collective-permute-start(bf16[64,1024]{1,0:T(8,128)(2,1)S(1)} %bitcast.17), channel_id=1, source_target_pairs={{0,2},{2,0},{1,3},{3,1},{4,6},{6,4},{5,7},{7,5},{8,10},{10,8},{9,1... | collective-permute-start | bytes 393224 | tf_op jit(solution)/shard_map/ppermute | solution.py:191
  104.6 8.6 %collective-permute-start.14 = (bf16[2,64,1024]{2,1,0:T(8,128)(2,1)S(1)}, bf16[2,64,1024]{2,1,0:T(8,128)(2,1)S(1)}, u32[]{:S(2)}, u32[]{:S(2)}) collective-permute-start(bf16[2,64,1024]{2,1,0:T(8,128)(2,1)S(1)} %pad_maximum_fusion.ritz), channel_id=1, source_target_pairs={{0,4},{4,8},{8,12},{12,0},{1,5},{5,9},{9,13},{13,1},{2,6},{6,10},{... | collective-permute-start | bytes 786440 | tf_op jit(solution)/shard_map/ppermute | solution.py:196
  105.9 9.3 %collective-permute-start.15 = (bf16[2,64,1024]{2,1,0:T(8,128)(2,1)S(1)}, bf16[2,64,1024]{2,1,0:T(8,128)(2,1)S(1)}, u32[]{:S(2)}, u32[]{:S(2)}) collective-permute-start(bf16[2,64,1024]{2,1,0:T(8,128)(2,1)S(1)} %pad_maximum_fusion.ritz), channel_id=1, source_target_pairs={{0,12},{4,0},{8,4},{12,8},{1,13},{5,1},{9,5},{13,9},{2,14},{6,2},{... | collective-permute-start | bytes 786440 | tf_op jit(solution)/shard_map/ppermute | solution.py:196
  106.7 12.1 %collective-permute-start.16 = (bf16[2,64,1024]{2,1,0:T(8,128)(2,1)S(1)}, bf16[2,64,1024]{2,1,0:T(8,128)(2,1)S(1)}, u32[]{:S(2)}, u32[]{:S(2)}) collective-permute-start(bf16[2,64,1024]{2,1,0:T(8,128)(2,1)S(1)} %pad_maximum_fusion.ritz), channel_id=1, source_target_pairs={{0,8},{4,12},{8,0},{12,4},{1,9},{5,13},{9,1},{13,5},{2,10},{6,14},... | collective-permute-start | bytes 786440 | tf_op jit(solution)/shard_map/ppermute | solution.py:196
  146.2 21.9 %all-to-all-start.2 = ((bf16[16,32,128]{2,1,0:T(8,128)(2,1)}), bf16[16,32,128]{2,1,0:T(8,128)(2,1)S(1)}, u32[]{:S(2)}, u32[]{:S(2)}) async-start(bf16[16,32,128]{2,1,0:T(8,128)(2,1)} %shard_map.75), calls=%async_computation.2 | async-start | bytes 262144 | tf_op jit(solution)/shard_map/all_to_all | solution.py:256

commit v3 on v2

--- a/solution.py
+++ b/solution.py
@@ -105,7 +105,7 @@
     )(*operands)
 
 
-def message_kernel(chips, place, mine, other, ritz, ritz_back, ritz_next, ritz_far, out, rows, own):
+def part_kernel(chips, place, mine, other, out, rows, own):
     held, cols = mine.shape[1], mine.shape[2]
 
     def fill(parity, source):
@@ -127,20 +127,30 @@
         fill(1, mine)
         fill(0, other)
 
-    base = chips * cols
     for s in range(0, chips, 2):
         part = product(own[pl.ds(s * cols, 2 * cols), :], rows[...], ROWS).astype(jnp.bfloat16)
         for q in range(2):
             for t in range(chips):
                 out[s + q, pl.ds(t * cols, cols), :] = part[q * cols : (q + 1) * cols, t * NB : (t + 1) * NB]
-    around = chips // 2
-    for away, source in ((0, ritz), (around - 1, ritz_back), (1, ritz_next), (2, ritz_far)):
+
+
+def turn_kernel(rows, ritz, ritz_next, ritz_far, ritz_back, *outs):
+    held, cols = outs[0].shape[0], outs[0].shape[1]
+    for away, source in enumerate((ritz, ritz_next, ritz_far, ritz_back)):
         turned = product(source[...].reshape(2 * cols, -1), rows[...], PLAIN).astype(jnp.bfloat16)
         for q in range(2):
-            to = lax.rem(place[0] + away, around) * 2 + (place[1] if q == 0 else 1 - place[1])
             for el in range(held):
-                piece = turned[q * cols : (q + 1) * cols, el * NB : (el + 1) * NB]
-                out[to, pl.ds(base + el * cols, cols), :] = piece
+                outs[2 * away + q][el] = turned[q * cols : (q + 1) * cols, el * NB : (el + 1) * NB]
+
+
+def collect_kernel(around, place, *refs):
+    pieces, out = refs[:-1], refs[-1]
+    held = pieces[0].shape[0]
+    for index, piece in enumerate(pieces):
+        away, q = index // 2, index % 2
+        line = lax.rem(place[0] + around - away, around) * 2 + (place[1] if q == 0 else 1 - place[1])
+        for el in range(held):
+            out[line * held + el] = piece[el].astype(jnp.float32)
 
 
 def margin_rows_kernel(chips, got, out):
@@ -238,28 +248,40 @@
     place = jnp.stack([lax.axis_index("x"), lax.axis_index("yl"), lax.axis_index("c")]).astype(jnp.int32)
     held = mine.shape[1]
     depth = held * NB
-    sent = call(
-        functools.partial(message_kernel, chips),
-        (place, mine, theirs, shared["pair"], shared[1], shared[around - 1], shared[2]),
-        jax.ShapeDtypeStruct((chips, (chips + held) * cols, NB), jnp.bfloat16),
-        pl.CostEstimate(flops=8 * (chips * cols) ** 2 * depth, bytes_accessed=4 << 20, transcendentals=0),
-        24,
-        (pltpu.VMEM((2 * chips * cols, depth), jnp.bfloat16), pltpu.VMEM((chips * cols, depth), jnp.bfloat16)),
-        [SMEM] + [VMEM] * 6,
+    small = pl.CostEstimate(flops=1 << 20, bytes_accessed=1 << 20, transcendentals=0)
+    flops = pl.CostEstimate(flops=4 * (chips * cols) ** 2 * depth, bytes_accessed=2 << 20, transcendentals=0)
+    sent, rows = call(
+        functools.partial(part_kernel, chips), (place, mine, theirs),
+        (
+            jax.ShapeDtypeStruct((chips, chips * cols, NB), jnp.bfloat16),
+            jax.ShapeDtypeStruct((2 * chips * cols, depth), jnp.bfloat16),
+        ),
+        flops, 16, (pltpu.VMEM((chips * cols, depth), jnp.bfloat16),), [SMEM, VMEM, VMEM],
     )
     got = lax.all_to_all(sent, CHIP, 0, 0, tiled=True)
-    small = pl.CostEstimate(flops=1 << 20, bytes_accessed=1 << 20, transcendentals=0)
-    rows = call(
+    turned = call(
+        turn_kernel, (rows, shared["pair"], shared[around - 1], shared[2], shared[1]),
+        (jax.ShapeDtypeStruct((held, cols, NB), jnp.bfloat16),) * chips, flops, 16,
+    )
+    pieces = [turned[0]]
+    for index in range(1, chips):
+        away, q = index // 2, index % 2
+        to = [(i, (i // 2 + away) % around * 2 + (i + q) % 2) for i in range(chips)]
+        pieces.append(lax.ppermute(turned[index], CHIP, to))
+    total = call(
         functools.partial(margin_rows_kernel, chips), (got,),
         jax.ShapeDtypeStruct((slabs, cols // 2, 2 * cols), jnp.bfloat16), small, 12,
     )
-    rows = lax.all_to_all(rows, ELEM, 0, 0, tiled=True)
+    total = lax.all_to_all(total, ELEM, 0, 0, tiled=True)
+    rotated = call(
+        functools.partial(collect_kernel, around), (place, *pieces),
+        jax.ShapeDtypeStruct((2 * PLANE, cols, NB), jnp.float32), small, 12, (), [SMEM] + [VMEM] * chips,
+    )
     margin = call(
-        functools.partial(margin_kernel, 1.0 / rows_total), (rows,),
+        functools.partial(margin_kernel, 1.0 / rows_total), (total,),
         jax.ShapeDtypeStruct((cols, cols), jnp.float32), small, 12,
     )
-    turned = got[:, chips * cols :].reshape(2 * PLANE, cols, NB).astype(jnp.float32)
-    return margin, jnp.swapaxes(turned, 1, 2)
+    return margin, jnp.swapaxes(rotated, 1, 2)
 
 
 def solution(mesh):

time: 170 us -> 163 us (0.959)
  the two profiles are of different devices: /device:TPU:4 before, /device:TPU:134 now
where the time goes in v3:
time: 163 us
  waiting for transfers between devices  57 us (35%)
  starting transfers between devices  54.3 us (33%)
  Pallas kernels  35.4 us (22%)
  blocking collectives  10.8 us (7%)
  local copies, waits for them, and re-layouts  4.15 us (3%)
    pallas_call x29, Pallas kernels, call(): pl.pallas_call(kernel, out_shape=out_shape, in_specs=in_specs or [VMEM] *...  35.4 us
    ppermute x6, waiting for transfers between devices, send(): halo['b', k] = lax.ppermute(val['a', k], ELEM, down)  16.8 us
    ppermute x1, waiting for transfers between devices, whole(): across = lax.ppermute(source, 'yl', [(0, 1), (1, 0)])  14.9 us
    ppermute x6, waiting for transfers between devices, send(): halo['a', k] = lax.ppermute(val['b', k], ELEM, up)  14.8 us
    ppermute x6, starting transfers between devices, send(): halo['a', k] = lax.ppermute(val['b', k], ELEM, up)  14 us
    ppermute x6, starting transfers between devices, send(): halo['b', k] = lax.ppermute(val['a', k], ELEM, down)  11.1 us
    all_to_all x1, blocking collectives, whole(): mine = lax.all_to_all(filtered, CHIP, 0, 0, tiled=True)  10.8 us
    ppermute x7, starting transfers between devices, whole(): pieces.append(lax.ppermute(turned[index], CHIP, to))  10.7 us
  transfers between devices with their start and end apart: 26, of which 16 were waited for; matrix products, arithmetic and copies ran while one was open for 0% of the time, Pallas kernels for 19%

profile of v3, /device:TPU:134, one launch (start us, length us, event | category | flops | bytes accessed | tf_op | source)
XLA Modules:
  0.0 162.6 jit_solution(15345026631601226928)
XLA Ops:
  1.7 3.3 %collective-permute-start.1 = (bf16[16,64,128]{2,1,0:T(8,128)(2,1)S(1)}, bf16[16,64,128]{2,1,0:T(8,128)(2,1)S(1)}, u32[]{:S(2)}, u32[]{:S(2)}) collective-permute-start(bf16[16,64,128]{2,1,0:T(8,128)(2,1)S(1)} %get-tuple-element.55.inner.own.current.rest_0_), channel_id=1, source_target_pairs={{0,16},{16,32},{32,48},{48,64},{64,80},{80,96},{96,112},{112,128},... | collective-permute-start | bytes 786440 | tf_op jit(solution)/shard_map/ppermute | solution.py:197
  5.0 2.4 %collective-permute-start = (bf16[16,64,128]{2,1,0:T(8,128)(2,1)S(1)}, bf16[16,64,128]{2,1,0:T(8,128)(2,1)S(1)}, u32[]{:S(2)}, u32[]{:S(2)}) collective-permute-start(bf16[16,64,128]{2,1,0:T(8,128)(2,1)S(1)} %get-tuple-element.56.own.current.inner.rest_0_), channel_id=1, source_target_pairs={{16,0},{32,16},{48,32},{64,48},{80,64},{96,80},{112,96},{128,112},... | collective-permute-start | bytes 786440 | tf_op jit(solution)/shard_map/ppermute | solution.py:195
  7.4 3.1 %copy-done = bf16[32,7,128,128]{3,2,1,0:T(8,128)(2,1)S(1)} copy-done((bf16[32,7,128,128]{3,2,1,0:T(8,128)(2,1)S(1)}, bf16[32,7,128,128]{3,2,1,0:T(8,128)(2,1)}, u32[]{:S(2)}) %copy-start) | copy-done | bytes 7340056
  12.0 4.1 %collective-permute-done.1.halo = bf16[16,64,128]{2,1,0:T(8,128)(2,1)S(1)} collective-permute-done((bf16[16,64,128]{2,1,0:T(8,128)(2,1)S(1)}, bf16[16,64,128]{2,1,0:T(8,128)(2,1)S(1)}, u32[]{:S(2)}, u32[]{:S(2)}) %collective-permute-start.1) | collective-permute-done | bytes 262176 | tf_op jit(solution)/shard_map/ppermute | solution.py:197
  17.0 3.6 %collective-permute-start.3 = (bf16[16,64,128]{2,1,0:T(8,128)(2,1)S(1)}, bf16[16,64,128]{2,1,0:T(8,128)(2,1)S(1)}, u32[]{:S(2)}, u32[]{:S(2)}) collective-permute-start(bf16[16,64,128]{2,1,0:T(8,128)(2,1)S(1)} %get-tuple-element.62.inner.own), channel_id=1, source_target_pairs={{16,0},{32,16},{48,32},{64,48},{80,64},{96,80},{112,96},{128,112},... | collective-permute-start | bytes 786440 | tf_op jit(solution)/shard_map/ppermute | solution.py:195
  25.1 4.2 %collective-permute-done.3.halo = bf16[16,64,128]{2,1,0:T(8,128)(2,1)S(1)} collective-permute-done((bf16[16,64,128]{2,1,0:T(8,128)(2,1)S(1)}, bf16[16,64,128]{2,1,0:T(8,128)(2,1)S(1)}, u32[]{:S(2)}, u32[]{:S(2)}) %collective-permute-start.3) | collective-permute-done | bytes 262176 | tf_op jit(solution)/shard_map/ppermute | solution.py:195
  34.9 3.4 %collective-permute-start.4 = (bf16[16,64,128]{2,1,0:T(8,128)(2,1)S(1)}, bf16[16,64,128]{2,1,0:T(8,128)(2,1)S(1)}, u32[]{:S(2)}, u32[]{:S(2)}) collective-permute-start(bf16[16,64,128]{2,1,0:T(8,128)(2,1)S(1)} %get-tuple-element.71.own.inner), channel_id=1, source_target_pairs={{16,0},{32,16},{48,32},{64,48},{80,64},{96,80},{112,96},{128,112},... | collective-permute-start | bytes 786440 | tf_op jit(solution)/shard_map/ppermute | solution.py:195
  42.7 3.2 %collective-permute-done.4.halo = bf16[16,64,128]{2,1,0:T(8,128)(2,1)S(1)} collective-permute-done((bf16[16,64,128]{2,1,0:T(8,128)(2,1)S(1)}, bf16[16,64,128]{2,1,0:T(8,128)(2,1)S(1)}, u32[]{:S(2)}, u32[]{:S(2)}) %collective-permute-start.4) | collective-permute-done | bytes 262176 | tf_op jit(solution)/shard_map/ppermute | solution.py:195
  46.7 2.3 %collective-permute-start.6 = (bf16[16,64,128]{2,1,0:T(8,128)(2,1)S(1)}, bf16[16,64,128]{2,1,0:T(8,128)(2,1)S(1)}, u32[]{:S(2)}, u32[]{:S(2)}) collective-permute-start(bf16[16,64,128]{2,1,0:T(8,128)(2,1)S(1)} %get-tuple-element.79.own.inner), channel_id=1, source_target_pairs={{0,16},{16,32},{32,48},{48,64},{64,80},{80,96},{96,112},{112,128},... | collective-permute-start | bytes 786440 | tf_op jit(solution)/shard_map/ppermute | solution.py:197
  52.2 2.2 %collective-permute-start.9 = (bf16[16,64,128]{2,1,0:T(8,128)(2,1)S(1)}, bf16[16,64,128]{2,1,0:T(8,128)(2,1)S(1)}, u32[]{:S(2)}, u32[]{:S(2)}) collective-permute-start(bf16[16,64,128]{2,1,0:T(8,128)(2,1)S(1)} %get-tuple-element.86.inner.own), channel_id=1, source_target_pairs={{0,16},{16,32},{32,48},{48,64},{64,80},{80,96},{96,112},{112,128},... | collective-permute-start | bytes 786440 | tf_op jit(solution)/shard_map/ppermute | solution.py:197
  55.9 2.9 %collective-permute-done.6.halo = bf16[16,64,128]{2,1,0:T(8,128)(2,1)S(1)} collective-permute-done((bf16[16,64,128]{2,1,0:T(8,128)(2,1)S(1)}, bf16[16,64,128]{2,1,0:T(8,128)(2,1)S(1)}, u32[]{:S(2)}, u32[]{:S(2)}) %collective-permute-start.6) | collective-permute-done | bytes 262176 | tf_op jit(solution)/shard_map/ppermute | solution.py:197
  62.7 6.4 %collective-permute-done.9.halo = bf16[16,64,128]{2,1,0:T(8,128)(2,1)S(1)} collective-permute-done((bf16[16,64,128]{2,1,0:T(8,128)(2,1)S(1)}, bf16[16,64,128]{2,1,0:T(8,128)(2,1)S(1)}, u32[]{:S(2)}, u32[]{:S(2)}) %collective-permute-start.9) | collective-permute-done | bytes 262176 | tf_op jit(solution)/shard_map/ppermute | solution.py:197
  72.4 4.2 %collective-permute-start.10 = (bf16[16,64,128]{2,1,0:T(8,128)(2,1)S(1)}, bf16[16,64,128]{2,1,0:T(8,128)(2,1)S(1)}, u32[]{:S(2)}, u32[]{:S(2)}) collective-permute-start(bf16[16,64,128]{2,1,0:T(8,128)(2,1)S(1)} %get-tuple-element.94.own.inner), channel_id=1, source_target_pairs={{0,16},{16,32},{32,48},{48,64},{64,80},{80,96},{96,112},{112,128},... | collective-permute-start | bytes 786440 | tf_op jit(solution)/shard_map/ppermute | solution.py:197
  78.1 8.6 %collective-permute-done.11.halo = bf16[16,64,128]{2,1,0:T(8,128)(2,1)S(1)} collective-permute-done((bf16[16,64,128]{2,1,0:T(8,128)(2,1)S(1)}, bf16[16,64,128]{2,1,0:T(8,128)(2,1)S(1)}, u32[]{:S(2)}, u32[]{:S(2)}) %collective-permute-start.11) | collective-permute-done | bytes 262176 | tf_op jit(solution)/shard_map/ppermute | solution.py:195
  89.9 10.8 %all_to_all.15 = bf16[32,64,128]{2,1,0:T(8,128)(2,1)S(1)} all-to-all(bf16[32,64,128]{2,1,0:T(8,128)(2,1)S(1)} %shard_map.73), channel_id=1, replica_groups=mesh['z'=8,'yh'=2,'x'=4,'yl'=2,'c'=2] {'x','yl'}, dimensions={0} | all-to-all | bytes 1048576 | tf_op jit(solution)/shard_map/all_to_all | solution.py:245
  102.6 3.3 %shard_map.74 = (bf16[8,512,128]{2,1,0:T(8,128)(2,1)}, bf16[1024,512]{1,0:T(8,128)(2,1)S(1)}) custom-call(s32[3]{0:T(128)S(1)} %pad_add_fusion.place, bf16[8,4,64,128]{3,2,1,0:T(8,128)(2,1)S(1)} %bitcast.11, bf16[8,4,64,128]{3,2,1,0:T(8,128)(2,1)S(1)} %collective-permute-done.12.other), custom_call_target="tpu_custom_call" | custom-call | flops 536870912 | bytes 2097152 | tf_op jit(solution)/shard_map/pallas_call | solution.py:97
  105.9 5.6 %all-to-all-start.1 = ((bf16[8,512,128]{2,1,0:T(8,128)(2,1)}), bf16[8,512,128]{2,1,0:T(8,128)(2,1)S(1)}, u32[]{:S(2)}, u32[]{:S(2)}) async-start(bf16[8,512,128]{2,1,0:T(8,128)(2,1)} %get-tuple-element.96), calls=%async_computation.1 | async-start | bytes 2097152 | tf_op jit(solution)/shard_map/all_to_all | solution.py:261
  113.0 14.9 %collective-permute-done.13 = bf16[64,1024]{1,0:T(8,128)(2,1)S(1)} collective-permute-done((bf16[64,1024]{1,0:T(8,128)(2,1)S(1)}, bf16[64,1024]{1,0:T(8,128)(2,1)S(1)}, u32[]{:S(2)}, u32[]{:S(2)}) %collective-permute-start.13) | collective-permute-done | bytes 131104 | tf_op jit(solution)/shard_map/ppermute | solution.py:201
  130.0 2.1 %collective-permute-start.16 = (bf16[2,64,1024]{2,1,0:T(8,128)(2,1)S(1)}, bf16[2,64,1024]{2,1,0:T(8,128)(2,1)S(1)}, u32[]{:S(2)}, u32[]{:S(2)}) collective-permute-start(bf16[2,64,1024]{2,1,0:T(8,128)(2,1)S(1)} %pad_maximum_fusion.ritz), channel_id=1, source_target_pairs={{0,4},{4,8},{8,12},{12,0},{1,5},{5,9},{9,13},{13,1},{2,6},{6,10},{... | collective-permute-start | bytes 786440 | tf_op jit(solution)/shard_map/ppermute | solution.py:206
  133.0 7.2 %all-to-all-start.2 = ((bf16[16,32,128]{2,1,0:T(8,128)(2,1)}), bf16[16,32,128]{2,1,0:T(8,128)(2,1)S(1)}, u32[]{:S(2)}, u32[]{:S(2)}) async-start(bf16[16,32,128]{2,1,0:T(8,128)(2,1)} %shard_map.75), calls=%async_computation.2 | async-start | bytes 262144 | tf_op jit(solution)/shard_map/all_to_all | solution.py:275
  140.2 2.2 %collective-permute-done.14.ritz_next = bf16[2,64,1024]{2,1,0:T(8,128)(2,1)S(1)} collective-permute-done((bf16[2,64,1024]{2,1,0:T(8,128)(2,1)S(1)}, bf16[2,64,1024]{2,1,0:T(8,128)(2,1)S(1)}, u32[]{:S(2)}, u32[]{:S(2)}) %collective-permute-start.14) | collective-permute-done | bytes 262176 | tf_op jit(solution)/shard_map/ppermute | solution.py:206
  144.8 2.6 %collective-permute-start.18 = (bf16[4,64,128]{2,1,0:T(8,128)(2,1)S(1)}, bf16[4,64,128]{2,1,0:T(8,128)(2,1)S(1)}, u32[]{:S(2)}, u32[]{:S(2)}) collective-permute-start(bf16[4,64,128]{2,1,0:T(8,128)(2,1)S(1)} %get-tuple-element.100), channel_id=1, source_target_pairs={{0,4},{2,6},{4,8},{6,10},{8,12},{10,14},{12,0},{14,2},{1,5},{3,7},... | collective-permute-start | bytes 196616 | tf_op jit(solution)/shard_map/ppermute | solution.py:270
  149.4 2.6 %collective-permute-start.21 = (bf16[4,64,128]{2,1,0:T(8,128)(2,1)S(1)}, bf16[4,64,128]{2,1,0:T(8,128)(2,1)S(1)}, u32[]{:S(2)}, u32[]{:S(2)}) collective-permute-start(bf16[4,64,128]{2,1,0:T(8,128)(2,1)S(1)} %get-tuple-element.103), channel_id=1, source_target_pairs={{0,10},{2,8},{4,14},{6,12},{8,2},{10,0},{12,6},{14,4},{1,11},{3,9}... | collective-permute-start | bytes 196616 | tf_op jit(solution)/shard_map/ppermute | solution.py:270
  157.9 2.4 %collective-permute-done.23.refs_7_ = bf16[4,64,128]{2,1,0:T(8,128)(2,1)S(1)} collective-permute-done((bf16[4,64,128]{2,1,0:T(8,128)(2,1)S(1)}, bf16[4,64,128]{2,1,0:T(8,128)(2,1)S(1)}, u32[]{:S(2)}, u32[]{:S(2)}) %collective-permute-start.23) | collective-permute-done | bytes 65568 | tf_op jit(solution)/shard_map/ppermute | solution.py:270
  (65 shorter events, 54.1 us)
Async XLA Ops:
  1.7 14.5 %collective-permute-start.1 = (bf16[16,64,128]{2,1,0:T(8,128)(2,1)S(1)}, bf16[16,64,128]{2,1,0:T(8,128)(2,1)S(1)}, u32[]{:S(2)}, u32[]{:S(2)}) collective-permute-start(bf16[16,64,128]{2,1,0:T(8,128)(2,1)S(1)} %get-tuple-element.55.inner.own.current.rest_0_), channel_id=1, source_target_pairs={{0,16},{16,32},{32,48},{48,64},{64,80},{80,96},{96,112},{112,128},... | collective-permute-start | bytes 786440 | tf_op jit(solution)/shard_map/ppermute | solution.py:197
  5.0 17.2 %collective-permute-start = (bf16[16,64,128]{2,1,0:T(8,128)(2,1)S(1)}, bf16[16,64,128]{2,1,0:T(8,128)(2,1)S(1)}, u32[]{:S(2)}, u32[]{:S(2)}) collective-permute-start(bf16[16,64,128]{2,1,0:T(8,128)(2,1)S(1)} %get-tuple-element.56.own.current.inner.rest_0_), channel_id=1, source_target_pairs={{16,0},{32,16},{48,32},{64,48},{80,64},{96,80},{112,96},{128,112},... | collective-permute-start | bytes 786440 | tf_op jit(solution)/shard_map/ppermute | solution.py:195
  17.0 12.3 %collective-permute-start.3 = (bf16[16,64,128]{2,1,0:T(8,128)(2,1)S(1)}, bf16[16,64,128]{2,1,0:T(8,128)(2,1)S(1)}, u32[]{:S(2)}, u32[]{:S(2)}) collective-permute-start(bf16[16,64,128]{2,1,0:T(8,128)(2,1)S(1)} %get-tuple-element.62.inner.own), channel_id=1, source_target_pairs={{16,0},{32,16},{48,32},{64,48},{80,64},{96,80},{112,96},{128,112},... | collective-permute-start | bytes 786440 | tf_op jit(solution)/shard_map/ppermute | solution.py:195
  23.0 11.1 %collective-permute-start.2 = (bf16[16,64,128]{2,1,0:T(8,128)(2,1)S(1)}, bf16[16,64,128]{2,1,0:T(8,128)(2,1)S(1)}, u32[]{:S(2)}, u32[]{:S(2)}) collective-permute-start(bf16[16,64,128]{2,1,0:T(8,128)(2,1)S(1)} %get-tuple-element.63.own.inner), channel_id=1, source_target_pairs={{0,16},{16,32},{32,48},{48,64},{64,80},{80,96},{96,112},{112,128},... | collective-permute-start | bytes 786440 | tf_op jit(solution)/shard_map/ppermute | solution.py:197
  30.1 10.2 %collective-permute-start.5 = (bf16[16,64,128]{2,1,0:T(8,128)(2,1)S(1)}, bf16[16,64,128]{2,1,0:T(8,128)(2,1)S(1)}, u32[]{:S(2)}, u32[]{:S(2)}) collective-permute-start(bf16[16,64,128]{2,1,0:T(8,128)(2,1)S(1)} %get-tuple-element.70.inner.own), channel_id=1, source_target_pairs={{0,16},{16,32},{32,48},{48,64},{64,80},{80,96},{96,112},{112,128},... | collective-permute-start | bytes 786440 | tf_op jit(solution)/shard_map/ppermute | solution.py:197
  34.9 11.0 %collective-permute-start.4 = (bf16[16,64,128]{2,1,0:T(8,128)(2,1)S(1)}, bf16[16,64,128]{2,1,0:T(8,128)(2,1)S(1)}, u32[]{:S(2)}, u32[]{:S(2)}) collective-permute-start(bf16[16,64,128]{2,1,0:T(8,128)(2,1)S(1)} %get-tuple-element.71.own.inner), channel_id=1, source_target_pairs={{16,0},{32,16},{48,32},{64,48},{80,64},{96,80},{112,96},{128,112},... | collective-permute-start | bytes 786440 | tf_op jit(solution)/shard_map/ppermute | solution.py:195
  41.1 10.3 %collective-permute-start.7 = (bf16[16,64,128]{2,1,0:T(8,128)(2,1)S(1)}, bf16[16,64,128]{2,1,0:T(8,128)(2,1)S(1)}, u32[]{:S(2)}, u32[]{:S(2)}) collective-permute-start(bf16[16,64,128]{2,1,0:T(8,128)(2,1)S(1)} %get-tuple-element.78.inner.own), channel_id=1, source_target_pairs={{16,0},{32,16},{48,32},{64,48},{80,64},{96,80},{112,96},{128,112},... | collective-permute-start | bytes 786440 | tf_op jit(solution)/shard_map/ppermute | solution.py:195
  46.7 12.2 %collective-permute-start.6 = (bf16[16,64,128]{2,1,0:T(8,128)(2,1)S(1)}, bf16[16,64,128]{2,1,0:T(8,128)(2,1)S(1)}, u32[]{:S(2)}, u32[]{:S(2)}) collective-permute-start(bf16[16,64,128]{2,1,0:T(8,128)(2,1)S(1)} %get-tuple-element.79.own.inner), channel_id=1, source_target_pairs={{0,16},{16,32},{32,48},{48,64},{64,80},{80,96},{96,112},{112,128},... | collective-permute-start | bytes 786440 | tf_op jit(solution)/shard_map/ppermute | solution.py:197
  52.2 16.9 %collective-permute-start.9 = (bf16[16,64,128]{2,1,0:T(8,128)(2,1)S(1)}, bf16[16,64,128]{2,1,0:T(8,128)(2,1)S(1)}, u32[]{:S(2)}, u32[]{:S(2)}) collective-permute-start(bf16[16,64,128]{2,1,0:T(8,128)(2,1)S(1)} %get-tuple-element.86.inner.own), channel_id=1, source_target_pairs={{0,16},{16,32},{32,48},{48,64},{64,80},{80,96},{96,112},{112,128},... | collective-permute-start | bytes 786440 | tf_op jit(solution)/shard_map/ppermute | solution.py:197
  59.7 11.9 %collective-permute-start.8 = (bf16[16,64,128]{2,1,0:T(8,128)(2,1)S(1)}, bf16[16,64,128]{2,1,0:T(8,128)(2,1)S(1)}, u32[]{:S(2)}, u32[]{:S(2)}) collective-permute-start(bf16[16,64,128]{2,1,0:T(8,128)(2,1)S(1)} %get-tuple-element.87.own.inner), channel_id=1, source_target_pairs={{16,0},{32,16},{48,32},{64,48},{80,64},{96,80},{112,96},{128,112},... | collective-permute-start | bytes 786440 | tf_op jit(solution)/shard_map/ppermute | solution.py:195
  69.9 16.8 %collective-permute-start.11 = (bf16[16,64,128]{2,1,0:T(8,128)(2,1)S(1)}, bf16[16,64,128]{2,1,0:T(8,128)(2,1)S(1)}, u32[]{:S(2)}, u32[]{:S(2)}) collective-permute-start(bf16[16,64,128]{2,1,0:T(8,128)(2,1)S(1)} %get-tuple-element.93.inner.own), channel_id=1, source_target_pairs={{16,0},{32,16},{48,32},{64,48},{80,64},{96,80},{112,96},{128,112},... | collective-permute-start | bytes 786440 | tf_op jit(solution)/shard_map/ppermute | solution.py:195
  72.4 16.7 %collective-permute-start.10 = (bf16[16,64,128]{2,1,0:T(8,128)(2,1)S(1)}, bf16[16,64,128]{2,1,0:T(8,128)(2,1)S(1)}, u32[]{:S(2)}, u32[]{:S(2)}) collective-permute-start(bf16[16,64,128]{2,1,0:T(8,128)(2,1)S(1)} %get-tuple-element.94.own.inner), channel_id=1, source_target_pairs={{0,16},{16,32},{32,48},{48,64},{64,80},{80,96},{96,112},{112,128},... | collective-permute-start | bytes 786440 | tf_op jit(solution)/shard_map/ppermute | solution.py:197
  105.9 26.2 %all-to-all-start.1 = ((bf16[8,512,128]{2,1,0:T(8,128)(2,1)}), bf16[8,512,128]{2,1,0:T(8,128)(2,1)S(1)}, u32[]{:S(2)}, u32[]{:S(2)}) async-start(bf16[8,512,128]{2,1,0:T(8,128)(2,1)} %get-tuple-element.96), calls=%async_computation.1 | async-start | bytes 2097152 | tf_op jit(solution)/shard_map/all_to_all | solution.py:261
  111.5 16.4 %collective-permute-start.13 = (bf16[64,1024]{1,0:T(8,128)(2,1)S(1)}, bf16[64,1024]{1,0:T(8,128)(2,1)S(1)}, u32[]{:S(2)}, u32[]{:S(2)}) collective-permute-start(bf16[64,1024]{1,0:T(8,128)(2,1)S(1)} %bitcast.14), channel_id=1, source_target_pairs={{0,2},{2,0},{1,3},{3,1},{4,6},{6,4},{5,7},{7,5},{8,10},{10,8},{9,1... | collective-permute-start | bytes 393224 | tf_op jit(solution)/shard_map/ppermute | solution.py:201
  128.0 14.4 %collective-permute-start.14 = (bf16[2,64,1024]{2,1,0:T(8,128)(2,1)S(1)}, bf16[2,64,1024]{2,1,0:T(8,128)(2,1)S(1)}, u32[]{:S(2)}, u32[]{:S(2)}) collective-permute-start(bf16[2,64,1024]{2,1,0:T(8,128)(2,1)S(1)} %pad_maximum_fusion.ritz), channel_id=1, source_target_pairs={{0,12},{4,0},{8,4},{12,8},{1,13},{5,1},{9,5},{13,9},{2,14},{6,2},{... | collective-permute-start | bytes 786440 | tf_op jit(solution)/shard_map/ppermute | solution.py:206
  128.9 13.5 %collective-permute-start.15 = (bf16[2,64,1024]{2,1,0:T(8,128)(2,1)S(1)}, bf16[2,64,1024]{2,1,0:T(8,128)(2,1)S(1)}, u32[]{:S(2)}, u32[]{:S(2)}) collective-permute-start(bf16[2,64,1024]{2,1,0:T(8,128)(2,1)S(1)} %pad_maximum_fusion.ritz), channel_id=1, source_target_pairs={{0,8},{4,12},{8,0},{12,4},{1,9},{5,13},{9,1},{13,5},{2,10},{6,14},... | collective-permute-start | bytes 786440 | tf_op jit(solution)/shard_map/ppermute | solution.py:206
  130.0 13.0 %collective-permute-start.16 = (bf16[2,64,1024]{2,1,0:T(8,128)(2,1)S(1)}, bf16[2,64,1024]{2,1,0:T(8,128)(2,1)S(1)}, u32[]{:S(2)}, u32[]{:S(2)}) collective-permute-start(bf16[2,64,1024]{2,1,0:T(8,128)(2,1)S(1)} %pad_maximum_fusion.ritz), channel_id=1, source_target_pairs={{0,4},{4,8},{8,12},{12,0},{1,5},{5,9},{9,13},{13,1},{2,6},{6,10},{... | collective-permute-start | bytes 786440 | tf_op jit(solution)/shard_map/ppermute | solution.py:206
  133.0 28.9 %all-to-all-start.2 = ((bf16[16,32,128]{2,1,0:T(8,128)(2,1)}), bf16[16,32,128]{2,1,0:T(8,128)(2,1)S(1)}, u32[]{:S(2)}, u32[]{:S(2)}) async-start(bf16[16,32,128]{2,1,0:T(8,128)(2,1)} %shard_map.75), calls=%async_computation.2 | async-start | bytes 262144 | tf_op jit(solution)/shard_map/all_to_all | solution.py:275
  143.7 8.2 %collective-permute-start.17 = (bf16[4,64,128]{2,1,0:T(8,128)(2,1)S(1)}, bf16[4,64,128]{2,1,0:T(8,128)(2,1)S(1)}, u32[]{:S(2)}, u32[]{:S(2)}) collective-permute-start(bf16[4,64,128]{2,1,0:T(8,128)(2,1)S(1)} %get-tuple-element.99), channel_id=1, source_target_pairs={{0,2},{2,0},{4,6},{6,4},{8,10},{10,8},{12,14},{14,12},{1,3},{3,1},... | collective-permute-start | bytes 196616 | tf_op jit(solution)/shard_map/ppermute | solution.py:270
  144.8 9.1 %collective-permute-start.18 = (bf16[4,64,128]{2,1,0:T(8,128)(2,1)S(1)}, bf16[4,64,128]{2,1,0:T(8,128)(2,1)S(1)}, u32[]{:S(2)}, u32[]{:S(2)}) collective-permute-start(bf16[4,64,128]{2,1,0:T(8,128)(2,1)S(1)} %get-tuple-element.100), channel_id=1, source_target_pairs={{0,4},{2,6},{4,8},{6,10},{8,12},{10,14},{12,0},{14,2},{1,5},{3,7},... | collective-permute-start | bytes 196616 | tf_op jit(solution)/shard_map/ppermute | solution.py:270
  147.5 7.0 %collective-permute-start.19 = (bf16[4,64,128]{2,1,0:T(8,128)(2,1)S(1)}, bf16[4,64,128]{2,1,0:T(8,128)(2,1)S(1)}, u32[]{:S(2)}, u32[]{:S(2)}) collective-permute-start(bf16[4,64,128]{2,1,0:T(8,128)(2,1)S(1)} %get-tuple-element.101), channel_id=1, source_target_pairs={{0,6},{2,4},{4,10},{6,8},{8,14},{10,12},{12,2},{14,0},{1,7},{3,5},... | collective-permute-start | bytes 196616 | tf_op jit(solution)/shard_map/ppermute | solution.py:270
  147.9 6.5 %collective-permute-start.20 = (bf16[4,64,128]{2,1,0:T(8,128)(2,1)S(1)}, bf16[4,64,128]{2,1,0:T(8,128)(2,1)S(1)}, u32[]{:S(2)}, u32[]{:S(2)}) collective-permute-start(bf16[4,64,128]{2,1,0:T(8,128)(2,1)S(1)} %get-tuple-element.102), channel_id=1, source_target_pairs={{0,8},{2,10},{4,12},{6,14},{8,0},{10,2},{12,4},{14,6},{1,9},{3,11}... | collective-permute-start | bytes 196616 | tf_op jit(solution)/shard_map/ppermute | solution.py:270
  149.4 6.8 %collective-permute-start.21 = (bf16[4,64,128]{2,1,0:T(8,128)(2,1)S(1)}, bf16[4,64,128]{2,1,0:T(8,128)(2,1)S(1)}, u32[]{:S(2)}, u32[]{:S(2)}) collective-permute-start(bf16[4,64,128]{2,1,0:T(8,128)(2,1)S(1)} %get-tuple-element.103), channel_id=1, source_target_pairs={{0,10},{2,8},{4,14},{6,12},{8,2},{10,0},{12,6},{14,4},{1,11},{3,9}... | collective-permute-start | bytes 196616 | tf_op jit(solution)/shard_map/ppermute | solution.py:270
  153.9 6.4 %collective-permute-start.23 = (bf16[4,64,128]{2,1,0:T(8,128)(2,1)S(1)}, bf16[4,64,128]{2,1,0:T(8,128)(2,1)S(1)}, u32[]{:S(2)}, u32[]{:S(2)}) collective-permute-start(bf16[4,64,128]{2,1,0:T(8,128)(2,1)S(1)} %get-tuple-element.105), channel_id=1, source_target_pairs={{0,14},{2,12},{4,2},{6,0},{8,6},{10,4},{12,10},{14,8},{1,15},{3,13... | collective-permute-start | bytes 196616 | tf_op jit(solution)/shard_map/ppermute | solution.py:270
  (4 other events, 33.4 us)

commit v4 on v3

--- a/solution.py
+++ b/solution.py
@@ -105,18 +105,14 @@
     )(*operands)
 
 
-def part_kernel(chips, place, mine, other, out, rows, own):
-    held, cols = mine.shape[1], mine.shape[2]
+def fill_rows(place, mine, other, rows):
+    chips, held, cols = mine.shape[0], mine.shape[1], mine.shape[2]
 
     def fill(parity, source):
         for t in range(chips):
             for el in range(held):
                 rows[pl.ds((2 * t + parity) * cols, cols), pl.ds(el * NB, NB)] = source[t, el]
 
-    for t in range(chips):
-        for el in range(held):
-            own[pl.ds(t * cols, cols), pl.ds(el * NB, NB)] = mine[t, el]
-
     @pl.when(place[2] == 0)
     def _():
         fill(0, mine)
@@ -127,11 +123,27 @@
         fill(1, mine)
         fill(0, other)
 
-    for s in range(0, chips, 2):
-        part = product(own[pl.ds(s * cols, 2 * cols), :], rows[...], ROWS).astype(jnp.bfloat16)
-        for q in range(2):
-            for t in range(chips):
-                out[s + q, pl.ds(t * cols, cols), :] = part[q * cols : (q + 1) * cols, t * NB : (t + 1) * NB]
+
+def part_blocks(around, away, place, rows, outs):
+    chips, cols = outs[0].shape[0], outs[0].shape[1]
+    line = lax.rem(place[0] + away, around) * 2
+    left = []
+    for q in range(2):
+        chip = line + (place[1] if q == 0 else 1 - place[1])
+        left.append(rows[pl.ds(pl.multiple_of((2 * chip + place[2]) * cols, cols), cols), :])
+    part = product(jnp.concatenate(left, axis=0), rows[...], ROWS).astype(jnp.bfloat16)
+    for q in range(2):
+        for t in range(chips):
+            outs[q][t] = part[q * cols : (q + 1) * cols, t * NB : (t + 1) * NB]
+
+
+def first_part_kernel(around, away, place, mine, other, rows, *outs):
+    fill_rows(place, mine, other, rows)
+    part_blocks(around, away, place, rows, outs)
+
+
+def part_kernel(around, away, place, rows, *outs):
+    part_blocks(around, away, place, rows, outs)
 
 
 def turn_kernel(rows, ritz, ritz_next, ritz_far, ritz_back, *outs):
@@ -153,13 +165,14 @@
             out[line * held + el] = piece[el].astype(jnp.float32)
 
 
-def margin_rows_kernel(chips, got, out):
+def margin_rows_kernel(*refs):
+    pieces, out = refs[:-1], refs[-1]
     cols = out.shape[2] // 2
     half = cols // 2
-    for t in range(chips):
-        total = got[0, pl.ds(t * cols, cols), :].astype(jnp.float32)
-        for s in range(1, chips):
-            total = total + got[s, pl.ds(t * cols, cols), :].astype(jnp.float32)
+    for t in range(len(pieces)):
+        total = pieces[0][t].astype(jnp.float32)
+        for piece in pieces[1:]:
+            total = total + piece[t].astype(jnp.float32)
         for core in range(2):
             block = total[:, core * cols : (core + 1) * cols]
             out[2 * t + core] = jnp.concatenate([block[:half], block[half:]], axis=1).astype(jnp.bfloat16)
@@ -250,26 +263,39 @@
     depth = held * NB
     small = pl.CostEstimate(flops=1 << 20, bytes_accessed=1 << 20, transcendentals=0)
     flops = pl.CostEstimate(flops=4 * (chips * cols) ** 2 * depth, bytes_accessed=2 << 20, transcendentals=0)
-    sent, rows = call(
-        functools.partial(part_kernel, chips), (place, mine, theirs),
-        (
-            jax.ShapeDtypeStruct((chips, chips * cols, NB), jnp.bfloat16),
-            jax.ShapeDtypeStruct((2 * chips * cols, depth), jnp.bfloat16),
-        ),
-        flops, 16, (pltpu.VMEM((chips * cols, depth), jnp.bfloat16),), [SMEM, VMEM, VMEM],
-    )
-    got = lax.all_to_all(sent, CHIP, 0, 0, tiled=True)
+
+    def to_chip(away, q):
+        return [(i, (i // 2 + away) % around * 2 + (i + q) % 2) for i in range(chips)]
+
+    block = jax.ShapeDtypeStruct((chips, cols, NB), jnp.bfloat16)
+    rows = None
+    parts = []
+    for away in (1, around - 1, 2, 0):
+        if rows is None:
+            rows, *blocks = call(
+                functools.partial(first_part_kernel, around, away), (place, mine, theirs),
+                (jax.ShapeDtypeStruct((2 * chips * cols, depth), jnp.bfloat16), block, block),
+                flops, 16, (), [SMEM, VMEM, VMEM],
+            )
+        else:
+            blocks = call(
+                functools.partial(part_kernel, around, away), (place, rows),
+                (block, block), flops, 16, (), [SMEM, VMEM],
+            )
+        for q in range(2):
+            if away == 0 and q == 0:
+                parts.append(blocks[0])
+                continue
+            parts.append(lax.ppermute(blocks[q], CHIP, to_chip(away, q)))
     turned = call(
         turn_kernel, (rows, shared["pair"], shared[around - 1], shared[2], shared[1]),
         (jax.ShapeDtypeStruct((held, cols, NB), jnp.bfloat16),) * chips, flops, 16,
     )
     pieces = [turned[0]]
     for index in range(1, chips):
-        away, q = index // 2, index % 2
-        to = [(i, (i // 2 + away) % around * 2 + (i + q) % 2) for i in range(chips)]
-        pieces.append(lax.ppermute(turned[index], CHIP, to))
+        pieces.append(lax.ppermute(turned[index], CHIP, to_chip(index // 2, index % 2)))
     total = call(
-        functools.partial(margin_rows_kernel, chips), (got,),
+        margin_rows_kernel, parts,
         jax.ShapeDtypeStruct((slabs, cols // 2, 2 * cols), jnp.bfloat16), small, 12,
     )
     total = lax.all_to_all(total, ELEM, 0, 0, tiled=True)

time: 163 us -> 166 us (1.018)
  the two profiles are of different devices: /device:TPU:134 before, /device:TPU:4 now
where the time goes in v4:
time: 166 us; the launch traced here: 163 us
  starting transfers between devices  69.1 us (42%)
  waiting for transfers between devices  41.2 us (25%)
  Pallas kernels  36.4 us (22%)
  blocking collectives  11 us (7%)
  local copies, waits for them, and re-layouts  4.15 us (3%)
    pallas_call x32, Pallas kernels, call(): pl.pallas_call(kernel, out_shape=out_shape, in_specs=in_specs or [VMEM] *...  36.4 us
    ppermute x6, starting transfers between devices, send(): halo['b', k] = lax.ppermute(val['a', k], ELEM, down)  25.5 us
    ppermute x6, waiting for transfers between devices, send(): halo['a', k] = lax.ppermute(val['b', k], ELEM, up)  17.8 us
    ppermute x7, waiting for transfers between devices, whole(): parts.append(lax.ppermute(blocks[q], CHIP, to_chip(away, q)))  12.6 us
    all_to_all x1, blocking collectives, whole(): mine = lax.all_to_all(filtered, CHIP, 0, 0, tiled=True)  11 us
    all_to_all x1, starting transfers between devices, whole(): total = lax.all_to_all(total, ELEM, 0, 0, tiled=True)  10.5 us
    ppermute x7, starting transfers between devices, whole(): lax.ppermute(turned[index], CHIP, to_chip(index // 2, index % 2))  10.1 us
    ppermute x7, starting transfers between devices, whole(): parts.append(lax.ppermute(blocks[q], CHIP, to_chip(away, q)))  9.55 us
  transfers between devices with their start and end apart: 32, of which 15 were waited for; matrix products, arithmetic and copies ran while one was open for 0% of the time, Pallas kernels for 21%

profile of v4, /device:TPU:4, one launch (start us, length us, event | category | flops | bytes accessed | tf_op | source)
XLA Modules:
  0.0 162.9 jit_solution(5014884988185997094)
XLA Ops:
  1.7 3.3 %collective-permute-start.1 = (bf16[16,64,128]{2,1,0:T(8,128)(2,1)S(1)}, bf16[16,64,128]{2,1,0:T(8,128)(2,1)S(1)}, u32[]{:S(2)}, u32[]{:S(2)}) collective-permute-start(bf16[16,64,128]{2,1,0:T(8,128)(2,1)S(1)} %get-tuple-element.62.inner.own.current.rest_0_), channel_id=1, source_target_pairs={{0,16},{16,32},{32,48},{48,64},{64,80},{80,96},{96,112},{112,128},... | collective-permute-start | bytes 786440 | tf_op jit(solution)/shard_map/ppermute | solution.py:210
  5.0 5.4 %collective-permute-start = (bf16[16,64,128]{2,1,0:T(8,128)(2,1)S(1)}, bf16[16,64,128]{2,1,0:T(8,128)(2,1)S(1)}, u32[]{:S(2)}, u32[]{:S(2)}) collective-permute-start(bf16[16,64,128]{2,1,0:T(8,128)(2,1)S(1)} %get-tuple-element.63.own.current.inner.rest_0_), channel_id=1, source_target_pairs={{16,0},{32,16},{48,32},{64,48},{80,64},{96,80},{112,96},{128,112},... | collective-permute-start | bytes 786440 | tf_op jit(solution)/shard_map/ppermute | solution.py:208
  10.4 3.1 %copy-done = bf16[32,7,128,128]{3,2,1,0:T(8,128)(2,1)S(1)} copy-done((bf16[32,7,128,128]{3,2,1,0:T(8,128)(2,1)S(1)}, bf16[32,7,128,128]{3,2,1,0:T(8,128)(2,1)}, u32[]{:S(2)}) %copy-start) | copy-done | bytes 7340056
  13.4 1.6 shard_map.50.partial
  15.0 1.7 %collective-permute-done.1.halo = bf16[16,64,128]{2,1,0:T(8,128)(2,1)S(1)} collective-permute-done((bf16[16,64,128]{2,1,0:T(8,128)(2,1)S(1)}, bf16[16,64,128]{2,1,0:T(8,128)(2,1)S(1)}, u32[]{:S(2)}, u32[]{:S(2)}) %collective-permute-start.1) | collective-permute-done | bytes 262176 | tf_op jit(solution)/shard_map/ppermute | solution.py:210
  17.5 8.8 %collective-permute-start.3 = (bf16[16,64,128]{2,1,0:T(8,128)(2,1)S(1)}, bf16[16,64,128]{2,1,0:T(8,128)(2,1)S(1)}, u32[]{:S(2)}, u32[]{:S(2)}) collective-permute-start(bf16[16,64,128]{2,1,0:T(8,128)(2,1)S(1)} %get-tuple-element.69.inner.own), channel_id=1, source_target_pairs={{16,0},{32,16},{48,32},{64,48},{80,64},{96,80},{112,96},{128,112},... | collective-permute-start | bytes 786440 | tf_op jit(solution)/shard_map/ppermute | solution.py:208
  26.3 1.6 shard_map.52.partial
  33.5 8.1 %collective-permute-done.2.halo = bf16[16,64,128]{2,1,0:T(8,128)(2,1)S(1)} collective-permute-done((bf16[16,64,128]{2,1,0:T(8,128)(2,1)S(1)}, bf16[16,64,128]{2,1,0:T(8,128)(2,1)S(1)}, u32[]{:S(2)}, u32[]{:S(2)}) %collective-permute-start.2) | collective-permute-done | bytes 262176 | tf_op jit(solution)/shard_map/ppermute | solution.py:210
  46.1 3.1 %collective-permute-start.7 = (bf16[16,64,128]{2,1,0:T(8,128)(2,1)S(1)}, bf16[16,64,128]{2,1,0:T(8,128)(2,1)S(1)}, u32[]{:S(2)}, u32[]{:S(2)}) collective-permute-start(bf16[16,64,128]{2,1,0:T(8,128)(2,1)S(1)} %get-tuple-element.85.inner.own), channel_id=1, source_target_pairs={{16,0},{32,16},{48,32},{64,48},{80,64},{96,80},{112,96},{128,112},... | collective-permute-start | bytes 786440 | tf_op jit(solution)/shard_map/ppermute | solution.py:208
  53.8 2.4 %collective-permute-done.7.halo = bf16[16,64,128]{2,1,0:T(8,128)(2,1)S(1)} collective-permute-done((bf16[16,64,128]{2,1,0:T(8,128)(2,1)S(1)}, bf16[16,64,128]{2,1,0:T(8,128)(2,1)S(1)}, u32[]{:S(2)}, u32[]{:S(2)}) %collective-permute-start.7) | collective-permute-done | bytes 262176 | tf_op jit(solution)/shard_map/ppermute | solution.py:208
  59.8 3.4 %collective-permute-done.6.halo = bf16[16,64,128]{2,1,0:T(8,128)(2,1)S(1)} collective-permute-done((bf16[16,64,128]{2,1,0:T(8,128)(2,1)S(1)}, bf16[16,64,128]{2,1,0:T(8,128)(2,1)S(1)}, u32[]{:S(2)}, u32[]{:S(2)}) %collective-permute-start.6) | collective-permute-done | bytes 262176 | tf_op jit(solution)/shard_map/ppermute | solution.py:210
  64.0 4.2 %collective-permute-start.8 = (bf16[16,64,128]{2,1,0:T(8,128)(2,1)S(1)}, bf16[16,64,128]{2,1,0:T(8,128)(2,1)S(1)}, u32[]{:S(2)}, u32[]{:S(2)}) collective-permute-start(bf16[16,64,128]{2,1,0:T(8,128)(2,1)S(1)} %get-tuple-element.94.own.inner), channel_id=1, source_target_pairs={{16,0},{32,16},{48,32},{64,48},{80,64},{96,80},{112,96},{128,112},... | collective-permute-start | bytes 786440 | tf_op jit(solution)/shard_map/ppermute | solution.py:208
  70.7 2.6 %collective-permute-start.11 = (bf16[16,64,128]{2,1,0:T(8,128)(2,1)S(1)}, bf16[16,64,128]{2,1,0:T(8,128)(2,1)S(1)}, u32[]{:S(2)}, u32[]{:S(2)}) collective-permute-start(bf16[16,64,128]{2,1,0:T(8,128)(2,1)S(1)} %get-tuple-element.100.inner.own), channel_id=1, source_target_pairs={{16,0},{32,16},{48,32},{64,48},{80,64},{96,80},{112,96},{128,112},... | collective-permute-start | bytes 786440 | tf_op jit(solution)/shard_map/ppermute | solution.py:208
  82.2 4.7 %collective-permute-done.10.halo = bf16[16,64,128]{2,1,0:T(8,128)(2,1)S(1)} collective-permute-done((bf16[16,64,128]{2,1,0:T(8,128)(2,1)S(1)}, bf16[16,64,128]{2,1,0:T(8,128)(2,1)S(1)}, u32[]{:S(2)}, u32[]{:S(2)}) %collective-permute-start.10) | collective-permute-done | bytes 262176 | tf_op jit(solution)/shard_map/ppermute | solution.py:210
  87.6 11.0 %all_to_all.10 = bf16[32,64,128]{2,1,0:T(8,128)(2,1)S(1)} all-to-all(bf16[32,64,128]{2,1,0:T(8,128)(2,1)S(1)} %shard_map.73), channel_id=1, replica_groups=mesh['z'=8,'yh'=2,'x'=4,'yl'=2,'c'=2] {'x','yl'}, dimensions={0} | all-to-all | bytes 1048576 | tf_op jit(solution)/shard_map/all_to_all | solution.py:258
  104.1 2.1 %collective-permute-start.16 = (bf16[8,64,128]{2,1,0:T(8,128)(2,1)S(1)}, bf16[8,64,128]{2,1,0:T(8,128)(2,1)S(1)}, u32[]{:S(2)}, u32[]{:S(2)}) collective-permute-start(bf16[8,64,128]{2,1,0:T(8,128)(2,1)S(1)} %get-tuple-element.107), channel_id=1, source_target_pairs={{0,14},{2,12},{4,2},{6,0},{8,6},{10,4},{12,10},{14,8},{1,15},{3,13... | collective-permute-start | bytes 393224 | tf_op jit(solution)/shard_map/ppermute | solution.py:289
  108.9 3.3 %collective-permute-start.18 = (bf16[8,64,128]{2,1,0:T(8,128)(2,1)S(1)}, bf16[8,64,128]{2,1,0:T(8,128)(2,1)S(1)}, u32[]{:S(2)}, u32[]{:S(2)}) collective-permute-start(bf16[8,64,128]{2,1,0:T(8,128)(2,1)S(1)} %get-tuple-element.109), channel_id=1, source_target_pairs={{0,10},{2,8},{4,14},{6,12},{8,2},{10,0},{12,6},{14,4},{1,11},{3,9}... | collective-permute-start | bytes 393224 | tf_op jit(solution)/shard_map/ppermute | solution.py:289
  116.1 4.3 %collective-permute-start.23 = (bf16[2,64,1024]{2,1,0:T(8,128)(2,1)S(1)}, bf16[2,64,1024]{2,1,0:T(8,128)(2,1)S(1)}, u32[]{:S(2)}, u32[]{:S(2)}) collective-permute-start(bf16[2,64,1024]{2,1,0:T(8,128)(2,1)S(1)} %pad_maximum_fusion.ritz), channel_id=1, source_target_pairs={{0,4},{4,8},{8,12},{12,0},{1,5},{5,9},{9,13},{13,1},{2,6},{6,10},{... | collective-permute-start | bytes 786440 | tf_op jit(solution)/shard_map/ppermute | solution.py:219
  121.4 9.9 %collective-permute-done.13.refs_0_ = bf16[8,64,128]{2,1,0:T(8,128)(2,1)S(1)} collective-permute-done((bf16[8,64,128]{2,1,0:T(8,128)(2,1)S(1)}, bf16[8,64,128]{2,1,0:T(8,128)(2,1)S(1)}, u32[]{:S(2)}, u32[]{:S(2)}) %collective-permute-start.13) | collective-permute-done | bytes 131104 | tf_op jit(solution)/shard_map/ppermute | solution.py:289
  131.3 2.7 %collective-permute-done.14.refs_1_ = bf16[8,64,128]{2,1,0:T(8,128)(2,1)S(1)} collective-permute-done((bf16[8,64,128]{2,1,0:T(8,128)(2,1)S(1)}, bf16[8,64,128]{2,1,0:T(8,128)(2,1)S(1)}, u32[]{:S(2)}, u32[]{:S(2)}) %collective-permute-start.14) | collective-permute-done | bytes 131104 | tf_op jit(solution)/shard_map/ppermute | solution.py:289
  134.9 10.5 %all-to-all-start.1 = ((bf16[16,32,128]{2,1,0:T(8,128)(2,1)}), bf16[16,32,128]{2,1,0:T(8,128)(2,1)S(1)}, u32[]{:S(2)}, u32[]{:S(2)}) async-start(bf16[16,32,128]{2,1,0:T(8,128)(2,1)} %shard_map.78), calls=%async_computation.1 | async-start | bytes 262144 | tf_op jit(solution)/shard_map/all_to_all | solution.py:301
  147.9 3.3 %collective-permute-start.26 = (bf16[4,64,128]{2,1,0:T(8,128)(2,1)S(1)}, bf16[4,64,128]{2,1,0:T(8,128)(2,1)S(1)}, u32[]{:S(2)}, u32[]{:S(2)}) collective-permute-start(bf16[4,64,128]{2,1,0:T(8,128)(2,1)S(1)} %get-tuple-element.115), channel_id=1, source_target_pairs={{0,6},{2,4},{4,10},{6,8},{8,14},{10,12},{12,2},{14,0},{1,7},{3,5},... | collective-permute-start | bytes 196616 | tf_op jit(solution)/shard_map/ppermute | solution.py:296
  151.2 3.8 %collective-permute-start.28 = (bf16[4,64,128]{2,1,0:T(8,128)(2,1)S(1)}, bf16[4,64,128]{2,1,0:T(8,128)(2,1)S(1)}, u32[]{:S(2)}, u32[]{:S(2)}) collective-permute-start(bf16[4,64,128]{2,1,0:T(8,128)(2,1)S(1)} %get-tuple-element.117), channel_id=1, source_target_pairs={{0,10},{2,8},{4,14},{6,12},{8,2},{10,0},{12,6},{14,4},{1,11},{3,9}... | collective-permute-start | bytes 196616 | tf_op jit(solution)/shard_map/ppermute | solution.py:296
  160.6 1.6 shard_map.81
  (80 shorter events, 55.7 us)
Async XLA Ops:
  1.7 15.0 %collective-permute-start.1 = (bf16[16,64,128]{2,1,0:T(8,128)(2,1)S(1)}, bf16[16,64,128]{2,1,0:T(8,128)(2,1)S(1)}, u32[]{:S(2)}, u32[]{:S(2)}) collective-permute-start(bf16[16,64,128]{2,1,0:T(8,128)(2,1)S(1)} %get-tuple-element.62.inner.own.current.rest_0_), channel_id=1, source_target_pairs={{0,16},{16,32},{32,48},{48,64},{64,80},{80,96},{96,112},{112,128},... | collective-permute-start | bytes 786440 | tf_op jit(solution)/shard_map/ppermute | solution.py:210
  5.0 22.9 %collective-permute-start = (bf16[16,64,128]{2,1,0:T(8,128)(2,1)S(1)}, bf16[16,64,128]{2,1,0:T(8,128)(2,1)S(1)}, u32[]{:S(2)}, u32[]{:S(2)}) collective-permute-start(bf16[16,64,128]{2,1,0:T(8,128)(2,1)S(1)} %get-tuple-element.63.own.current.inner.rest_0_), channel_id=1, source_target_pairs={{16,0},{32,16},{48,32},{64,48},{80,64},{96,80},{112,96},{128,112},... | collective-permute-start | bytes 786440 | tf_op jit(solution)/shard_map/ppermute | solution.py:208
  17.5 13.6 %collective-permute-start.3 = (bf16[16,64,128]{2,1,0:T(8,128)(2,1)S(1)}, bf16[16,64,128]{2,1,0:T(8,128)(2,1)S(1)}, u32[]{:S(2)}, u32[]{:S(2)}) collective-permute-start(bf16[16,64,128]{2,1,0:T(8,128)(2,1)S(1)} %get-tuple-element.69.inner.own), channel_id=1, source_target_pairs={{16,0},{32,16},{48,32},{64,48},{80,64},{96,80},{112,96},{128,112},... | collective-permute-start | bytes 786440 | tf_op jit(solution)/shard_map/ppermute | solution.py:208
  28.7 12.9 %collective-permute-start.2 = (bf16[16,64,128]{2,1,0:T(8,128)(2,1)S(1)}, bf16[16,64,128]{2,1,0:T(8,128)(2,1)S(1)}, u32[]{:S(2)}, u32[]{:S(2)}) collective-permute-start(bf16[16,64,128]{2,1,0:T(8,128)(2,1)S(1)} %get-tuple-element.70.own.inner), channel_id=1, source_target_pairs={{0,16},{16,32},{32,48},{48,64},{64,80},{80,96},{96,112},{112,128},... | collective-permute-start | bytes 786440 | tf_op jit(solution)/shard_map/ppermute | solution.py:210
  31.9 13.4 %collective-permute-start.5 = (bf16[16,64,128]{2,1,0:T(8,128)(2,1)S(1)}, bf16[16,64,128]{2,1,0:T(8,128)(2,1)S(1)}, u32[]{:S(2)}, u32[]{:S(2)}) collective-permute-start(bf16[16,64,128]{2,1,0:T(8,128)(2,1)S(1)} %get-tuple-element.77.inner.own), channel_id=1, source_target_pairs={{0,16},{16,32},{32,48},{48,64},{64,80},{80,96},{96,112},{112,128},... | collective-permute-start | bytes 786440 | tf_op jit(solution)/shard_map/ppermute | solution.py:210
  42.4 8.8 %collective-permute-start.4 = (bf16[16,64,128]{2,1,0:T(8,128)(2,1)S(1)}, bf16[16,64,128]{2,1,0:T(8,128)(2,1)S(1)}, u32[]{:S(2)}, u32[]{:S(2)}) collective-permute-start(bf16[16,64,128]{2,1,0:T(8,128)(2,1)S(1)} %get-tuple-element.78.own.inner), channel_id=1, source_target_pairs={{16,0},{32,16},{48,32},{64,48},{80,64},{96,80},{112,96},{128,112},... | collective-permute-start | bytes 786440 | tf_op jit(solution)/shard_map/ppermute | solution.py:208
  46.1 10.0 %collective-permute-start.7 = (bf16[16,64,128]{2,1,0:T(8,128)(2,1)S(1)}, bf16[16,64,128]{2,1,0:T(8,128)(2,1)S(1)}, u32[]{:S(2)}, u32[]{:S(2)}) collective-permute-start(bf16[16,64,128]{2,1,0:T(8,128)(2,1)S(1)} %get-tuple-element.85.inner.own), channel_id=1, source_target_pairs={{16,0},{32,16},{48,32},{64,48},{80,64},{96,80},{112,96},{128,112},... | collective-permute-start | bytes 786440 | tf_op jit(solution)/shard_map/ppermute | solution.py:208
  52.0 11.2 %collective-permute-start.6 = (bf16[16,64,128]{2,1,0:T(8,128)(2,1)S(1)}, bf16[16,64,128]{2,1,0:T(8,128)(2,1)S(1)}, u32[]{:S(2)}, u32[]{:S(2)}) collective-permute-start(bf16[16,64,128]{2,1,0:T(8,128)(2,1)S(1)} %get-tuple-element.86.own.inner), channel_id=1, source_target_pairs={{0,16},{16,32},{32,48},{48,64},{64,80},{80,96},{96,112},{112,128},... | collective-permute-start | bytes 786440 | tf_op jit(solution)/shard_map/ppermute | solution.py:210
  57.0 12.9 %collective-permute-start.9 = (bf16[16,64,128]{2,1,0:T(8,128)(2,1)S(1)}, bf16[16,64,128]{2,1,0:T(8,128)(2,1)S(1)}, u32[]{:S(2)}, u32[]{:S(2)}) collective-permute-start(bf16[16,64,128]{2,1,0:T(8,128)(2,1)S(1)} %get-tuple-element.93.inner.own), channel_id=1, source_target_pairs={{0,16},{16,32},{32,48},{48,64},{64,80},{80,96},{96,112},{112,128},... | collective-permute-start | bytes 786440 | tf_op jit(solution)/shard_map/ppermute | solution.py:210
  64.0 10.8 %collective-permute-start.8 = (bf16[16,64,128]{2,1,0:T(8,128)(2,1)S(1)}, bf16[16,64,128]{2,1,0:T(8,128)(2,1)S(1)}, u32[]{:S(2)}, u32[]{:S(2)}) collective-permute-start(bf16[16,64,128]{2,1,0:T(8,128)(2,1)S(1)} %get-tuple-element.94.own.inner), channel_id=1, source_target_pairs={{16,0},{32,16},{48,32},{64,48},{80,64},{96,80},{112,96},{128,112},... | collective-permute-start | bytes 786440 | tf_op jit(solution)/shard_map/ppermute | solution.py:208
  70.7 9.1 %collective-permute-start.11 = (bf16[16,64,128]{2,1,0:T(8,128)(2,1)S(1)}, bf16[16,64,128]{2,1,0:T(8,128)(2,1)S(1)}, u32[]{:S(2)}, u32[]{:S(2)}) collective-permute-start(bf16[16,64,128]{2,1,0:T(8,128)(2,1)S(1)} %get-tuple-element.100.inner.own), channel_id=1, source_target_pairs={{16,0},{32,16},{48,32},{64,48},{80,64},{96,80},{112,96},{128,112},... | collective-permute-start | bytes 786440 | tf_op jit(solution)/shard_map/ppermute | solution.py:208
  75.6 11.2 %collective-permute-start.10 = (bf16[16,64,128]{2,1,0:T(8,128)(2,1)S(1)}, bf16[16,64,128]{2,1,0:T(8,128)(2,1)S(1)}, u32[]{:S(2)}, u32[]{:S(2)}) collective-permute-start(bf16[16,64,128]{2,1,0:T(8,128)(2,1)S(1)} %get-tuple-element.101.own.inner), channel_id=1, source_target_pairs={{0,16},{16,32},{32,48},{48,64},{64,80},{80,96},{96,112},{112,128},... | collective-permute-start | bytes 786440 | tf_op jit(solution)/shard_map/ppermute | solution.py:210
  98.6 13.6 %collective-permute-start.20 = (bf16[64,1024]{1,0:T(8,128)(2,1)S(1)}, bf16[64,1024]{1,0:T(8,128)(2,1)S(1)}, u32[]{:S(2)}, u32[]{:S(2)}) collective-permute-start(bf16[64,1024]{1,0:T(8,128)(2,1)S(1)} %bitcast.14), channel_id=1, source_target_pairs={{0,2},{2,0},{1,3},{3,1},{4,6},{6,4},{5,7},{7,5},{8,10},{10,8},{9,1... | collective-permute-start | bytes 393224 | tf_op jit(solution)/shard_map/ppermute | solution.py:214
  102.8 10.6 %collective-permute-start.15 = (bf16[8,64,128]{2,1,0:T(8,128)(2,1)S(1)}, bf16[8,64,128]{2,1,0:T(8,128)(2,1)S(1)}, u32[]{:S(2)}, u32[]{:S(2)}) collective-permute-start(bf16[8,64,128]{2,1,0:T(8,128)(2,1)S(1)} %get-tuple-element.106), channel_id=1, source_target_pairs={{0,12},{2,14},{4,0},{6,2},{8,4},{10,6},{12,8},{14,10},{1,13},{3,15... | collective-permute-start | bytes 393224 | tf_op jit(solution)/shard_map/ppermute | solution.py:289
  104.1 10.6 %collective-permute-start.16 = (bf16[8,64,128]{2,1,0:T(8,128)(2,1)S(1)}, bf16[8,64,128]{2,1,0:T(8,128)(2,1)S(1)}, u32[]{:S(2)}, u32[]{:S(2)}) collective-permute-start(bf16[8,64,128]{2,1,0:T(8,128)(2,1)S(1)} %get-tuple-element.107), channel_id=1, source_target_pairs={{0,14},{2,12},{4,2},{6,0},{8,6},{10,4},{12,10},{14,8},{1,15},{3,13... | collective-permute-start | bytes 393224 | tf_op jit(solution)/shard_map/ppermute | solution.py:289
  107.1 9.0 %collective-permute-start.17 = (bf16[8,64,128]{2,1,0:T(8,128)(2,1)S(1)}, bf16[8,64,128]{2,1,0:T(8,128)(2,1)S(1)}, u32[]{:S(2)}, u32[]{:S(2)}) collective-permute-start(bf16[8,64,128]{2,1,0:T(8,128)(2,1)S(1)} %get-tuple-element.108), channel_id=1, source_target_pairs={{0,8},{2,10},{4,12},{6,14},{8,0},{10,2},{12,4},{14,6},{1,9},{3,11}... | collective-permute-start | bytes 393224 | tf_op jit(solution)/shard_map/ppermute | solution.py:289
  108.9 11.4 %collective-permute-start.18 = (bf16[8,64,128]{2,1,0:T(8,128)(2,1)S(1)}, bf16[8,64,128]{2,1,0:T(8,128)(2,1)S(1)}, u32[]{:S(2)}, u32[]{:S(2)}) collective-permute-start(bf16[8,64,128]{2,1,0:T(8,128)(2,1)S(1)} %get-tuple-element.109), channel_id=1, source_target_pairs={{0,10},{2,8},{4,14},{6,12},{8,2},{10,0},{12,6},{14,4},{1,11},{3,9}... | collective-permute-start | bytes 393224 | tf_op jit(solution)/shard_map/ppermute | solution.py:289
  113.4 32.0 %collective-permute-start.21 = (bf16[2,64,1024]{2,1,0:T(8,128)(2,1)S(1)}, bf16[2,64,1024]{2,1,0:T(8,128)(2,1)S(1)}, u32[]{:S(2)}, u32[]{:S(2)}) collective-permute-start(bf16[2,64,1024]{2,1,0:T(8,128)(2,1)S(1)} %pad_maximum_fusion.ritz), channel_id=1, source_target_pairs={{0,12},{4,0},{8,4},{12,8},{1,13},{5,1},{9,5},{13,9},{2,14},{6,2},{... | collective-permute-start | bytes 786440 | tf_op jit(solution)/shard_map/ppermute | solution.py:219
  114.6 30.7 %collective-permute-start.22 = (bf16[2,64,1024]{2,1,0:T(8,128)(2,1)S(1)}, bf16[2,64,1024]{2,1,0:T(8,128)(2,1)S(1)}, u32[]{:S(2)}, u32[]{:S(2)}) collective-permute-start(bf16[2,64,1024]{2,1,0:T(8,128)(2,1)S(1)} %pad_maximum_fusion.ritz), channel_id=1, source_target_pairs={{0,8},{4,12},{8,0},{12,4},{1,9},{5,13},{9,1},{13,5},{2,10},{6,14},... | collective-permute-start | bytes 786440 | tf_op jit(solution)/shard_map/ppermute | solution.py:219
  116.1 29.3 %collective-permute-start.23 = (bf16[2,64,1024]{2,1,0:T(8,128)(2,1)S(1)}, bf16[2,64,1024]{2,1,0:T(8,128)(2,1)S(1)}, u32[]{:S(2)}, u32[]{:S(2)}) collective-permute-start(bf16[2,64,1024]{2,1,0:T(8,128)(2,1)S(1)} %pad_maximum_fusion.ritz), channel_id=1, source_target_pairs={{0,4},{4,8},{8,12},{12,0},{1,5},{5,9},{9,13},{13,1},{2,6},{6,10},{... | collective-permute-start | bytes 786440 | tf_op jit(solution)/shard_map/ppermute | solution.py:219
  120.4 11.0 %collective-permute-start.13 = (bf16[8,64,128]{2,1,0:T(8,128)(2,1)S(1)}, bf16[8,64,128]{2,1,0:T(8,128)(2,1)S(1)}, u32[]{:S(2)}, u32[]{:S(2)}) collective-permute-start(bf16[8,64,128]{2,1,0:T(8,128)(2,1)S(1)} %get-tuple-element.103), channel_id=1, source_target_pairs={{0,4},{2,6},{4,8},{6,10},{8,12},{10,14},{12,0},{14,2},{1,5},{3,7},... | collective-permute-start | bytes 393224 | tf_op jit(solution)/shard_map/ppermute | solution.py:289
  121.0 13.0 %collective-permute-start.14 = (bf16[8,64,128]{2,1,0:T(8,128)(2,1)S(1)}, bf16[8,64,128]{2,1,0:T(8,128)(2,1)S(1)}, u32[]{:S(2)}, u32[]{:S(2)}) collective-permute-start(bf16[8,64,128]{2,1,0:T(8,128)(2,1)S(1)} %get-tuple-element.104), channel_id=1, source_target_pairs={{0,6},{2,4},{4,10},{6,8},{8,14},{10,12},{12,2},{14,0},{1,7},{3,5},... | collective-permute-start | bytes 393224 | tf_op jit(solution)/shard_map/ppermute | solution.py:289
  134.9 27.3 %all-to-all-start.1 = ((bf16[16,32,128]{2,1,0:T(8,128)(2,1)}), bf16[16,32,128]{2,1,0:T(8,128)(2,1)S(1)}, u32[]{:S(2)}, u32[]{:S(2)}) async-start(bf16[16,32,128]{2,1,0:T(8,128)(2,1)} %shard_map.78), calls=%async_computation.1 | async-start | bytes 262144 | tf_op jit(solution)/shard_map/all_to_all | solution.py:301
  146.1 8.9 %collective-permute-start.24 = (bf16[4,64,128]{2,1,0:T(8,128)(2,1)S(1)}, bf16[4,64,128]{2,1,0:T(8,128)(2,1)S(1)}, u32[]{:S(2)}, u32[]{:S(2)}) collective-permute-start(bf16[4,64,128]{2,1,0:T(8,128)(2,1)S(1)} %get-tuple-element.113), channel_id=1, source_target_pairs={{0,2},{2,0},{4,6},{6,4},{8,10},{10,8},{12,14},{14,12},{1,3},{3,1},... | collective-permute-start | bytes 196616 | tf_op jit(solution)/shard_map/ppermute | solution.py:296
  (10 other events, 68.6 us)

commit v5 on v4

--- a/solution.py
+++ b/solution.py
@@ -150,19 +150,31 @@
     held, cols = outs[0].shape[0], outs[0].shape[1]
     for away, source in enumerate((ritz, ritz_next, ritz_far, ritz_back)):
         turned = product(source[...].reshape(2 * cols, -1), rows[...], PLAIN).astype(jnp.bfloat16)
-        for q in range(2):
+        for el in range(held):
+            outs[away][el] = turned[:cols, el * NB : (el + 1) * NB]
+            outs[4][away, el] = turned[cols:, el * NB : (el + 1) * NB]
+
+
+def join_kernel(crossed, *refs):
+    count = len(refs) // 2
+    for away in range(count):
+        refs[count + away][0] = refs[away][...]
+        refs[count + away][1] = crossed[away + 1]
+
+
+def collect_kernel(around, place, here, crossed, *refs):
+    pieces, out = refs[:-1], refs[-1]
+    held = here.shape[0]
+    for q in range(2):
+        near = place[1] if q == 0 else 1 - place[1]
+        for away in range(around):
+            line = lax.rem(place[0] + around - away, around) * 2 + near
             for el in range(held):
-                outs[2 * away + q][el] = turned[q * cols : (q + 1) * cols, el * NB : (el + 1) * NB]
-
-
-def collect_kernel(around, place, *refs):
-    pieces, out = refs[:-1], refs[-1]
-    held = pieces[0].shape[0]
-    for index, piece in enumerate(pieces):
-        away, q = index // 2, index % 2
-        line = lax.rem(place[0] + around - away, around) * 2 + (place[1] if q == 0 else 1 - place[1])
-        for el in range(held):
-            out[line * held + el] = piece[el].astype(jnp.float32)
+                if away:
+                    piece = pieces[away - 1][q, el]
+                else:
+                    piece = crossed[0, el] if q else here[el]
+                out[line * held + el] = piece.astype(jnp.float32)
 
 
 def margin_rows_kernel(*refs):
@@ -270,7 +282,7 @@
     block = jax.ShapeDtypeStruct((chips, cols, NB), jnp.bfloat16)
     rows = None
     parts = []
-    for away in (1, around - 1, 2, 0):
+    for away in (2, 1, around - 1, 0):
         if rows is None:
             rows, *blocks = call(
                 functools.partial(first_part_kernel, around, away), (place, mine, theirs),
@@ -287,21 +299,27 @@
                 parts.append(blocks[0])
                 continue
             parts.append(lax.ppermute(blocks[q], CHIP, to_chip(away, q)))
-    turned = call(
+    piece = jax.ShapeDtypeStruct((held, cols, NB), jnp.bfloat16)
+    *turned, across = call(
         turn_kernel, (rows, shared["pair"], shared[around - 1], shared[2], shared[1]),
-        (jax.ShapeDtypeStruct((held, cols, NB), jnp.bfloat16),) * chips, flops, 16,
-    )
-    pieces = [turned[0]]
-    for index in range(1, chips):
-        pieces.append(lax.ppermute(turned[index], CHIP, to_chip(index // 2, index % 2)))
+        (piece,) * around + (piece.update(shape=(around, *piece.shape)),), flops, 16,
+    )
+    crossed = lax.ppermute(across, "yl", [(0, 1), (1, 0)])
     total = call(
         margin_rows_kernel, parts,
         jax.ShapeDtypeStruct((slabs, cols // 2, 2 * cols), jnp.bfloat16), small, 12,
     )
     total = lax.all_to_all(total, ELEM, 0, 0, tiled=True)
+    joined = call(
+        join_kernel, (crossed, *turned[1:]),
+        (piece.update(shape=(2, *piece.shape)),) * (around - 1), small, 12,
+    )
+    pieces = []
+    for away in range(1, around):
+        pieces.append(lax.ppermute(joined[away - 1], "x", [(i, (i + away) % around) for i in range(around)]))
     rotated = call(
-        functools.partial(collect_kernel, around), (place, *pieces),
-        jax.ShapeDtypeStruct((2 * PLANE, cols, NB), jnp.float32), small, 12, (), [SMEM] + [VMEM] * chips,
+        functools.partial(collect_kernel, around), (place, turned[0], crossed, *pieces),
+        jax.ShapeDtypeStruct((2 * PLANE, cols, NB), jnp.float32), small, 12, (), [SMEM] + [VMEM] * (around + 1),
     )
     margin = call(
         functools.partial(margin_kernel, 1.0 / rows_total), (total,),

time: 166 us -> 167 us (level); the launches traced: 163 us -> 166 us
  waiting for transfers between devices: 41.2 us -> 48 us
  starting transfers between devices: 69.1 us -> 65 us
    all_to_all x1, waiting for transfers between devices: 0.01 us -> 6.12 us  [whole(): total = lax.all_to_all(total, ELEM, 0, 0, tiled=True)]
    ppermute x1, waiting for transfers between devices: 0.01 us -> 5.6 us  [whole(): across = lax.ppermute(source, 'yl', [(0, 1), (1, 0)])]
    ppermute x7 -> x4, waiting for transfers between devices: 4.4 us -> 0.01 us  [the longest x3 0.01 us: whole(): lax.ppermute(joined[away - 1], 'x', [(i, (i + away) % around) for i in ra...]
    ppermute x3, waiting for transfers between devices: 0.01 us -> 3.97 us  [whole(): lax.ppermute(shared['pair'], 'x', [(i, (i + shift) % around) for i in ran...]
    ppermute x7 -> x4, starting transfers between devices: 10.1 us -> 6.2 us  [the longest x3 4.95 us: whole(): lax.ppermute(joined[away - 1], 'x', [(i, (i + away) % around) for i in ra...]
    ppermute x7, waiting for transfers between devices: 12.6 us -> 9.63 us  [whole(): parts.append(lax.ppermute(blocks[q], CHIP, to_chip(away, q)))]
    ppermute x3, starting transfers between devices: 6.98 us -> 4.91 us  [whole(): lax.ppermute(shared['pair'], 'x', [(i, (i + shift) % around) for i in ran...]
    ppermute x7, starting transfers between devices: 9.55 us -> 11.3 us  [whole(): parts.append(lax.ppermute(blocks[q], CHIP, to_chip(away, q)))]
  transfers between devices with their start and end apart: 32 -> 29, of which waited for: 15 -> 12; matrix products, arithmetic and copies ran while one was open for 0% -> 0% of each run, Pallas kernels for 21% -> 21%
where the time goes in v5:
time: 167 us; the launch traced here: 166 us
  starting transfers between devices  65 us (39%)
  waiting for transfers between devices  48 us (29%)
  Pallas kernels  36.5 us (22%)
  blocking collectives  11 us (7%)
  local copies, waits for them, and re-layouts  4.15 us (2%)
    pallas_call x33, Pallas kernels, call(): pl.pallas_call(kernel, out_shape=out_shape, in_specs=in_specs or [VMEM] *...  36.5 us
    ppermute x6, starting transfers between devices, send(): halo['b', k] = lax.ppermute(val['a', k], ELEM, down)  25.5 us
    ppermute x6, waiting for transfers between devices, send(): halo['a', k] = lax.ppermute(val['b', k], ELEM, up)  17.8 us
    ppermute x7, starting transfers between devices, whole(): parts.append(lax.ppermute(blocks[q], CHIP, to_chip(away, q)))  11.3 us
    all_to_all x1, blocking collectives, whole(): mine = lax.all_to_all(filtered, CHIP, 0, 0, tiled=True)  11 us
    all_to_all x1, starting transfers between devices, whole(): total = lax.all_to_all(total, ELEM, 0, 0, tiled=True)  10.5 us
    ppermute x7, waiting for transfers between devices, whole(): parts.append(lax.ppermute(blocks[q], CHIP, to_chip(away, q)))  9.63 us
    ppermute x6, starting transfers between devices, send(): halo['a', k] = lax.ppermute(val['b', k], ELEM, up)  6.23 us
  transfers between devices with their start and end apart: 29, of which 12 were waited for; matrix products, arithmetic and copies ran while one was open for 0% of the time, Pallas kernels for 21%

profile of v5, /device:TPU:4, one launch (start us, length us, event | category | flops | bytes accessed | tf_op | source)
XLA Modules:
  0.0 165.6 jit_solution(17007956605590620146)
XLA Ops:
  1.7 3.3 %collective-permute-start.1 = (bf16[16,64,128]{2,1,0:T(8,128)(2,1)S(1)}, bf16[16,64,128]{2,1,0:T(8,128)(2,1)S(1)}, u32[]{:S(2)}, u32[]{:S(2)}) collective-permute-start(bf16[16,64,128]{2,1,0:T(8,128)(2,1)S(1)} %get-tuple-element.62.inner.own.current.rest_0_), channel_id=1, source_target_pairs={{0,16},{16,32},{32,48},{48,64},{64,80},{80,96},{96,112},{112,128},... | collective-permute-start | bytes 786440 | tf_op jit(solution)/shard_map/ppermute | solution.py:222
  5.0 5.4 %collective-permute-start = (bf16[16,64,128]{2,1,0:T(8,128)(2,1)S(1)}, bf16[16,64,128]{2,1,0:T(8,128)(2,1)S(1)}, u32[]{:S(2)}, u32[]{:S(2)}) collective-permute-start(bf16[16,64,128]{2,1,0:T(8,128)(2,1)S(1)} %get-tuple-element.63.own.current.inner.rest_0_), channel_id=1, source_target_pairs={{16,0},{32,16},{48,32},{64,48},{80,64},{96,80},{112,96},{128,112},... | collective-permute-start | bytes 786440 | tf_op jit(solution)/shard_map/ppermute | solution.py:220
  10.4 3.1 %copy-done = bf16[32,7,128,128]{3,2,1,0:T(8,128)(2,1)S(1)} copy-done((bf16[32,7,128,128]{3,2,1,0:T(8,128)(2,1)S(1)}, bf16[32,7,128,128]{3,2,1,0:T(8,128)(2,1)}, u32[]{:S(2)}) %copy-start) | copy-done | bytes 7340056
  17.5 8.8 %collective-permute-start.3 = (bf16[16,64,128]{2,1,0:T(8,128)(2,1)S(1)}, bf16[16,64,128]{2,1,0:T(8,128)(2,1)S(1)}, u32[]{:S(2)}, u32[]{:S(2)}) collective-permute-start(bf16[16,64,128]{2,1,0:T(8,128)(2,1)S(1)} %get-tuple-element.69.inner.own), channel_id=1, source_target_pairs={{16,0},{32,16},{48,32},{64,48},{80,64},{96,80},{112,96},{128,112},... | collective-permute-start | bytes 786440 | tf_op jit(solution)/shard_map/ppermute | solution.py:220
  33.5 8.1 %collective-permute-done.2.halo = bf16[16,64,128]{2,1,0:T(8,128)(2,1)S(1)} collective-permute-done((bf16[16,64,128]{2,1,0:T(8,128)(2,1)S(1)}, bf16[16,64,128]{2,1,0:T(8,128)(2,1)S(1)}, u32[]{:S(2)}, u32[]{:S(2)}) %collective-permute-start.2) | collective-permute-done | bytes 262176 | tf_op jit(solution)/shard_map/ppermute | solution.py:222
  46.1 3.1 %collective-permute-start.7 = (bf16[16,64,128]{2,1,0:T(8,128)(2,1)S(1)}, bf16[16,64,128]{2,1,0:T(8,128)(2,1)S(1)}, u32[]{:S(2)}, u32[]{:S(2)}) collective-permute-start(bf16[16,64,128]{2,1,0:T(8,128)(2,1)S(1)} %get-tuple-element.85.inner.own), channel_id=1, source_target_pairs={{16,0},{32,16},{48,32},{64,48},{80,64},{96,80},{112,96},{128,112},... | collective-permute-start | bytes 786440 | tf_op jit(solution)/shard_map/ppermute | solution.py:220
  53.8 2.4 %collective-permute-done.7.halo = bf16[16,64,128]{2,1,0:T(8,128)(2,1)S(1)} collective-permute-done((bf16[16,64,128]{2,1,0:T(8,128)(2,1)S(1)}, bf16[16,64,128]{2,1,0:T(8,128)(2,1)S(1)}, u32[]{:S(2)}, u32[]{:S(2)}) %collective-permute-start.7) | collective-permute-done | bytes 262176 | tf_op jit(solution)/shard_map/ppermute | solution.py:220
  59.8 3.4 %collective-permute-done.6.halo = bf16[16,64,128]{2,1,0:T(8,128)(2,1)S(1)} collective-permute-done((bf16[16,64,128]{2,1,0:T(8,128)(2,1)S(1)}, bf16[16,64,128]{2,1,0:T(8,128)(2,1)S(1)}, u32[]{:S(2)}, u32[]{:S(2)}) %collective-permute-start.6) | collective-permute-done | bytes 262176 | tf_op jit(solution)/shard_map/ppermute | solution.py:222
  64.0 4.2 %collective-permute-start.8 = (bf16[16,64,128]{2,1,0:T(8,128)(2,1)S(1)}, bf16[16,64,128]{2,1,0:T(8,128)(2,1)S(1)}, u32[]{:S(2)}, u32[]{:S(2)}) collective-permute-start(bf16[16,64,128]{2,1,0:T(8,128)(2,1)S(1)} %get-tuple-element.94.own.inner), channel_id=1, source_target_pairs={{16,0},{32,16},{48,32},{64,48},{80,64},{96,80},{112,96},{128,112},... | collective-permute-start | bytes 786440 | tf_op jit(solution)/shard_map/ppermute | solution.py:220
  70.7 2.6 %collective-permute-start.11 = (bf16[16,64,128]{2,1,0:T(8,128)(2,1)S(1)}, bf16[16,64,128]{2,1,0:T(8,128)(2,1)S(1)}, u32[]{:S(2)}, u32[]{:S(2)}) collective-permute-start(bf16[16,64,128]{2,1,0:T(8,128)(2,1)S(1)} %get-tuple-element.100.inner.own), channel_id=1, source_target_pairs={{16,0},{32,16},{48,32},{64,48},{80,64},{96,80},{112,96},{128,112},... | collective-permute-start | bytes 786440 | tf_op jit(solution)/shard_map/ppermute | solution.py:220
  82.2 4.7 %collective-permute-done.10.halo = bf16[16,64,128]{2,1,0:T(8,128)(2,1)S(1)} collective-permute-done((bf16[16,64,128]{2,1,0:T(8,128)(2,1)S(1)}, bf16[16,64,128]{2,1,0:T(8,128)(2,1)S(1)}, u32[]{:S(2)}, u32[]{:S(2)}) %collective-permute-start.10) | collective-permute-done | bytes 262176 | tf_op jit(solution)/shard_map/ppermute | solution.py:222
  87.6 11.0 %all_to_all.10 = bf16[32,64,128]{2,1,0:T(8,128)(2,1)S(1)} all-to-all(bf16[32,64,128]{2,1,0:T(8,128)(2,1)S(1)} %shard_map.73), channel_id=1, replica_groups=mesh['z'=8,'yh'=2,'x'=4,'yl'=2,'c'=2] {'x','yl'}, dimensions={0} | all-to-all | bytes 1048576 | tf_op jit(solution)/shard_map/all_to_all | solution.py:270
  98.9 5.6 %collective-permute-done.20 = bf16[64,1024]{1,0:T(8,128)(2,1)S(1)} collective-permute-done((bf16[64,1024]{1,0:T(8,128)(2,1)S(1)}, bf16[64,1024]{1,0:T(8,128)(2,1)S(1)}, u32[]{:S(2)}, u32[]{:S(2)}) %collective-permute-start.20) | collective-permute-done | bytes 131104 | tf_op jit(solution)/shard_map/ppermute | solution.py:226
  105.9 2.1 %collective-permute-start.22 = (bf16[2,64,1024]{2,1,0:T(8,128)(2,1)S(1)}, bf16[2,64,1024]{2,1,0:T(8,128)(2,1)S(1)}, u32[]{:S(2)}, u32[]{:S(2)}) collective-permute-start(bf16[2,64,1024]{2,1,0:T(8,128)(2,1)S(1)} %pad_maximum_fusion.ritz), channel_id=1, source_target_pairs={{0,8},{4,12},{8,0},{12,4},{1,9},{5,13},{9,1},{13,5},{2,10},{6,14},... | collective-permute-start | bytes 786440 | tf_op jit(solution)/shard_map/ppermute | solution.py:231
  114.7 2.0 %collective-permute-start.17 = (bf16[8,64,128]{2,1,0:T(8,128)(2,1)S(1)}, bf16[8,64,128]{2,1,0:T(8,128)(2,1)S(1)}, u32[]{:S(2)}, u32[]{:S(2)}) collective-permute-start(bf16[8,64,128]{2,1,0:T(8,128)(2,1)S(1)} %get-tuple-element.108), channel_id=1, source_target_pairs={{0,12},{2,14},{4,0},{6,2},{8,4},{10,6},{12,8},{14,10},{1,13},{3,15... | collective-permute-start | bytes 393224 | tf_op jit(solution)/shard_map/ppermute | solution.py:301
  116.7 4.0 %collective-permute-done.23.ritz_back = bf16[2,64,1024]{2,1,0:T(8,128)(2,1)S(1)} collective-permute-done((bf16[2,64,1024]{2,1,0:T(8,128)(2,1)S(1)}, bf16[2,64,1024]{2,1,0:T(8,128)(2,1)S(1)}, u32[]{:S(2)}, u32[]{:S(2)}) %collective-permute-start.23) | collective-permute-done | bytes 262176 | tf_op jit(solution)/shard_map/ppermute | solution.py:231
  123.7 2.5 %collective-permute-start.18 = (bf16[8,64,128]{2,1,0:T(8,128)(2,1)S(1)}, bf16[8,64,128]{2,1,0:T(8,128)(2,1)S(1)}, u32[]{:S(2)}, u32[]{:S(2)}) collective-permute-start(bf16[8,64,128]{2,1,0:T(8,128)(2,1)S(1)} %get-tuple-element.109), channel_id=1, source_target_pairs={{0,14},{2,12},{4,2},{6,0},{8,6},{10,4},{12,10},{14,8},{1,15},{3,13... | collective-permute-start | bytes 393224 | tf_op jit(solution)/shard_map/ppermute | solution.py:301
  127.4 2.1 %collective-permute-start.13 = (bf16[8,64,128]{2,1,0:T(8,128)(2,1)S(1)}, bf16[8,64,128]{2,1,0:T(8,128)(2,1)S(1)}, u32[]{:S(2)}, u32[]{:S(2)}) collective-permute-start(bf16[8,64,128]{2,1,0:T(8,128)(2,1)S(1)} %get-tuple-element.103), channel_id=1, source_target_pairs={{0,8},{2,10},{4,12},{6,14},{8,0},{10,2},{12,4},{14,6},{1,9},{3,11}... | collective-permute-start | bytes 393224 | tf_op jit(solution)/shard_map/ppermute | solution.py:301
  129.4 1.8 %collective-permute-start.14 = (bf16[8,64,128]{2,1,0:T(8,128)(2,1)S(1)}, bf16[8,64,128]{2,1,0:T(8,128)(2,1)S(1)}, u32[]{:S(2)}, u32[]{:S(2)}) collective-permute-start(bf16[8,64,128]{2,1,0:T(8,128)(2,1)S(1)} %get-tuple-element.104), channel_id=1, source_target_pairs={{0,10},{2,8},{4,14},{6,12},{8,2},{10,0},{12,6},{14,4},{1,11},{3,9}... | collective-permute-start | bytes 393224 | tf_op jit(solution)/shard_map/ppermute | solution.py:301
  131.2 9.6 %collective-permute-done.19.refs_7_ = bf16[8,64,128]{2,1,0:T(8,128)(2,1)S(1)} collective-permute-done((bf16[8,64,128]{2,1,0:T(8,128)(2,1)S(1)}, bf16[8,64,128]{2,1,0:T(8,128)(2,1)S(1)}, u32[]{:S(2)}, u32[]{:S(2)}) %collective-permute-start.19) | collective-permute-done | bytes 131104 | tf_op jit(solution)/shard_map/ppermute | solution.py:301
  141.7 10.5 %all-to-all-start.1 = ((bf16[16,32,128]{2,1,0:T(8,128)(2,1)}), bf16[16,32,128]{2,1,0:T(8,128)(2,1)S(1)}, u32[]{:S(2)}, u32[]{:S(2)}) async-start(bf16[16,32,128]{2,1,0:T(8,128)(2,1)} %shard_map.78), calls=%async_computation.1 | async-start | bytes 262144 | tf_op jit(solution)/shard_map/all_to_all | solution.py:312
  152.3 2.3 %collective-permute-start.26 = (bf16[2,4,64,128]{3,2,1,0:T(8,128)(2,1)S(1)}, bf16[2,4,64,128]{3,2,1,0:T(8,128)(2,1)S(1)}, u32[]{:S(2)}, u32[]{:S(2)}) collective-permute-start(bf16[2,4,64,128]{3,2,1,0:T(8,128)(2,1)S(1)} %get-tuple-element.118), channel_id=1, source_target_pairs={{0,8},{4,12},{8,0},{12,4},{1,9},{5,13},{9,1},{13,5},{2,10},{6,14},... | collective-permute-start | bytes 393224 | tf_op jit(solution)/shard_map/ppermute | solution.py:319
  154.7 2.5 %collective-permute-start.27 = (bf16[2,4,64,128]{3,2,1,0:T(8,128)(2,1)S(1)}, bf16[2,4,64,128]{3,2,1,0:T(8,128)(2,1)S(1)}, u32[]{:S(2)}, u32[]{:S(2)}) collective-permute-start(bf16[2,4,64,128]{3,2,1,0:T(8,128)(2,1)S(1)} %get-tuple-element.119), channel_id=1, source_target_pairs={{0,12},{4,0},{8,4},{12,8},{1,13},{5,1},{9,5},{13,9},{2,14},{6,2},{... | collective-permute-start | bytes 393224 | tf_op jit(solution)/shard_map/ppermute | solution.py:319
  157.2 6.1 %all-to-all-done.1.got = bf16[16,32,128]{2,1,0:T(8,128)(2,1)S(1)} async-done(((bf16[16,32,128]{2,1,0:T(8,128)(2,1)}), bf16[16,32,128]{2,1,0:T(8,128)(2,1)S(1)}, u32[]{:S(2)}, u32[]{:S(2)}) %all-to-all-start.1) | async-done | bytes 131104 | tf_op jit(solution)/shard_map/all_to_all | solution.py:312
  (75 shorter events, 53.5 us)
Async XLA Ops:
  1.7 15.0 %collective-permute-start.1 = (bf16[16,64,128]{2,1,0:T(8,128)(2,1)S(1)}, bf16[16,64,128]{2,1,0:T(8,128)(2,1)S(1)}, u32[]{:S(2)}, u32[]{:S(2)}) collective-permute-start(bf16[16,64,128]{2,1,0:T(8,128)(2,1)S(1)} %get-tuple-element.62.inner.own.current.rest_0_), channel_id=1, source_target_pairs={{0,16},{16,32},{32,48},{48,64},{64,80},{80,96},{96,112},{112,128},... | collective-permute-start | bytes 786440 | tf_op jit(solution)/shard_map/ppermute | solution.py:222
  5.0 22.9 %collective-permute-start = (bf16[16,64,128]{2,1,0:T(8,128)(2,1)S(1)}, bf16[16,64,128]{2,1,0:T(8,128)(2,1)S(1)}, u32[]{:S(2)}, u32[]{:S(2)}) collective-permute-start(bf16[16,64,128]{2,1,0:T(8,128)(2,1)S(1)} %get-tuple-element.63.own.current.inner.rest_0_), channel_id=1, source_target_pairs={{16,0},{32,16},{48,32},{64,48},{80,64},{96,80},{112,96},{128,112},... | collective-permute-start | bytes 786440 | tf_op jit(solution)/shard_map/ppermute | solution.py:220
  17.5 13.6 %collective-permute-start.3 = (bf16[16,64,128]{2,1,0:T(8,128)(2,1)S(1)}, bf16[16,64,128]{2,1,0:T(8,128)(2,1)S(1)}, u32[]{:S(2)}, u32[]{:S(2)}) collective-permute-start(bf16[16,64,128]{2,1,0:T(8,128)(2,1)S(1)} %get-tuple-element.69.inner.own), channel_id=1, source_target_pairs={{16,0},{32,16},{48,32},{64,48},{80,64},{96,80},{112,96},{128,112},... | collective-permute-start | bytes 786440 | tf_op jit(solution)/shard_map/ppermute | solution.py:220
  28.7 12.9 %collective-permute-start.2 = (bf16[16,64,128]{2,1,0:T(8,128)(2,1)S(1)}, bf16[16,64,128]{2,1,0:T(8,128)(2,1)S(1)}, u32[]{:S(2)}, u32[]{:S(2)}) collective-permute-start(bf16[16,64,128]{2,1,0:T(8,128)(2,1)S(1)} %get-tuple-element.70.own.inner), channel_id=1, source_target_pairs={{0,16},{16,32},{32,48},{48,64},{64,80},{80,96},{96,112},{112,128},... | collective-permute-start | bytes 786440 | tf_op jit(solution)/shard_map/ppermute | solution.py:222
  31.9 13.4 %collective-permute-start.5 = (bf16[16,64,128]{2,1,0:T(8,128)(2,1)S(1)}, bf16[16,64,128]{2,1,0:T(8,128)(2,1)S(1)}, u32[]{:S(2)}, u32[]{:S(2)}) collective-permute-start(bf16[16,64,128]{2,1,0:T(8,128)(2,1)S(1)} %get-tuple-element.77.inner.own), channel_id=1, source_target_pairs={{0,16},{16,32},{32,48},{48,64},{64,80},{80,96},{96,112},{112,128},... | collective-permute-start | bytes 786440 | tf_op jit(solution)/shard_map/ppermute | solution.py:222
  46.1 10.0 %collective-permute-start.7 = (bf16[16,64,128]{2,1,0:T(8,128)(2,1)S(1)}, bf16[16,64,128]{2,1,0:T(8,128)(2,1)S(1)}, u32[]{:S(2)}, u32[]{:S(2)}) collective-permute-start(bf16[16,64,128]{2,1,0:T(8,128)(2,1)S(1)} %get-tuple-element.85.inner.own), channel_id=1, source_target_pairs={{16,0},{32,16},{48,32},{64,48},{80,64},{96,80},{112,96},{128,112},... | collective-permute-start | bytes 786440 | tf_op jit(solution)/shard_map/ppermute | solution.py:220
  52.0 11.2 %collective-permute-start.6 = (bf16[16,64,128]{2,1,0:T(8,128)(2,1)S(1)}, bf16[16,64,128]{2,1,0:T(8,128)(2,1)S(1)}, u32[]{:S(2)}, u32[]{:S(2)}) collective-permute-start(bf16[16,64,128]{2,1,0:T(8,128)(2,1)S(1)} %get-tuple-element.86.own.inner), channel_id=1, source_target_pairs={{0,16},{16,32},{32,48},{48,64},{64,80},{80,96},{96,112},{112,128},... | collective-permute-start | bytes 786440 | tf_op jit(solution)/shard_map/ppermute | solution.py:222
  57.0 12.9 %collective-permute-start.9 = (bf16[16,64,128]{2,1,0:T(8,128)(2,1)S(1)}, bf16[16,64,128]{2,1,0:T(8,128)(2,1)S(1)}, u32[]{:S(2)}, u32[]{:S(2)}) collective-permute-start(bf16[16,64,128]{2,1,0:T(8,128)(2,1)S(1)} %get-tuple-element.93.inner.own), channel_id=1, source_target_pairs={{0,16},{16,32},{32,48},{48,64},{64,80},{80,96},{96,112},{112,128},... | collective-permute-start | bytes 786440 | tf_op jit(solution)/shard_map/ppermute | solution.py:222
  64.0 10.8 %collective-permute-start.8 = (bf16[16,64,128]{2,1,0:T(8,128)(2,1)S(1)}, bf16[16,64,128]{2,1,0:T(8,128)(2,1)S(1)}, u32[]{:S(2)}, u32[]{:S(2)}) collective-permute-start(bf16[16,64,128]{2,1,0:T(8,128)(2,1)S(1)} %get-tuple-element.94.own.inner), channel_id=1, source_target_pairs={{16,0},{32,16},{48,32},{64,48},{80,64},{96,80},{112,96},{128,112},... | collective-permute-start | bytes 786440 | tf_op jit(solution)/shard_map/ppermute | solution.py:220
  75.6 11.2 %collective-permute-start.10 = (bf16[16,64,128]{2,1,0:T(8,128)(2,1)S(1)}, bf16[16,64,128]{2,1,0:T(8,128)(2,1)S(1)}, u32[]{:S(2)}, u32[]{:S(2)}) collective-permute-start(bf16[16,64,128]{2,1,0:T(8,128)(2,1)S(1)} %get-tuple-element.101.own.inner), channel_id=1, source_target_pairs={{0,16},{16,32},{32,48},{48,64},{64,80},{80,96},{96,112},{112,128},... | collective-permute-start | bytes 786440 | tf_op jit(solution)/shard_map/ppermute | solution.py:222
  98.6 10.9 %collective-permute-start.12 = (bf16[8,4,64,128]{3,2,1,0:T(8,128)(2,1)S(1)}, bf16[8,4,64,128]{3,2,1,0:T(8,128)(2,1)S(1)}, u32[]{:S(2)}, u32[]{:S(2)}) collective-permute-start(bf16[8,4,64,128]{3,2,1,0:T(8,128)(2,1)S(1)} %bitcast.10), channel_id=1, source_target_pairs={{0,1},{1,0},{2,3},{3,2},{4,5},{5,4},{6,7},{7,6},{8,9},{9,8},{10,11... | collective-permute-start | bytes 1572872 | tf_op jit(solution)/shard_map/ppermute | solution.py:272
  104.6 10.1 %collective-permute-start.21 = (bf16[2,64,1024]{2,1,0:T(8,128)(2,1)S(1)}, bf16[2,64,1024]{2,1,0:T(8,128)(2,1)S(1)}, u32[]{:S(2)}, u32[]{:S(2)}) collective-permute-start(bf16[2,64,1024]{2,1,0:T(8,128)(2,1)S(1)} %pad_maximum_fusion.ritz), channel_id=1, source_target_pairs={{0,12},{4,0},{8,4},{12,8},{1,13},{5,1},{9,5},{13,9},{2,14},{6,2},{... | collective-permute-start | bytes 786440 | tf_op jit(solution)/shard_map/ppermute | solution.py:231
  105.9 10.8 %collective-permute-start.22 = (bf16[2,64,1024]{2,1,0:T(8,128)(2,1)S(1)}, bf16[2,64,1024]{2,1,0:T(8,128)(2,1)S(1)}, u32[]{:S(2)}, u32[]{:S(2)}) collective-permute-start(bf16[2,64,1024]{2,1,0:T(8,128)(2,1)S(1)} %pad_maximum_fusion.ritz), channel_id=1, source_target_pairs={{0,8},{4,12},{8,0},{12,4},{1,9},{5,13},{9,1},{13,5},{2,10},{6,14},... | collective-permute-start | bytes 786440 | tf_op jit(solution)/shard_map/ppermute | solution.py:231
  108.0 12.7 %collective-permute-start.23 = (bf16[2,64,1024]{2,1,0:T(8,128)(2,1)S(1)}, bf16[2,64,1024]{2,1,0:T(8,128)(2,1)S(1)}, u32[]{:S(2)}, u32[]{:S(2)}) collective-permute-start(bf16[2,64,1024]{2,1,0:T(8,128)(2,1)S(1)} %pad_maximum_fusion.ritz), channel_id=1, source_target_pairs={{0,4},{4,8},{8,12},{12,0},{1,5},{5,9},{9,13},{13,1},{2,6},{6,10},{... | collective-permute-start | bytes 786440 | tf_op jit(solution)/shard_map/ppermute | solution.py:231
  111.8 14.4 %collective-permute-start.15 = (bf16[8,64,128]{2,1,0:T(8,128)(2,1)S(1)}, bf16[8,64,128]{2,1,0:T(8,128)(2,1)S(1)}, u32[]{:S(2)}, u32[]{:S(2)}) collective-permute-start(bf16[8,64,128]{2,1,0:T(8,128)(2,1)S(1)} %get-tuple-element.106), channel_id=1, source_target_pairs={{0,4},{2,6},{4,8},{6,10},{8,12},{10,14},{12,0},{14,2},{1,5},{3,7},... | collective-permute-start | bytes 393224 | tf_op jit(solution)/shard_map/ppermute | solution.py:301
  114.0 13.4 %collective-permute-start.16 = (bf16[8,64,128]{2,1,0:T(8,128)(2,1)S(1)}, bf16[8,64,128]{2,1,0:T(8,128)(2,1)S(1)}, u32[]{:S(2)}, u32[]{:S(2)}) collective-permute-start(bf16[8,64,128]{2,1,0:T(8,128)(2,1)S(1)} %get-tuple-element.107), channel_id=1, source_target_pairs={{0,6},{2,4},{4,10},{6,8},{8,14},{10,12},{12,2},{14,0},{1,7},{3,5},... | collective-permute-start | bytes 393224 | tf_op jit(solution)/shard_map/ppermute | solution.py:301
  114.7 14.8 %collective-permute-start.17 = (bf16[8,64,128]{2,1,0:T(8,128)(2,1)S(1)}, bf16[8,64,128]{2,1,0:T(8,128)(2,1)S(1)}, u32[]{:S(2)}, u32[]{:S(2)}) collective-permute-start(bf16[8,64,128]{2,1,0:T(8,128)(2,1)S(1)} %get-tuple-element.108), channel_id=1, source_target_pairs={{0,12},{2,14},{4,0},{6,2},{8,4},{10,6},{12,8},{14,10},{1,13},{3,15... | collective-permute-start | bytes 393224 | tf_op jit(solution)/shard_map/ppermute | solution.py:301
  121.4 30.8 %collective-permute-start.24 = (bf16[4,4,64,128]{3,2,1,0:T(8,128)(2,1)S(1)}, bf16[4,4,64,128]{3,2,1,0:T(8,128)(2,1)S(1)}, u32[]{:S(2)}, u32[]{:S(2)}) collective-permute-start(bf16[4,4,64,128]{3,2,1,0:T(8,128)(2,1)S(1)} %get-tuple-element.113), channel_id=1, source_target_pairs={{0,2},{2,0},{1,3},{3,1},{4,6},{6,4},{5,7},{7,5},{8,10},{10,8},{9,1... | collective-permute-start | bytes 786440 | tf_op jit(solution)/shard_map/ppermute | solution.py:307
  126.2 14.6 %collective-permute-start.19 = (bf16[8,64,128]{2,1,0:T(8,128)(2,1)S(1)}, bf16[8,64,128]{2,1,0:T(8,128)(2,1)S(1)}, u32[]{:S(2)}, u32[]{:S(2)}) collective-permute-start(bf16[8,64,128]{2,1,0:T(8,128)(2,1)S(1)} %get-tuple-element.111), channel_id=1, source_target_pairs={{0,2},{2,0},{4,6},{6,4},{8,10},{10,8},{12,14},{14,12},{1,3},{3,1},... | collective-permute-start | bytes 393224 | tf_op jit(solution)/shard_map/ppermute | solution.py:301
  127.4 13.5 %collective-permute-start.13 = (bf16[8,64,128]{2,1,0:T(8,128)(2,1)S(1)}, bf16[8,64,128]{2,1,0:T(8,128)(2,1)S(1)}, u32[]{:S(2)}, u32[]{:S(2)}) collective-permute-start(bf16[8,64,128]{2,1,0:T(8,128)(2,1)S(1)} %get-tuple-element.103), channel_id=1, source_target_pairs={{0,8},{2,10},{4,12},{6,14},{8,0},{10,2},{12,4},{14,6},{1,9},{3,11}... | collective-permute-start | bytes 393224 | tf_op jit(solution)/shard_map/ppermute | solution.py:301
  129.4 11.4 %collective-permute-start.14 = (bf16[8,64,128]{2,1,0:T(8,128)(2,1)S(1)}, bf16[8,64,128]{2,1,0:T(8,128)(2,1)S(1)}, u32[]{:S(2)}, u32[]{:S(2)}) collective-permute-start(bf16[8,64,128]{2,1,0:T(8,128)(2,1)S(1)} %get-tuple-element.104), channel_id=1, source_target_pairs={{0,10},{2,8},{4,14},{6,12},{8,2},{10,0},{12,6},{14,4},{1,11},{3,9}... | collective-permute-start | bytes 393224 | tf_op jit(solution)/shard_map/ppermute | solution.py:301
  141.7 21.6 %all-to-all-start.1 = ((bf16[16,32,128]{2,1,0:T(8,128)(2,1)}), bf16[16,32,128]{2,1,0:T(8,128)(2,1)S(1)}, u32[]{:S(2)}, u32[]{:S(2)}) async-start(bf16[16,32,128]{2,1,0:T(8,128)(2,1)} %shard_map.78), calls=%async_computation.1 | async-start | bytes 262144 | tf_op jit(solution)/shard_map/all_to_all | solution.py:312
  152.3 11.8 %collective-permute-start.25 = (bf16[2,4,64,128]{3,2,1,0:T(8,128)(2,1)S(1)}, bf16[2,4,64,128]{3,2,1,0:T(8,128)(2,1)S(1)}, u32[]{:S(2)}, u32[]{:S(2)}) collective-permute-start(bf16[2,4,64,128]{3,2,1,0:T(8,128)(2,1)S(1)} %get-tuple-element.117), channel_id=1, source_target_pairs={{0,4},{4,8},{8,12},{12,0},{1,5},{5,9},{9,13},{13,1},{2,6},{6,10},{... | collective-permute-start | bytes 393224 | tf_op jit(solution)/shard_map/ppermute | solution.py:319
  152.3 11.7 %collective-permute-start.26 = (bf16[2,4,64,128]{3,2,1,0:T(8,128)(2,1)S(1)}, bf16[2,4,64,128]{3,2,1,0:T(8,128)(2,1)S(1)}, u32[]{:S(2)}, u32[]{:S(2)}) collective-permute-start(bf16[2,4,64,128]{3,2,1,0:T(8,128)(2,1)S(1)} %get-tuple-element.118), channel_id=1, source_target_pairs={{0,8},{4,12},{8,0},{12,4},{1,9},{5,13},{9,1},{13,5},{2,10},{6,14},... | collective-permute-start | bytes 393224 | tf_op jit(solution)/shard_map/ppermute | solution.py:319
  (7 other events, 60.2 us)

commit v6 on v5

--- a/solution.py
+++ b/solution.py
@@ -113,12 +113,12 @@
             for el in range(held):
                 rows[pl.ds((2 * t + parity) * cols, cols), pl.ds(el * NB, NB)] = source[t, el]
 
-    @pl.when(place[2] == 0)
+    @pl.when(place[3] == 0)
     def _():
         fill(0, mine)
         fill(1, other)
 
-    @pl.when(place[2] != 0)
+    @pl.when(place[3] != 0)
     def _():
         fill(1, mine)
         fill(0, other)
@@ -207,23 +207,23 @@
     rows_total = float(slabs * hamiltonian.shape[0] * NB)
     cols = start.shape[2]
     layer = jax.ShapeDtypeStruct((PLANE, cols, NB), jnp.float32)
-    up = [(i, (i + 1) % slabs) for i in range(slabs)]
-    down = [((i + 1) % slabs, i) for i in range(slabs)]
-    begin = jnp.swapaxes(start, 1, 2)
+    up = [(2 * i + c, 2 * ((i + 1) % slabs) + 1 - c) for i in range(slabs) for c in range(2)]
+    down = [(to, source) for source, to in up]
     base = {"a": 0, "b": PLANE}
-    val = {("a", 0): begin[:PLANE], ("b", 0): begin[PLANE:]}
-    full = dict(val)
     halo = {}
 
     def send(name, k):
         if name == "a":
-            halo["b", k] = lax.ppermute(val["a", k], ELEM, down)
+            halo["b", k] = lax.ppermute(val["a", k], ELEM + ("c",), down)
         else:
-            halo["a", k] = lax.ppermute(val["b", k], ELEM, up)
+            halo["a", k] = lax.ppermute(val["b", k], ELEM + ("c",), up)
 
     shared = {}
     source = jnp.swapaxes(ritz, 0, 1)
     across = lax.ppermute(source, "yl", [(0, 1), (1, 0)])
+    begin = lax.ppermute(jnp.swapaxes(start, 1, 2), ("yh", "c"), [(0, 0), (1, 1), (2, 3), (3, 2)])
+    val = {("a", 0): begin[:PLANE], ("b", 0): begin[PLANE:]}
+    full = dict(val)
     send("b", 0)
     send("a", 0)
     shared["pair"] = jnp.stack([source, across])
@@ -270,7 +270,8 @@
     mine = lax.all_to_all(filtered, CHIP, 0, 0, tiled=True)
     mine = mine.reshape(chips, 2 * PLANE // chips, cols, NB)
     theirs = lax.ppermute(mine, "c", [(0, 1), (1, 0)])
-    place = jnp.stack([lax.axis_index("x"), lax.axis_index("yl"), lax.axis_index("c")]).astype(jnp.int32)
+    core = lax.axis_index("c")
+    place = jnp.stack([lax.axis_index("x"), lax.axis_index("yl"), core, (core + lax.axis_index("yh")) % 2]).astype(jnp.int32)
     held = mine.shape[1]
     depth = held * NB
     small = pl.CostEstimate(flops=1 << 20, bytes_accessed=1 << 20, transcendentals=0)
@@ -282,7 +283,7 @@
     block = jax.ShapeDtypeStruct((chips, cols, NB), jnp.bfloat16)
     rows = None
     parts = []
-    for away in (2, 1, around - 1, 0):
+    for away in (0, 2, 1, around - 1):
         if rows is None:
             rows, *blocks = call(
                 functools.partial(first_part_kernel, around, away), (place, mine, theirs),
@@ -294,7 +295,7 @@
                 functools.partial(part_kernel, around, away), (place, rows),
                 (block, block), flops, 16, (), [SMEM, VMEM],
             )
-        for q in range(2):
+        for q in (1, 0):
             if away == 0 and q == 0:
                 parts.append(blocks[0])
                 continue

time: 167 us -> 167 us (level)
  blocking collectives: 11 us -> 13 us
    all_to_all x1, starting transfers between devices: 10.5 us -> 5.49 us  [whole(): total = lax.all_to_all(total, ELEM, 0, 0, tiled=True)]
    ppermute x12 -> x13, starting transfers between devices: 31.7 us -> 36.4 us  [the longest x6 28.1 us: send(): halo['b', k] = lax.ppermute(val['a', k], ELEM + ('c',), down)]
    ppermute x7, waiting for transfers between devices: 9.63 us -> 7.4 us  [whole(): parts.append(lax.ppermute(blocks[q], CHIP, to_chip(away, q)))]
    all_to_all x1, blocking collectives: 11 us -> 13 us  [whole(): mine = lax.all_to_all(filtered, CHIP, 0, 0, tiled=True)]
    ppermute x12 -> x13, waiting for transfers between devices: 22.6 us -> 24.3 us  [the longest x6 16.5 us: send(): halo['a', k] = lax.ppermute(val['b', k], ELEM + ('c',), up)]
  transfers between devices with their start and end apart: 29 -> 30, of which waited for: 12 -> 12; matrix products, arithmetic and copies ran while one was open for 0% -> 0% of each run, Pallas kernels for 21% -> 20%
where the time goes in v6:
time: 167 us; the launch traced here: 166 us
  starting transfers between devices  65.5 us (39%)
  waiting for transfers between devices  47.3 us (28%)
  Pallas kernels  36.5 us (22%)
  blocking collectives  13 us (8%)
  local copies, waits for them, and re-layouts  3.12 us (2%)
    pallas_call x33, Pallas kernels, call(): pl.pallas_call(kernel, out_shape=out_shape, in_specs=in_specs or [VMEM] *...  36.5 us
    ppermute x6, starting transfers between devices, send(): halo['b', k] = lax.ppermute(val['a', k], ELEM + ('c',), down)  28.1 us
    ppermute x6, waiting for transfers between devices, send(): halo['a', k] = lax.ppermute(val['b', k], ELEM + ('c',), up)  16.5 us
    all_to_all x1, blocking collectives, whole(): mine = lax.all_to_all(filtered, CHIP, 0, 0, tiled=True)  13 us
    ppermute x7, starting transfers between devices, whole(): parts.append(lax.ppermute(blocks[q], CHIP, to_chip(away, q)))  11.9 us
    ppermute x6, waiting for transfers between devices, send(): halo['b', k] = lax.ppermute(val['a', k], ELEM + ('c',), down)  7.74 us
    ppermute x7, waiting for transfers between devices, whole(): parts.append(lax.ppermute(blocks[q], CHIP, to_chip(away, q)))  7.4 us
    ppermute x6, starting transfers between devices, send(): halo['a', k] = lax.ppermute(val['b', k], ELEM + ('c',), up)  6.54 us
  transfers between devices with their start and end apart: 30, of which 12 were waited for; matrix products, arithmetic and copies ran while one was open for 0% of the time, Pallas kernels for 20%

profile of v6, /device:TPU:4, one launch (start us, length us, event | category | flops | bytes accessed | tf_op | source)
XLA Modules:
  0.0 166.5 jit_solution(8189988681217979538)
XLA Ops:
  2.4 5.3 %collective-permute-start.2 = (bf16[16,64,128]{2,1,0:T(8,128)(2,1)S(1)}, bf16[16,64,128]{2,1,0:T(8,128)(2,1)S(1)}, u32[]{:S(2)}, u32[]{:S(2)}) collective-permute-start(bf16[16,64,128]{2,1,0:T(8,128)(2,1)S(1)} %get-tuple-element.62.inner.own.current.rest_0_), channel_id=1, source_target_pairs={{0,17},{1,16},{16,33},{17,32},{32,49},{33,48},{48,65},{49,64},{64,... | collective-permute-start | bytes 786440 | tf_op jit(solution)/shard_map/ppermute | solution.py:219
  7.7 5.4 %collective-permute-start.1 = (bf16[16,64,128]{2,1,0:T(8,128)(2,1)S(1)}, bf16[16,64,128]{2,1,0:T(8,128)(2,1)S(1)}, u32[]{:S(2)}, u32[]{:S(2)}) collective-permute-start(bf16[16,64,128]{2,1,0:T(8,128)(2,1)S(1)} %get-tuple-element.63.own.current.inner.rest_0_), channel_id=1, source_target_pairs={{17,0},{16,1},{33,16},{32,17},{49,32},{48,33},{65,48},{64,49},{81,... | collective-permute-start | bytes 786440 | tf_op jit(solution)/shard_map/ppermute | solution.py:217
  13.1 3.1 %copy-done = bf16[32,7,128,128]{3,2,1,0:T(8,128)(2,1)S(1)} copy-done((bf16[32,7,128,128]{3,2,1,0:T(8,128)(2,1)S(1)}, bf16[32,7,128,128]{3,2,1,0:T(8,128)(2,1)}, u32[]{:S(2)}) %copy-start) | copy-done | bytes 7340056
  20.5 8.8 %collective-permute-start.4 = (bf16[16,64,128]{2,1,0:T(8,128)(2,1)S(1)}, bf16[16,64,128]{2,1,0:T(8,128)(2,1)S(1)}, u32[]{:S(2)}, u32[]{:S(2)}) collective-permute-start(bf16[16,64,128]{2,1,0:T(8,128)(2,1)S(1)} %get-tuple-element.69.inner.own), channel_id=1, source_target_pairs={{17,0},{16,1},{33,16},{32,17},{49,32},{48,33},{65,48},{64,49},{81,... | collective-permute-start | bytes 786440 | tf_op jit(solution)/shard_map/ppermute | solution.py:217
  38.2 5.3 %collective-permute-done.3.halo = bf16[16,64,128]{2,1,0:T(8,128)(2,1)S(1)} collective-permute-done((bf16[16,64,128]{2,1,0:T(8,128)(2,1)S(1)}, bf16[16,64,128]{2,1,0:T(8,128)(2,1)S(1)}, u32[]{:S(2)}, u32[]{:S(2)}) %collective-permute-start.3) | collective-permute-done | bytes 262176 | tf_op jit(solution)/shard_map/ppermute | solution.py:219
  44.3 3.7 %collective-permute-start.5 = (bf16[16,64,128]{2,1,0:T(8,128)(2,1)S(1)}, bf16[16,64,128]{2,1,0:T(8,128)(2,1)S(1)}, u32[]{:S(2)}, u32[]{:S(2)}) collective-permute-start(bf16[16,64,128]{2,1,0:T(8,128)(2,1)S(1)} %get-tuple-element.78.own.inner), channel_id=1, source_target_pairs={{17,0},{16,1},{33,16},{32,17},{49,32},{48,33},{65,48},{64,49},{81,... | collective-permute-start | bytes 786440 | tf_op jit(solution)/shard_map/ppermute | solution.py:217
  50.4 3.2 %collective-permute-start.8 = (bf16[16,64,128]{2,1,0:T(8,128)(2,1)S(1)}, bf16[16,64,128]{2,1,0:T(8,128)(2,1)S(1)}, u32[]{:S(2)}, u32[]{:S(2)}) collective-permute-start(bf16[16,64,128]{2,1,0:T(8,128)(2,1)S(1)} %get-tuple-element.85.inner.own), channel_id=1, source_target_pairs={{17,0},{16,1},{33,16},{32,17},{49,32},{48,33},{65,48},{64,49},{81,... | collective-permute-start | bytes 786440 | tf_op jit(solution)/shard_map/ppermute | solution.py:217
  57.7 2.8 %collective-permute-done.8.halo = bf16[16,64,128]{2,1,0:T(8,128)(2,1)S(1)} collective-permute-done((bf16[16,64,128]{2,1,0:T(8,128)(2,1)S(1)}, bf16[16,64,128]{2,1,0:T(8,128)(2,1)S(1)}, u32[]{:S(2)}, u32[]{:S(2)}) %collective-permute-start.8) | collective-permute-done | bytes 262176 | tf_op jit(solution)/shard_map/ppermute | solution.py:217
  63.3 4.3 %collective-permute-done.7.halo = bf16[16,64,128]{2,1,0:T(8,128)(2,1)S(1)} collective-permute-done((bf16[16,64,128]{2,1,0:T(8,128)(2,1)S(1)}, bf16[16,64,128]{2,1,0:T(8,128)(2,1)S(1)}, u32[]{:S(2)}, u32[]{:S(2)}) %collective-permute-start.7) | collective-permute-done | bytes 262176 | tf_op jit(solution)/shard_map/ppermute | solution.py:219
  68.4 3.9 %collective-permute-start.9 = (bf16[16,64,128]{2,1,0:T(8,128)(2,1)S(1)}, bf16[16,64,128]{2,1,0:T(8,128)(2,1)S(1)}, u32[]{:S(2)}, u32[]{:S(2)}) collective-permute-start(bf16[16,64,128]{2,1,0:T(8,128)(2,1)S(1)} %get-tuple-element.94.own.inner), channel_id=1, source_target_pairs={{17,0},{16,1},{33,16},{32,17},{49,32},{48,33},{65,48},{64,49},{81,... | collective-permute-start | bytes 786440 | tf_op jit(solution)/shard_map/ppermute | solution.py:217
  74.7 3.2 %collective-permute-start.12 = (bf16[16,64,128]{2,1,0:T(8,128)(2,1)S(1)}, bf16[16,64,128]{2,1,0:T(8,128)(2,1)S(1)}, u32[]{:S(2)}, u32[]{:S(2)}) collective-permute-start(bf16[16,64,128]{2,1,0:T(8,128)(2,1)S(1)} %get-tuple-element.100.inner.own), channel_id=1, source_target_pairs={{17,0},{16,1},{33,16},{32,17},{49,32},{48,33},{65,48},{64,49},{81,... | collective-permute-start | bytes 786440 | tf_op jit(solution)/shard_map/ppermute | solution.py:217
  82.3 2.5 %collective-permute-done.12.halo = bf16[16,64,128]{2,1,0:T(8,128)(2,1)S(1)} collective-permute-done((bf16[16,64,128]{2,1,0:T(8,128)(2,1)S(1)}, bf16[16,64,128]{2,1,0:T(8,128)(2,1)S(1)}, u32[]{:S(2)}, u32[]{:S(2)}) %collective-permute-start.12) | collective-permute-done | bytes 262176 | tf_op jit(solution)/shard_map/ppermute | solution.py:217
  87.2 5.0 %collective-permute-done.11.halo = bf16[16,64,128]{2,1,0:T(8,128)(2,1)S(1)} collective-permute-done((bf16[16,64,128]{2,1,0:T(8,128)(2,1)S(1)}, bf16[16,64,128]{2,1,0:T(8,128)(2,1)S(1)}, u32[]{:S(2)}, u32[]{:S(2)}) %collective-permute-start.11) | collective-permute-done | bytes 262176 | tf_op jit(solution)/shard_map/ppermute | solution.py:219
  93.0 13.0 %all_to_all.10 = bf16[32,64,128]{2,1,0:T(8,128)(2,1)S(1)} all-to-all(bf16[32,64,128]{2,1,0:T(8,128)(2,1)S(1)} %shard_map.73), channel_id=1, replica_groups=mesh['z'=8,'yh'=2,'x'=4,'yl'=2,'c'=2] {'x','yl'}, dimensions={0} | all-to-all | bytes 1048576 | tf_op jit(solution)/shard_map/all_to_all | solution.py:270
  106.3 5.6 %collective-permute-done.21 = bf16[64,1024]{1,0:T(8,128)(2,1)S(1)} collective-permute-done((bf16[64,1024]{1,0:T(8,128)(2,1)S(1)}, bf16[64,1024]{1,0:T(8,128)(2,1)S(1)}, u32[]{:S(2)}, u32[]{:S(2)}) %collective-permute-start.21) | collective-permute-done | bytes 131104 | tf_op jit(solution)/shard_map/ppermute | solution.py:223
  120.7 3.6 %collective-permute-start.16 = (bf16[8,64,128]{2,1,0:T(8,128)(2,1)S(1)}, bf16[8,64,128]{2,1,0:T(8,128)(2,1)S(1)}, u32[]{:S(2)}, u32[]{:S(2)}) collective-permute-start(bf16[8,64,128]{2,1,0:T(8,128)(2,1)S(1)} %get-tuple-element.107), channel_id=1, source_target_pairs={{0,8},{2,10},{4,12},{6,14},{8,0},{10,2},{12,4},{14,6},{1,9},{3,11}... | collective-permute-start | bytes 393224 | tf_op jit(solution)/shard_map/ppermute | solution.py:302
  125.5 3.8 %collective-permute-done.24.ritz_back = bf16[2,64,1024]{2,1,0:T(8,128)(2,1)S(1)} collective-permute-done((bf16[2,64,1024]{2,1,0:T(8,128)(2,1)S(1)}, bf16[2,64,1024]{2,1,0:T(8,128)(2,1)S(1)}, u32[]{:S(2)}, u32[]{:S(2)}) %collective-permute-start.24) | collective-permute-done | bytes 262176 | tf_op jit(solution)/shard_map/ppermute | solution.py:231
  133.2 2.8 %collective-permute-start.19 = (bf16[8,64,128]{2,1,0:T(8,128)(2,1)S(1)}, bf16[8,64,128]{2,1,0:T(8,128)(2,1)S(1)}, u32[]{:S(2)}, u32[]{:S(2)}) collective-permute-start(bf16[8,64,128]{2,1,0:T(8,128)(2,1)S(1)} %get-tuple-element.110), channel_id=1, source_target_pairs={{0,14},{2,12},{4,2},{6,0},{8,6},{10,4},{12,10},{14,8},{1,15},{3,13... | collective-permute-start | bytes 393224 | tf_op jit(solution)/shard_map/ppermute | solution.py:302
  136.0 2.5 %collective-permute-start.20 = (bf16[8,64,128]{2,1,0:T(8,128)(2,1)S(1)}, bf16[8,64,128]{2,1,0:T(8,128)(2,1)S(1)}, u32[]{:S(2)}, u32[]{:S(2)}) collective-permute-start(bf16[8,64,128]{2,1,0:T(8,128)(2,1)S(1)} %get-tuple-element.111), channel_id=1, source_target_pairs={{0,12},{2,14},{4,0},{6,2},{8,4},{10,6},{12,8},{14,10},{1,13},{3,15... | collective-permute-start | bytes 393224 | tf_op jit(solution)/shard_map/ppermute | solution.py:302
  139.3 2.7 %collective-permute-done.19.refs_6_ = bf16[8,64,128]{2,1,0:T(8,128)(2,1)S(1)} collective-permute-done((bf16[8,64,128]{2,1,0:T(8,128)(2,1)S(1)}, bf16[8,64,128]{2,1,0:T(8,128)(2,1)S(1)}, u32[]{:S(2)}, u32[]{:S(2)}) %collective-permute-start.19) | collective-permute-done | bytes 131104 | tf_op jit(solution)/shard_map/ppermute | solution.py:302
  142.0 4.7 %collective-permute-done.14.refs_0_ = bf16[8,64,128]{2,1,0:T(8,128)(2,1)S(1)} collective-permute-done((bf16[8,64,128]{2,1,0:T(8,128)(2,1)S(1)}, bf16[8,64,128]{2,1,0:T(8,128)(2,1)S(1)}, u32[]{:S(2)}, u32[]{:S(2)}) %collective-permute-start.14) | collective-permute-done | bytes 131104 | tf_op jit(solution)/shard_map/ppermute | solution.py:302
  147.5 5.5 %all-to-all-start.1 = ((bf16[16,32,128]{2,1,0:T(8,128)(2,1)}), bf16[16,32,128]{2,1,0:T(8,128)(2,1)S(1)}, u32[]{:S(2)}, u32[]{:S(2)}) async-start(bf16[16,32,128]{2,1,0:T(8,128)(2,1)} %shard_map.78), calls=%async_computation.1 | async-start | bytes 262144 | tf_op jit(solution)/shard_map/all_to_all | solution.py:313
  155.4 2.5 %collective-permute-start.28 = (bf16[2,4,64,128]{3,2,1,0:T(8,128)(2,1)S(1)}, bf16[2,4,64,128]{3,2,1,0:T(8,128)(2,1)S(1)}, u32[]{:S(2)}, u32[]{:S(2)}) collective-permute-start(bf16[2,4,64,128]{3,2,1,0:T(8,128)(2,1)S(1)} %get-tuple-element.119), channel_id=1, source_target_pairs={{0,12},{4,0},{8,4},{12,8},{1,13},{5,1},{9,5},{13,9},{2,14},{6,2},{... | collective-permute-start | bytes 393224 | tf_op jit(solution)/shard_map/ppermute | solution.py:320
  157.9 6.2 %all-to-all-done.1.got = bf16[16,32,128]{2,1,0:T(8,128)(2,1)S(1)} async-done(((bf16[16,32,128]{2,1,0:T(8,128)(2,1)}), bf16[16,32,128]{2,1,0:T(8,128)(2,1)S(1)}, u32[]{:S(2)}, u32[]{:S(2)}) %all-to-all-start.1) | async-done | bytes 131104 | tf_op jit(solution)/shard_map/all_to_all | solution.py:313
  (77 shorter events, 56.2 us)
Async XLA Ops:
  2.4 17.3 %collective-permute-start.2 = (bf16[16,64,128]{2,1,0:T(8,128)(2,1)S(1)}, bf16[16,64,128]{2,1,0:T(8,128)(2,1)S(1)}, u32[]{:S(2)}, u32[]{:S(2)}) collective-permute-start(bf16[16,64,128]{2,1,0:T(8,128)(2,1)S(1)} %get-tuple-element.62.inner.own.current.rest_0_), channel_id=1, source_target_pairs={{0,17},{1,16},{16,33},{17,32},{32,49},{33,48},{48,65},{49,64},{64,... | collective-permute-start | bytes 786440 | tf_op jit(solution)/shard_map/ppermute | solution.py:219
  7.7 23.2 %collective-permute-start.1 = (bf16[16,64,128]{2,1,0:T(8,128)(2,1)S(1)}, bf16[16,64,128]{2,1,0:T(8,128)(2,1)S(1)}, u32[]{:S(2)}, u32[]{:S(2)}) collective-permute-start(bf16[16,64,128]{2,1,0:T(8,128)(2,1)S(1)} %get-tuple-element.63.own.current.inner.rest_0_), channel_id=1, source_target_pairs={{17,0},{16,1},{33,16},{32,17},{49,32},{48,33},{65,48},{64,49},{81,... | collective-permute-start | bytes 786440 | tf_op jit(solution)/shard_map/ppermute | solution.py:217
  20.5 15.2 %collective-permute-start.4 = (bf16[16,64,128]{2,1,0:T(8,128)(2,1)S(1)}, bf16[16,64,128]{2,1,0:T(8,128)(2,1)S(1)}, u32[]{:S(2)}, u32[]{:S(2)}) collective-permute-start(bf16[16,64,128]{2,1,0:T(8,128)(2,1)S(1)} %get-tuple-element.69.inner.own), channel_id=1, source_target_pairs={{17,0},{16,1},{33,16},{32,17},{49,32},{48,33},{65,48},{64,49},{81,... | collective-permute-start | bytes 786440 | tf_op jit(solution)/shard_map/ppermute | solution.py:217
  31.7 11.8 %collective-permute-start.3 = (bf16[16,64,128]{2,1,0:T(8,128)(2,1)S(1)}, bf16[16,64,128]{2,1,0:T(8,128)(2,1)S(1)}, u32[]{:S(2)}, u32[]{:S(2)}) collective-permute-start(bf16[16,64,128]{2,1,0:T(8,128)(2,1)S(1)} %get-tuple-element.70.own.inner), channel_id=1, source_target_pairs={{0,17},{1,16},{16,33},{17,32},{32,49},{33,48},{48,65},{49,64},{64,... | collective-permute-start | bytes 786440 | tf_op jit(solution)/shard_map/ppermute | solution.py:219
  36.5 13.0 %collective-permute-start.6 = (bf16[16,64,128]{2,1,0:T(8,128)(2,1)S(1)}, bf16[16,64,128]{2,1,0:T(8,128)(2,1)S(1)}, u32[]{:S(2)}, u32[]{:S(2)}) collective-permute-start(bf16[16,64,128]{2,1,0:T(8,128)(2,1)S(1)} %get-tuple-element.77.inner.own), channel_id=1, source_target_pairs={{0,17},{1,16},{16,33},{17,32},{32,49},{33,48},{48,65},{49,64},{64,... | collective-permute-start | bytes 786440 | tf_op jit(solution)/shard_map/ppermute | solution.py:219
  44.3 10.9 %collective-permute-start.5 = (bf16[16,64,128]{2,1,0:T(8,128)(2,1)S(1)}, bf16[16,64,128]{2,1,0:T(8,128)(2,1)S(1)}, u32[]{:S(2)}, u32[]{:S(2)}) collective-permute-start(bf16[16,64,128]{2,1,0:T(8,128)(2,1)S(1)} %get-tuple-element.78.own.inner), channel_id=1, source_target_pairs={{17,0},{16,1},{33,16},{32,17},{49,32},{48,33},{65,48},{64,49},{81,... | collective-permute-start | bytes 786440 | tf_op jit(solution)/shard_map/ppermute | solution.py:217
  50.4 10.2 %collective-permute-start.8 = (bf16[16,64,128]{2,1,0:T(8,128)(2,1)S(1)}, bf16[16,64,128]{2,1,0:T(8,128)(2,1)S(1)}, u32[]{:S(2)}, u32[]{:S(2)}) collective-permute-start(bf16[16,64,128]{2,1,0:T(8,128)(2,1)S(1)} %get-tuple-element.85.inner.own), channel_id=1, source_target_pairs={{17,0},{16,1},{33,16},{32,17},{49,32},{48,33},{65,48},{64,49},{81,... | collective-permute-start | bytes 786440 | tf_op jit(solution)/shard_map/ppermute | solution.py:217
  56.0 11.7 %collective-permute-start.7 = (bf16[16,64,128]{2,1,0:T(8,128)(2,1)S(1)}, bf16[16,64,128]{2,1,0:T(8,128)(2,1)S(1)}, u32[]{:S(2)}, u32[]{:S(2)}) collective-permute-start(bf16[16,64,128]{2,1,0:T(8,128)(2,1)S(1)} %get-tuple-element.86.own.inner), channel_id=1, source_target_pairs={{0,17},{1,16},{16,33},{17,32},{32,49},{33,48},{48,65},{49,64},{64,... | collective-permute-start | bytes 786440 | tf_op jit(solution)/shard_map/ppermute | solution.py:219
  61.4 12.5 %collective-permute-start.10 = (bf16[16,64,128]{2,1,0:T(8,128)(2,1)S(1)}, bf16[16,64,128]{2,1,0:T(8,128)(2,1)S(1)}, u32[]{:S(2)}, u32[]{:S(2)}) collective-permute-start(bf16[16,64,128]{2,1,0:T(8,128)(2,1)S(1)} %get-tuple-element.93.inner.own), channel_id=1, source_target_pairs={{0,17},{1,16},{16,33},{17,32},{32,49},{33,48},{48,65},{49,64},{64,... | collective-permute-start | bytes 786440 | tf_op jit(solution)/shard_map/ppermute | solution.py:219
  68.4 11.0 %collective-permute-start.9 = (bf16[16,64,128]{2,1,0:T(8,128)(2,1)S(1)}, bf16[16,64,128]{2,1,0:T(8,128)(2,1)S(1)}, u32[]{:S(2)}, u32[]{:S(2)}) collective-permute-start(bf16[16,64,128]{2,1,0:T(8,128)(2,1)S(1)} %get-tuple-element.94.own.inner), channel_id=1, source_target_pairs={{17,0},{16,1},{33,16},{32,17},{49,32},{48,33},{65,48},{64,49},{81,... | collective-permute-start | bytes 786440 | tf_op jit(solution)/shard_map/ppermute | solution.py:217
  74.7 10.1 %collective-permute-start.12 = (bf16[16,64,128]{2,1,0:T(8,128)(2,1)S(1)}, bf16[16,64,128]{2,1,0:T(8,128)(2,1)S(1)}, u32[]{:S(2)}, u32[]{:S(2)}) collective-permute-start(bf16[16,64,128]{2,1,0:T(8,128)(2,1)S(1)} %get-tuple-element.100.inner.own), channel_id=1, source_target_pairs={{17,0},{16,1},{33,16},{32,17},{49,32},{48,33},{65,48},{64,49},{81,... | collective-permute-start | bytes 786440 | tf_op jit(solution)/shard_map/ppermute | solution.py:217
  80.3 11.9 %collective-permute-start.11 = (bf16[16,64,128]{2,1,0:T(8,128)(2,1)S(1)}, bf16[16,64,128]{2,1,0:T(8,128)(2,1)S(1)}, u32[]{:S(2)}, u32[]{:S(2)}) collective-permute-start(bf16[16,64,128]{2,1,0:T(8,128)(2,1)S(1)} %get-tuple-element.101.own.inner), channel_id=1, source_target_pairs={{0,17},{1,16},{16,33},{17,32},{32,49},{33,48},{48,65},{49,64},{64,... | collective-permute-start | bytes 786440 | tf_op jit(solution)/shard_map/ppermute | solution.py:219
  105.9 10.8 %collective-permute-start.13 = (bf16[8,4,64,128]{3,2,1,0:T(8,128)(2,1)S(1)}, bf16[8,4,64,128]{3,2,1,0:T(8,128)(2,1)S(1)}, u32[]{:S(2)}, u32[]{:S(2)}) collective-permute-start(bf16[8,4,64,128]{3,2,1,0:T(8,128)(2,1)S(1)} %bitcast.11), channel_id=1, source_target_pairs={{0,1},{1,0},{2,3},{3,2},{4,5},{5,4},{6,7},{7,6},{8,9},{9,8},{10,11... | collective-permute-start | bytes 1572872 | tf_op jit(solution)/shard_map/ppermute | solution.py:272
  111.9 12.5 %collective-permute-start.22 = (bf16[2,64,1024]{2,1,0:T(8,128)(2,1)S(1)}, bf16[2,64,1024]{2,1,0:T(8,128)(2,1)S(1)}, u32[]{:S(2)}, u32[]{:S(2)}) collective-permute-start(bf16[2,64,1024]{2,1,0:T(8,128)(2,1)S(1)} %pad_maximum_fusion.ritz), channel_id=1, source_target_pairs={{0,12},{4,0},{8,4},{12,8},{1,13},{5,1},{9,5},{13,9},{2,14},{6,2},{... | collective-permute-start | bytes 786440 | tf_op jit(solution)/shard_map/ppermute | solution.py:231
  112.9 12.6 %collective-permute-start.23 = (bf16[2,64,1024]{2,1,0:T(8,128)(2,1)S(1)}, bf16[2,64,1024]{2,1,0:T(8,128)(2,1)S(1)}, u32[]{:S(2)}, u32[]{:S(2)}) collective-permute-start(bf16[2,64,1024]{2,1,0:T(8,128)(2,1)S(1)} %pad_maximum_fusion.ritz), channel_id=1, source_target_pairs={{0,8},{4,12},{8,0},{12,4},{1,9},{5,13},{9,1},{13,5},{2,10},{6,14},... | collective-permute-start | bytes 786440 | tf_op jit(solution)/shard_map/ppermute | solution.py:231
  114.9 14.3 %collective-permute-start.24 = (bf16[2,64,1024]{2,1,0:T(8,128)(2,1)S(1)}, bf16[2,64,1024]{2,1,0:T(8,128)(2,1)S(1)}, u32[]{:S(2)}, u32[]{:S(2)}) collective-permute-start(bf16[2,64,1024]{2,1,0:T(8,128)(2,1)S(1)} %pad_maximum_fusion.ritz), channel_id=1, source_target_pairs={{0,4},{4,8},{8,12},{12,0},{1,5},{5,9},{9,13},{13,1},{2,6},{6,10},{... | collective-permute-start | bytes 786440 | tf_op jit(solution)/shard_map/ppermute | solution.py:231
  119.0 14.2 %collective-permute-start.15 = (bf16[8,64,128]{2,1,0:T(8,128)(2,1)S(1)}, bf16[8,64,128]{2,1,0:T(8,128)(2,1)S(1)}, u32[]{:S(2)}, u32[]{:S(2)}) collective-permute-start(bf16[8,64,128]{2,1,0:T(8,128)(2,1)S(1)} %get-tuple-element.106), channel_id=1, source_target_pairs={{0,10},{2,8},{4,14},{6,12},{8,2},{10,0},{12,6},{14,4},{1,11},{3,9}... | collective-permute-start | bytes 393224 | tf_op jit(solution)/shard_map/ppermute | solution.py:302
  120.7 15.2 %collective-permute-start.16 = (bf16[8,64,128]{2,1,0:T(8,128)(2,1)S(1)}, bf16[8,64,128]{2,1,0:T(8,128)(2,1)S(1)}, u32[]{:S(2)}, u32[]{:S(2)}) collective-permute-start(bf16[8,64,128]{2,1,0:T(8,128)(2,1)S(1)} %get-tuple-element.107), channel_id=1, source_target_pairs={{0,8},{2,10},{4,12},{6,14},{8,0},{10,2},{12,4},{14,6},{1,9},{3,11}... | collective-permute-start | bytes 393224 | tf_op jit(solution)/shard_map/ppermute | solution.py:302
  124.3 14.1 %collective-permute-start.17 = (bf16[8,64,128]{2,1,0:T(8,128)(2,1)S(1)}, bf16[8,64,128]{2,1,0:T(8,128)(2,1)S(1)}, u32[]{:S(2)}, u32[]{:S(2)}) collective-permute-start(bf16[8,64,128]{2,1,0:T(8,128)(2,1)S(1)} %get-tuple-element.108), channel_id=1, source_target_pairs={{0,6},{2,4},{4,10},{6,8},{8,14},{10,12},{12,2},{14,0},{1,7},{3,5},... | collective-permute-start | bytes 393224 | tf_op jit(solution)/shard_map/ppermute | solution.py:302
  130.0 23.0 %collective-permute-start.25 = (bf16[4,4,64,128]{3,2,1,0:T(8,128)(2,1)S(1)}, bf16[4,4,64,128]{3,2,1,0:T(8,128)(2,1)S(1)}, u32[]{:S(2)}, u32[]{:S(2)}) collective-permute-start(bf16[4,4,64,128]{3,2,1,0:T(8,128)(2,1)S(1)} %get-tuple-element.113), channel_id=1, source_target_pairs={{0,2},{2,0},{1,3},{3,1},{4,6},{6,4},{5,7},{7,5},{8,10},{10,8},{9,1... | collective-permute-start | bytes 786440 | tf_op jit(solution)/shard_map/ppermute | solution.py:308
  147.5 16.6 %all-to-all-start.1 = ((bf16[16,32,128]{2,1,0:T(8,128)(2,1)}), bf16[16,32,128]{2,1,0:T(8,128)(2,1)S(1)}, u32[]{:S(2)}, u32[]{:S(2)}) async-start(bf16[16,32,128]{2,1,0:T(8,128)(2,1)} %shard_map.78), calls=%async_computation.1 | async-start | bytes 262144 | tf_op jit(solution)/shard_map/all_to_all | solution.py:313
  153.1 11.8 %collective-permute-start.26 = (bf16[2,4,64,128]{3,2,1,0:T(8,128)(2,1)S(1)}, bf16[2,4,64,128]{3,2,1,0:T(8,128)(2,1)S(1)}, u32[]{:S(2)}, u32[]{:S(2)}) collective-permute-start(bf16[2,4,64,128]{3,2,1,0:T(8,128)(2,1)S(1)} %get-tuple-element.117), channel_id=1, source_target_pairs={{0,4},{4,8},{8,12},{12,0},{1,5},{5,9},{9,13},{13,1},{2,6},{6,10},{... | collective-permute-start | bytes 393224 | tf_op jit(solution)/shard_map/ppermute | solution.py:320
  153.2 11.7 %collective-permute-start.27 = (bf16[2,4,64,128]{3,2,1,0:T(8,128)(2,1)S(1)}, bf16[2,4,64,128]{3,2,1,0:T(8,128)(2,1)S(1)}, u32[]{:S(2)}, u32[]{:S(2)}) collective-permute-start(bf16[2,4,64,128]{3,2,1,0:T(8,128)(2,1)S(1)} %get-tuple-element.118), channel_id=1, source_target_pairs={{0,8},{4,12},{8,0},{12,4},{1,9},{5,13},{9,1},{13,5},{2,10},{6,14},... | collective-permute-start | bytes 393224 | tf_op jit(solution)/shard_map/ppermute | solution.py:320
  155.4 9.5 %collective-permute-start.28 = (bf16[2,4,64,128]{3,2,1,0:T(8,128)(2,1)S(1)}, bf16[2,4,64,128]{3,2,1,0:T(8,128)(2,1)S(1)}, u32[]{:S(2)}, u32[]{:S(2)}) collective-permute-start(bf16[2,4,64,128]{3,2,1,0:T(8,128)(2,1)S(1)} %get-tuple-element.119), channel_id=1, source_target_pairs={{0,12},{4,0},{8,4},{12,8},{1,13},{5,1},{9,5},{13,9},{2,14},{6,2},{... | collective-permute-start | bytes 393224 | tf_op jit(solution)/shard_map/ppermute | solution.py:320
  (8 other events, 58.9 us)

commit v7 on v5

--- a/solution.py
+++ b/solution.py
@@ -155,11 +155,9 @@
             outs[4][away, el] = turned[cols:, el * NB : (el + 1) * NB]
 
 
-def join_kernel(crossed, *refs):
-    count = len(refs) // 2
-    for away in range(count):
-        refs[count + away][0] = refs[away][...]
-        refs[count + away][1] = crossed[away + 1]
+def part_ways_kernel(crossed, *outs):
+    for away, out in enumerate(outs):
+        out[...] = crossed[away + 1]
 
 
 def collect_kernel(around, place, here, crossed, *refs):
@@ -171,7 +169,7 @@
             line = lax.rem(place[0] + around - away, around) * 2 + near
             for el in range(held):
                 if away:
-                    piece = pieces[away - 1][q, el]
+                    piece = pieces[q * (around - 1) + away - 1][el]
                 else:
                     piece = crossed[0, el] if q else here[el]
                 out[line * held + el] = piece.astype(jnp.float32)
@@ -210,9 +208,9 @@
     up = [(i, (i + 1) % slabs) for i in range(slabs)]
     down = [((i + 1) % slabs, i) for i in range(slabs)]
     begin = jnp.swapaxes(start, 1, 2)
-    base = {"a": 0, "b": PLANE}
     val = {("a", 0): begin[:PLANE], ("b", 0): begin[PLANE:]}
     full = dict(val)
+    base = {"a": 0, "b": PLANE}
     halo = {}
 
     def send(name, k):
@@ -282,7 +280,7 @@
     block = jax.ShapeDtypeStruct((chips, cols, NB), jnp.bfloat16)
     rows = None
     parts = []
-    for away in (2, 1, around - 1, 0):
+    for away in (0, 2, 1, around - 1):
         if rows is None:
             rows, *blocks = call(
                 functools.partial(first_part_kernel, around, away), (place, mine, theirs),
@@ -294,7 +292,7 @@
                 functools.partial(part_kernel, around, away), (place, rows),
                 (block, block), flops, 16, (), [SMEM, VMEM],
             )
-        for q in range(2):
+        for q in (1, 0):
             if away == 0 and q == 0:
                 parts.append(blocks[0])
                 continue
@@ -305,21 +303,24 @@
         (piece,) * around + (piece.update(shape=(around, *piece.shape)),), flops, 16,
     )
     crossed = lax.ppermute(across, "yl", [(0, 1), (1, 0)])
+    pieces = []
+
+    def along(away, value):
+        pieces.append(lax.ppermute(value, "x", [(i, (i + away) % around) for i in range(around)]))
+
+    for away in range(1, around):
+        along(away, turned[away])
     total = call(
         margin_rows_kernel, parts,
         jax.ShapeDtypeStruct((slabs, cols // 2, 2 * cols), jnp.bfloat16), small, 12,
     )
     total = lax.all_to_all(total, ELEM, 0, 0, tiled=True)
-    joined = call(
-        join_kernel, (crossed, *turned[1:]),
-        (piece.update(shape=(2, *piece.shape)),) * (around - 1), small, 12,
-    )
-    pieces = []
+    ways = call(part_ways_kernel, (crossed,), (piece,) * (around - 1), small, 12)
     for away in range(1, around):
-        pieces.append(lax.ppermute(joined[away - 1], "x", [(i, (i + away) % around) for i in range(around)]))
+        along(away, ways[away - 1])
     rotated = call(
         functools.partial(collect_kernel, around), (place, turned[0], crossed, *pieces),
-        jax.ShapeDtypeStruct((2 * PLANE, cols, NB), jnp.float32), small, 12, (), [SMEM] + [VMEM] * (around + 1),
+        jax.ShapeDtypeStruct((2 * PLANE, cols, NB), jnp.float32), small, 12, (), [SMEM] + [VMEM] * (2 * around),
     )
     margin = call(
         functools.partial(margin_kernel, 1.0 / rows_total), (total,),

time: 167 us -> 164 us (0.982)
  waiting for transfers between devices: 48 us -> 35.3 us
  starting transfers between devices: 65 us -> 73.7 us
    all_to_all x1, waiting for transfers between devices: 6.12 us -> 0.01 us  [whole(): total = lax.all_to_all(total, ELEM, 0, 0, tiled=True)]
    ppermute x7, waiting for transfers between devices: 9.63 us -> 3.51 us  [whole(): parts.append(lax.ppermute(blocks[q], CHIP, to_chip(away, q)))]
    ppermute x7, starting transfers between devices: 11.3 us -> 16.4 us  [whole(): parts.append(lax.ppermute(blocks[q], CHIP, to_chip(away, q)))]
    ppermute x3 -> x6, starting transfers between devices: 4.95 us -> 9.05 us  [along(): lax.ppermute(value, 'x', [(i, (i + away) % around) for i in range(around)])]
    ppermute x3, waiting for transfers between devices: 3.97 us -> 0.01 us  [whole(): lax.ppermute(shared['pair'], 'x', [(i, (i + shift) % around) for i in ran...]
    ppermute x3 -> x6, waiting for transfers between devices: 0.01 us -> 3.51 us  [along(): lax.ppermute(value, 'x', [(i, (i + away) % around) for i in range(around)])]
  transfers between devices with their start and end apart: 29 -> 32, of which waited for: 12 -> 15; matrix products, arithmetic and copies ran while one was open for 0% -> 0% of each run, Pallas kernels for 21% -> 22%
where the time goes in v7:
time: 164 us; the launch traced here: 162 us
  starting transfers between devices  73.7 us (45%)
  Pallas kernels  36.5 us (22%)
  waiting for transfers between devices  35.3 us (22%)
  blocking collectives  11 us (7%)
  local copies, waits for them, and re-layouts  4.15 us (3%)
    pallas_call x33, Pallas kernels, call(): pl.pallas_call(kernel, out_shape=out_shape, in_specs=in_specs or [VMEM] *...  36.5 us
    ppermute x6, starting transfers between devices, send(): halo['b', k] = lax.ppermute(val['a', k], ELEM, down)  25.5 us
    ppermute x6, waiting for transfers between devices, send(): halo['a', k] = lax.ppermute(val['b', k], ELEM, up)  17.8 us
    ppermute x7, starting transfers between devices, whole(): parts.append(lax.ppermute(blocks[q], CHIP, to_chip(away, q)))  16.4 us
    all_to_all x1, blocking collectives, whole(): mine = lax.all_to_all(filtered, CHIP, 0, 0, tiled=True)  11 us
    all_to_all x1, starting transfers between devices, whole(): total = lax.all_to_all(total, ELEM, 0, 0, tiled=True)  10.7 us
    ppermute x6, starting transfers between devices, along(): lax.ppermute(value, 'x', [(i, (i + away) % around) for i in range(around)])  9.05 us
    ppermute x6, starting transfers between devices, send(): halo['a', k] = lax.ppermute(val['b', k], ELEM, up)  6.23 us
  transfers between devices with their start and end apart: 32, of which 15 were waited for; matrix products, arithmetic and copies ran while one was open for 0% of the time, Pallas kernels for 22%

profile of v7, /device:TPU:4, one launch (start us, length us, event | category | flops | bytes accessed | tf_op | source)
XLA Modules:
  0.0 161.6 jit_solution(72558709510320458)
XLA Ops:
  1.7 3.3 %collective-permute-start.1 = (bf16[16,64,128]{2,1,0:T(8,128)(2,1)S(1)}, bf16[16,64,128]{2,1,0:T(8,128)(2,1)S(1)}, u32[]{:S(2)}, u32[]{:S(2)}) collective-permute-start(bf16[16,64,128]{2,1,0:T(8,128)(2,1)S(1)} %get-tuple-element.62.inner.own.current.rest_0_), channel_id=1, source_target_pairs={{0,16},{16,32},{32,48},{48,64},{64,80},{80,96},{96,112},{112,128},... | collective-permute-start | bytes 786440 | tf_op jit(solution)/shard_map/ppermute | solution.py:220
  5.0 5.4 %collective-permute-start = (bf16[16,64,128]{2,1,0:T(8,128)(2,1)S(1)}, bf16[16,64,128]{2,1,0:T(8,128)(2,1)S(1)}, u32[]{:S(2)}, u32[]{:S(2)}) collective-permute-start(bf16[16,64,128]{2,1,0:T(8,128)(2,1)S(1)} %get-tuple-element.63.own.current.inner.rest_0_), channel_id=1, source_target_pairs={{16,0},{32,16},{48,32},{64,48},{80,64},{96,80},{112,96},{128,112},... | collective-permute-start | bytes 786440 | tf_op jit(solution)/shard_map/ppermute | solution.py:218
  10.4 3.1 %copy-done = bf16[32,7,128,128]{3,2,1,0:T(8,128)(2,1)S(1)} copy-done((bf16[32,7,128,128]{3,2,1,0:T(8,128)(2,1)S(1)}, bf16[32,7,128,128]{3,2,1,0:T(8,128)(2,1)}, u32[]{:S(2)}) %copy-start) | copy-done | bytes 7340056
  15.0 1.7 %collective-permute-done.1.halo = bf16[16,64,128]{2,1,0:T(8,128)(2,1)S(1)} collective-permute-done((bf16[16,64,128]{2,1,0:T(8,128)(2,1)S(1)}, bf16[16,64,128]{2,1,0:T(8,128)(2,1)S(1)}, u32[]{:S(2)}, u32[]{:S(2)}) %collective-permute-start.1) | collective-permute-done | bytes 262176 | tf_op jit(solution)/shard_map/ppermute | solution.py:220
  17.5 8.8 %collective-permute-start.3 = (bf16[16,64,128]{2,1,0:T(8,128)(2,1)S(1)}, bf16[16,64,128]{2,1,0:T(8,128)(2,1)S(1)}, u32[]{:S(2)}, u32[]{:S(2)}) collective-permute-start(bf16[16,64,128]{2,1,0:T(8,128)(2,1)S(1)} %get-tuple-element.69.inner.own), channel_id=1, source_target_pairs={{16,0},{32,16},{48,32},{64,48},{80,64},{96,80},{112,96},{128,112},... | collective-permute-start | bytes 786440 | tf_op jit(solution)/shard_map/ppermute | solution.py:218
  33.5 8.1 %collective-permute-done.2.halo = bf16[16,64,128]{2,1,0:T(8,128)(2,1)S(1)} collective-permute-done((bf16[16,64,128]{2,1,0:T(8,128)(2,1)S(1)}, bf16[16,64,128]{2,1,0:T(8,128)(2,1)S(1)}, u32[]{:S(2)}, u32[]{:S(2)}) %collective-permute-start.2) | collective-permute-done | bytes 262176 | tf_op jit(solution)/shard_map/ppermute | solution.py:220
  46.1 3.1 %collective-permute-start.7 = (bf16[16,64,128]{2,1,0:T(8,128)(2,1)S(1)}, bf16[16,64,128]{2,1,0:T(8,128)(2,1)S(1)}, u32[]{:S(2)}, u32[]{:S(2)}) collective-permute-start(bf16[16,64,128]{2,1,0:T(8,128)(2,1)S(1)} %get-tuple-element.85.inner.own), channel_id=1, source_target_pairs={{16,0},{32,16},{48,32},{64,48},{80,64},{96,80},{112,96},{128,112},... | collective-permute-start | bytes 786440 | tf_op jit(solution)/shard_map/ppermute | solution.py:218
  53.8 2.4 %collective-permute-done.7.halo = bf16[16,64,128]{2,1,0:T(8,128)(2,1)S(1)} collective-permute-done((bf16[16,64,128]{2,1,0:T(8,128)(2,1)S(1)}, bf16[16,64,128]{2,1,0:T(8,128)(2,1)S(1)}, u32[]{:S(2)}, u32[]{:S(2)}) %collective-permute-start.7) | collective-permute-done | bytes 262176 | tf_op jit(solution)/shard_map/ppermute | solution.py:218
  59.8 3.4 %collective-permute-done.6.halo = bf16[16,64,128]{2,1,0:T(8,128)(2,1)S(1)} collective-permute-done((bf16[16,64,128]{2,1,0:T(8,128)(2,1)S(1)}, bf16[16,64,128]{2,1,0:T(8,128)(2,1)S(1)}, u32[]{:S(2)}, u32[]{:S(2)}) %collective-permute-start.6) | collective-permute-done | bytes 262176 | tf_op jit(solution)/shard_map/ppermute | solution.py:220
  64.0 4.2 %collective-permute-start.8 = (bf16[16,64,128]{2,1,0:T(8,128)(2,1)S(1)}, bf16[16,64,128]{2,1,0:T(8,128)(2,1)S(1)}, u32[]{:S(2)}, u32[]{:S(2)}) collective-permute-start(bf16[16,64,128]{2,1,0:T(8,128)(2,1)S(1)} %get-tuple-element.94.own.inner), channel_id=1, source_target_pairs={{16,0},{32,16},{48,32},{64,48},{80,64},{96,80},{112,96},{128,112},... | collective-permute-start | bytes 786440 | tf_op jit(solution)/shard_map/ppermute | solution.py:218
  70.7 2.6 %collective-permute-start.11 = (bf16[16,64,128]{2,1,0:T(8,128)(2,1)S(1)}, bf16[16,64,128]{2,1,0:T(8,128)(2,1)S(1)}, u32[]{:S(2)}, u32[]{:S(2)}) collective-permute-start(bf16[16,64,128]{2,1,0:T(8,128)(2,1)S(1)} %get-tuple-element.100.inner.own), channel_id=1, source_target_pairs={{16,0},{32,16},{48,32},{64,48},{80,64},{96,80},{112,96},{128,112},... | collective-permute-start | bytes 786440 | tf_op jit(solution)/shard_map/ppermute | solution.py:218
  82.2 4.7 %collective-permute-done.10.halo = bf16[16,64,128]{2,1,0:T(8,128)(2,1)S(1)} collective-permute-done((bf16[16,64,128]{2,1,0:T(8,128)(2,1)S(1)}, bf16[16,64,128]{2,1,0:T(8,128)(2,1)S(1)}, u32[]{:S(2)}, u32[]{:S(2)}) %collective-permute-start.10) | collective-permute-done | bytes 262176 | tf_op jit(solution)/shard_map/ppermute | solution.py:220
  87.6 11.0 %all_to_all.10 = bf16[32,64,128]{2,1,0:T(8,128)(2,1)S(1)} all-to-all(bf16[32,64,128]{2,1,0:T(8,128)(2,1)S(1)} %shard_map.73), channel_id=1, replica_groups=mesh['z'=8,'yh'=2,'x'=4,'yl'=2,'c'=2] {'x','yl'}, dimensions={0} | all-to-all | bytes 1048576 | tf_op jit(solution)/shard_map/all_to_all | solution.py:268
  98.9 5.6 %collective-permute-done.20 = bf16[64,1024]{1,0:T(8,128)(2,1)S(1)} collective-permute-done((bf16[64,1024]{1,0:T(8,128)(2,1)S(1)}, bf16[64,1024]{1,0:T(8,128)(2,1)S(1)}, u32[]{:S(2)}, u32[]{:S(2)}) %collective-permute-start.20) | collective-permute-done | bytes 131104 | tf_op jit(solution)/shard_map/ppermute | solution.py:224
  105.9 2.1 %collective-permute-start.22 = (bf16[2,64,1024]{2,1,0:T(8,128)(2,1)S(1)}, bf16[2,64,1024]{2,1,0:T(8,128)(2,1)S(1)}, u32[]{:S(2)}, u32[]{:S(2)}) collective-permute-start(bf16[2,64,1024]{2,1,0:T(8,128)(2,1)S(1)} %pad_maximum_fusion.ritz), channel_id=1, source_target_pairs={{0,8},{4,12},{8,0},{12,4},{1,9},{5,13},{9,1},{13,5},{2,10},{6,14},... | collective-permute-start | bytes 786440 | tf_op jit(solution)/shard_map/ppermute | solution.py:229
  112.4 3.5 %collective-permute-start.15 = (bf16[8,64,128]{2,1,0:T(8,128)(2,1)S(1)}, bf16[8,64,128]{2,1,0:T(8,128)(2,1)S(1)}, u32[]{:S(2)}, u32[]{:S(2)}) collective-permute-start(bf16[8,64,128]{2,1,0:T(8,128)(2,1)S(1)} %get-tuple-element.107), channel_id=1, source_target_pairs={{0,8},{2,10},{4,12},{6,14},{8,0},{10,2},{12,4},{14,6},{1,9},{3,11}... | collective-permute-start | bytes 393224 | tf_op jit(solution)/shard_map/ppermute | solution.py:299
  119.5 2.7 %collective-permute-start.17 = (bf16[8,64,128]{2,1,0:T(8,128)(2,1)S(1)}, bf16[8,64,128]{2,1,0:T(8,128)(2,1)S(1)}, u32[]{:S(2)}, u32[]{:S(2)}) collective-permute-start(bf16[8,64,128]{2,1,0:T(8,128)(2,1)S(1)} %get-tuple-element.109), channel_id=1, source_target_pairs={{0,4},{2,6},{4,8},{6,10},{8,12},{10,14},{12,0},{14,2},{1,5},{3,7},... | collective-permute-start | bytes 393224 | tf_op jit(solution)/shard_map/ppermute | solution.py:299
  122.3 4.6 %collective-permute-start.18 = (bf16[8,64,128]{2,1,0:T(8,128)(2,1)S(1)}, bf16[8,64,128]{2,1,0:T(8,128)(2,1)S(1)}, u32[]{:S(2)}, u32[]{:S(2)}) collective-permute-start(bf16[8,64,128]{2,1,0:T(8,128)(2,1)S(1)} %get-tuple-element.110), channel_id=1, source_target_pairs={{0,14},{2,12},{4,2},{6,0},{8,6},{10,4},{12,10},{14,8},{1,15},{3,13... | collective-permute-start | bytes 393224 | tf_op jit(solution)/shard_map/ppermute | solution.py:299
  126.8 1.9 %collective-permute-start.19 = (bf16[8,64,128]{2,1,0:T(8,128)(2,1)S(1)}, bf16[8,64,128]{2,1,0:T(8,128)(2,1)S(1)}, u32[]{:S(2)}, u32[]{:S(2)}) collective-permute-start(bf16[8,64,128]{2,1,0:T(8,128)(2,1)S(1)} %get-tuple-element.111), channel_id=1, source_target_pairs={{0,12},{2,14},{4,0},{6,2},{8,4},{10,6},{12,8},{14,10},{1,13},{3,15... | collective-permute-start | bytes 393224 | tf_op jit(solution)/shard_map/ppermute | solution.py:299
  131.8 1.9 %collective-permute-done.19.refs_7_ = bf16[8,64,128]{2,1,0:T(8,128)(2,1)S(1)} collective-permute-done((bf16[8,64,128]{2,1,0:T(8,128)(2,1)S(1)}, bf16[8,64,128]{2,1,0:T(8,128)(2,1)S(1)}, u32[]{:S(2)}, u32[]{:S(2)}) %collective-permute-start.19) | collective-permute-done | bytes 131104 | tf_op jit(solution)/shard_map/ppermute | solution.py:299
  136.0 10.7 %all-to-all-start.1 = ((bf16[16,32,128]{2,1,0:T(8,128)(2,1)}), bf16[16,32,128]{2,1,0:T(8,128)(2,1)S(1)}, u32[]{:S(2)}, u32[]{:S(2)}) async-start(bf16[16,32,128]{2,1,0:T(8,128)(2,1)} %shard_map.78), calls=%async_computation.1 | async-start | bytes 262144 | tf_op jit(solution)/shard_map/all_to_all | solution.py:317
  146.7 2.3 %collective-permute-start.25 = (bf16[4,64,128]{2,1,0:T(8,128)(2,1)S(1)}, bf16[4,64,128]{2,1,0:T(8,128)(2,1)S(1)}, u32[]{:S(2)}, u32[]{:S(2)}) collective-permute-start(bf16[4,64,128]{2,1,0:T(8,128)(2,1)S(1)} %get-tuple-element.114), channel_id=1, source_target_pairs={{0,4},{4,8},{8,12},{12,0},{1,5},{5,9},{9,13},{13,1},{2,6},{6,10},{... | collective-permute-start | bytes 196616 | tf_op jit(solution)/shard_map/ppermute | solution.py:309
  150.1 2.1 %collective-permute-start.27 = (bf16[4,64,128]{2,1,0:T(8,128)(2,1)S(1)}, bf16[4,64,128]{2,1,0:T(8,128)(2,1)S(1)}, u32[]{:S(2)}, u32[]{:S(2)}) collective-permute-start(bf16[4,64,128]{2,1,0:T(8,128)(2,1)S(1)} %get-tuple-element.116), channel_id=1, source_target_pairs={{0,12},{4,0},{8,4},{12,8},{1,13},{5,1},{9,5},{13,9},{2,14},{6,2},{... | collective-permute-start | bytes 196616 | tf_op jit(solution)/shard_map/ppermute | solution.py:309
  152.3 2.4 %collective-permute-start.29 = (bf16[4,64,128]{2,1,0:T(8,128)(2,1)S(1)}, bf16[4,64,128]{2,1,0:T(8,128)(2,1)S(1)}, u32[]{:S(2)}, u32[]{:S(2)}) collective-permute-start(bf16[4,64,128]{2,1,0:T(8,128)(2,1)S(1)} %get-tuple-element.118), channel_id=1, source_target_pairs={{0,8},{4,12},{8,0},{12,4},{1,9},{5,13},{9,1},{13,5},{2,10},{6,14},... | collective-permute-start | bytes 196616 | tf_op jit(solution)/shard_map/ppermute | solution.py:309
  (81 shorter events, 59.1 us)
Async XLA Ops:
  1.7 15.0 %collective-permute-start.1 = (bf16[16,64,128]{2,1,0:T(8,128)(2,1)S(1)}, bf16[16,64,128]{2,1,0:T(8,128)(2,1)S(1)}, u32[]{:S(2)}, u32[]{:S(2)}) collective-permute-start(bf16[16,64,128]{2,1,0:T(8,128)(2,1)S(1)} %get-tuple-element.62.inner.own.current.rest_0_), channel_id=1, source_target_pairs={{0,16},{16,32},{32,48},{48,64},{64,80},{80,96},{96,112},{112,128},... | collective-permute-start | bytes 786440 | tf_op jit(solution)/shard_map/ppermute | solution.py:220
  5.0 22.9 %collective-permute-start = (bf16[16,64,128]{2,1,0:T(8,128)(2,1)S(1)}, bf16[16,64,128]{2,1,0:T(8,128)(2,1)S(1)}, u32[]{:S(2)}, u32[]{:S(2)}) collective-permute-start(bf16[16,64,128]{2,1,0:T(8,128)(2,1)S(1)} %get-tuple-element.63.own.current.inner.rest_0_), channel_id=1, source_target_pairs={{16,0},{32,16},{48,32},{64,48},{80,64},{96,80},{112,96},{128,112},... | collective-permute-start | bytes 786440 | tf_op jit(solution)/shard_map/ppermute | solution.py:218
  17.5 13.6 %collective-permute-start.3 = (bf16[16,64,128]{2,1,0:T(8,128)(2,1)S(1)}, bf16[16,64,128]{2,1,0:T(8,128)(2,1)S(1)}, u32[]{:S(2)}, u32[]{:S(2)}) collective-permute-start(bf16[16,64,128]{2,1,0:T(8,128)(2,1)S(1)} %get-tuple-element.69.inner.own), channel_id=1, source_target_pairs={{16,0},{32,16},{48,32},{64,48},{80,64},{96,80},{112,96},{128,112},... | collective-permute-start | bytes 786440 | tf_op jit(solution)/shard_map/ppermute | solution.py:218
  28.7 12.9 %collective-permute-start.2 = (bf16[16,64,128]{2,1,0:T(8,128)(2,1)S(1)}, bf16[16,64,128]{2,1,0:T(8,128)(2,1)S(1)}, u32[]{:S(2)}, u32[]{:S(2)}) collective-permute-start(bf16[16,64,128]{2,1,0:T(8,128)(2,1)S(1)} %get-tuple-element.70.own.inner), channel_id=1, source_target_pairs={{0,16},{16,32},{32,48},{48,64},{64,80},{80,96},{96,112},{112,128},... | collective-permute-start | bytes 786440 | tf_op jit(solution)/shard_map/ppermute | solution.py:220
  31.9 13.4 %collective-permute-start.5 = (bf16[16,64,128]{2,1,0:T(8,128)(2,1)S(1)}, bf16[16,64,128]{2,1,0:T(8,128)(2,1)S(1)}, u32[]{:S(2)}, u32[]{:S(2)}) collective-permute-start(bf16[16,64,128]{2,1,0:T(8,128)(2,1)S(1)} %get-tuple-element.77.inner.own), channel_id=1, source_target_pairs={{0,16},{16,32},{32,48},{48,64},{64,80},{80,96},{96,112},{112,128},... | collective-permute-start | bytes 786440 | tf_op jit(solution)/shard_map/ppermute | solution.py:220
  42.4 8.8 %collective-permute-start.4 = (bf16[16,64,128]{2,1,0:T(8,128)(2,1)S(1)}, bf16[16,64,128]{2,1,0:T(8,128)(2,1)S(1)}, u32[]{:S(2)}, u32[]{:S(2)}) collective-permute-start(bf16[16,64,128]{2,1,0:T(8,128)(2,1)S(1)} %get-tuple-element.78.own.inner), channel_id=1, source_target_pairs={{16,0},{32,16},{48,32},{64,48},{80,64},{96,80},{112,96},{128,112},... | collective-permute-start | bytes 786440 | tf_op jit(solution)/shard_map/ppermute | solution.py:218
  46.1 10.0 %collective-permute-start.7 = (bf16[16,64,128]{2,1,0:T(8,128)(2,1)S(1)}, bf16[16,64,128]{2,1,0:T(8,128)(2,1)S(1)}, u32[]{:S(2)}, u32[]{:S(2)}) collective-permute-start(bf16[16,64,128]{2,1,0:T(8,128)(2,1)S(1)} %get-tuple-element.85.inner.own), channel_id=1, source_target_pairs={{16,0},{32,16},{48,32},{64,48},{80,64},{96,80},{112,96},{128,112},... | collective-permute-start | bytes 786440 | tf_op jit(solution)/shard_map/ppermute | solution.py:218
  52.0 11.2 %collective-permute-start.6 = (bf16[16,64,128]{2,1,0:T(8,128)(2,1)S(1)}, bf16[16,64,128]{2,1,0:T(8,128)(2,1)S(1)}, u32[]{:S(2)}, u32[]{:S(2)}) collective-permute-start(bf16[16,64,128]{2,1,0:T(8,128)(2,1)S(1)} %get-tuple-element.86.own.inner), channel_id=1, source_target_pairs={{0,16},{16,32},{32,48},{48,64},{64,80},{80,96},{96,112},{112,128},... | collective-permute-start | bytes 786440 | tf_op jit(solution)/shard_map/ppermute | solution.py:220
  57.0 12.9 %collective-permute-start.9 = (bf16[16,64,128]{2,1,0:T(8,128)(2,1)S(1)}, bf16[16,64,128]{2,1,0:T(8,128)(2,1)S(1)}, u32[]{:S(2)}, u32[]{:S(2)}) collective-permute-start(bf16[16,64,128]{2,1,0:T(8,128)(2,1)S(1)} %get-tuple-element.93.inner.own), channel_id=1, source_target_pairs={{0,16},{16,32},{32,48},{48,64},{64,80},{80,96},{96,112},{112,128},... | collective-permute-start | bytes 786440 | tf_op jit(solution)/shard_map/ppermute | solution.py:220
  64.0 10.8 %collective-permute-start.8 = (bf16[16,64,128]{2,1,0:T(8,128)(2,1)S(1)}, bf16[16,64,128]{2,1,0:T(8,128)(2,1)S(1)}, u32[]{:S(2)}, u32[]{:S(2)}) collective-permute-start(bf16[16,64,128]{2,1,0:T(8,128)(2,1)S(1)} %get-tuple-element.94.own.inner), channel_id=1, source_target_pairs={{16,0},{32,16},{48,32},{64,48},{80,64},{96,80},{112,96},{128,112},... | collective-permute-start | bytes 786440 | tf_op jit(solution)/shard_map/ppermute | solution.py:218
  70.7 9.1 %collective-permute-start.11 = (bf16[16,64,128]{2,1,0:T(8,128)(2,1)S(1)}, bf16[16,64,128]{2,1,0:T(8,128)(2,1)S(1)}, u32[]{:S(2)}, u32[]{:S(2)}) collective-permute-start(bf16[16,64,128]{2,1,0:T(8,128)(2,1)S(1)} %get-tuple-element.100.inner.own), channel_id=1, source_target_pairs={{16,0},{32,16},{48,32},{64,48},{80,64},{96,80},{112,96},{128,112},... | collective-permute-start | bytes 786440 | tf_op jit(solution)/shard_map/ppermute | solution.py:218
  75.6 11.2 %collective-permute-start.10 = (bf16[16,64,128]{2,1,0:T(8,128)(2,1)S(1)}, bf16[16,64,128]{2,1,0:T(8,128)(2,1)S(1)}, u32[]{:S(2)}, u32[]{:S(2)}) collective-permute-start(bf16[16,64,128]{2,1,0:T(8,128)(2,1)S(1)} %get-tuple-element.101.own.inner), channel_id=1, source_target_pairs={{0,16},{16,32},{32,48},{48,64},{64,80},{80,96},{96,112},{112,128},... | collective-permute-start | bytes 786440 | tf_op jit(solution)/shard_map/ppermute | solution.py:220
  98.6 10.9 %collective-permute-start.12 = (bf16[8,4,64,128]{3,2,1,0:T(8,128)(2,1)S(1)}, bf16[8,4,64,128]{3,2,1,0:T(8,128)(2,1)S(1)}, u32[]{:S(2)}, u32[]{:S(2)}) collective-permute-start(bf16[8,4,64,128]{3,2,1,0:T(8,128)(2,1)S(1)} %bitcast.10), channel_id=1, source_target_pairs={{0,1},{1,0},{2,3},{3,2},{4,5},{5,4},{6,7},{7,6},{8,9},{9,8},{10,11... | collective-permute-start | bytes 1572872 | tf_op jit(solution)/shard_map/ppermute | solution.py:270
  104.6 12.4 %collective-permute-start.21 = (bf16[2,64,1024]{2,1,0:T(8,128)(2,1)S(1)}, bf16[2,64,1024]{2,1,0:T(8,128)(2,1)S(1)}, u32[]{:S(2)}, u32[]{:S(2)}) collective-permute-start(bf16[2,64,1024]{2,1,0:T(8,128)(2,1)S(1)} %pad_maximum_fusion.ritz), channel_id=1, source_target_pairs={{0,12},{4,0},{8,4},{12,8},{1,13},{5,1},{9,5},{13,9},{2,14},{6,2},{... | collective-permute-start | bytes 786440 | tf_op jit(solution)/shard_map/ppermute | solution.py:229
  105.9 13.7 %collective-permute-start.22 = (bf16[2,64,1024]{2,1,0:T(8,128)(2,1)S(1)}, bf16[2,64,1024]{2,1,0:T(8,128)(2,1)S(1)}, u32[]{:S(2)}, u32[]{:S(2)}) collective-permute-start(bf16[2,64,1024]{2,1,0:T(8,128)(2,1)S(1)} %pad_maximum_fusion.ritz), channel_id=1, source_target_pairs={{0,8},{4,12},{8,0},{12,4},{1,9},{5,13},{9,1},{13,5},{2,10},{6,14},... | collective-permute-start | bytes 786440 | tf_op jit(solution)/shard_map/ppermute | solution.py:229
  108.0 14.3 %collective-permute-start.23 = (bf16[2,64,1024]{2,1,0:T(8,128)(2,1)S(1)}, bf16[2,64,1024]{2,1,0:T(8,128)(2,1)S(1)}, u32[]{:S(2)}, u32[]{:S(2)}) collective-permute-start(bf16[2,64,1024]{2,1,0:T(8,128)(2,1)S(1)} %pad_maximum_fusion.ritz), channel_id=1, source_target_pairs={{0,4},{4,8},{8,12},{12,0},{1,5},{5,9},{9,13},{13,1},{2,6},{6,10},{... | collective-permute-start | bytes 786440 | tf_op jit(solution)/shard_map/ppermute | solution.py:229
  111.8 15.0 %collective-permute-start.14 = (bf16[8,64,128]{2,1,0:T(8,128)(2,1)S(1)}, bf16[8,64,128]{2,1,0:T(8,128)(2,1)S(1)}, u32[]{:S(2)}, u32[]{:S(2)}) collective-permute-start(bf16[8,64,128]{2,1,0:T(8,128)(2,1)S(1)} %get-tuple-element.106), channel_id=1, source_target_pairs={{0,10},{2,8},{4,14},{6,12},{8,2},{10,0},{12,6},{14,4},{1,11},{3,9}... | collective-permute-start | bytes 393224 | tf_op jit(solution)/shard_map/ppermute | solution.py:299
  112.4 16.4 %collective-permute-start.15 = (bf16[8,64,128]{2,1,0:T(8,128)(2,1)S(1)}, bf16[8,64,128]{2,1,0:T(8,128)(2,1)S(1)}, u32[]{:S(2)}, u32[]{:S(2)}) collective-permute-start(bf16[8,64,128]{2,1,0:T(8,128)(2,1)S(1)} %get-tuple-element.107), channel_id=1, source_target_pairs={{0,8},{2,10},{4,12},{6,14},{8,0},{10,2},{12,4},{14,6},{1,9},{3,11}... | collective-permute-start | bytes 393224 | tf_op jit(solution)/shard_map/ppermute | solution.py:299
  117.0 14.1 %collective-permute-start.16 = (bf16[8,64,128]{2,1,0:T(8,128)(2,1)S(1)}, bf16[8,64,128]{2,1,0:T(8,128)(2,1)S(1)}, u32[]{:S(2)}, u32[]{:S(2)}) collective-permute-start(bf16[8,64,128]{2,1,0:T(8,128)(2,1)S(1)} %get-tuple-element.108), channel_id=1, source_target_pairs={{0,6},{2,4},{4,10},{6,8},{8,14},{10,12},{12,2},{14,0},{1,7},{3,5},... | collective-permute-start | bytes 393224 | tf_op jit(solution)/shard_map/ppermute | solution.py:299
  119.5 12.3 %collective-permute-start.17 = (bf16[8,64,128]{2,1,0:T(8,128)(2,1)S(1)}, bf16[8,64,128]{2,1,0:T(8,128)(2,1)S(1)}, u32[]{:S(2)}, u32[]{:S(2)}) collective-permute-start(bf16[8,64,128]{2,1,0:T(8,128)(2,1)S(1)} %get-tuple-element.109), channel_id=1, source_target_pairs={{0,4},{2,6},{4,8},{6,10},{8,12},{10,14},{12,0},{14,2},{1,5},{3,7},... | collective-permute-start | bytes 393224 | tf_op jit(solution)/shard_map/ppermute | solution.py:299
  122.3 9.5 %collective-permute-start.18 = (bf16[8,64,128]{2,1,0:T(8,128)(2,1)S(1)}, bf16[8,64,128]{2,1,0:T(8,128)(2,1)S(1)}, u32[]{:S(2)}, u32[]{:S(2)}) collective-permute-start(bf16[8,64,128]{2,1,0:T(8,128)(2,1)S(1)} %get-tuple-element.110), channel_id=1, source_target_pairs={{0,14},{2,12},{4,2},{6,0},{8,6},{10,4},{12,10},{14,8},{1,15},{3,13... | collective-permute-start | bytes 393224 | tf_op jit(solution)/shard_map/ppermute | solution.py:299
  131.1 21.1 %collective-permute-start.24 = (bf16[4,4,64,128]{3,2,1,0:T(8,128)(2,1)S(1)}, bf16[4,4,64,128]{3,2,1,0:T(8,128)(2,1)S(1)}, u32[]{:S(2)}, u32[]{:S(2)}) collective-permute-start(bf16[4,4,64,128]{3,2,1,0:T(8,128)(2,1)S(1)} %get-tuple-element.113), channel_id=1, source_target_pairs={{0,2},{2,0},{1,3},{3,1},{4,6},{6,4},{5,7},{7,5},{8,10},{10,8},{9,1... | collective-permute-start | bytes 786440 | tf_op jit(solution)/shard_map/ppermute | solution.py:305
  136.0 24.9 %all-to-all-start.1 = ((bf16[16,32,128]{2,1,0:T(8,128)(2,1)}), bf16[16,32,128]{2,1,0:T(8,128)(2,1)S(1)}, u32[]{:S(2)}, u32[]{:S(2)}) async-start(bf16[16,32,128]{2,1,0:T(8,128)(2,1)} %shard_map.78), calls=%async_computation.1 | async-start | bytes 262144 | tf_op jit(solution)/shard_map/all_to_all | solution.py:317
  146.7 7.9 %collective-permute-start.25 = (bf16[4,64,128]{2,1,0:T(8,128)(2,1)S(1)}, bf16[4,64,128]{2,1,0:T(8,128)(2,1)S(1)}, u32[]{:S(2)}, u32[]{:S(2)}) collective-permute-start(bf16[4,64,128]{2,1,0:T(8,128)(2,1)S(1)} %get-tuple-element.114), channel_id=1, source_target_pairs={{0,4},{4,8},{8,12},{12,0},{1,5},{5,9},{9,13},{13,1},{2,6},{6,10},{... | collective-permute-start | bytes 196616 | tf_op jit(solution)/shard_map/ppermute | solution.py:309
  (10 other events, 66.2 us)

commit v8 on v5

--- a/solution.py
+++ b/solution.py
@@ -22,7 +22,6 @@
 CHIP = ("x", "yl")
 VMEM = pl.BlockSpec(memory_space=pltpu.VMEM)
 SMEM = pl.BlockSpec(memory_space=pltpu.SMEM)
-ROWS = (((1,), (1,)), ((), ()))
 PLAIN = (((1,), (0,)), ((), ()))
 
 
@@ -38,19 +37,16 @@
         below = lax.rem(gy + 1, GY) * GZ
         for gz in range(GZ):
             e = gy * GZ + gz
-            values = {
-                0: own[e],
-                inside: inner[e],
-                3: own[above + gz],
-                4: own[below + gz],
-                5: own[gy * GZ + (gz - 1) % GZ],
-                6: own[gy * GZ + (gz + 1) % GZ],
-            }
+            left_z, right_z = gy * GZ + (gz - 1) % GZ, gy * GZ + (gz + 1) % GZ
+            terms = (
+                (own[e], ham[base + e, 0], inner[e], ham[PLANE - base + e, 3 - inside]),
+                (own[above + gz], ham[base + above + gz, 4], own[below + gz], ham[base + below + gz, 3]),
+                (own[left_z], ham[base + left_z, 6], own[right_z], ham[base + right_z, 5]),
+            )
             total = None
-            for pair in ((0, inside), (3, 4), (5, 6)):
-                left = jnp.concatenate([values[d] for d in pair], axis=1)
-                right = jnp.concatenate([ham[base + e, d] for d in pair], axis=1)
-                term = product(left, right, ROWS)
+            for v0, h0, v1, h1 in terms:
+                left, right = jnp.concatenate([v0, v1], axis=1), jnp.concatenate([h0, h1], axis=0)
+                term = product(left, right, PLAIN)
                 total = term if total is None else total + term
             total = scale * total - shift * current[e].astype(jnp.float32)
             if has_previous:
@@ -61,11 +57,22 @@
     lax.fori_loop(0, GY, line, 0)
 
 
-def outside_kernel(base, direction, scale, ham, halo, partial, rounded, *full):
+def edges_kernel(ham, edge_a, edge_b):
     def line(gy, carry):
         for gz in range(GZ):
             e = gy * GZ + gz
-            value = partial[e] + scale * product(halo[e], ham[base + e, direction], ROWS)
+            edge_a[e] = ham[e, 1].T
+            edge_b[e] = ham[PLANE + e, 2].T
+        return carry
+
+    lax.fori_loop(0, GY, line, 0)
+
+
+def outside_kernel(scale, edge, halo, partial, rounded, *full):
+    def line(gy, carry):
+        for gz in range(GZ):
+            e = gy * GZ + gz
+            value = partial[e] + scale * product(halo[e], edge[e], PLAIN)
             rounded[e] = value.astype(jnp.bfloat16)
             if full:
                 full[0][e] = value
@@ -74,11 +81,11 @@
     lax.fori_loop(0, GY, line, 0)
 
 
-def last_kernel(base, direction, scale, ham, halo, partial, other, filtered):
+def last_kernel(base, scale, edge, halo, partial, other, filtered):
     def line(gy, carry):
         for gz in range(GZ):
             e = gy * GZ + gz
-            value = partial[e] + scale * product(halo[e], ham[base + e, direction], ROWS)
+            value = partial[e] + scale * product(halo[e], edge[e], PLAIN)
             filtered[base + e] = value.astype(jnp.bfloat16)
             filtered[PLANE - base + e] = other[e]
         return carry
@@ -105,7 +112,7 @@
     )(*operands)
 
 
-def fill_rows(place, mine, other, rows):
+def turn_kernel(place, mine, other, ritz, ritz_next, ritz_far, ritz_back, rows, *outs):
     chips, held, cols = mine.shape[0], mine.shape[1], mine.shape[2]
 
     def fill(parity, source):
@@ -123,36 +130,35 @@
         fill(1, mine)
         fill(0, other)
 
-
-def part_blocks(around, away, place, rows, outs):
+    for away, source in enumerate((ritz, ritz_next, ritz_far, ritz_back)):
+        turned = product(source[...].reshape(2 * cols, -1), rows[...], PLAIN).astype(jnp.bfloat16)
+        for el in range(held):
+            outs[away][el] = turned[:cols, el * NB : (el + 1) * NB]
+            outs[4][away, el] = turned[cols:, el * NB : (el + 1) * NB]
+
+
+def part_blocks(around, away, place, rows, across, outs):
     chips, cols = outs[0].shape[0], outs[0].shape[1]
     line = lax.rem(place[0] + away, around) * 2
     left = []
     for q in range(2):
         chip = line + (place[1] if q == 0 else 1 - place[1])
         left.append(rows[pl.ds(pl.multiple_of((2 * chip + place[2]) * cols, cols), cols), :])
-    part = product(jnp.concatenate(left, axis=0), rows[...], ROWS).astype(jnp.bfloat16)
+    part = product(jnp.concatenate(left, axis=0), across[...], PLAIN).astype(jnp.bfloat16)
     for q in range(2):
         for t in range(chips):
             outs[q][t] = part[q * cols : (q + 1) * cols, t * NB : (t + 1) * NB]
 
 
-def first_part_kernel(around, away, place, mine, other, rows, *outs):
-    fill_rows(place, mine, other, rows)
-    part_blocks(around, away, place, rows, outs)
-
-
-def part_kernel(around, away, place, rows, *outs):
-    part_blocks(around, away, place, rows, outs)
-
-
-def turn_kernel(rows, ritz, ritz_next, ritz_far, ritz_back, *outs):
-    held, cols = outs[0].shape[0], outs[0].shape[1]
-    for away, source in enumerate((ritz, ritz_next, ritz_far, ritz_back)):
-        turned = product(source[...].reshape(2 * cols, -1), rows[...], PLAIN).astype(jnp.bfloat16)
-        for el in range(held):
-            outs[away][el] = turned[:cols, el * NB : (el + 1) * NB]
-            outs[4][away, el] = turned[cols:, el * NB : (el + 1) * NB]
+def first_part_kernel(around, away, place, rows, across, *outs):
+    for t in range(rows.shape[0] // NB):
+        for el in range(rows.shape[1] // NB):
+            across[pl.ds(el * NB, NB), pl.ds(t * NB, NB)] = rows[pl.ds(t * NB, NB), pl.ds(el * NB, NB)].T
+    part_blocks(around, away, place, rows, across, outs)
+
+
+def part_kernel(around, away, place, rows, across, *outs):
+    part_blocks(around, away, place, rows, across, outs)
 
 
 def join_kernel(crossed, *refs):
@@ -210,9 +216,9 @@
     up = [(i, (i + 1) % slabs) for i in range(slabs)]
     down = [((i + 1) % slabs, i) for i in range(slabs)]
     begin = jnp.swapaxes(start, 1, 2)
-    base = {"a": 0, "b": PLANE}
     val = {("a", 0): begin[:PLANE], ("b", 0): begin[PLANE:]}
     full = dict(val)
+    base = {"a": 0, "b": PLANE}
     halo = {}
 
     def send(name, k):
@@ -234,9 +240,12 @@
     for k in range(1, DEG + 1):
         order += [("a", k), ("b", k)] if k % 2 else [("b", k), ("a", k)]
     token = None
+    blocks = jax.ShapeDtypeStruct((PLANE, NB, NB), jnp.bfloat16)
+    edges = call(edges_kernel, (hamiltonian,), (blocks, blocks), cost(PLANE, cols, 2), 12)
+    edges = dict(zip("ab", edges))
     for count, (name, k) in enumerate(order):
         other = "b" if name == "a" else "a"
-        inside, outside = (2, 1) if name == "a" else (1, 2)
+        inside = 2 if name == "a" else 1
         own, inner = val[name, k - 1], val[other, k - 1]
         if token is not None:
             own, inner, _ = lax.optimization_barrier((own, inner, token))
@@ -248,17 +257,17 @@
             functools.partial(inside_kernel, base[name], inside, scale, scale * center_shift, k > 1),
             operands, layer, cost(PLANE, cols, 6), 12,
         )
-        edge = [hamiltonian, halo[name, k - 1], part]
+        edge = [edges[name], halo[name, k - 1], part]
         if count == 2 * DEG - 1:
             filtered = call(
-                functools.partial(last_kernel, base[name], outside, scale),
+                functools.partial(last_kernel, base[name], scale),
                 edge + [val[other, k]],
                 jax.ShapeDtypeStruct((2 * PLANE, cols, NB), jnp.bfloat16), cost(PLANE, cols, 1), 12,
             )
             break
         kept = (layer,) if k < DEG else ()
         token, *kept = call(
-            functools.partial(outside_kernel, base[name], outside, scale),
+            functools.partial(outside_kernel, scale),
             edge, (layer.update(dtype=jnp.bfloat16), *kept), cost(PLANE, cols, 1), 12,
         )
         val[name, k] = token
@@ -279,44 +288,51 @@
     def to_chip(away, q):
         return [(i, (i // 2 + away) % around * 2 + (i + q) % 2) for i in range(chips)]
 
+    piece = jax.ShapeDtypeStruct((held, cols, NB), jnp.bfloat16)
+    rows, *turned, other_y = call(
+        turn_kernel,
+        (place, mine, theirs, shared["pair"], shared[around - 1], shared[2], shared[1]),
+        (
+            jax.ShapeDtypeStruct((2 * chips * cols, depth), jnp.bfloat16),
+            *(piece,) * around,
+            piece.update(shape=(around, *piece.shape)),
+        ),
+        flops, 16, (), [SMEM] + [VMEM] * 6,
+    )
+    crossed = lax.ppermute(other_y, "yl", [(0, 1), (1, 0)])
+
     block = jax.ShapeDtypeStruct((chips, cols, NB), jnp.bfloat16)
-    rows = None
+    across = None
     parts = []
-    for away in (2, 1, around - 1, 0):
-        if rows is None:
-            rows, *blocks = call(
-                functools.partial(first_part_kernel, around, away), (place, mine, theirs),
-                (jax.ShapeDtypeStruct((2 * chips * cols, depth), jnp.bfloat16), block, block),
-                flops, 16, (), [SMEM, VMEM, VMEM],
+    for away in (0, 2, 1, around - 1):
+        if across is None:
+            across, *blocks = call(
+                functools.partial(first_part_kernel, around, away), (place, rows),
+                (jax.ShapeDtypeStruct((depth, 2 * chips * cols), jnp.bfloat16), block, block),
+                flops, 16, (), [SMEM, VMEM],
             )
         else:
             blocks = call(
-                functools.partial(part_kernel, around, away), (place, rows),
-                (block, block), flops, 16, (), [SMEM, VMEM],
+                functools.partial(part_kernel, around, away), (place, rows, across),
+                (block, block), flops, 16, (), [SMEM, VMEM, VMEM],
             )
-        for q in range(2):
+        for q in (1, 0):
             if away == 0 and q == 0:
                 parts.append(blocks[0])
                 continue
             parts.append(lax.ppermute(blocks[q], CHIP, to_chip(away, q)))
-    piece = jax.ShapeDtypeStruct((held, cols, NB), jnp.bfloat16)
-    *turned, across = call(
-        turn_kernel, (rows, shared["pair"], shared[around - 1], shared[2], shared[1]),
-        (piece,) * around + (piece.update(shape=(around, *piece.shape)),), flops, 16,
-    )
-    crossed = lax.ppermute(across, "yl", [(0, 1), (1, 0)])
+    joined = call(
+        join_kernel, (crossed, *turned[1:]),
+        (piece.update(shape=(2, *piece.shape)),) * (around - 1), small, 12,
+    )
+    pieces = []
+    for away in range(1, around):
+        pieces.append(lax.ppermute(joined[away - 1], "x", [(i, (i + away) % around) for i in range(around)]))
     total = call(
         margin_rows_kernel, parts,
         jax.ShapeDtypeStruct((slabs, cols // 2, 2 * cols), jnp.bfloat16), small, 12,
     )
     total = lax.all_to_all(total, ELEM, 0, 0, tiled=True)
-    joined = call(
-        join_kernel, (crossed, *turned[1:]),
-        (piece.update(shape=(2, *piece.shape)),) * (around - 1), small, 12,
-    )
-    pieces = []
-    for away in range(1, around):
-        pieces.append(lax.ppermute(joined[away - 1], "x", [(i, (i + away) % around) for i in range(around)]))
     rotated = call(
         functools.partial(collect_kernel, around), (place, turned[0], crossed, *pieces),
         jax.ShapeDtypeStruct((2 * PLANE, cols, NB), jnp.float32), small, 12, (), [SMEM] + [VMEM] * (around + 1),

time: 167 us -> 173 us (1.036)
  starting transfers between devices: 65 us -> 74.6 us
  Pallas kernels: 36.5 us -> 29.9 us
  waiting for transfers between devices: 48 us -> 51.6 us
    ppermute x3, waiting for transfers between devices: 3.97 us -> 10.8 us  [whole(): lax.ppermute(shared['pair'], 'x', [(i, (i + shift) % around) for i in ran...]
    ppermute x6, starting transfers between devices: 6.23 us -> 12.9 us  [send(): halo['a', k] = lax.ppermute(val['b', k], ELEM, up)]
    pallas_call x33 -> x34, Pallas kernels: 36.5 us -> 29.9 us  [call(): pl.pallas_call(kernel, out_shape=out_shape, in_specs=in_specs or [VMEM] *...]
    ppermute x7, waiting for transfers between devices: 9.63 us -> 6.49 us  [whole(): parts.append(lax.ppermute(blocks[q], CHIP, to_chip(away, q)))]
    ppermute x6, waiting for transfers between devices: 17.8 us -> 14.9 us  [send(): halo['a', k] = lax.ppermute(val['b', k], ELEM, up)]
    ppermute x6, starting transfers between devices: 25.5 us -> 28.1 us  [send(): halo['b', k] = lax.ppermute(val['a', k], ELEM, down)]
    ppermute x6, waiting for transfers between devices: 4.8 us -> 7.34 us  [send(): halo['b', k] = lax.ppermute(val['a', k], ELEM, down)]
  transfers between devices with their start and end apart: 29 -> 29, of which waited for: 12 -> 17; matrix products, arithmetic and copies ran while one was open for 0% -> 0% of each run, Pallas kernels for 21% -> 14%
where the time goes in v8:
time: 173 us; the launch traced here: 172 us
  starting transfers between devices  74.6 us (43%)
  waiting for transfers between devices  51.6 us (30%)
  Pallas kernels  29.9 us (17%)
  blocking collectives  11 us (6%)
  local copies, waits for them, and re-layouts  4.17 us (2%)
    pallas_call x34, Pallas kernels, call(): pl.pallas_call(kernel, out_shape=out_shape, in_specs=in_specs or [VMEM] *...  29.9 us
    ppermute x6, starting transfers between devices, send(): halo['b', k] = lax.ppermute(val['a', k], ELEM, down)  28.1 us
    ppermute x6, waiting for transfers between devices, send(): halo['a', k] = lax.ppermute(val['b', k], ELEM, up)  14.9 us
    ppermute x6, starting transfers between devices, send(): halo['a', k] = lax.ppermute(val['b', k], ELEM, up)  12.9 us
    ppermute x7, starting transfers between devices, whole(): parts.append(lax.ppermute(blocks[q], CHIP, to_chip(away, q)))  11.4 us
    all_to_all x1, starting transfers between devices, whole(): total = lax.all_to_all(total, ELEM, 0, 0, tiled=True)  11.1 us
    all_to_all x1, blocking collectives, whole(): mine = lax.all_to_all(filtered, CHIP, 0, 0, tiled=True)  11 us
    ppermute x3, waiting for transfers between devices, whole(): lax.ppermute(shared['pair'], 'x', [(i, (i + shift) % around) for i in ran...  10.8 us
  transfers between devices with their start and end apart: 29, of which 17 were waited for; matrix products, arithmetic and copies ran while one was open for 0% of the time, Pallas kernels for 14%

profile of v8, /device:TPU:4, one launch (start us, length us, event | category | flops | bytes accessed | tf_op | source)
XLA Modules:
  0.0 172.4 jit_solution(15317007090344218851)
XLA Ops:
  1.7 3.3 %collective-permute-start.1 = (bf16[16,64,128]{2,1,0:T(8,128)(2,1)S(1)}, bf16[16,64,128]{2,1,0:T(8,128)(2,1)S(1)}, u32[]{:S(2)}, u32[]{:S(2)}) collective-permute-start(bf16[16,64,128]{2,1,0:T(8,128)(2,1)S(1)} %get-tuple-element.67.inner.own.current.rest_0_), channel_id=1, source_target_pairs={{0,16},{16,32},{32,48},{48,64},{64,80},{80,96},{96,112},{112,128},... | collective-permute-start | bytes 786440 | tf_op jit(solution)/shard_map/ppermute | solution.py:228
  5.0 5.4 %collective-permute-start = (bf16[16,64,128]{2,1,0:T(8,128)(2,1)S(1)}, bf16[16,64,128]{2,1,0:T(8,128)(2,1)S(1)}, u32[]{:S(2)}, u32[]{:S(2)}) collective-permute-start(bf16[16,64,128]{2,1,0:T(8,128)(2,1)S(1)} %get-tuple-element.68.own.current.inner.rest_0_), channel_id=1, source_target_pairs={{16,0},{32,16},{48,32},{64,48},{80,64},{96,80},{112,96},{128,112},... | collective-permute-start | bytes 786440 | tf_op jit(solution)/shard_map/ppermute | solution.py:226
  10.4 3.1 %copy-done = bf16[32,7,128,128]{3,2,1,0:T(8,128)(2,1)S(1)} copy-done((bf16[32,7,128,128]{3,2,1,0:T(8,128)(2,1)S(1)}, bf16[32,7,128,128]{3,2,1,0:T(8,128)(2,1)}, u32[]{:S(2)}) %copy-start) | copy-done | bytes 7340056
  17.4 8.8 %collective-permute-start.3 = (bf16[16,64,128]{2,1,0:T(8,128)(2,1)S(1)}, bf16[16,64,128]{2,1,0:T(8,128)(2,1)S(1)}, u32[]{:S(2)}, u32[]{:S(2)}) collective-permute-start(bf16[16,64,128]{2,1,0:T(8,128)(2,1)S(1)} %get-tuple-element.74.inner.own), channel_id=1, source_target_pairs={{16,0},{32,16},{48,32},{64,48},{80,64},{96,80},{112,96},{128,112},... | collective-permute-start | bytes 786440 | tf_op jit(solution)/shard_map/ppermute | solution.py:226
  32.8 7.6 %collective-permute-done.2.halo = bf16[16,64,128]{2,1,0:T(8,128)(2,1)S(1)} collective-permute-done((bf16[16,64,128]{2,1,0:T(8,128)(2,1)S(1)}, bf16[16,64,128]{2,1,0:T(8,128)(2,1)S(1)}, u32[]{:S(2)}, u32[]{:S(2)}) %collective-permute-start.2) | collective-permute-done | bytes 262176 | tf_op jit(solution)/shard_map/ppermute | solution.py:228
  41.0 2.4 %collective-permute-start.4 = (bf16[16,64,128]{2,1,0:T(8,128)(2,1)S(1)}, bf16[16,64,128]{2,1,0:T(8,128)(2,1)S(1)}, u32[]{:S(2)}, u32[]{:S(2)}) collective-permute-start(bf16[16,64,128]{2,1,0:T(8,128)(2,1)S(1)} %get-tuple-element.83.own.inner), channel_id=1, source_target_pairs={{16,0},{32,16},{48,32},{64,48},{80,64},{96,80},{112,96},{128,112},... | collective-permute-start | bytes 786440 | tf_op jit(solution)/shard_map/ppermute | solution.py:226
  45.2 3.7 %collective-permute-start.7 = (bf16[16,64,128]{2,1,0:T(8,128)(2,1)S(1)}, bf16[16,64,128]{2,1,0:T(8,128)(2,1)S(1)}, u32[]{:S(2)}, u32[]{:S(2)}) collective-permute-start(bf16[16,64,128]{2,1,0:T(8,128)(2,1)S(1)} %get-tuple-element.90.inner.own), channel_id=1, source_target_pairs={{16,0},{32,16},{48,32},{64,48},{80,64},{96,80},{112,96},{128,112},... | collective-permute-start | bytes 786440 | tf_op jit(solution)/shard_map/ppermute | solution.py:226
  51.2 2.4 %collective-permute-start.6 = (bf16[16,64,128]{2,1,0:T(8,128)(2,1)S(1)}, bf16[16,64,128]{2,1,0:T(8,128)(2,1)S(1)}, u32[]{:S(2)}, u32[]{:S(2)}) collective-permute-start(bf16[16,64,128]{2,1,0:T(8,128)(2,1)S(1)} %get-tuple-element.91.own.inner), channel_id=1, source_target_pairs={{0,16},{16,32},{32,48},{48,64},{64,80},{80,96},{96,112},{112,128},... | collective-permute-start | bytes 786440 | tf_op jit(solution)/shard_map/ppermute | solution.py:228
  56.1 3.3 %collective-permute-start.9 = (bf16[16,64,128]{2,1,0:T(8,128)(2,1)S(1)}, bf16[16,64,128]{2,1,0:T(8,128)(2,1)S(1)}, u32[]{:S(2)}, u32[]{:S(2)}) collective-permute-start(bf16[16,64,128]{2,1,0:T(8,128)(2,1)S(1)} %get-tuple-element.98.inner.own), channel_id=1, source_target_pairs={{0,16},{16,32},{32,48},{48,64},{64,80},{80,96},{96,112},{112,128},... | collective-permute-start | bytes 786440 | tf_op jit(solution)/shard_map/ppermute | solution.py:228
  63.3 4.3 %collective-permute-start.8 = (bf16[16,64,128]{2,1,0:T(8,128)(2,1)S(1)}, bf16[16,64,128]{2,1,0:T(8,128)(2,1)S(1)}, u32[]{:S(2)}, u32[]{:S(2)}) collective-permute-start(bf16[16,64,128]{2,1,0:T(8,128)(2,1)S(1)} %get-tuple-element.99.own.inner), channel_id=1, source_target_pairs={{16,0},{32,16},{48,32},{64,48},{80,64},{96,80},{112,96},{128,112},... | collective-permute-start | bytes 786440 | tf_op jit(solution)/shard_map/ppermute | solution.py:226
  69.4 3.4 %collective-permute-start.11 = (bf16[16,64,128]{2,1,0:T(8,128)(2,1)S(1)}, bf16[16,64,128]{2,1,0:T(8,128)(2,1)S(1)}, u32[]{:S(2)}, u32[]{:S(2)}) collective-permute-start(bf16[16,64,128]{2,1,0:T(8,128)(2,1)S(1)} %get-tuple-element.105.inner.own), channel_id=1, source_target_pairs={{16,0},{32,16},{48,32},{64,48},{80,64},{96,80},{112,96},{128,112},... | collective-permute-start | bytes 786440 | tf_op jit(solution)/shard_map/ppermute | solution.py:226
  73.9 4.3 %collective-permute-done.8.halo = bf16[16,64,128]{2,1,0:T(8,128)(2,1)S(1)} collective-permute-done((bf16[16,64,128]{2,1,0:T(8,128)(2,1)S(1)}, bf16[16,64,128]{2,1,0:T(8,128)(2,1)S(1)}, u32[]{:S(2)}, u32[]{:S(2)}) %collective-permute-start.8) | collective-permute-done | bytes 262176 | tf_op jit(solution)/shard_map/ppermute | solution.py:226
  78.9 3.8 %collective-permute-start.10 = (bf16[16,64,128]{2,1,0:T(8,128)(2,1)S(1)}, bf16[16,64,128]{2,1,0:T(8,128)(2,1)S(1)}, u32[]{:S(2)}, u32[]{:S(2)}) collective-permute-start(bf16[16,64,128]{2,1,0:T(8,128)(2,1)S(1)} %get-tuple-element.106.own.inner), channel_id=1, source_target_pairs={{0,16},{16,32},{32,48},{48,64},{64,80},{80,96},{96,112},{112,128},... | collective-permute-start | bytes 786440 | tf_op jit(solution)/shard_map/ppermute | solution.py:228
  85.6 3.5 %collective-permute-done.10.halo = bf16[16,64,128]{2,1,0:T(8,128)(2,1)S(1)} collective-permute-done((bf16[16,64,128]{2,1,0:T(8,128)(2,1)S(1)}, bf16[16,64,128]{2,1,0:T(8,128)(2,1)S(1)}, u32[]{:S(2)}, u32[]{:S(2)}) %collective-permute-start.10) | collective-permute-done | bytes 262176 | tf_op jit(solution)/shard_map/ppermute | solution.py:228
  89.8 11.0 %all_to_all.10 = bf16[32,64,128]{2,1,0:T(8,128)(2,1)S(1)} all-to-all(bf16[32,64,128]{2,1,0:T(8,128)(2,1)S(1)} %shard_map.74), channel_id=1, replica_groups=mesh['z'=8,'yh'=2,'x'=4,'yl'=2,'c'=2] {'x','yl'}, dimensions={0} | all-to-all | bytes 1048576 | tf_op jit(solution)/shard_map/all_to_all | solution.py:279
  101.1 5.6 %collective-permute-done.13 = bf16[64,1024]{1,0:T(8,128)(2,1)S(1)} collective-permute-done((bf16[64,1024]{1,0:T(8,128)(2,1)S(1)}, bf16[64,1024]{1,0:T(8,128)(2,1)S(1)}, u32[]{:S(2)}, u32[]{:S(2)}) %collective-permute-start.13) | collective-permute-done | bytes 131104 | tf_op jit(solution)/shard_map/ppermute | solution.py:232
  111.6 4.4 %collective-permute-done.14.ritz_next = bf16[2,64,1024]{2,1,0:T(8,128)(2,1)S(1)} collective-permute-done((bf16[2,64,1024]{2,1,0:T(8,128)(2,1)S(1)}, bf16[2,64,1024]{2,1,0:T(8,128)(2,1)S(1)}, u32[]{:S(2)}, u32[]{:S(2)}) %collective-permute-start.14) | collective-permute-done | bytes 262176 | tf_op jit(solution)/shard_map/ppermute | solution.py:237
  116.0 2.5 %collective-permute-done.15.ritz_far = bf16[2,64,1024]{2,1,0:T(8,128)(2,1)S(1)} collective-permute-done((bf16[2,64,1024]{2,1,0:T(8,128)(2,1)S(1)}, bf16[2,64,1024]{2,1,0:T(8,128)(2,1)S(1)}, u32[]{:S(2)}, u32[]{:S(2)}) %collective-permute-start.15) | collective-permute-done | bytes 262176 | tf_op jit(solution)/shard_map/ppermute | solution.py:237
  118.4 4.0 %collective-permute-done.16.ritz_back = bf16[2,64,1024]{2,1,0:T(8,128)(2,1)S(1)} collective-permute-done((bf16[2,64,1024]{2,1,0:T(8,128)(2,1)S(1)}, bf16[2,64,1024]{2,1,0:T(8,128)(2,1)S(1)}, u32[]{:S(2)}, u32[]{:S(2)}) %collective-permute-start.16) | collective-permute-done | bytes 262176 | tf_op jit(solution)/shard_map/ppermute | solution.py:237
  132.8 2.7 %collective-permute-start.21 = (bf16[8,64,128]{2,1,0:T(8,128)(2,1)S(1)}, bf16[8,64,128]{2,1,0:T(8,128)(2,1)S(1)}, u32[]{:S(2)}, u32[]{:S(2)}) collective-permute-start(bf16[8,64,128]{2,1,0:T(8,128)(2,1)S(1)} %get-tuple-element.115), channel_id=1, source_target_pairs={{0,4},{2,6},{4,8},{6,10},{8,12},{10,14},{12,0},{14,2},{1,5},{3,7},... | collective-permute-start | bytes 393224 | tf_op jit(solution)/shard_map/ppermute | solution.py:323
  136.6 2.5 %collective-permute-start.19 = (bf16[8,64,128]{2,1,0:T(8,128)(2,1)S(1)}, bf16[8,64,128]{2,1,0:T(8,128)(2,1)S(1)}, u32[]{:S(2)}, u32[]{:S(2)}) collective-permute-start(bf16[8,64,128]{2,1,0:T(8,128)(2,1)S(1)} %get-tuple-element.113), channel_id=1, source_target_pairs={{0,8},{2,10},{4,12},{6,14},{8,0},{10,2},{12,4},{14,6},{1,9},{3,11}... | collective-permute-start | bytes 393224 | tf_op jit(solution)/shard_map/ppermute | solution.py:323
  140.5 3.3 %collective-permute-done.18.refs_2_ = bf16[8,64,128]{2,1,0:T(8,128)(2,1)S(1)} collective-permute-done((bf16[8,64,128]{2,1,0:T(8,128)(2,1)S(1)}, bf16[8,64,128]{2,1,0:T(8,128)(2,1)S(1)}, u32[]{:S(2)}, u32[]{:S(2)}) %collective-permute-start.18) | collective-permute-done | bytes 131104 | tf_op jit(solution)/shard_map/ppermute | solution.py:323
  147.9 11.1 %all-to-all-start.1 = ((bf16[16,32,128]{2,1,0:T(8,128)(2,1)}), bf16[16,32,128]{2,1,0:T(8,128)(2,1)S(1)}, u32[]{:S(2)}, u32[]{:S(2)}) async-start(bf16[16,32,128]{2,1,0:T(8,128)(2,1)} %shard_map.80), calls=%async_computation.1 | async-start | bytes 262144 | tf_op jit(solution)/shard_map/all_to_all | solution.py:335
  163.6 6.5 %all-to-all-done.1.got = bf16[16,32,128]{2,1,0:T(8,128)(2,1)S(1)} async-done(((bf16[16,32,128]{2,1,0:T(8,128)(2,1)}), bf16[16,32,128]{2,1,0:T(8,128)(2,1)S(1)}, u32[]{:S(2)}, u32[]{:S(2)}) %all-to-all-start.1) | async-done | bytes 131104 | tf_op jit(solution)/shard_map/all_to_all | solution.py:335
  (81 shorter events, 58.6 us)
Async XLA Ops:
  1.7 15.0 %collective-permute-start.1 = (bf16[16,64,128]{2,1,0:T(8,128)(2,1)S(1)}, bf16[16,64,128]{2,1,0:T(8,128)(2,1)S(1)}, u32[]{:S(2)}, u32[]{:S(2)}) collective-permute-start(bf16[16,64,128]{2,1,0:T(8,128)(2,1)S(1)} %get-tuple-element.67.inner.own.current.rest_0_), channel_id=1, source_target_pairs={{0,16},{16,32},{32,48},{48,64},{64,80},{80,96},{96,112},{112,128},... | collective-permute-start | bytes 786440 | tf_op jit(solution)/shard_map/ppermute | solution.py:228
  5.0 22.3 %collective-permute-start = (bf16[16,64,128]{2,1,0:T(8,128)(2,1)S(1)}, bf16[16,64,128]{2,1,0:T(8,128)(2,1)S(1)}, u32[]{:S(2)}, u32[]{:S(2)}) collective-permute-start(bf16[16,64,128]{2,1,0:T(8,128)(2,1)S(1)} %get-tuple-element.68.own.current.inner.rest_0_), channel_id=1, source_target_pairs={{16,0},{32,16},{48,32},{64,48},{80,64},{96,80},{112,96},{128,112},... | collective-permute-start | bytes 786440 | tf_op jit(solution)/shard_map/ppermute | solution.py:226
  17.4 13.6 %collective-permute-start.3 = (bf16[16,64,128]{2,1,0:T(8,128)(2,1)S(1)}, bf16[16,64,128]{2,1,0:T(8,128)(2,1)S(1)}, u32[]{:S(2)}, u32[]{:S(2)}) collective-permute-start(bf16[16,64,128]{2,1,0:T(8,128)(2,1)S(1)} %get-tuple-element.74.inner.own), channel_id=1, source_target_pairs={{16,0},{32,16},{48,32},{64,48},{80,64},{96,80},{112,96},{128,112},... | collective-permute-start | bytes 786440 | tf_op jit(solution)/shard_map/ppermute | solution.py:226
  28.0 12.4 %collective-permute-start.2 = (bf16[16,64,128]{2,1,0:T(8,128)(2,1)S(1)}, bf16[16,64,128]{2,1,0:T(8,128)(2,1)S(1)}, u32[]{:S(2)}, u32[]{:S(2)}) collective-permute-start(bf16[16,64,128]{2,1,0:T(8,128)(2,1)S(1)} %get-tuple-element.75.own.inner), channel_id=1, source_target_pairs={{0,16},{16,32},{32,48},{48,64},{64,80},{80,96},{96,112},{112,128},... | collective-permute-start | bytes 786440 | tf_op jit(solution)/shard_map/ppermute | solution.py:228
  31.6 12.9 %collective-permute-start.5 = (bf16[16,64,128]{2,1,0:T(8,128)(2,1)S(1)}, bf16[16,64,128]{2,1,0:T(8,128)(2,1)S(1)}, u32[]{:S(2)}, u32[]{:S(2)}) collective-permute-start(bf16[16,64,128]{2,1,0:T(8,128)(2,1)S(1)} %get-tuple-element.82.inner.own), channel_id=1, source_target_pairs={{0,16},{16,32},{32,48},{48,64},{64,80},{80,96},{96,112},{112,128},... | collective-permute-start | bytes 786440 | tf_op jit(solution)/shard_map/ppermute | solution.py:228
  41.0 9.5 %collective-permute-start.4 = (bf16[16,64,128]{2,1,0:T(8,128)(2,1)S(1)}, bf16[16,64,128]{2,1,0:T(8,128)(2,1)S(1)}, u32[]{:S(2)}, u32[]{:S(2)}) collective-permute-start(bf16[16,64,128]{2,1,0:T(8,128)(2,1)S(1)} %get-tuple-element.83.own.inner), channel_id=1, source_target_pairs={{16,0},{32,16},{48,32},{64,48},{80,64},{96,80},{112,96},{128,112},... | collective-permute-start | bytes 786440 | tf_op jit(solution)/shard_map/ppermute | solution.py:226
  45.2 10.2 %collective-permute-start.7 = (bf16[16,64,128]{2,1,0:T(8,128)(2,1)S(1)}, bf16[16,64,128]{2,1,0:T(8,128)(2,1)S(1)}, u32[]{:S(2)}, u32[]{:S(2)}) collective-permute-start(bf16[16,64,128]{2,1,0:T(8,128)(2,1)S(1)} %get-tuple-element.90.inner.own), channel_id=1, source_target_pairs={{16,0},{32,16},{48,32},{64,48},{80,64},{96,80},{112,96},{128,112},... | collective-permute-start | bytes 786440 | tf_op jit(solution)/shard_map/ppermute | solution.py:226
  51.2 11.4 %collective-permute-start.6 = (bf16[16,64,128]{2,1,0:T(8,128)(2,1)S(1)}, bf16[16,64,128]{2,1,0:T(8,128)(2,1)S(1)}, u32[]{:S(2)}, u32[]{:S(2)}) collective-permute-start(bf16[16,64,128]{2,1,0:T(8,128)(2,1)S(1)} %get-tuple-element.91.own.inner), channel_id=1, source_target_pairs={{0,16},{16,32},{32,48},{48,64},{64,80},{80,96},{96,112},{112,128},... | collective-permute-start | bytes 786440 | tf_op jit(solution)/shard_map/ppermute | solution.py:228
  56.1 12.6 %collective-permute-start.9 = (bf16[16,64,128]{2,1,0:T(8,128)(2,1)S(1)}, bf16[16,64,128]{2,1,0:T(8,128)(2,1)S(1)}, u32[]{:S(2)}, u32[]{:S(2)}) collective-permute-start(bf16[16,64,128]{2,1,0:T(8,128)(2,1)S(1)} %get-tuple-element.98.inner.own), channel_id=1, source_target_pairs={{0,16},{16,32},{32,48},{48,64},{64,80},{80,96},{96,112},{112,128},... | collective-permute-start | bytes 786440 | tf_op jit(solution)/shard_map/ppermute | solution.py:228
  63.3 14.9 %collective-permute-start.8 = (bf16[16,64,128]{2,1,0:T(8,128)(2,1)S(1)}, bf16[16,64,128]{2,1,0:T(8,128)(2,1)S(1)}, u32[]{:S(2)}, u32[]{:S(2)}) collective-permute-start(bf16[16,64,128]{2,1,0:T(8,128)(2,1)S(1)} %get-tuple-element.99.own.inner), channel_id=1, source_target_pairs={{16,0},{32,16},{48,32},{64,48},{80,64},{96,80},{112,96},{128,112},... | collective-permute-start | bytes 786440 | tf_op jit(solution)/shard_map/ppermute | solution.py:226
  69.4 14.4 %collective-permute-start.11 = (bf16[16,64,128]{2,1,0:T(8,128)(2,1)S(1)}, bf16[16,64,128]{2,1,0:T(8,128)(2,1)S(1)}, u32[]{:S(2)}, u32[]{:S(2)}) collective-permute-start(bf16[16,64,128]{2,1,0:T(8,128)(2,1)S(1)} %get-tuple-element.105.inner.own), channel_id=1, source_target_pairs={{16,0},{32,16},{48,32},{64,48},{80,64},{96,80},{112,96},{128,112},... | collective-permute-start | bytes 786440 | tf_op jit(solution)/shard_map/ppermute | solution.py:226
  78.9 10.2 %collective-permute-start.10 = (bf16[16,64,128]{2,1,0:T(8,128)(2,1)S(1)}, bf16[16,64,128]{2,1,0:T(8,128)(2,1)S(1)}, u32[]{:S(2)}, u32[]{:S(2)}) collective-permute-start(bf16[16,64,128]{2,1,0:T(8,128)(2,1)S(1)} %get-tuple-element.106.own.inner), channel_id=1, source_target_pairs={{0,16},{16,32},{32,48},{48,64},{64,80},{80,96},{96,112},{112,128},... | collective-permute-start | bytes 786440 | tf_op jit(solution)/shard_map/ppermute | solution.py:228
  100.8 21.6 %collective-permute-start.12 = (bf16[8,4,64,128]{3,2,1,0:T(8,128)(2,1)S(1)}, bf16[8,4,64,128]{3,2,1,0:T(8,128)(2,1)S(1)}, u32[]{:S(2)}, u32[]{:S(2)}) collective-permute-start(bf16[8,4,64,128]{3,2,1,0:T(8,128)(2,1)S(1)} %bitcast.12), channel_id=1, source_target_pairs={{0,1},{1,0},{2,3},{3,2},{4,5},{5,4},{6,7},{7,6},{8,9},{9,8},{10,11... | collective-permute-start | bytes 1572872 | tf_op jit(solution)/shard_map/ppermute | solution.py:281
  106.7 9.3 %collective-permute-start.14 = (bf16[2,64,1024]{2,1,0:T(8,128)(2,1)S(1)}, bf16[2,64,1024]{2,1,0:T(8,128)(2,1)S(1)}, u32[]{:S(2)}, u32[]{:S(2)}) collective-permute-start(bf16[2,64,1024]{2,1,0:T(8,128)(2,1)S(1)} %pad_maximum_fusion.ritz), channel_id=1, source_target_pairs={{0,12},{4,0},{8,4},{12,8},{1,13},{5,1},{9,5},{13,9},{2,14},{6,2},{... | collective-permute-start | bytes 786440 | tf_op jit(solution)/shard_map/ppermute | solution.py:237
  107.7 10.7 %collective-permute-start.15 = (bf16[2,64,1024]{2,1,0:T(8,128)(2,1)S(1)}, bf16[2,64,1024]{2,1,0:T(8,128)(2,1)S(1)}, u32[]{:S(2)}, u32[]{:S(2)}) collective-permute-start(bf16[2,64,1024]{2,1,0:T(8,128)(2,1)S(1)} %pad_maximum_fusion.ritz), channel_id=1, source_target_pairs={{0,8},{4,12},{8,0},{12,4},{1,9},{5,13},{9,1},{13,5},{2,10},{6,14},... | collective-permute-start | bytes 786440 | tf_op jit(solution)/shard_map/ppermute | solution.py:237
  110.0 12.4 %collective-permute-start.16 = (bf16[2,64,1024]{2,1,0:T(8,128)(2,1)S(1)}, bf16[2,64,1024]{2,1,0:T(8,128)(2,1)S(1)}, u32[]{:S(2)}, u32[]{:S(2)}) collective-permute-start(bf16[2,64,1024]{2,1,0:T(8,128)(2,1)S(1)} %pad_maximum_fusion.ritz), channel_id=1, source_target_pairs={{0,4},{4,8},{8,12},{12,0},{1,5},{5,9},{9,13},{13,1},{2,6},{6,10},{... | collective-permute-start | bytes 786440 | tf_op jit(solution)/shard_map/ppermute | solution.py:237
  125.9 9.6 %collective-permute-start.22 = (bf16[8,64,128]{2,1,0:T(8,128)(2,1)S(1)}, bf16[8,64,128]{2,1,0:T(8,128)(2,1)S(1)}, u32[]{:S(2)}, u32[]{:S(2)}) collective-permute-start(bf16[8,64,128]{2,1,0:T(8,128)(2,1)S(1)} %get-tuple-element.116), channel_id=1, source_target_pairs={{0,14},{2,12},{4,2},{6,0},{8,6},{10,4},{12,10},{14,8},{1,15},{3,13... | collective-permute-start | bytes 393224 | tf_op jit(solution)/shard_map/ppermute | solution.py:323
  127.5 9.1 %collective-permute-start.23 = (bf16[8,64,128]{2,1,0:T(8,128)(2,1)S(1)}, bf16[8,64,128]{2,1,0:T(8,128)(2,1)S(1)}, u32[]{:S(2)}, u32[]{:S(2)}) collective-permute-start(bf16[8,64,128]{2,1,0:T(8,128)(2,1)S(1)} %get-tuple-element.117), channel_id=1, source_target_pairs={{0,12},{2,14},{4,0},{6,2},{8,4},{10,6},{12,8},{14,10},{1,13},{3,15... | collective-permute-start | bytes 393224 | tf_op jit(solution)/shard_map/ppermute | solution.py:323
  130.4 8.7 %collective-permute-start.20 = (bf16[8,64,128]{2,1,0:T(8,128)(2,1)S(1)}, bf16[8,64,128]{2,1,0:T(8,128)(2,1)S(1)}, u32[]{:S(2)}, u32[]{:S(2)}) collective-permute-start(bf16[8,64,128]{2,1,0:T(8,128)(2,1)S(1)} %get-tuple-element.114), channel_id=1, source_target_pairs={{0,6},{2,4},{4,10},{6,8},{8,14},{10,12},{12,2},{14,0},{1,7},{3,5},... | collective-permute-start | bytes 393224 | tf_op jit(solution)/shard_map/ppermute | solution.py:323
  130.5 28.5 %collective-permute-start.24 = (bf16[4,4,64,128]{3,2,1,0:T(8,128)(2,1)S(1)}, bf16[4,4,64,128]{3,2,1,0:T(8,128)(2,1)S(1)}, u32[]{:S(2)}, u32[]{:S(2)}) collective-permute-start(bf16[4,4,64,128]{3,2,1,0:T(8,128)(2,1)S(1)} %get-tuple-element.119), channel_id=1, source_target_pairs={{0,2},{2,0},{1,3},{3,1},{4,6},{6,4},{5,7},{7,5},{8,10},{10,8},{9,1... | collective-permute-start | bytes 786440 | tf_op jit(solution)/shard_map/ppermute | solution.py:302
  147.9 22.2 %all-to-all-start.1 = ((bf16[16,32,128]{2,1,0:T(8,128)(2,1)}), bf16[16,32,128]{2,1,0:T(8,128)(2,1)S(1)}, u32[]{:S(2)}, u32[]{:S(2)}) async-start(bf16[16,32,128]{2,1,0:T(8,128)(2,1)} %shard_map.80), calls=%async_computation.1 | async-start | bytes 262144 | tf_op jit(solution)/shard_map/all_to_all | solution.py:335
  159.0 11.8 %collective-permute-start.25 = (bf16[2,4,64,128]{3,2,1,0:T(8,128)(2,1)S(1)}, bf16[2,4,64,128]{3,2,1,0:T(8,128)(2,1)S(1)}, u32[]{:S(2)}, u32[]{:S(2)}) collective-permute-start(bf16[2,4,64,128]{3,2,1,0:T(8,128)(2,1)S(1)} %get-tuple-element.123), channel_id=1, source_target_pairs={{0,4},{4,8},{8,12},{12,0},{1,5},{5,9},{9,13},{13,1},{2,6},{6,10},{... | collective-permute-start | bytes 393224 | tf_op jit(solution)/shard_map/ppermute | solution.py:330
  160.3 10.5 %collective-permute-start.26 = (bf16[2,4,64,128]{3,2,1,0:T(8,128)(2,1)S(1)}, bf16[2,4,64,128]{3,2,1,0:T(8,128)(2,1)S(1)}, u32[]{:S(2)}, u32[]{:S(2)}) collective-permute-start(bf16[2,4,64,128]{3,2,1,0:T(8,128)(2,1)S(1)} %get-tuple-element.124), channel_id=1, source_target_pairs={{0,8},{4,12},{8,0},{12,4},{1,9},{5,13},{9,1},{13,5},{2,10},{6,14},... | collective-permute-start | bytes 393224 | tf_op jit(solution)/shard_map/ppermute | solution.py:330
  161.3 9.5 %collective-permute-start.27 = (bf16[2,4,64,128]{3,2,1,0:T(8,128)(2,1)S(1)}, bf16[2,4,64,128]{3,2,1,0:T(8,128)(2,1)S(1)}, u32[]{:S(2)}, u32[]{:S(2)}) collective-permute-start(bf16[2,4,64,128]{3,2,1,0:T(8,128)(2,1)S(1)} %get-tuple-element.125), channel_id=1, source_target_pairs={{0,12},{4,0},{8,4},{12,8},{1,13},{5,1},{9,5},{13,9},{2,14},{6,2},{... | collective-permute-start | bytes 393224 | tf_op jit(solution)/shard_map/ppermute | solution.py:330
  (9 other events, 83.4 us)

commit v9 on v8

--- a/solution.py
+++ b/solution.py
@@ -112,7 +112,8 @@
     )(*operands)
 
 
-def turn_kernel(place, mine, other, ritz, ritz_next, ritz_far, ritz_back, rows, *outs):
+def part_kernel(around, place, mine, other, rows, *refs):
+    outs, across = refs[:-1], refs[-1]
     chips, held, cols = mine.shape[0], mine.shape[1], mine.shape[2]
 
     def fill(parity, source):
@@ -130,6 +131,23 @@
         fill(1, mine)
         fill(0, other)
 
+    for t in range(chips):
+        for el in range(held):
+            across[pl.ds(el * NB, NB), pl.ds(t * NB, NB)] = rows[pl.ds(t * NB, NB), pl.ds(el * NB, NB)].T
+    for away in range(around):
+        line = lax.rem(place[0] + away, around) * 2
+        left = []
+        for q in range(2):
+            chip = line + (place[1] if q == 0 else 1 - place[1])
+            left.append(rows[pl.ds(pl.multiple_of((2 * chip + place[2]) * cols, cols), cols), :])
+        part = product(jnp.concatenate(left, axis=0), across[...], PLAIN).astype(jnp.bfloat16)
+        for q in range(2):
+            for t in range(chips):
+                outs[2 * away + q][t] = part[q * cols : (q + 1) * cols, t * NB : (t + 1) * NB]
+
+
+def turn_kernel(rows, ritz, ritz_next, ritz_far, ritz_back, *outs):
+    held, cols = outs[0].shape[0], outs[0].shape[1]
     for away, source in enumerate((ritz, ritz_next, ritz_far, ritz_back)):
         turned = product(source[...].reshape(2 * cols, -1), rows[...], PLAIN).astype(jnp.bfloat16)
         for el in range(held):
@@ -137,35 +155,9 @@
             outs[4][away, el] = turned[cols:, el * NB : (el + 1) * NB]
 
 
-def part_blocks(around, away, place, rows, across, outs):
-    chips, cols = outs[0].shape[0], outs[0].shape[1]
-    line = lax.rem(place[0] + away, around) * 2
-    left = []
-    for q in range(2):
-        chip = line + (place[1] if q == 0 else 1 - place[1])
-        left.append(rows[pl.ds(pl.multiple_of((2 * chip + place[2]) * cols, cols), cols), :])
-    part = product(jnp.concatenate(left, axis=0), across[...], PLAIN).astype(jnp.bfloat16)
-    for q in range(2):
-        for t in range(chips):
-            outs[q][t] = part[q * cols : (q + 1) * cols, t * NB : (t + 1) * NB]
-
-
-def first_part_kernel(around, away, place, rows, across, *outs):
-    for t in range(rows.shape[0] // NB):
-        for el in range(rows.shape[1] // NB):
-            across[pl.ds(el * NB, NB), pl.ds(t * NB, NB)] = rows[pl.ds(t * NB, NB), pl.ds(el * NB, NB)].T
-    part_blocks(around, away, place, rows, across, outs)
-
-
-def part_kernel(around, away, place, rows, across, *outs):
-    part_blocks(around, away, place, rows, across, outs)
-
-
-def join_kernel(crossed, *refs):
-    count = len(refs) // 2
-    for away in range(count):
-        refs[count + away][0] = refs[away][...]
-        refs[count + away][1] = crossed[away + 1]
+def part_ways_kernel(crossed, *outs):
+    for away, out in enumerate(outs):
+        out[...] = crossed[away + 1]
 
 
 def collect_kernel(around, place, here, crossed, *refs):
@@ -177,7 +169,7 @@
             line = lax.rem(place[0] + around - away, around) * 2 + near
             for el in range(held):
                 if away:
-                    piece = pieces[away - 1][q, el]
+                    piece = pieces[q * (around - 1) + away - 1][el]
                 else:
                     piece = crossed[0, el] if q else here[el]
                 out[line * held + el] = piece.astype(jnp.float32)
@@ -288,60 +280,48 @@
     def to_chip(away, q):
         return [(i, (i // 2 + away) % around * 2 + (i + q) % 2) for i in range(chips)]
 
+    block = jax.ShapeDtypeStruct((chips, cols, NB), jnp.bfloat16)
+    rows, *blocks = call(
+        functools.partial(part_kernel, around), (place, mine, theirs),
+        (jax.ShapeDtypeStruct((2 * chips * cols, depth), jnp.bfloat16), *(block,) * chips),
+        flops, 16, (pltpu.VMEM((depth, 2 * chips * cols), jnp.bfloat16),), [SMEM, VMEM, VMEM],
+    )
+    parts = [blocks[0]]
+    for away, q in SENT:
+        parts.append(lax.ppermute(blocks[2 * away + q], CHIP, to_chip(away, q)))
     piece = jax.ShapeDtypeStruct((held, cols, NB), jnp.bfloat16)
-    rows, *turned, other_y = call(
-        turn_kernel,
-        (place, mine, theirs, shared["pair"], shared[around - 1], shared[2], shared[1]),
-        (
-            jax.ShapeDtypeStruct((2 * chips * cols, depth), jnp.bfloat16),
-            *(piece,) * around,
-            piece.update(shape=(around, *piece.shape)),
-        ),
-        flops, 16, (), [SMEM] + [VMEM] * 6,
+    *turned, other_y = call(
+        turn_kernel, (rows, shared["pair"], shared[around - 1], shared[2], shared[1]),
+        (piece,) * around + (piece.update(shape=(around, *piece.shape)),), flops, 16,
     )
     crossed = lax.ppermute(other_y, "yl", [(0, 1), (1, 0)])
-
-    block = jax.ShapeDtypeStruct((chips, cols, NB), jnp.bfloat16)
-    across = None
-    parts = []
-    for away in (0, 2, 1, around - 1):
-        if across is None:
-            across, *blocks = call(
-                functools.partial(first_part_kernel, around, away), (place, rows),
-                (jax.ShapeDtypeStruct((depth, 2 * chips * cols), jnp.bfloat16), block, block),
-                flops, 16, (), [SMEM, VMEM],
-            )
-        else:
-            blocks = call(
-                functools.partial(part_kernel, around, away), (place, rows, across),
-                (block, block), flops, 16, (), [SMEM, VMEM, VMEM],
-            )
-        for q in (1, 0):
-            if away == 0 and q == 0:
-                parts.append(blocks[0])
-                continue
-            parts.append(lax.ppermute(blocks[q], CHIP, to_chip(away, q)))
-    joined = call(
-        join_kernel, (crossed, *turned[1:]),
-        (piece.update(shape=(2, *piece.shape)),) * (around - 1), small, 12,
-    )
     pieces = []
+
+    def along(away, value):
+        pieces.append(lax.ppermute(value, "x", [(i, (i + away) % around) for i in range(around)]))
+
     for away in range(1, around):
-        pieces.append(lax.ppermute(joined[away - 1], "x", [(i, (i + away) % around) for i in range(around)]))
+        along(away, turned[away])
     total = call(
         margin_rows_kernel, parts,
         jax.ShapeDtypeStruct((slabs, cols // 2, 2 * cols), jnp.bfloat16), small, 12,
     )
     total = lax.all_to_all(total, ELEM, 0, 0, tiled=True)
+    ways = call(part_ways_kernel, (crossed,), (piece,) * (around - 1), small, 12)
+    for away in range(1, around):
+        along(away, ways[away - 1])
     rotated = call(
         functools.partial(collect_kernel, around), (place, turned[0], crossed, *pieces),
-        jax.ShapeDtypeStruct((2 * PLANE, cols, NB), jnp.float32), small, 12, (), [SMEM] + [VMEM] * (around + 1),
+        jax.ShapeDtypeStruct((2 * PLANE, cols, NB), jnp.float32), small, 12, (), [SMEM] + [VMEM] * (2 * around),
     )
     margin = call(
         functools.partial(margin_kernel, 1.0 / rows_total), (total,),
         jax.ShapeDtypeStruct((cols, cols), jnp.float32), small, 12,
     )
     return margin, jnp.swapaxes(rotated, 1, 2)
+
+
+SENT = ((2, 1), (0, 1), (1, 1), (3, 1), (2, 0), (1, 0), (3, 0))
 
 
 def solution(mesh):

time: 173 us -> 163 us (0.942)
  waiting for transfers between devices: 51.6 us -> 37 us
  starting transfers between devices: 74.6 us -> 81.2 us
  Pallas kernels: 29.9 us -> 27.2 us
    ppermute x3, waiting for transfers between devices: 10.8 us -> 0.82 us  [whole(): lax.ppermute(shared['pair'], 'x', [(i, (i + shift) % around) for i in ran...]
    ppermute x10 -> x13, starting transfers between devices: 16 us -> 24.1 us  [the longest x7 14.8 us: whole(): parts.append(lax.ppermute(blocks[2 * away + q], CHIP, to_chip(away, q)))]
    all_to_all x1, waiting for transfers between devices: 6.45 us -> 0.01 us  [whole(): total = lax.all_to_all(total, ELEM, 0, 0, tiled=True)]
    pallas_call x34 -> x31, Pallas kernels: 29.9 us -> 27.2 us  [call(): pl.pallas_call(kernel, out_shape=out_shape, in_specs=in_specs or [VMEM] *...]
    ppermute x10 -> x13, waiting for transfers between devices: 6.5 us -> 8.36 us  [the longest x7 4.7 us: whole(): parts.append(lax.ppermute(blocks[2 * away + q], CHIP, to_chip(away, q)))]
  transfers between devices with their start and end apart: 29 -> 32, of which waited for: 17 -> 18; matrix products, arithmetic and copies ran while one was open for 0% -> 0% of each run, Pallas kernels for 14% -> 16%
where the time goes in v9:
time: 163 us; the launch traced here: 162 us
  starting transfers between devices  81.2 us (50%)
  waiting for transfers between devices  37 us (23%)
  Pallas kernels  27.2 us (17%)
  blocking collectives  11 us (7%)
  local copies, waits for them, and re-layouts  4.17 us (3%)
    ppermute x6, starting transfers between devices, send(): halo['b', k] = lax.ppermute(val['a', k], ELEM, down)  28.1 us
    pallas_call x31, Pallas kernels, call(): pl.pallas_call(kernel, out_shape=out_shape, in_specs=in_specs or [VMEM] *...  27.2 us
    ppermute x6, waiting for transfers between devices, send(): halo['a', k] = lax.ppermute(val['b', k], ELEM, up)  14.9 us
    ppermute x7, starting transfers between devices, whole(): parts.append(lax.ppermute(blocks[2 * away + q], CHIP, to_chip(away, q)))  14.8 us
    ppermute x6, starting transfers between devices, send(): halo['a', k] = lax.ppermute(val['b', k], ELEM, up)  12.9 us
    all_to_all x1, starting transfers between devices, whole(): total = lax.all_to_all(total, ELEM, 0, 0, tiled=True)  11.1 us
    all_to_all x1, blocking collectives, whole(): mine = lax.all_to_all(filtered, CHIP, 0, 0, tiled=True)  11 us
    ppermute x6, starting transfers between devices, along(): lax.ppermute(value, 'x', [(i, (i + away) % around) for i in range(around)])  9.23 us
  transfers between devices with their start and end apart: 32, of which 18 were waited for; matrix products, arithmetic and copies ran while one was open for 0% of the time, Pallas kernels for 16%

profile of v9, /device:TPU:4, one launch (start us, length us, event | category | flops | bytes accessed | tf_op | source)
XLA Modules:
  0.0 161.6 jit_solution(10412566270769609897)
XLA Ops:
  1.7 3.3 %collective-permute-start.1 = (bf16[16,64,128]{2,1,0:T(8,128)(2,1)S(1)}, bf16[16,64,128]{2,1,0:T(8,128)(2,1)S(1)}, u32[]{:S(2)}, u32[]{:S(2)}) collective-permute-start(bf16[16,64,128]{2,1,0:T(8,128)(2,1)S(1)} %get-tuple-element.66.inner.own.current.rest_0_), channel_id=1, source_target_pairs={{0,16},{16,32},{32,48},{48,64},{64,80},{80,96},{96,112},{112,128},... | collective-permute-start | bytes 786440 | tf_op jit(solution)/shard_map/ppermute | solution.py:220
  5.0 5.4 %collective-permute-start = (bf16[16,64,128]{2,1,0:T(8,128)(2,1)S(1)}, bf16[16,64,128]{2,1,0:T(8,128)(2,1)S(1)}, u32[]{:S(2)}, u32[]{:S(2)}) collective-permute-start(bf16[16,64,128]{2,1,0:T(8,128)(2,1)S(1)} %get-tuple-element.67.own.current.inner.rest_0_), channel_id=1, source_target_pairs={{16,0},{32,16},{48,32},{64,48},{80,64},{96,80},{112,96},{128,112},... | collective-permute-start | bytes 786440 | tf_op jit(solution)/shard_map/ppermute | solution.py:218
  10.4 3.1 %copy-done = bf16[32,7,128,128]{3,2,1,0:T(8,128)(2,1)S(1)} copy-done((bf16[32,7,128,128]{3,2,1,0:T(8,128)(2,1)S(1)}, bf16[32,7,128,128]{3,2,1,0:T(8,128)(2,1)}, u32[]{:S(2)}) %copy-start) | copy-done | bytes 7340056
  17.4 8.8 %collective-permute-start.3 = (bf16[16,64,128]{2,1,0:T(8,128)(2,1)S(1)}, bf16[16,64,128]{2,1,0:T(8,128)(2,1)S(1)}, u32[]{:S(2)}, u32[]{:S(2)}) collective-permute-start(bf16[16,64,128]{2,1,0:T(8,128)(2,1)S(1)} %get-tuple-element.73.inner.own), channel_id=1, source_target_pairs={{16,0},{32,16},{48,32},{64,48},{80,64},{96,80},{112,96},{128,112},... | collective-permute-start | bytes 786440 | tf_op jit(solution)/shard_map/ppermute | solution.py:218
  32.8 7.6 %collective-permute-done.2.halo = bf16[16,64,128]{2,1,0:T(8,128)(2,1)S(1)} collective-permute-done((bf16[16,64,128]{2,1,0:T(8,128)(2,1)S(1)}, bf16[16,64,128]{2,1,0:T(8,128)(2,1)S(1)}, u32[]{:S(2)}, u32[]{:S(2)}) %collective-permute-start.2) | collective-permute-done | bytes 262176 | tf_op jit(solution)/shard_map/ppermute | solution.py:220
  41.0 2.4 %collective-permute-start.4 = (bf16[16,64,128]{2,1,0:T(8,128)(2,1)S(1)}, bf16[16,64,128]{2,1,0:T(8,128)(2,1)S(1)}, u32[]{:S(2)}, u32[]{:S(2)}) collective-permute-start(bf16[16,64,128]{2,1,0:T(8,128)(2,1)S(1)} %get-tuple-element.82.own.inner), channel_id=1, source_target_pairs={{16,0},{32,16},{48,32},{64,48},{80,64},{96,80},{112,96},{128,112},... | collective-permute-start | bytes 786440 | tf_op jit(solution)/shard_map/ppermute | solution.py:218
  45.2 3.7 %collective-permute-start.7 = (bf16[16,64,128]{2,1,0:T(8,128)(2,1)S(1)}, bf16[16,64,128]{2,1,0:T(8,128)(2,1)S(1)}, u32[]{:S(2)}, u32[]{:S(2)}) collective-permute-start(bf16[16,64,128]{2,1,0:T(8,128)(2,1)S(1)} %get-tuple-element.89.inner.own), channel_id=1, source_target_pairs={{16,0},{32,16},{48,32},{64,48},{80,64},{96,80},{112,96},{128,112},... | collective-permute-start | bytes 786440 | tf_op jit(solution)/shard_map/ppermute | solution.py:218
  51.2 2.4 %collective-permute-start.6 = (bf16[16,64,128]{2,1,0:T(8,128)(2,1)S(1)}, bf16[16,64,128]{2,1,0:T(8,128)(2,1)S(1)}, u32[]{:S(2)}, u32[]{:S(2)}) collective-permute-start(bf16[16,64,128]{2,1,0:T(8,128)(2,1)S(1)} %get-tuple-element.90.own.inner), channel_id=1, source_target_pairs={{0,16},{16,32},{32,48},{48,64},{64,80},{80,96},{96,112},{112,128},... | collective-permute-start | bytes 786440 | tf_op jit(solution)/shard_map/ppermute | solution.py:220
  56.1 3.3 %collective-permute-start.9 = (bf16[16,64,128]{2,1,0:T(8,128)(2,1)S(1)}, bf16[16,64,128]{2,1,0:T(8,128)(2,1)S(1)}, u32[]{:S(2)}, u32[]{:S(2)}) collective-permute-start(bf16[16,64,128]{2,1,0:T(8,128)(2,1)S(1)} %get-tuple-element.97.inner.own), channel_id=1, source_target_pairs={{0,16},{16,32},{32,48},{48,64},{64,80},{80,96},{96,112},{112,128},... | collective-permute-start | bytes 786440 | tf_op jit(solution)/shard_map/ppermute | solution.py:220
  60.5 2.1 %collective-permute-done.6.halo = bf16[16,64,128]{2,1,0:T(8,128)(2,1)S(1)} collective-permute-done((bf16[16,64,128]{2,1,0:T(8,128)(2,1)S(1)}, bf16[16,64,128]{2,1,0:T(8,128)(2,1)S(1)}, u32[]{:S(2)}, u32[]{:S(2)}) %collective-permute-start.6) | collective-permute-done | bytes 262176 | tf_op jit(solution)/shard_map/ppermute | solution.py:220
  63.3 4.3 %collective-permute-start.8 = (bf16[16,64,128]{2,1,0:T(8,128)(2,1)S(1)}, bf16[16,64,128]{2,1,0:T(8,128)(2,1)S(1)}, u32[]{:S(2)}, u32[]{:S(2)}) collective-permute-start(bf16[16,64,128]{2,1,0:T(8,128)(2,1)S(1)} %get-tuple-element.98.own.inner), channel_id=1, source_target_pairs={{16,0},{32,16},{48,32},{64,48},{80,64},{96,80},{112,96},{128,112},... | collective-permute-start | bytes 786440 | tf_op jit(solution)/shard_map/ppermute | solution.py:218
  69.4 3.4 %collective-permute-start.11 = (bf16[16,64,128]{2,1,0:T(8,128)(2,1)S(1)}, bf16[16,64,128]{2,1,0:T(8,128)(2,1)S(1)}, u32[]{:S(2)}, u32[]{:S(2)}) collective-permute-start(bf16[16,64,128]{2,1,0:T(8,128)(2,1)S(1)} %get-tuple-element.104.inner.own), channel_id=1, source_target_pairs={{16,0},{32,16},{48,32},{64,48},{80,64},{96,80},{112,96},{128,112},... | collective-permute-start | bytes 786440 | tf_op jit(solution)/shard_map/ppermute | solution.py:218
  73.9 4.3 %collective-permute-done.8.halo = bf16[16,64,128]{2,1,0:T(8,128)(2,1)S(1)} collective-permute-done((bf16[16,64,128]{2,1,0:T(8,128)(2,1)S(1)}, bf16[16,64,128]{2,1,0:T(8,128)(2,1)S(1)}, u32[]{:S(2)}, u32[]{:S(2)}) %collective-permute-start.8) | collective-permute-done | bytes 262176 | tf_op jit(solution)/shard_map/ppermute | solution.py:218
  78.9 3.8 %collective-permute-start.10 = (bf16[16,64,128]{2,1,0:T(8,128)(2,1)S(1)}, bf16[16,64,128]{2,1,0:T(8,128)(2,1)S(1)}, u32[]{:S(2)}, u32[]{:S(2)}) collective-permute-start(bf16[16,64,128]{2,1,0:T(8,128)(2,1)S(1)} %get-tuple-element.105.own.inner), channel_id=1, source_target_pairs={{0,16},{16,32},{32,48},{48,64},{64,80},{80,96},{96,112},{112,128},... | collective-permute-start | bytes 786440 | tf_op jit(solution)/shard_map/ppermute | solution.py:220
  85.6 3.5 %collective-permute-done.10.halo = bf16[16,64,128]{2,1,0:T(8,128)(2,1)S(1)} collective-permute-done((bf16[16,64,128]{2,1,0:T(8,128)(2,1)S(1)}, bf16[16,64,128]{2,1,0:T(8,128)(2,1)S(1)}, u32[]{:S(2)}, u32[]{:S(2)}) %collective-permute-start.10) | collective-permute-done | bytes 262176 | tf_op jit(solution)/shard_map/ppermute | solution.py:220
  89.8 11.0 %all_to_all.10 = bf16[32,64,128]{2,1,0:T(8,128)(2,1)S(1)} all-to-all(bf16[32,64,128]{2,1,0:T(8,128)(2,1)S(1)} %shard_map.74), channel_id=1, replica_groups=mesh['z'=8,'yh'=2,'x'=4,'yl'=2,'c'=2] {'x','yl'}, dimensions={0} | all-to-all | bytes 1048576 | tf_op jit(solution)/shard_map/all_to_all | solution.py:271
  101.1 5.6 %collective-permute-done.20 = bf16[64,1024]{1,0:T(8,128)(2,1)S(1)} collective-permute-done((bf16[64,1024]{1,0:T(8,128)(2,1)S(1)}, bf16[64,1024]{1,0:T(8,128)(2,1)S(1)}, u32[]{:S(2)}, u32[]{:S(2)}) %collective-permute-start.20) | collective-permute-done | bytes 131104 | tf_op jit(solution)/shard_map/ppermute | solution.py:224
  107.7 2.3 %collective-permute-start.22 = (bf16[2,64,1024]{2,1,0:T(8,128)(2,1)S(1)}, bf16[2,64,1024]{2,1,0:T(8,128)(2,1)S(1)}, u32[]{:S(2)}, u32[]{:S(2)}) collective-permute-start(bf16[2,64,1024]{2,1,0:T(8,128)(2,1)S(1)} %pad_maximum_fusion.ritz), channel_id=1, source_target_pairs={{0,8},{4,12},{8,0},{12,4},{1,9},{5,13},{9,1},{13,5},{2,10},{6,14},... | collective-permute-start | bytes 786440 | tf_op jit(solution)/shard_map/ppermute | solution.py:229
  116.0 2.7 %collective-permute-start.15 = (bf16[8,64,128]{2,1,0:T(8,128)(2,1)S(1)}, bf16[8,64,128]{2,1,0:T(8,128)(2,1)S(1)}, u32[]{:S(2)}, u32[]{:S(2)}) collective-permute-start(bf16[8,64,128]{2,1,0:T(8,128)(2,1)S(1)} %get-tuple-element.110), channel_id=1, source_target_pairs={{0,6},{2,4},{4,10},{6,8},{8,14},{10,12},{12,2},{14,0},{1,7},{3,5},... | collective-permute-start | bytes 393224 | tf_op jit(solution)/shard_map/ppermute | solution.py:291
  118.7 6.4 %collective-permute-start.16 = (bf16[8,64,128]{2,1,0:T(8,128)(2,1)S(1)}, bf16[8,64,128]{2,1,0:T(8,128)(2,1)S(1)}, u32[]{:S(2)}, u32[]{:S(2)}) collective-permute-start(bf16[8,64,128]{2,1,0:T(8,128)(2,1)S(1)} %get-tuple-element.111), channel_id=1, source_target_pairs={{0,14},{2,12},{4,2},{6,0},{8,6},{10,4},{12,10},{14,8},{1,15},{3,13... | collective-permute-start | bytes 393224 | tf_op jit(solution)/shard_map/ppermute | solution.py:291
  135.3 11.1 %all-to-all-start.1 = ((bf16[16,32,128]{2,1,0:T(8,128)(2,1)}), bf16[16,32,128]{2,1,0:T(8,128)(2,1)S(1)}, u32[]{:S(2)}, u32[]{:S(2)}) async-start(bf16[16,32,128]{2,1,0:T(8,128)(2,1)} %shard_map.76), calls=%async_computation.1 | async-start | bytes 262144 | tf_op jit(solution)/shard_map/all_to_all | solution.py:309
  146.4 3.0 %collective-permute-start.25 = (bf16[4,64,128]{2,1,0:T(8,128)(2,1)S(1)}, bf16[4,64,128]{2,1,0:T(8,128)(2,1)S(1)}, u32[]{:S(2)}, u32[]{:S(2)}) collective-permute-start(bf16[4,64,128]{2,1,0:T(8,128)(2,1)S(1)} %get-tuple-element.118), channel_id=1, source_target_pairs={{0,4},{4,8},{8,12},{12,0},{1,5},{5,9},{9,13},{13,1},{2,6},{6,10},{... | collective-permute-start | bytes 196616 | tf_op jit(solution)/shard_map/ppermute | solution.py:301
  151.7 3.4 %collective-permute-start.29 = (bf16[4,64,128]{2,1,0:T(8,128)(2,1)S(1)}, bf16[4,64,128]{2,1,0:T(8,128)(2,1)S(1)}, u32[]{:S(2)}, u32[]{:S(2)}) collective-permute-start(bf16[4,64,128]{2,1,0:T(8,128)(2,1)S(1)} %get-tuple-element.122), channel_id=1, source_target_pairs={{0,8},{4,12},{8,0},{12,4},{1,9},{5,13},{9,1},{13,5},{2,10},{6,14},... | collective-permute-start | bytes 196616 | tf_op jit(solution)/shard_map/ppermute | solution.py:301
  155.9 2.1 %collective-permute-done.29.refs_4_ = bf16[4,64,128]{2,1,0:T(8,128)(2,1)S(1)} collective-permute-done((bf16[4,64,128]{2,1,0:T(8,128)(2,1)S(1)}, bf16[4,64,128]{2,1,0:T(8,128)(2,1)S(1)}, u32[]{:S(2)}, u32[]{:S(2)}) %collective-permute-start.29) | collective-permute-done | bytes 65568 | tf_op jit(solution)/shard_map/ppermute | solution.py:301
  (84 shorter events, 51.7 us)
Async XLA Ops:
  1.7 15.0 %collective-permute-start.1 = (bf16[16,64,128]{2,1,0:T(8,128)(2,1)S(1)}, bf16[16,64,128]{2,1,0:T(8,128)(2,1)S(1)}, u32[]{:S(2)}, u32[]{:S(2)}) collective-permute-start(bf16[16,64,128]{2,1,0:T(8,128)(2,1)S(1)} %get-tuple-element.66.inner.own.current.rest_0_), channel_id=1, source_target_pairs={{0,16},{16,32},{32,48},{48,64},{64,80},{80,96},{96,112},{112,128},... | collective-permute-start | bytes 786440 | tf_op jit(solution)/shard_map/ppermute | solution.py:220
  5.0 22.3 %collective-permute-start = (bf16[16,64,128]{2,1,0:T(8,128)(2,1)S(1)}, bf16[16,64,128]{2,1,0:T(8,128)(2,1)S(1)}, u32[]{:S(2)}, u32[]{:S(2)}) collective-permute-start(bf16[16,64,128]{2,1,0:T(8,128)(2,1)S(1)} %get-tuple-element.67.own.current.inner.rest_0_), channel_id=1, source_target_pairs={{16,0},{32,16},{48,32},{64,48},{80,64},{96,80},{112,96},{128,112},... | collective-permute-start | bytes 786440 | tf_op jit(solution)/shard_map/ppermute | solution.py:218
  17.4 13.6 %collective-permute-start.3 = (bf16[16,64,128]{2,1,0:T(8,128)(2,1)S(1)}, bf16[16,64,128]{2,1,0:T(8,128)(2,1)S(1)}, u32[]{:S(2)}, u32[]{:S(2)}) collective-permute-start(bf16[16,64,128]{2,1,0:T(8,128)(2,1)S(1)} %get-tuple-element.73.inner.own), channel_id=1, source_target_pairs={{16,0},{32,16},{48,32},{64,48},{80,64},{96,80},{112,96},{128,112},... | collective-permute-start | bytes 786440 | tf_op jit(solution)/shard_map/ppermute | solution.py:218
  28.0 12.4 %collective-permute-start.2 = (bf16[16,64,128]{2,1,0:T(8,128)(2,1)S(1)}, bf16[16,64,128]{2,1,0:T(8,128)(2,1)S(1)}, u32[]{:S(2)}, u32[]{:S(2)}) collective-permute-start(bf16[16,64,128]{2,1,0:T(8,128)(2,1)S(1)} %get-tuple-element.74.own.inner), channel_id=1, source_target_pairs={{0,16},{16,32},{32,48},{48,64},{64,80},{80,96},{96,112},{112,128},... | collective-permute-start | bytes 786440 | tf_op jit(solution)/shard_map/ppermute | solution.py:220
  31.6 12.9 %collective-permute-start.5 = (bf16[16,64,128]{2,1,0:T(8,128)(2,1)S(1)}, bf16[16,64,128]{2,1,0:T(8,128)(2,1)S(1)}, u32[]{:S(2)}, u32[]{:S(2)}) collective-permute-start(bf16[16,64,128]{2,1,0:T(8,128)(2,1)S(1)} %get-tuple-element.81.inner.own), channel_id=1, source_target_pairs={{0,16},{16,32},{32,48},{48,64},{64,80},{80,96},{96,112},{112,128},... | collective-permute-start | bytes 786440 | tf_op jit(solution)/shard_map/ppermute | solution.py:220
  41.0 9.5 %collective-permute-start.4 = (bf16[16,64,128]{2,1,0:T(8,128)(2,1)S(1)}, bf16[16,64,128]{2,1,0:T(8,128)(2,1)S(1)}, u32[]{:S(2)}, u32[]{:S(2)}) collective-permute-start(bf16[16,64,128]{2,1,0:T(8,128)(2,1)S(1)} %get-tuple-element.82.own.inner), channel_id=1, source_target_pairs={{16,0},{32,16},{48,32},{64,48},{80,64},{96,80},{112,96},{128,112},... | collective-permute-start | bytes 786440 | tf_op jit(solution)/shard_map/ppermute | solution.py:218
  45.2 10.2 %collective-permute-start.7 = (bf16[16,64,128]{2,1,0:T(8,128)(2,1)S(1)}, bf16[16,64,128]{2,1,0:T(8,128)(2,1)S(1)}, u32[]{:S(2)}, u32[]{:S(2)}) collective-permute-start(bf16[16,64,128]{2,1,0:T(8,128)(2,1)S(1)} %get-tuple-element.89.inner.own), channel_id=1, source_target_pairs={{16,0},{32,16},{48,32},{64,48},{80,64},{96,80},{112,96},{128,112},... | collective-permute-start | bytes 786440 | tf_op jit(solution)/shard_map/ppermute | solution.py:218
  51.2 11.4 %collective-permute-start.6 = (bf16[16,64,128]{2,1,0:T(8,128)(2,1)S(1)}, bf16[16,64,128]{2,1,0:T(8,128)(2,1)S(1)}, u32[]{:S(2)}, u32[]{:S(2)}) collective-permute-start(bf16[16,64,128]{2,1,0:T(8,128)(2,1)S(1)} %get-tuple-element.90.own.inner), channel_id=1, source_target_pairs={{0,16},{16,32},{32,48},{48,64},{64,80},{80,96},{96,112},{112,128},... | collective-permute-start | bytes 786440 | tf_op jit(solution)/shard_map/ppermute | solution.py:220
  56.1 12.6 %collective-permute-start.9 = (bf16[16,64,128]{2,1,0:T(8,128)(2,1)S(1)}, bf16[16,64,128]{2,1,0:T(8,128)(2,1)S(1)}, u32[]{:S(2)}, u32[]{:S(2)}) collective-permute-start(bf16[16,64,128]{2,1,0:T(8,128)(2,1)S(1)} %get-tuple-element.97.inner.own), channel_id=1, source_target_pairs={{0,16},{16,32},{32,48},{48,64},{64,80},{80,96},{96,112},{112,128},... | collective-permute-start | bytes 786440 | tf_op jit(solution)/shard_map/ppermute | solution.py:220
  63.3 14.9 %collective-permute-start.8 = (bf16[16,64,128]{2,1,0:T(8,128)(2,1)S(1)}, bf16[16,64,128]{2,1,0:T(8,128)(2,1)S(1)}, u32[]{:S(2)}, u32[]{:S(2)}) collective-permute-start(bf16[16,64,128]{2,1,0:T(8,128)(2,1)S(1)} %get-tuple-element.98.own.inner), channel_id=1, source_target_pairs={{16,0},{32,16},{48,32},{64,48},{80,64},{96,80},{112,96},{128,112},... | collective-permute-start | bytes 786440 | tf_op jit(solution)/shard_map/ppermute | solution.py:218
  69.4 14.4 %collective-permute-start.11 = (bf16[16,64,128]{2,1,0:T(8,128)(2,1)S(1)}, bf16[16,64,128]{2,1,0:T(8,128)(2,1)S(1)}, u32[]{:S(2)}, u32[]{:S(2)}) collective-permute-start(bf16[16,64,128]{2,1,0:T(8,128)(2,1)S(1)} %get-tuple-element.104.inner.own), channel_id=1, source_target_pairs={{16,0},{32,16},{48,32},{64,48},{80,64},{96,80},{112,96},{128,112},... | collective-permute-start | bytes 786440 | tf_op jit(solution)/shard_map/ppermute | solution.py:218
  78.9 10.2 %collective-permute-start.10 = (bf16[16,64,128]{2,1,0:T(8,128)(2,1)S(1)}, bf16[16,64,128]{2,1,0:T(8,128)(2,1)S(1)}, u32[]{:S(2)}, u32[]{:S(2)}) collective-permute-start(bf16[16,64,128]{2,1,0:T(8,128)(2,1)S(1)} %get-tuple-element.105.own.inner), channel_id=1, source_target_pairs={{0,16},{16,32},{32,48},{48,64},{64,80},{80,96},{96,112},{112,128},... | collective-permute-start | bytes 786440 | tf_op jit(solution)/shard_map/ppermute | solution.py:220
  100.8 10.8 %collective-permute-start.12 = (bf16[8,4,64,128]{3,2,1,0:T(8,128)(2,1)S(1)}, bf16[8,4,64,128]{3,2,1,0:T(8,128)(2,1)S(1)}, u32[]{:S(2)}, u32[]{:S(2)}) collective-permute-start(bf16[8,4,64,128]{3,2,1,0:T(8,128)(2,1)S(1)} %bitcast.12), channel_id=1, source_target_pairs={{0,1},{1,0},{2,3},{3,2},{4,5},{5,4},{6,7},{7,6},{8,9},{9,8},{10,11... | collective-permute-start | bytes 1572872 | tf_op jit(solution)/shard_map/ppermute | solution.py:273
  106.7 9.3 %collective-permute-start.21 = (bf16[2,64,1024]{2,1,0:T(8,128)(2,1)S(1)}, bf16[2,64,1024]{2,1,0:T(8,128)(2,1)S(1)}, u32[]{:S(2)}, u32[]{:S(2)}) collective-permute-start(bf16[2,64,1024]{2,1,0:T(8,128)(2,1)S(1)} %pad_maximum_fusion.ritz), channel_id=1, source_target_pairs={{0,12},{4,0},{8,4},{12,8},{1,13},{5,1},{9,5},{13,9},{2,14},{6,2},{... | collective-permute-start | bytes 786440 | tf_op jit(solution)/shard_map/ppermute | solution.py:229
  107.7 11.0 %collective-permute-start.22 = (bf16[2,64,1024]{2,1,0:T(8,128)(2,1)S(1)}, bf16[2,64,1024]{2,1,0:T(8,128)(2,1)S(1)}, u32[]{:S(2)}, u32[]{:S(2)}) collective-permute-start(bf16[2,64,1024]{2,1,0:T(8,128)(2,1)S(1)} %pad_maximum_fusion.ritz), channel_id=1, source_target_pairs={{0,8},{4,12},{8,0},{12,4},{1,9},{5,13},{9,1},{13,5},{2,10},{6,14},... | collective-permute-start | bytes 786440 | tf_op jit(solution)/shard_map/ppermute | solution.py:229
  110.0 15.1 %collective-permute-start.23 = (bf16[2,64,1024]{2,1,0:T(8,128)(2,1)S(1)}, bf16[2,64,1024]{2,1,0:T(8,128)(2,1)S(1)}, u32[]{:S(2)}, u32[]{:S(2)}) collective-permute-start(bf16[2,64,1024]{2,1,0:T(8,128)(2,1)S(1)} %pad_maximum_fusion.ritz), channel_id=1, source_target_pairs={{0,4},{4,8},{8,12},{12,0},{1,5},{5,9},{9,13},{13,1},{2,6},{6,10},{... | collective-permute-start | bytes 786440 | tf_op jit(solution)/shard_map/ppermute | solution.py:229
  113.4 15.5 %collective-permute-start.13 = (bf16[8,64,128]{2,1,0:T(8,128)(2,1)S(1)}, bf16[8,64,128]{2,1,0:T(8,128)(2,1)S(1)}, u32[]{:S(2)}, u32[]{:S(2)}) collective-permute-start(bf16[8,64,128]{2,1,0:T(8,128)(2,1)S(1)} %get-tuple-element.108), channel_id=1, source_target_pairs={{0,10},{2,8},{4,14},{6,12},{8,2},{10,0},{12,6},{14,4},{1,11},{3,9}... | collective-permute-start | bytes 393224 | tf_op jit(solution)/shard_map/ppermute | solution.py:291
  114.1 14.8 %collective-permute-start.14 = (bf16[8,64,128]{2,1,0:T(8,128)(2,1)S(1)}, bf16[8,64,128]{2,1,0:T(8,128)(2,1)S(1)}, u32[]{:S(2)}, u32[]{:S(2)}) collective-permute-start(bf16[8,64,128]{2,1,0:T(8,128)(2,1)S(1)} %get-tuple-element.109), channel_id=1, source_target_pairs={{0,2},{2,0},{4,6},{6,4},{8,10},{10,8},{12,14},{14,12},{1,3},{3,1},... | collective-permute-start | bytes 393224 | tf_op jit(solution)/shard_map/ppermute | solution.py:291
  116.0 16.2 %collective-permute-start.15 = (bf16[8,64,128]{2,1,0:T(8,128)(2,1)S(1)}, bf16[8,64,128]{2,1,0:T(8,128)(2,1)S(1)}, u32[]{:S(2)}, u32[]{:S(2)}) collective-permute-start(bf16[8,64,128]{2,1,0:T(8,128)(2,1)S(1)} %get-tuple-element.110), channel_id=1, source_target_pairs={{0,6},{2,4},{4,10},{6,8},{8,14},{10,12},{12,2},{14,0},{1,7},{3,5},... | collective-permute-start | bytes 393224 | tf_op jit(solution)/shard_map/ppermute | solution.py:291
  118.7 13.5 %collective-permute-start.16 = (bf16[8,64,128]{2,1,0:T(8,128)(2,1)S(1)}, bf16[8,64,128]{2,1,0:T(8,128)(2,1)S(1)}, u32[]{:S(2)}, u32[]{:S(2)}) collective-permute-start(bf16[8,64,128]{2,1,0:T(8,128)(2,1)S(1)} %get-tuple-element.111), channel_id=1, source_target_pairs={{0,14},{2,12},{4,2},{6,0},{8,6},{10,4},{12,10},{14,8},{1,15},{3,13... | collective-permute-start | bytes 393224 | tf_op jit(solution)/shard_map/ppermute | solution.py:291
  125.1 8.5 %collective-permute-start.17 = (bf16[8,64,128]{2,1,0:T(8,128)(2,1)S(1)}, bf16[8,64,128]{2,1,0:T(8,128)(2,1)S(1)}, u32[]{:S(2)}, u32[]{:S(2)}) collective-permute-start(bf16[8,64,128]{2,1,0:T(8,128)(2,1)S(1)} %get-tuple-element.112), channel_id=1, source_target_pairs={{0,8},{2,10},{4,12},{6,14},{8,0},{10,2},{12,4},{14,6},{1,9},{3,11}... | collective-permute-start | bytes 393224 | tf_op jit(solution)/shard_map/ppermute | solution.py:291
  132.2 18.9 %collective-permute-start.24 = (bf16[4,4,64,128]{3,2,1,0:T(8,128)(2,1)S(1)}, bf16[4,4,64,128]{3,2,1,0:T(8,128)(2,1)S(1)}, u32[]{:S(2)}, u32[]{:S(2)}) collective-permute-start(bf16[4,4,64,128]{3,2,1,0:T(8,128)(2,1)S(1)} %get-tuple-element.117), channel_id=1, source_target_pairs={{0,2},{2,0},{1,3},{3,1},{4,6},{6,4},{5,7},{7,5},{8,10},{10,8},{9,1... | collective-permute-start | bytes 786440 | tf_op jit(solution)/shard_map/ppermute | solution.py:297
  135.3 25.6 %all-to-all-start.1 = ((bf16[16,32,128]{2,1,0:T(8,128)(2,1)}), bf16[16,32,128]{2,1,0:T(8,128)(2,1)S(1)}, u32[]{:S(2)}, u32[]{:S(2)}) async-start(bf16[16,32,128]{2,1,0:T(8,128)(2,1)} %shard_map.76), calls=%async_computation.1 | async-start | bytes 262144 | tf_op jit(solution)/shard_map/all_to_all | solution.py:309
  146.4 8.6 %collective-permute-start.25 = (bf16[4,64,128]{2,1,0:T(8,128)(2,1)S(1)}, bf16[4,64,128]{2,1,0:T(8,128)(2,1)S(1)}, u32[]{:S(2)}, u32[]{:S(2)}) collective-permute-start(bf16[4,64,128]{2,1,0:T(8,128)(2,1)S(1)} %get-tuple-element.118), channel_id=1, source_target_pairs={{0,4},{4,8},{8,12},{12,0},{1,5},{5,9},{9,13},{13,1},{2,6},{6,10},{... | collective-permute-start | bytes 196616 | tf_op jit(solution)/shard_map/ppermute | solution.py:301
  (12 other events, 90.0 us)

commit v10 on v9

--- a/solution.py
+++ b/solution.py
@@ -160,19 +160,23 @@
         out[...] = crossed[away + 1]
 
 
+def collect_line(around, index, place):
+    q, away = index // around, index % around
+    return lax.rem(place[0] + around - away, around) * 2 + place[1] + q - 2 * q * place[1]
+
+
 def collect_kernel(around, place, here, crossed, *refs):
     pieces, out = refs[:-1], refs[-1]
-    held = here.shape[0]
-    for q in range(2):
-        near = place[1] if q == 0 else 1 - place[1]
-        for away in range(around):
-            line = lax.rem(place[0] + around - away, around) * 2 + near
-            for el in range(held):
-                if away:
-                    piece = pieces[q * (around - 1) + away - 1][el]
-                else:
-                    piece = crossed[0, el] if q else here[el]
-                out[line * held + el] = piece.astype(jnp.float32)
+    for index in range(2 * around):
+        q, away = index // around, index % around
+
+        @pl.when(pl.program_id(0) == index)
+        def _():
+            if away:
+                piece = pieces[q * (around - 1) + away - 1][...]
+            else:
+                piece = crossed[0] if q else here[...]
+            out[...] = piece.astype(jnp.float32)
 
 
 def margin_rows_kernel(*refs):
@@ -208,7 +212,9 @@
     up = [(i, (i + 1) % slabs) for i in range(slabs)]
     down = [((i + 1) % slabs, i) for i in range(slabs)]
     begin = jnp.swapaxes(start, 1, 2)
-    val = {("a", 0): begin[:PLANE], ("b", 0): begin[PLANE:]}
+    first = begin[PLANE:]
+    begin, _ = lax.optimization_barrier((begin, first))
+    val = {("a", 0): begin[:PLANE], ("b", 0): first}
     full = dict(val)
     base = {"a": 0, "b": PLANE}
     halo = {}
@@ -310,10 +316,19 @@
     ways = call(part_ways_kernel, (crossed,), (piece,) * (around - 1), small, 12)
     for away in range(1, around):
         along(away, ways[away - 1])
-    rotated = call(
-        functools.partial(collect_kernel, around), (place, turned[0], crossed, *pieces),
-        jax.ShapeDtypeStruct((2 * PLANE, cols, NB), jnp.float32), small, 12, (), [SMEM] + [VMEM] * (2 * around),
-    )
+    rotated = pl.pallas_call(
+        functools.partial(collect_kernel, around),
+        grid_spec=pltpu.PrefetchScalarGridSpec(
+            num_scalar_prefetch=1,
+            grid=(chips,),
+            in_specs=[VMEM] * (2 * around),
+            out_specs=pl.BlockSpec((held, cols, NB), lambda i, place: (collect_line(around, i, place), 0, 0)),
+        ),
+        out_shape=jax.ShapeDtypeStruct((2 * PLANE, cols, NB), jnp.float32),
+        cost_estimate=small,
+        compiler_params=pltpu.CompilerParams(vmem_limit_bytes=12 << 20),
+        name="collect",
+    )(place, turned[0], crossed, *pieces)
     margin = call(
         functools.partial(margin_kernel, 1.0 / rows_total), (total,),
         jax.ShapeDtypeStruct((cols, cols), jnp.float32), small, 12,

time: 163 us -> 166 us (1.018)
  Pallas kernels: 27.2 us -> 29 us
    pallas_call x0 -> x1, Pallas kernels: none -> 3.47 us  [whole(): pl.pallas_call(functools.partial(collect_kernel, around), grid_spec=pltpu...]
    pallas_call x31 -> x30, Pallas kernels: 27.2 us -> 25.6 us  [call(): pl.pallas_call(kernel, out_shape=out_shape, in_specs=in_specs or [VMEM] *...]
  transfers between devices with their start and end apart: 32 -> 32, of which waited for: 18 -> 18; matrix products, arithmetic and copies ran while one was open for 0% -> 1% of each run, Pallas kernels for 16% -> 17%
where the time goes in v10:
time: 166 us; the launch traced here: 164 us
  starting transfers between devices  82.2 us (50%)
  waiting for transfers between devices  36.1 us (22%)
  Pallas kernels  29 us (17%)
  blocking collectives  11 us (7%)
  local copies, waits for them, and re-layouts  5.04 us (3%)
    ppermute x6, starting transfers between devices, send(): halo['b', k] = lax.ppermute(val['a', k], ELEM, down)  28.1 us
    pallas_call x30, Pallas kernels, call(): pl.pallas_call(kernel, out_shape=out_shape, in_specs=in_specs or [VMEM] *...  25.6 us
    ppermute x7, starting transfers between devices, whole(): parts.append(lax.ppermute(blocks[2 * away + q], CHIP, to_chip(away, q)))  14.8 us
    ppermute x6, waiting for transfers between devices, send(): halo['a', k] = lax.ppermute(val['b', k], ELEM, up)  13.9 us
    ppermute x6, starting transfers between devices, send(): halo['a', k] = lax.ppermute(val['b', k], ELEM, up)  12.9 us
    all_to_all x1, starting transfers between devices, whole(): total = lax.all_to_all(total, ELEM, 0, 0, tiled=True)  12 us
    all_to_all x1, blocking collectives, whole(): mine = lax.all_to_all(filtered, CHIP, 0, 0, tiled=True)  11 us
    ppermute x6, starting transfers between devices, along(): lax.ppermute(value, 'x', [(i, (i + away) % around) for i in range(around)])  9.23 us
  transfers between devices with their start and end apart: 32, of which 18 were waited for; matrix products, arithmetic and copies ran while one was open for 1% of the time, Pallas kernels for 17%

profile of v10, /device:TPU:4, one launch (start us, length us, event | category | flops | bytes accessed | tf_op | source)
XLA Modules:
  0.0 164.3 jit_solution(2584760494317386413)
XLA Ops:
  1.6 3.3 %collective-permute-start.1 = (bf16[16,64,128]{2,1,0:T(8,128)(2,1)S(1)}, bf16[16,64,128]{2,1,0:T(8,128)(2,1)S(1)}, u32[]{:S(2)}, u32[]{:S(2)}) collective-permute-start(bf16[16,64,128]{2,1,0:T(8,128)(2,1)S(1)} %slice.8.inner.own.current.rest_0_), channel_id=1, source_target_pairs={{0,16},{16,32},{32,48},{48,64},{64,80},{80,96},{96,112},{112,128},... | collective-permute-start | bytes 786440 | tf_op jit(solution)/shard_map/ppermute | solution.py:226
  5.8 5.4 %collective-permute-start = (bf16[16,64,128]{2,1,0:T(8,128)(2,1)S(1)}, bf16[16,64,128]{2,1,0:T(8,128)(2,1)S(1)}, u32[]{:S(2)}, u32[]{:S(2)}) collective-permute-start(bf16[16,64,128]{2,1,0:T(8,128)(2,1)S(1)} %slice.7.own.current.inner.rest_0_), channel_id=1, source_target_pairs={{16,0},{32,16},{48,32},{64,48},{80,64},{96,80},{112,96},{128,112},... | collective-permute-start | bytes 786440 | tf_op jit(solution)/shard_map/ppermute | solution.py:224
  11.2 3.1 %copy-done = bf16[32,7,128,128]{3,2,1,0:T(8,128)(2,1)S(1)} copy-done((bf16[32,7,128,128]{3,2,1,0:T(8,128)(2,1)S(1)}, bf16[32,7,128,128]{3,2,1,0:T(8,128)(2,1)}, u32[]{:S(2)}) %copy-start) | copy-done | bytes 7340056
  17.3 8.8 %collective-permute-start.3 = (bf16[16,64,128]{2,1,0:T(8,128)(2,1)S(1)}, bf16[16,64,128]{2,1,0:T(8,128)(2,1)S(1)}, u32[]{:S(2)}, u32[]{:S(2)}) collective-permute-start(bf16[16,64,128]{2,1,0:T(8,128)(2,1)S(1)} %get-tuple-element.75.inner.own), channel_id=1, source_target_pairs={{16,0},{32,16},{48,32},{64,48},{80,64},{96,80},{112,96},{128,112},... | collective-permute-start | bytes 786440 | tf_op jit(solution)/shard_map/ppermute | solution.py:224
  32.7 7.6 %collective-permute-done.2.halo = bf16[16,64,128]{2,1,0:T(8,128)(2,1)S(1)} collective-permute-done((bf16[16,64,128]{2,1,0:T(8,128)(2,1)S(1)}, bf16[16,64,128]{2,1,0:T(8,128)(2,1)S(1)}, u32[]{:S(2)}, u32[]{:S(2)}) %collective-permute-start.2) | collective-permute-done | bytes 262176 | tf_op jit(solution)/shard_map/ppermute | solution.py:226
  40.9 2.4 %collective-permute-start.4 = (bf16[16,64,128]{2,1,0:T(8,128)(2,1)S(1)}, bf16[16,64,128]{2,1,0:T(8,128)(2,1)S(1)}, u32[]{:S(2)}, u32[]{:S(2)}) collective-permute-start(bf16[16,64,128]{2,1,0:T(8,128)(2,1)S(1)} %get-tuple-element.84.own.inner), channel_id=1, source_target_pairs={{16,0},{32,16},{48,32},{64,48},{80,64},{96,80},{112,96},{128,112},... | collective-permute-start | bytes 786440 | tf_op jit(solution)/shard_map/ppermute | solution.py:224
  45.1 3.7 %collective-permute-start.7 = (bf16[16,64,128]{2,1,0:T(8,128)(2,1)S(1)}, bf16[16,64,128]{2,1,0:T(8,128)(2,1)S(1)}, u32[]{:S(2)}, u32[]{:S(2)}) collective-permute-start(bf16[16,64,128]{2,1,0:T(8,128)(2,1)S(1)} %get-tuple-element.91.inner.own), channel_id=1, source_target_pairs={{16,0},{32,16},{48,32},{64,48},{80,64},{96,80},{112,96},{128,112},... | collective-permute-start | bytes 786440 | tf_op jit(solution)/shard_map/ppermute | solution.py:224
  51.1 2.4 %collective-permute-start.6 = (bf16[16,64,128]{2,1,0:T(8,128)(2,1)S(1)}, bf16[16,64,128]{2,1,0:T(8,128)(2,1)S(1)}, u32[]{:S(2)}, u32[]{:S(2)}) collective-permute-start(bf16[16,64,128]{2,1,0:T(8,128)(2,1)S(1)} %get-tuple-element.92.own.inner), channel_id=1, source_target_pairs={{0,16},{16,32},{32,48},{48,64},{64,80},{80,96},{96,112},{112,128},... | collective-permute-start | bytes 786440 | tf_op jit(solution)/shard_map/ppermute | solution.py:226
  56.0 3.3 %collective-permute-start.9 = (bf16[16,64,128]{2,1,0:T(8,128)(2,1)S(1)}, bf16[16,64,128]{2,1,0:T(8,128)(2,1)S(1)}, u32[]{:S(2)}, u32[]{:S(2)}) collective-permute-start(bf16[16,64,128]{2,1,0:T(8,128)(2,1)S(1)} %get-tuple-element.99.inner.own), channel_id=1, source_target_pairs={{0,16},{16,32},{32,48},{48,64},{64,80},{80,96},{96,112},{112,128},... | collective-permute-start | bytes 786440 | tf_op jit(solution)/shard_map/ppermute | solution.py:226
  60.4 2.1 %collective-permute-done.6.halo = bf16[16,64,128]{2,1,0:T(8,128)(2,1)S(1)} collective-permute-done((bf16[16,64,128]{2,1,0:T(8,128)(2,1)S(1)}, bf16[16,64,128]{2,1,0:T(8,128)(2,1)S(1)}, u32[]{:S(2)}, u32[]{:S(2)}) %collective-permute-start.6) | collective-permute-done | bytes 262176 | tf_op jit(solution)/shard_map/ppermute | solution.py:226
  63.2 4.3 %collective-permute-start.8 = (bf16[16,64,128]{2,1,0:T(8,128)(2,1)S(1)}, bf16[16,64,128]{2,1,0:T(8,128)(2,1)S(1)}, u32[]{:S(2)}, u32[]{:S(2)}) collective-permute-start(bf16[16,64,128]{2,1,0:T(8,128)(2,1)S(1)} %get-tuple-element.100.own.inner), channel_id=1, source_target_pairs={{16,0},{32,16},{48,32},{64,48},{80,64},{96,80},{112,96},{128,112},... | collective-permute-start | bytes 786440 | tf_op jit(solution)/shard_map/ppermute | solution.py:224
  69.3 3.4 %collective-permute-start.11 = (bf16[16,64,128]{2,1,0:T(8,128)(2,1)S(1)}, bf16[16,64,128]{2,1,0:T(8,128)(2,1)S(1)}, u32[]{:S(2)}, u32[]{:S(2)}) collective-permute-start(bf16[16,64,128]{2,1,0:T(8,128)(2,1)S(1)} %get-tuple-element.106.inner.own), channel_id=1, source_target_pairs={{16,0},{32,16},{48,32},{64,48},{80,64},{96,80},{112,96},{128,112},... | collective-permute-start | bytes 786440 | tf_op jit(solution)/shard_map/ppermute | solution.py:224
  73.8 4.3 %collective-permute-done.8.halo = bf16[16,64,128]{2,1,0:T(8,128)(2,1)S(1)} collective-permute-done((bf16[16,64,128]{2,1,0:T(8,128)(2,1)S(1)}, bf16[16,64,128]{2,1,0:T(8,128)(2,1)S(1)}, u32[]{:S(2)}, u32[]{:S(2)}) %collective-permute-start.8) | collective-permute-done | bytes 262176 | tf_op jit(solution)/shard_map/ppermute | solution.py:224
  78.8 3.8 %collective-permute-start.10 = (bf16[16,64,128]{2,1,0:T(8,128)(2,1)S(1)}, bf16[16,64,128]{2,1,0:T(8,128)(2,1)S(1)}, u32[]{:S(2)}, u32[]{:S(2)}) collective-permute-start(bf16[16,64,128]{2,1,0:T(8,128)(2,1)S(1)} %get-tuple-element.107.own.inner), channel_id=1, source_target_pairs={{0,16},{16,32},{32,48},{48,64},{64,80},{80,96},{96,112},{112,128},... | collective-permute-start | bytes 786440 | tf_op jit(solution)/shard_map/ppermute | solution.py:226
  85.5 3.5 %collective-permute-done.10.halo = bf16[16,64,128]{2,1,0:T(8,128)(2,1)S(1)} collective-permute-done((bf16[16,64,128]{2,1,0:T(8,128)(2,1)S(1)}, bf16[16,64,128]{2,1,0:T(8,128)(2,1)S(1)}, u32[]{:S(2)}, u32[]{:S(2)}) %collective-permute-start.10) | collective-permute-done | bytes 262176 | tf_op jit(solution)/shard_map/ppermute | solution.py:226
  89.7 11.0 %all_to_all.10 = bf16[32,64,128]{2,1,0:T(8,128)(2,1)S(1)} all-to-all(bf16[32,64,128]{2,1,0:T(8,128)(2,1)S(1)} %shard_map.74), channel_id=1, replica_groups=mesh['z'=8,'yh'=2,'x'=4,'yl'=2,'c'=2] {'x','yl'}, dimensions={0} | all-to-all | bytes 1048576 | tf_op jit(solution)/shard_map/all_to_all | solution.py:277
  101.0 5.6 %collective-permute-done.20 = bf16[64,1024]{1,0:T(8,128)(2,1)S(1)} collective-permute-done((bf16[64,1024]{1,0:T(8,128)(2,1)S(1)}, bf16[64,1024]{1,0:T(8,128)(2,1)S(1)}, u32[]{:S(2)}, u32[]{:S(2)}) %collective-permute-start.20) | collective-permute-done | bytes 131104 | tf_op jit(solution)/shard_map/ppermute | solution.py:230
  107.6 2.3 %collective-permute-start.22 = (bf16[2,64,1024]{2,1,0:T(8,128)(2,1)S(1)}, bf16[2,64,1024]{2,1,0:T(8,128)(2,1)S(1)}, u32[]{:S(2)}, u32[]{:S(2)}) collective-permute-start(bf16[2,64,1024]{2,1,0:T(8,128)(2,1)S(1)} %pad_maximum_fusion.ritz), channel_id=1, source_target_pairs={{0,8},{4,12},{8,0},{12,4},{1,9},{5,13},{9,1},{13,5},{2,10},{6,14},... | collective-permute-start | bytes 786440 | tf_op jit(solution)/shard_map/ppermute | solution.py:235
  115.9 2.7 %collective-permute-start.15 = (bf16[8,64,128]{2,1,0:T(8,128)(2,1)S(1)}, bf16[8,64,128]{2,1,0:T(8,128)(2,1)S(1)}, u32[]{:S(2)}, u32[]{:S(2)}) collective-permute-start(bf16[8,64,128]{2,1,0:T(8,128)(2,1)S(1)} %get-tuple-element.112), channel_id=1, source_target_pairs={{0,6},{2,4},{4,10},{6,8},{8,14},{10,12},{12,2},{14,0},{1,7},{3,5},... | collective-permute-start | bytes 393224 | tf_op jit(solution)/shard_map/ppermute | solution.py:297
  118.6 6.4 %collective-permute-start.16 = (bf16[8,64,128]{2,1,0:T(8,128)(2,1)S(1)}, bf16[8,64,128]{2,1,0:T(8,128)(2,1)S(1)}, u32[]{:S(2)}, u32[]{:S(2)}) collective-permute-start(bf16[8,64,128]{2,1,0:T(8,128)(2,1)S(1)} %get-tuple-element.113), channel_id=1, source_target_pairs={{0,14},{2,12},{4,2},{6,0},{8,6},{10,4},{12,10},{14,8},{1,15},{3,13... | collective-permute-start | bytes 393224 | tf_op jit(solution)/shard_map/ppermute | solution.py:297
  135.2 12.0 %all-to-all-start.1 = ((bf16[16,32,128]{2,1,0:T(8,128)(2,1)}), bf16[16,32,128]{2,1,0:T(8,128)(2,1)S(1)}, u32[]{:S(2)}, u32[]{:S(2)}) async-start(bf16[16,32,128]{2,1,0:T(8,128)(2,1)} %shard_map.76), calls=%async_computation.1 | async-start | bytes 262144 | tf_op jit(solution)/shard_map/all_to_all | solution.py:315
  147.3 3.0 %collective-permute-start.25 = (bf16[4,64,128]{2,1,0:T(8,128)(2,1)S(1)}, bf16[4,64,128]{2,1,0:T(8,128)(2,1)S(1)}, u32[]{:S(2)}, u32[]{:S(2)}) collective-permute-start(bf16[4,64,128]{2,1,0:T(8,128)(2,1)S(1)} %get-tuple-element.120), channel_id=1, source_target_pairs={{0,4},{4,8},{8,12},{12,0},{1,5},{5,9},{9,13},{13,1},{2,6},{6,10},{... | collective-permute-start | bytes 196616 | tf_op jit(solution)/shard_map/ppermute | solution.py:307
  152.5 3.4 %collective-permute-start.29 = (bf16[4,64,128]{2,1,0:T(8,128)(2,1)S(1)}, bf16[4,64,128]{2,1,0:T(8,128)(2,1)S(1)}, u32[]{:S(2)}, u32[]{:S(2)}) collective-permute-start(bf16[4,64,128]{2,1,0:T(8,128)(2,1)S(1)} %get-tuple-element.124), channel_id=1, source_target_pairs={{0,8},{4,12},{8,0},{12,4},{1,9},{5,13},{9,1},{13,5},{2,10},{6,14},... | collective-permute-start | bytes 196616 | tf_op jit(solution)/shard_map/ppermute | solution.py:307
  160.2 3.5 %collect.1 = f32[32,64,128]{2,1,0:T(8,128)} custom-call(s32[3]{0:T(128)S(1)} %pad_add_fusion.place, bf16[4,64,128]{2,1,0:T(8,128)(2,1)S(1)} %get-tuple-element.118.here, bf16[4,4,64,128]{3,2,1,0:T(8,128)(2,1)S(1)} %collective-permute-done.24.crossed, bf16[4,64,128]{2,1,0:T(8,128)(2,1)S(1)} %collective-permute-done.25.refs_0_, ...), custom_call_target="tpu_custom_call" | custom-call | flops 1048576 | bytes 1048576 | tf_op jit(solution)/shard_map/collect/pallas_call | solution.py:319
  (85 shorter events, 52.1 us)
Async XLA Ops:
  1.6 15.0 %collective-permute-start.1 = (bf16[16,64,128]{2,1,0:T(8,128)(2,1)S(1)}, bf16[16,64,128]{2,1,0:T(8,128)(2,1)S(1)}, u32[]{:S(2)}, u32[]{:S(2)}) collective-permute-start(bf16[16,64,128]{2,1,0:T(8,128)(2,1)S(1)} %slice.8.inner.own.current.rest_0_), channel_id=1, source_target_pairs={{0,16},{16,32},{32,48},{48,64},{64,80},{80,96},{96,112},{112,128},... | collective-permute-start | bytes 786440 | tf_op jit(solution)/shard_map/ppermute | solution.py:226
  5.8 21.3 %collective-permute-start = (bf16[16,64,128]{2,1,0:T(8,128)(2,1)S(1)}, bf16[16,64,128]{2,1,0:T(8,128)(2,1)S(1)}, u32[]{:S(2)}, u32[]{:S(2)}) collective-permute-start(bf16[16,64,128]{2,1,0:T(8,128)(2,1)S(1)} %slice.7.own.current.inner.rest_0_), channel_id=1, source_target_pairs={{16,0},{32,16},{48,32},{64,48},{80,64},{96,80},{112,96},{128,112},... | collective-permute-start | bytes 786440 | tf_op jit(solution)/shard_map/ppermute | solution.py:224
  17.3 13.6 %collective-permute-start.3 = (bf16[16,64,128]{2,1,0:T(8,128)(2,1)S(1)}, bf16[16,64,128]{2,1,0:T(8,128)(2,1)S(1)}, u32[]{:S(2)}, u32[]{:S(2)}) collective-permute-start(bf16[16,64,128]{2,1,0:T(8,128)(2,1)S(1)} %get-tuple-element.75.inner.own), channel_id=1, source_target_pairs={{16,0},{32,16},{48,32},{64,48},{80,64},{96,80},{112,96},{128,112},... | collective-permute-start | bytes 786440 | tf_op jit(solution)/shard_map/ppermute | solution.py:224
  27.9 12.4 %collective-permute-start.2 = (bf16[16,64,128]{2,1,0:T(8,128)(2,1)S(1)}, bf16[16,64,128]{2,1,0:T(8,128)(2,1)S(1)}, u32[]{:S(2)}, u32[]{:S(2)}) collective-permute-start(bf16[16,64,128]{2,1,0:T(8,128)(2,1)S(1)} %get-tuple-element.76.own.inner), channel_id=1, source_target_pairs={{0,16},{16,32},{32,48},{48,64},{64,80},{80,96},{96,112},{112,128},... | collective-permute-start | bytes 786440 | tf_op jit(solution)/shard_map/ppermute | solution.py:226
  31.5 12.9 %collective-permute-start.5 = (bf16[16,64,128]{2,1,0:T(8,128)(2,1)S(1)}, bf16[16,64,128]{2,1,0:T(8,128)(2,1)S(1)}, u32[]{:S(2)}, u32[]{:S(2)}) collective-permute-start(bf16[16,64,128]{2,1,0:T(8,128)(2,1)S(1)} %get-tuple-element.83.inner.own), channel_id=1, source_target_pairs={{0,16},{16,32},{32,48},{48,64},{64,80},{80,96},{96,112},{112,128},... | collective-permute-start | bytes 786440 | tf_op jit(solution)/shard_map/ppermute | solution.py:226
  40.9 9.5 %collective-permute-start.4 = (bf16[16,64,128]{2,1,0:T(8,128)(2,1)S(1)}, bf16[16,64,128]{2,1,0:T(8,128)(2,1)S(1)}, u32[]{:S(2)}, u32[]{:S(2)}) collective-permute-start(bf16[16,64,128]{2,1,0:T(8,128)(2,1)S(1)} %get-tuple-element.84.own.inner), channel_id=1, source_target_pairs={{16,0},{32,16},{48,32},{64,48},{80,64},{96,80},{112,96},{128,112},... | collective-permute-start | bytes 786440 | tf_op jit(solution)/shard_map/ppermute | solution.py:224
  45.1 10.2 %collective-permute-start.7 = (bf16[16,64,128]{2,1,0:T(8,128)(2,1)S(1)}, bf16[16,64,128]{2,1,0:T(8,128)(2,1)S(1)}, u32[]{:S(2)}, u32[]{:S(2)}) collective-permute-start(bf16[16,64,128]{2,1,0:T(8,128)(2,1)S(1)} %get-tuple-element.91.inner.own), channel_id=1, source_target_pairs={{16,0},{32,16},{48,32},{64,48},{80,64},{96,80},{112,96},{128,112},... | collective-permute-start | bytes 786440 | tf_op jit(solution)/shard_map/ppermute | solution.py:224
  51.1 11.4 %collective-permute-start.6 = (bf16[16,64,128]{2,1,0:T(8,128)(2,1)S(1)}, bf16[16,64,128]{2,1,0:T(8,128)(2,1)S(1)}, u32[]{:S(2)}, u32[]{:S(2)}) collective-permute-start(bf16[16,64,128]{2,1,0:T(8,128)(2,1)S(1)} %get-tuple-element.92.own.inner), channel_id=1, source_target_pairs={{0,16},{16,32},{32,48},{48,64},{64,80},{80,96},{96,112},{112,128},... | collective-permute-start | bytes 786440 | tf_op jit(solution)/shard_map/ppermute | solution.py:226
  56.0 12.6 %collective-permute-start.9 = (bf16[16,64,128]{2,1,0:T(8,128)(2,1)S(1)}, bf16[16,64,128]{2,1,0:T(8,128)(2,1)S(1)}, u32[]{:S(2)}, u32[]{:S(2)}) collective-permute-start(bf16[16,64,128]{2,1,0:T(8,128)(2,1)S(1)} %get-tuple-element.99.inner.own), channel_id=1, source_target_pairs={{0,16},{16,32},{32,48},{48,64},{64,80},{80,96},{96,112},{112,128},... | collective-permute-start | bytes 786440 | tf_op jit(solution)/shard_map/ppermute | solution.py:226
  63.2 14.9 %collective-permute-start.8 = (bf16[16,64,128]{2,1,0:T(8,128)(2,1)S(1)}, bf16[16,64,128]{2,1,0:T(8,128)(2,1)S(1)}, u32[]{:S(2)}, u32[]{:S(2)}) collective-permute-start(bf16[16,64,128]{2,1,0:T(8,128)(2,1)S(1)} %get-tuple-element.100.own.inner), channel_id=1, source_target_pairs={{16,0},{32,16},{48,32},{64,48},{80,64},{96,80},{112,96},{128,112},... | collective-permute-start | bytes 786440 | tf_op jit(solution)/shard_map/ppermute | solution.py:224
  69.3 14.4 %collective-permute-start.11 = (bf16[16,64,128]{2,1,0:T(8,128)(2,1)S(1)}, bf16[16,64,128]{2,1,0:T(8,128)(2,1)S(1)}, u32[]{:S(2)}, u32[]{:S(2)}) collective-permute-start(bf16[16,64,128]{2,1,0:T(8,128)(2,1)S(1)} %get-tuple-element.106.inner.own), channel_id=1, source_target_pairs={{16,0},{32,16},{48,32},{64,48},{80,64},{96,80},{112,96},{128,112},... | collective-permute-start | bytes 786440 | tf_op jit(solution)/shard_map/ppermute | solution.py:224
  78.8 10.2 %collective-permute-start.10 = (bf16[16,64,128]{2,1,0:T(8,128)(2,1)S(1)}, bf16[16,64,128]{2,1,0:T(8,128)(2,1)S(1)}, u32[]{:S(2)}, u32[]{:S(2)}) collective-permute-start(bf16[16,64,128]{2,1,0:T(8,128)(2,1)S(1)} %get-tuple-element.107.own.inner), channel_id=1, source_target_pairs={{0,16},{16,32},{32,48},{48,64},{64,80},{80,96},{96,112},{112,128},... | collective-permute-start | bytes 786440 | tf_op jit(solution)/shard_map/ppermute | solution.py:226
  100.7 10.8 %collective-permute-start.12 = (bf16[8,4,64,128]{3,2,1,0:T(8,128)(2,1)S(1)}, bf16[8,4,64,128]{3,2,1,0:T(8,128)(2,1)S(1)}, u32[]{:S(2)}, u32[]{:S(2)}) collective-permute-start(bf16[8,4,64,128]{3,2,1,0:T(8,128)(2,1)S(1)} %bitcast.12), channel_id=1, source_target_pairs={{0,1},{1,0},{2,3},{3,2},{4,5},{5,4},{6,7},{7,6},{8,9},{9,8},{10,11... | collective-permute-start | bytes 1572872 | tf_op jit(solution)/shard_map/ppermute | solution.py:279
  106.6 9.3 %collective-permute-start.21 = (bf16[2,64,1024]{2,1,0:T(8,128)(2,1)S(1)}, bf16[2,64,1024]{2,1,0:T(8,128)(2,1)S(1)}, u32[]{:S(2)}, u32[]{:S(2)}) collective-permute-start(bf16[2,64,1024]{2,1,0:T(8,128)(2,1)S(1)} %pad_maximum_fusion.ritz), channel_id=1, source_target_pairs={{0,12},{4,0},{8,4},{12,8},{1,13},{5,1},{9,5},{13,9},{2,14},{6,2},{... | collective-permute-start | bytes 786440 | tf_op jit(solution)/shard_map/ppermute | solution.py:235
  107.6 11.0 %collective-permute-start.22 = (bf16[2,64,1024]{2,1,0:T(8,128)(2,1)S(1)}, bf16[2,64,1024]{2,1,0:T(8,128)(2,1)S(1)}, u32[]{:S(2)}, u32[]{:S(2)}) collective-permute-start(bf16[2,64,1024]{2,1,0:T(8,128)(2,1)S(1)} %pad_maximum_fusion.ritz), channel_id=1, source_target_pairs={{0,8},{4,12},{8,0},{12,4},{1,9},{5,13},{9,1},{13,5},{2,10},{6,14},... | collective-permute-start | bytes 786440 | tf_op jit(solution)/shard_map/ppermute | solution.py:235
  109.9 15.1 %collective-permute-start.23 = (bf16[2,64,1024]{2,1,0:T(8,128)(2,1)S(1)}, bf16[2,64,1024]{2,1,0:T(8,128)(2,1)S(1)}, u32[]{:S(2)}, u32[]{:S(2)}) collective-permute-start(bf16[2,64,1024]{2,1,0:T(8,128)(2,1)S(1)} %pad_maximum_fusion.ritz), channel_id=1, source_target_pairs={{0,4},{4,8},{8,12},{12,0},{1,5},{5,9},{9,13},{13,1},{2,6},{6,10},{... | collective-permute-start | bytes 786440 | tf_op jit(solution)/shard_map/ppermute | solution.py:235
  113.3 15.5 %collective-permute-start.13 = (bf16[8,64,128]{2,1,0:T(8,128)(2,1)S(1)}, bf16[8,64,128]{2,1,0:T(8,128)(2,1)S(1)}, u32[]{:S(2)}, u32[]{:S(2)}) collective-permute-start(bf16[8,64,128]{2,1,0:T(8,128)(2,1)S(1)} %get-tuple-element.110), channel_id=1, source_target_pairs={{0,10},{2,8},{4,14},{6,12},{8,2},{10,0},{12,6},{14,4},{1,11},{3,9}... | collective-permute-start | bytes 393224 | tf_op jit(solution)/shard_map/ppermute | solution.py:297
  114.0 14.8 %collective-permute-start.14 = (bf16[8,64,128]{2,1,0:T(8,128)(2,1)S(1)}, bf16[8,64,128]{2,1,0:T(8,128)(2,1)S(1)}, u32[]{:S(2)}, u32[]{:S(2)}) collective-permute-start(bf16[8,64,128]{2,1,0:T(8,128)(2,1)S(1)} %get-tuple-element.111), channel_id=1, source_target_pairs={{0,2},{2,0},{4,6},{6,4},{8,10},{10,8},{12,14},{14,12},{1,3},{3,1},... | collective-permute-start | bytes 393224 | tf_op jit(solution)/shard_map/ppermute | solution.py:297
  115.9 16.2 %collective-permute-start.15 = (bf16[8,64,128]{2,1,0:T(8,128)(2,1)S(1)}, bf16[8,64,128]{2,1,0:T(8,128)(2,1)S(1)}, u32[]{:S(2)}, u32[]{:S(2)}) collective-permute-start(bf16[8,64,128]{2,1,0:T(8,128)(2,1)S(1)} %get-tuple-element.112), channel_id=1, source_target_pairs={{0,6},{2,4},{4,10},{6,8},{8,14},{10,12},{12,2},{14,0},{1,7},{3,5},... | collective-permute-start | bytes 393224 | tf_op jit(solution)/shard_map/ppermute | solution.py:297
  118.6 13.5 %collective-permute-start.16 = (bf16[8,64,128]{2,1,0:T(8,128)(2,1)S(1)}, bf16[8,64,128]{2,1,0:T(8,128)(2,1)S(1)}, u32[]{:S(2)}, u32[]{:S(2)}) collective-permute-start(bf16[8,64,128]{2,1,0:T(8,128)(2,1)S(1)} %get-tuple-element.113), channel_id=1, source_target_pairs={{0,14},{2,12},{4,2},{6,0},{8,6},{10,4},{12,10},{14,8},{1,15},{3,13... | collective-permute-start | bytes 393224 | tf_op jit(solution)/shard_map/ppermute | solution.py:297
  125.0 8.5 %collective-permute-start.17 = (bf16[8,64,128]{2,1,0:T(8,128)(2,1)S(1)}, bf16[8,64,128]{2,1,0:T(8,128)(2,1)S(1)}, u32[]{:S(2)}, u32[]{:S(2)}) collective-permute-start(bf16[8,64,128]{2,1,0:T(8,128)(2,1)S(1)} %get-tuple-element.114), channel_id=1, source_target_pairs={{0,8},{2,10},{4,12},{6,14},{8,0},{10,2},{12,4},{14,6},{1,9},{3,11}... | collective-permute-start | bytes 393224 | tf_op jit(solution)/shard_map/ppermute | solution.py:297
  132.1 19.8 %collective-permute-start.24 = (bf16[4,4,64,128]{3,2,1,0:T(8,128)(2,1)S(1)}, bf16[4,4,64,128]{3,2,1,0:T(8,128)(2,1)S(1)}, u32[]{:S(2)}, u32[]{:S(2)}) collective-permute-start(bf16[4,4,64,128]{3,2,1,0:T(8,128)(2,1)S(1)} %get-tuple-element.119), channel_id=1, source_target_pairs={{0,2},{2,0},{1,3},{3,1},{4,6},{6,4},{5,7},{7,5},{8,10},{10,8},{9,1... | collective-permute-start | bytes 786440 | tf_op jit(solution)/shard_map/ppermute | solution.py:303
  135.2 28.4 %all-to-all-start.1 = ((bf16[16,32,128]{2,1,0:T(8,128)(2,1)}), bf16[16,32,128]{2,1,0:T(8,128)(2,1)S(1)}, u32[]{:S(2)}, u32[]{:S(2)}) async-start(bf16[16,32,128]{2,1,0:T(8,128)(2,1)} %shard_map.76), calls=%async_computation.1 | async-start | bytes 262144 | tf_op jit(solution)/shard_map/all_to_all | solution.py:315
  147.3 8.6 %collective-permute-start.25 = (bf16[4,64,128]{2,1,0:T(8,128)(2,1)S(1)}, bf16[4,64,128]{2,1,0:T(8,128)(2,1)S(1)}, u32[]{:S(2)}, u32[]{:S(2)}) collective-permute-start(bf16[4,64,128]{2,1,0:T(8,128)(2,1)S(1)} %get-tuple-element.120), channel_id=1, source_target_pairs={{0,4},{4,8},{8,12},{12,0},{1,5},{5,9},{9,13},{13,1},{2,6},{6,10},{... | collective-permute-start | bytes 196616 | tf_op jit(solution)/shard_map/ppermute | solution.py:307
  (12 other events, 88.0 us)

commit v11 on v9

--- a/solution.py
+++ b/solution.py
@@ -155,9 +155,11 @@
             outs[4][away, el] = turned[cols:, el * NB : (el + 1) * NB]
 
 
-def part_ways_kernel(crossed, *outs):
-    for away, out in enumerate(outs):
-        out[...] = crossed[away + 1]
+def join_kernel(crossed, *refs):
+    count = len(refs) // 2
+    for away in range(count):
+        refs[count + away][0] = refs[away][...]
+        refs[count + away][1] = crossed[away + 1]
 
 
 def collect_kernel(around, place, here, crossed, *refs):
@@ -169,7 +171,7 @@
             line = lax.rem(place[0] + around - away, around) * 2 + near
             for el in range(held):
                 if away:
-                    piece = pieces[q * (around - 1) + away - 1][el]
+                    piece = pieces[away - 1][q, el]
                 else:
                     piece = crossed[0, el] if q else here[el]
                 out[line * held + el] = piece.astype(jnp.float32)
@@ -300,19 +302,20 @@
     def along(away, value):
         pieces.append(lax.ppermute(value, "x", [(i, (i + away) % around) for i in range(around)]))
 
-    for away in range(1, around):
-        along(away, turned[away])
     total = call(
         margin_rows_kernel, parts,
         jax.ShapeDtypeStruct((slabs, cols // 2, 2 * cols), jnp.bfloat16), small, 12,
     )
     total = lax.all_to_all(total, ELEM, 0, 0, tiled=True)
-    ways = call(part_ways_kernel, (crossed,), (piece,) * (around - 1), small, 12)
+    joined = call(
+        join_kernel, (crossed, *turned[1:]),
+        (piece.update(shape=(2, *piece.shape)),) * (around - 1), small, 12,
+    )
     for away in range(1, around):
-        along(away, ways[away - 1])
+        along(away, joined[away - 1])
     rotated = call(
         functools.partial(collect_kernel, around), (place, turned[0], crossed, *pieces),
-        jax.ShapeDtypeStruct((2 * PLANE, cols, NB), jnp.float32), small, 12, (), [SMEM] + [VMEM] * (2 * around),
+        jax.ShapeDtypeStruct((2 * PLANE, cols, NB), jnp.float32), small, 12, (), [SMEM] + [VMEM] * (around + 1),
     )
     margin = call(
         functools.partial(margin_kernel, 1.0 / rows_total), (total,),

time: 163 us -> 164 us (level)
  waiting for transfers between devices: 37 us -> 46 us
  starting transfers between devices: 81.2 us -> 72.9 us
    all_to_all x1, waiting for transfers between devices: 0.01 us -> 6.14 us  [whole(): total = lax.all_to_all(total, ELEM, 0, 0, tiled=True)]
    ppermute x7, starting transfers between devices: 14.8 us -> 9.3 us  [whole(): parts.append(lax.ppermute(blocks[2 * away + q], CHIP, to_chip(away, q)))]
    ppermute x3, waiting for transfers between devices: 0.82 us -> 6.02 us  [whole(): lax.ppermute(shared['pair'], 'x', [(i, (i + shift) % around) for i in ran...]
    ppermute x6 -> x3, starting transfers between devices: 9.23 us -> 4.93 us  [along(): lax.ppermute(value, 'x', [(i, (i + away) % around) for i in range(around)])]
    ppermute x6 -> x3, waiting for transfers between devices: 3.66 us -> 0.01 us  [along(): lax.ppermute(value, 'x', [(i, (i + away) % around) for i in range(around)])]
  transfers between devices with their start and end apart: 32 -> 29, of which waited for: 18 -> 18; matrix products, arithmetic and copies ran while one was open for 0% -> 0% of each run, Pallas kernels for 16% -> 15%
where the time goes in v11:
time: 164 us; the launch traced here: 162 us
  starting transfers between devices  72.9 us (44%)
  waiting for transfers between devices  46 us (28%)
  Pallas kernels  27.2 us (17%)
  blocking collectives  11 us (7%)
  local copies, waits for them, and re-layouts  4.17 us (3%)
    ppermute x6, starting transfers between devices, send(): halo['b', k] = lax.ppermute(val['a', k], ELEM, down)  28.1 us
    pallas_call x31, Pallas kernels, call(): pl.pallas_call(kernel, out_shape=out_shape, in_specs=in_specs or [VMEM] *...  27.2 us
    ppermute x6, waiting for transfers between devices, send(): halo['a', k] = lax.ppermute(val['b', k], ELEM, up)  14.9 us
    ppermute x6, starting transfers between devices, send(): halo['a', k] = lax.ppermute(val['b', k], ELEM, up)  12.9 us
    all_to_all x1, starting transfers between devices, whole(): total = lax.all_to_all(total, ELEM, 0, 0, tiled=True)  11.1 us
    all_to_all x1, blocking collectives, whole(): mine = lax.all_to_all(filtered, CHIP, 0, 0, tiled=True)  11 us
    ppermute x7, starting transfers between devices, whole(): parts.append(lax.ppermute(blocks[2 * away + q], CHIP, to_chip(away, q)))  9.3 us
    ppermute x6, waiting for transfers between devices, send(): halo['b', k] = lax.ppermute(val['a', k], ELEM, down)  7.34 us
  transfers between devices with their start and end apart: 29, of which 18 were waited for; matrix products, arithmetic and copies ran while one was open for 0% of the time, Pallas kernels for 15%

profile of v11, /device:TPU:4, one launch (start us, length us, event | category | flops | bytes accessed | tf_op | source)
XLA Modules:
  0.0 162.3 jit_solution(16238448451982168690)
XLA Ops:
  1.7 3.3 %collective-permute-start.1 = (bf16[16,64,128]{2,1,0:T(8,128)(2,1)S(1)}, bf16[16,64,128]{2,1,0:T(8,128)(2,1)S(1)}, u32[]{:S(2)}, u32[]{:S(2)}) collective-permute-start(bf16[16,64,128]{2,1,0:T(8,128)(2,1)S(1)} %get-tuple-element.66.inner.own.current.rest_0_), channel_id=1, source_target_pairs={{0,16},{16,32},{32,48},{48,64},{64,80},{80,96},{96,112},{112,128},... | collective-permute-start | bytes 786440 | tf_op jit(solution)/shard_map/ppermute | solution.py:222
  5.0 5.4 %collective-permute-start = (bf16[16,64,128]{2,1,0:T(8,128)(2,1)S(1)}, bf16[16,64,128]{2,1,0:T(8,128)(2,1)S(1)}, u32[]{:S(2)}, u32[]{:S(2)}) collective-permute-start(bf16[16,64,128]{2,1,0:T(8,128)(2,1)S(1)} %get-tuple-element.67.own.current.inner.rest_0_), channel_id=1, source_target_pairs={{16,0},{32,16},{48,32},{64,48},{80,64},{96,80},{112,96},{128,112},... | collective-permute-start | bytes 786440 | tf_op jit(solution)/shard_map/ppermute | solution.py:220
  10.4 3.1 %copy-done = bf16[32,7,128,128]{3,2,1,0:T(8,128)(2,1)S(1)} copy-done((bf16[32,7,128,128]{3,2,1,0:T(8,128)(2,1)S(1)}, bf16[32,7,128,128]{3,2,1,0:T(8,128)(2,1)}, u32[]{:S(2)}) %copy-start) | copy-done | bytes 7340056
  17.4 8.8 %collective-permute-start.3 = (bf16[16,64,128]{2,1,0:T(8,128)(2,1)S(1)}, bf16[16,64,128]{2,1,0:T(8,128)(2,1)S(1)}, u32[]{:S(2)}, u32[]{:S(2)}) collective-permute-start(bf16[16,64,128]{2,1,0:T(8,128)(2,1)S(1)} %get-tuple-element.73.inner.own), channel_id=1, source_target_pairs={{16,0},{32,16},{48,32},{64,48},{80,64},{96,80},{112,96},{128,112},... | collective-permute-start | bytes 786440 | tf_op jit(solution)/shard_map/ppermute | solution.py:220
  32.8 7.6 %collective-permute-done.2.halo = bf16[16,64,128]{2,1,0:T(8,128)(2,1)S(1)} collective-permute-done((bf16[16,64,128]{2,1,0:T(8,128)(2,1)S(1)}, bf16[16,64,128]{2,1,0:T(8,128)(2,1)S(1)}, u32[]{:S(2)}, u32[]{:S(2)}) %collective-permute-start.2) | collective-permute-done | bytes 262176 | tf_op jit(solution)/shard_map/ppermute | solution.py:222
  41.0 2.4 %collective-permute-start.4 = (bf16[16,64,128]{2,1,0:T(8,128)(2,1)S(1)}, bf16[16,64,128]{2,1,0:T(8,128)(2,1)S(1)}, u32[]{:S(2)}, u32[]{:S(2)}) collective-permute-start(bf16[16,64,128]{2,1,0:T(8,128)(2,1)S(1)} %get-tuple-element.82.own.inner), channel_id=1, source_target_pairs={{16,0},{32,16},{48,32},{64,48},{80,64},{96,80},{112,96},{128,112},... | collective-permute-start | bytes 786440 | tf_op jit(solution)/shard_map/ppermute | solution.py:220
  45.2 3.7 %collective-permute-start.7 = (bf16[16,64,128]{2,1,0:T(8,128)(2,1)S(1)}, bf16[16,64,128]{2,1,0:T(8,128)(2,1)S(1)}, u32[]{:S(2)}, u32[]{:S(2)}) collective-permute-start(bf16[16,64,128]{2,1,0:T(8,128)(2,1)S(1)} %get-tuple-element.89.inner.own), channel_id=1, source_target_pairs={{16,0},{32,16},{48,32},{64,48},{80,64},{96,80},{112,96},{128,112},... | collective-permute-start | bytes 786440 | tf_op jit(solution)/shard_map/ppermute | solution.py:220
  51.2 2.4 %collective-permute-start.6 = (bf16[16,64,128]{2,1,0:T(8,128)(2,1)S(1)}, bf16[16,64,128]{2,1,0:T(8,128)(2,1)S(1)}, u32[]{:S(2)}, u32[]{:S(2)}) collective-permute-start(bf16[16,64,128]{2,1,0:T(8,128)(2,1)S(1)} %get-tuple-element.90.own.inner), channel_id=1, source_target_pairs={{0,16},{16,32},{32,48},{48,64},{64,80},{80,96},{96,112},{112,128},... | collective-permute-start | bytes 786440 | tf_op jit(solution)/shard_map/ppermute | solution.py:222
  56.1 3.3 %collective-permute-start.9 = (bf16[16,64,128]{2,1,0:T(8,128)(2,1)S(1)}, bf16[16,64,128]{2,1,0:T(8,128)(2,1)S(1)}, u32[]{:S(2)}, u32[]{:S(2)}) collective-permute-start(bf16[16,64,128]{2,1,0:T(8,128)(2,1)S(1)} %get-tuple-element.97.inner.own), channel_id=1, source_target_pairs={{0,16},{16,32},{32,48},{48,64},{64,80},{80,96},{96,112},{112,128},... | collective-permute-start | bytes 786440 | tf_op jit(solution)/shard_map/ppermute | solution.py:222
  60.5 2.1 %collective-permute-done.6.halo = bf16[16,64,128]{2,1,0:T(8,128)(2,1)S(1)} collective-permute-done((bf16[16,64,128]{2,1,0:T(8,128)(2,1)S(1)}, bf16[16,64,128]{2,1,0:T(8,128)(2,1)S(1)}, u32[]{:S(2)}, u32[]{:S(2)}) %collective-permute-start.6) | collective-permute-done | bytes 262176 | tf_op jit(solution)/shard_map/ppermute | solution.py:222
  63.3 4.3 %collective-permute-start.8 = (bf16[16,64,128]{2,1,0:T(8,128)(2,1)S(1)}, bf16[16,64,128]{2,1,0:T(8,128)(2,1)S(1)}, u32[]{:S(2)}, u32[]{:S(2)}) collective-permute-start(bf16[16,64,128]{2,1,0:T(8,128)(2,1)S(1)} %get-tuple-element.98.own.inner), channel_id=1, source_target_pairs={{16,0},{32,16},{48,32},{64,48},{80,64},{96,80},{112,96},{128,112},... | collective-permute-start | bytes 786440 | tf_op jit(solution)/shard_map/ppermute | solution.py:220
  69.4 3.4 %collective-permute-start.11 = (bf16[16,64,128]{2,1,0:T(8,128)(2,1)S(1)}, bf16[16,64,128]{2,1,0:T(8,128)(2,1)S(1)}, u32[]{:S(2)}, u32[]{:S(2)}) collective-permute-start(bf16[16,64,128]{2,1,0:T(8,128)(2,1)S(1)} %get-tuple-element.104.inner.own), channel_id=1, source_target_pairs={{16,0},{32,16},{48,32},{64,48},{80,64},{96,80},{112,96},{128,112},... | collective-permute-start | bytes 786440 | tf_op jit(solution)/shard_map/ppermute | solution.py:220
  73.9 4.3 %collective-permute-done.8.halo = bf16[16,64,128]{2,1,0:T(8,128)(2,1)S(1)} collective-permute-done((bf16[16,64,128]{2,1,0:T(8,128)(2,1)S(1)}, bf16[16,64,128]{2,1,0:T(8,128)(2,1)S(1)}, u32[]{:S(2)}, u32[]{:S(2)}) %collective-permute-start.8) | collective-permute-done | bytes 262176 | tf_op jit(solution)/shard_map/ppermute | solution.py:220
  78.9 3.8 %collective-permute-start.10 = (bf16[16,64,128]{2,1,0:T(8,128)(2,1)S(1)}, bf16[16,64,128]{2,1,0:T(8,128)(2,1)S(1)}, u32[]{:S(2)}, u32[]{:S(2)}) collective-permute-start(bf16[16,64,128]{2,1,0:T(8,128)(2,1)S(1)} %get-tuple-element.105.own.inner), channel_id=1, source_target_pairs={{0,16},{16,32},{32,48},{48,64},{64,80},{80,96},{96,112},{112,128},... | collective-permute-start | bytes 786440 | tf_op jit(solution)/shard_map/ppermute | solution.py:222
  85.6 3.5 %collective-permute-done.10.halo = bf16[16,64,128]{2,1,0:T(8,128)(2,1)S(1)} collective-permute-done((bf16[16,64,128]{2,1,0:T(8,128)(2,1)S(1)}, bf16[16,64,128]{2,1,0:T(8,128)(2,1)S(1)}, u32[]{:S(2)}, u32[]{:S(2)}) %collective-permute-start.10) | collective-permute-done | bytes 262176 | tf_op jit(solution)/shard_map/ppermute | solution.py:222
  89.8 11.0 %all_to_all.10 = bf16[32,64,128]{2,1,0:T(8,128)(2,1)S(1)} all-to-all(bf16[32,64,128]{2,1,0:T(8,128)(2,1)S(1)} %shard_map.74), channel_id=1, replica_groups=mesh['z'=8,'yh'=2,'x'=4,'yl'=2,'c'=2] {'x','yl'}, dimensions={0} | all-to-all | bytes 1048576 | tf_op jit(solution)/shard_map/all_to_all | solution.py:273
  101.1 5.6 %collective-permute-done.20 = bf16[64,1024]{1,0:T(8,128)(2,1)S(1)} collective-permute-done((bf16[64,1024]{1,0:T(8,128)(2,1)S(1)}, bf16[64,1024]{1,0:T(8,128)(2,1)S(1)}, u32[]{:S(2)}, u32[]{:S(2)}) %collective-permute-start.20) | collective-permute-done | bytes 131104 | tf_op jit(solution)/shard_map/ppermute | solution.py:226
  107.7 2.3 %collective-permute-start.22 = (bf16[2,64,1024]{2,1,0:T(8,128)(2,1)S(1)}, bf16[2,64,1024]{2,1,0:T(8,128)(2,1)S(1)}, u32[]{:S(2)}, u32[]{:S(2)}) collective-permute-start(bf16[2,64,1024]{2,1,0:T(8,128)(2,1)S(1)} %pad_maximum_fusion.ritz), channel_id=1, source_target_pairs={{0,8},{4,12},{8,0},{12,4},{1,9},{5,13},{9,1},{13,5},{2,10},{6,14},... | collective-permute-start | bytes 786440 | tf_op jit(solution)/shard_map/ppermute | solution.py:231
  116.0 2.7 %collective-permute-start.15 = (bf16[8,64,128]{2,1,0:T(8,128)(2,1)S(1)}, bf16[8,64,128]{2,1,0:T(8,128)(2,1)S(1)}, u32[]{:S(2)}, u32[]{:S(2)}) collective-permute-start(bf16[8,64,128]{2,1,0:T(8,128)(2,1)S(1)} %get-tuple-element.110), channel_id=1, source_target_pairs={{0,6},{2,4},{4,10},{6,8},{8,14},{10,12},{12,2},{14,0},{1,7},{3,5},... | collective-permute-start | bytes 393224 | tf_op jit(solution)/shard_map/ppermute | solution.py:293
  118.7 5.2 %collective-permute-done.23.ritz_back = bf16[2,64,1024]{2,1,0:T(8,128)(2,1)S(1)} collective-permute-done((bf16[2,64,1024]{2,1,0:T(8,128)(2,1)S(1)}, bf16[2,64,1024]{2,1,0:T(8,128)(2,1)S(1)}, u32[]{:S(2)}, u32[]{:S(2)}) %collective-permute-start.23) | collective-permute-done | bytes 262176 | tf_op jit(solution)/shard_map/ppermute | solution.py:231
  127.7 2.0 %collective-permute-start.17 = (bf16[8,64,128]{2,1,0:T(8,128)(2,1)S(1)}, bf16[8,64,128]{2,1,0:T(8,128)(2,1)S(1)}, u32[]{:S(2)}, u32[]{:S(2)}) collective-permute-start(bf16[8,64,128]{2,1,0:T(8,128)(2,1)S(1)} %get-tuple-element.112), channel_id=1, source_target_pairs={{0,8},{2,10},{4,12},{6,14},{8,0},{10,2},{12,4},{14,6},{1,9},{3,11}... | collective-permute-start | bytes 393224 | tf_op jit(solution)/shard_map/ppermute | solution.py:293
  137.8 11.1 %all-to-all-start.1 = ((bf16[16,32,128]{2,1,0:T(8,128)(2,1)}), bf16[16,32,128]{2,1,0:T(8,128)(2,1)S(1)}, u32[]{:S(2)}, u32[]{:S(2)}) async-start(bf16[16,32,128]{2,1,0:T(8,128)(2,1)} %shard_map.76), calls=%async_computation.1 | async-start | bytes 262144 | tf_op jit(solution)/shard_map/all_to_all | solution.py:309
  148.9 2.4 %collective-permute-start.25 = (bf16[2,4,64,128]{3,2,1,0:T(8,128)(2,1)S(1)}, bf16[2,4,64,128]{3,2,1,0:T(8,128)(2,1)S(1)}, u32[]{:S(2)}, u32[]{:S(2)}) collective-permute-start(bf16[2,4,64,128]{3,2,1,0:T(8,128)(2,1)S(1)} %get-tuple-element.121), channel_id=1, source_target_pairs={{0,4},{4,8},{8,12},{12,0},{1,5},{5,9},{9,13},{13,1},{2,6},{6,10},{... | collective-permute-start | bytes 393224 | tf_op jit(solution)/shard_map/ppermute | solution.py:303
  153.9 6.1 %all-to-all-done.1.got = bf16[16,32,128]{2,1,0:T(8,128)(2,1)S(1)} async-done(((bf16[16,32,128]{2,1,0:T(8,128)(2,1)}), bf16[16,32,128]{2,1,0:T(8,128)(2,1)S(1)}, u32[]{:S(2)}, u32[]{:S(2)}) %all-to-all-start.1) | async-done | bytes 131104 | tf_op jit(solution)/shard_map/all_to_all | solution.py:309
  (78 shorter events, 51.5 us)
Async XLA Ops:
  1.7 15.0 %collective-permute-start.1 = (bf16[16,64,128]{2,1,0:T(8,128)(2,1)S(1)}, bf16[16,64,128]{2,1,0:T(8,128)(2,1)S(1)}, u32[]{:S(2)}, u32[]{:S(2)}) collective-permute-start(bf16[16,64,128]{2,1,0:T(8,128)(2,1)S(1)} %get-tuple-element.66.inner.own.current.rest_0_), channel_id=1, source_target_pairs={{0,16},{16,32},{32,48},{48,64},{64,80},{80,96},{96,112},{112,128},... | collective-permute-start | bytes 786440 | tf_op jit(solution)/shard_map/ppermute | solution.py:222
  5.0 22.3 %collective-permute-start = (bf16[16,64,128]{2,1,0:T(8,128)(2,1)S(1)}, bf16[16,64,128]{2,1,0:T(8,128)(2,1)S(1)}, u32[]{:S(2)}, u32[]{:S(2)}) collective-permute-start(bf16[16,64,128]{2,1,0:T(8,128)(2,1)S(1)} %get-tuple-element.67.own.current.inner.rest_0_), channel_id=1, source_target_pairs={{16,0},{32,16},{48,32},{64,48},{80,64},{96,80},{112,96},{128,112},... | collective-permute-start | bytes 786440 | tf_op jit(solution)/shard_map/ppermute | solution.py:220
  17.4 13.6 %collective-permute-start.3 = (bf16[16,64,128]{2,1,0:T(8,128)(2,1)S(1)}, bf16[16,64,128]{2,1,0:T(8,128)(2,1)S(1)}, u32[]{:S(2)}, u32[]{:S(2)}) collective-permute-start(bf16[16,64,128]{2,1,0:T(8,128)(2,1)S(1)} %get-tuple-element.73.inner.own), channel_id=1, source_target_pairs={{16,0},{32,16},{48,32},{64,48},{80,64},{96,80},{112,96},{128,112},... | collective-permute-start | bytes 786440 | tf_op jit(solution)/shard_map/ppermute | solution.py:220
  28.0 12.4 %collective-permute-start.2 = (bf16[16,64,128]{2,1,0:T(8,128)(2,1)S(1)}, bf16[16,64,128]{2,1,0:T(8,128)(2,1)S(1)}, u32[]{:S(2)}, u32[]{:S(2)}) collective-permute-start(bf16[16,64,128]{2,1,0:T(8,128)(2,1)S(1)} %get-tuple-element.74.own.inner), channel_id=1, source_target_pairs={{0,16},{16,32},{32,48},{48,64},{64,80},{80,96},{96,112},{112,128},... | collective-permute-start | bytes 786440 | tf_op jit(solution)/shard_map/ppermute | solution.py:222
  31.6 12.9 %collective-permute-start.5 = (bf16[16,64,128]{2,1,0:T(8,128)(2,1)S(1)}, bf16[16,64,128]{2,1,0:T(8,128)(2,1)S(1)}, u32[]{:S(2)}, u32[]{:S(2)}) collective-permute-start(bf16[16,64,128]{2,1,0:T(8,128)(2,1)S(1)} %get-tuple-element.81.inner.own), channel_id=1, source_target_pairs={{0,16},{16,32},{32,48},{48,64},{64,80},{80,96},{96,112},{112,128},... | collective-permute-start | bytes 786440 | tf_op jit(solution)/shard_map/ppermute | solution.py:222
  41.0 9.5 %collective-permute-start.4 = (bf16[16,64,128]{2,1,0:T(8,128)(2,1)S(1)}, bf16[16,64,128]{2,1,0:T(8,128)(2,1)S(1)}, u32[]{:S(2)}, u32[]{:S(2)}) collective-permute-start(bf16[16,64,128]{2,1,0:T(8,128)(2,1)S(1)} %get-tuple-element.82.own.inner), channel_id=1, source_target_pairs={{16,0},{32,16},{48,32},{64,48},{80,64},{96,80},{112,96},{128,112},... | collective-permute-start | bytes 786440 | tf_op jit(solution)/shard_map/ppermute | solution.py:220
  45.2 10.2 %collective-permute-start.7 = (bf16[16,64,128]{2,1,0:T(8,128)(2,1)S(1)}, bf16[16,64,128]{2,1,0:T(8,128)(2,1)S(1)}, u32[]{:S(2)}, u32[]{:S(2)}) collective-permute-start(bf16[16,64,128]{2,1,0:T(8,128)(2,1)S(1)} %get-tuple-element.89.inner.own), channel_id=1, source_target_pairs={{16,0},{32,16},{48,32},{64,48},{80,64},{96,80},{112,96},{128,112},... | collective-permute-start | bytes 786440 | tf_op jit(solution)/shard_map/ppermute | solution.py:220
  51.2 11.4 %collective-permute-start.6 = (bf16[16,64,128]{2,1,0:T(8,128)(2,1)S(1)}, bf16[16,64,128]{2,1,0:T(8,128)(2,1)S(1)}, u32[]{:S(2)}, u32[]{:S(2)}) collective-permute-start(bf16[16,64,128]{2,1,0:T(8,128)(2,1)S(1)} %get-tuple-element.90.own.inner), channel_id=1, source_target_pairs={{0,16},{16,32},{32,48},{48,64},{64,80},{80,96},{96,112},{112,128},... | collective-permute-start | bytes 786440 | tf_op jit(solution)/shard_map/ppermute | solution.py:222
  56.1 12.6 %collective-permute-start.9 = (bf16[16,64,128]{2,1,0:T(8,128)(2,1)S(1)}, bf16[16,64,128]{2,1,0:T(8,128)(2,1)S(1)}, u32[]{:S(2)}, u32[]{:S(2)}) collective-permute-start(bf16[16,64,128]{2,1,0:T(8,128)(2,1)S(1)} %get-tuple-element.97.inner.own), channel_id=1, source_target_pairs={{0,16},{16,32},{32,48},{48,64},{64,80},{80,96},{96,112},{112,128},... | collective-permute-start | bytes 786440 | tf_op jit(solution)/shard_map/ppermute | solution.py:222
  63.3 14.9 %collective-permute-start.8 = (bf16[16,64,128]{2,1,0:T(8,128)(2,1)S(1)}, bf16[16,64,128]{2,1,0:T(8,128)(2,1)S(1)}, u32[]{:S(2)}, u32[]{:S(2)}) collective-permute-start(bf16[16,64,128]{2,1,0:T(8,128)(2,1)S(1)} %get-tuple-element.98.own.inner), channel_id=1, source_target_pairs={{16,0},{32,16},{48,32},{64,48},{80,64},{96,80},{112,96},{128,112},... | collective-permute-start | bytes 786440 | tf_op jit(solution)/shard_map/ppermute | solution.py:220
  69.4 14.4 %collective-permute-start.11 = (bf16[16,64,128]{2,1,0:T(8,128)(2,1)S(1)}, bf16[16,64,128]{2,1,0:T(8,128)(2,1)S(1)}, u32[]{:S(2)}, u32[]{:S(2)}) collective-permute-start(bf16[16,64,128]{2,1,0:T(8,128)(2,1)S(1)} %get-tuple-element.104.inner.own), channel_id=1, source_target_pairs={{16,0},{32,16},{48,32},{64,48},{80,64},{96,80},{112,96},{128,112},... | collective-permute-start | bytes 786440 | tf_op jit(solution)/shard_map/ppermute | solution.py:220
  78.9 10.2 %collective-permute-start.10 = (bf16[16,64,128]{2,1,0:T(8,128)(2,1)S(1)}, bf16[16,64,128]{2,1,0:T(8,128)(2,1)S(1)}, u32[]{:S(2)}, u32[]{:S(2)}) collective-permute-start(bf16[16,64,128]{2,1,0:T(8,128)(2,1)S(1)} %get-tuple-element.105.own.inner), channel_id=1, source_target_pairs={{0,16},{16,32},{32,48},{48,64},{64,80},{80,96},{96,112},{112,128},... | collective-permute-start | bytes 786440 | tf_op jit(solution)/shard_map/ppermute | solution.py:222
  100.8 10.8 %collective-permute-start.12 = (bf16[8,4,64,128]{3,2,1,0:T(8,128)(2,1)S(1)}, bf16[8,4,64,128]{3,2,1,0:T(8,128)(2,1)S(1)}, u32[]{:S(2)}, u32[]{:S(2)}) collective-permute-start(bf16[8,4,64,128]{3,2,1,0:T(8,128)(2,1)S(1)} %bitcast.12), channel_id=1, source_target_pairs={{0,1},{1,0},{2,3},{3,2},{4,5},{5,4},{6,7},{7,6},{8,9},{9,8},{10,11... | collective-permute-start | bytes 1572872 | tf_op jit(solution)/shard_map/ppermute | solution.py:275
  106.7 9.3 %collective-permute-start.21 = (bf16[2,64,1024]{2,1,0:T(8,128)(2,1)S(1)}, bf16[2,64,1024]{2,1,0:T(8,128)(2,1)S(1)}, u32[]{:S(2)}, u32[]{:S(2)}) collective-permute-start(bf16[2,64,1024]{2,1,0:T(8,128)(2,1)S(1)} %pad_maximum_fusion.ritz), channel_id=1, source_target_pairs={{0,12},{4,0},{8,4},{12,8},{1,13},{5,1},{9,5},{13,9},{2,14},{6,2},{... | collective-permute-start | bytes 786440 | tf_op jit(solution)/shard_map/ppermute | solution.py:231
  107.7 11.0 %collective-permute-start.22 = (bf16[2,64,1024]{2,1,0:T(8,128)(2,1)S(1)}, bf16[2,64,1024]{2,1,0:T(8,128)(2,1)S(1)}, u32[]{:S(2)}, u32[]{:S(2)}) collective-permute-start(bf16[2,64,1024]{2,1,0:T(8,128)(2,1)S(1)} %pad_maximum_fusion.ritz), channel_id=1, source_target_pairs={{0,8},{4,12},{8,0},{12,4},{1,9},{5,13},{9,1},{13,5},{2,10},{6,14},... | collective-permute-start | bytes 786440 | tf_op jit(solution)/shard_map/ppermute | solution.py:231
  110.0 13.9 %collective-permute-start.23 = (bf16[2,64,1024]{2,1,0:T(8,128)(2,1)S(1)}, bf16[2,64,1024]{2,1,0:T(8,128)(2,1)S(1)}, u32[]{:S(2)}, u32[]{:S(2)}) collective-permute-start(bf16[2,64,1024]{2,1,0:T(8,128)(2,1)S(1)} %pad_maximum_fusion.ritz), channel_id=1, source_target_pairs={{0,4},{4,8},{8,12},{12,0},{1,5},{5,9},{9,13},{13,1},{2,6},{6,10},{... | collective-permute-start | bytes 786440 | tf_op jit(solution)/shard_map/ppermute | solution.py:231
  113.4 14.3 %collective-permute-start.13 = (bf16[8,64,128]{2,1,0:T(8,128)(2,1)S(1)}, bf16[8,64,128]{2,1,0:T(8,128)(2,1)S(1)}, u32[]{:S(2)}, u32[]{:S(2)}) collective-permute-start(bf16[8,64,128]{2,1,0:T(8,128)(2,1)S(1)} %get-tuple-element.108), channel_id=1, source_target_pairs={{0,10},{2,8},{4,14},{6,12},{8,2},{10,0},{12,6},{14,4},{1,11},{3,9}... | collective-permute-start | bytes 393224 | tf_op jit(solution)/shard_map/ppermute | solution.py:293
  114.1 15.7 %collective-permute-start.14 = (bf16[8,64,128]{2,1,0:T(8,128)(2,1)S(1)}, bf16[8,64,128]{2,1,0:T(8,128)(2,1)S(1)}, u32[]{:S(2)}, u32[]{:S(2)}) collective-permute-start(bf16[8,64,128]{2,1,0:T(8,128)(2,1)S(1)} %get-tuple-element.109), channel_id=1, source_target_pairs={{0,2},{2,0},{4,6},{6,4},{8,10},{10,8},{12,14},{14,12},{1,3},{3,1},... | collective-permute-start | bytes 393224 | tf_op jit(solution)/shard_map/ppermute | solution.py:293
  116.0 15.4 %collective-permute-start.15 = (bf16[8,64,128]{2,1,0:T(8,128)(2,1)S(1)}, bf16[8,64,128]{2,1,0:T(8,128)(2,1)S(1)}, u32[]{:S(2)}, u32[]{:S(2)}) collective-permute-start(bf16[8,64,128]{2,1,0:T(8,128)(2,1)S(1)} %get-tuple-element.110), channel_id=1, source_target_pairs={{0,6},{2,4},{4,10},{6,8},{8,14},{10,12},{12,2},{14,0},{1,7},{3,5},... | collective-permute-start | bytes 393224 | tf_op jit(solution)/shard_map/ppermute | solution.py:293
  124.7 24.2 %collective-permute-start.24 = (bf16[4,4,64,128]{3,2,1,0:T(8,128)(2,1)S(1)}, bf16[4,4,64,128]{3,2,1,0:T(8,128)(2,1)S(1)}, u32[]{:S(2)}, u32[]{:S(2)}) collective-permute-start(bf16[4,4,64,128]{3,2,1,0:T(8,128)(2,1)S(1)} %get-tuple-element.117), channel_id=1, source_target_pairs={{0,2},{2,0},{1,3},{3,1},{4,6},{6,4},{5,7},{7,5},{8,10},{10,8},{9,1... | collective-permute-start | bytes 786440 | tf_op jit(solution)/shard_map/ppermute | solution.py:299
  137.8 22.2 %all-to-all-start.1 = ((bf16[16,32,128]{2,1,0:T(8,128)(2,1)}), bf16[16,32,128]{2,1,0:T(8,128)(2,1)S(1)}, u32[]{:S(2)}, u32[]{:S(2)}) async-start(bf16[16,32,128]{2,1,0:T(8,128)(2,1)} %shard_map.76), calls=%async_computation.1 | async-start | bytes 262144 | tf_op jit(solution)/shard_map/all_to_all | solution.py:309
  148.9 11.8 %collective-permute-start.25 = (bf16[2,4,64,128]{3,2,1,0:T(8,128)(2,1)S(1)}, bf16[2,4,64,128]{3,2,1,0:T(8,128)(2,1)S(1)}, u32[]{:S(2)}, u32[]{:S(2)}) collective-permute-start(bf16[2,4,64,128]{3,2,1,0:T(8,128)(2,1)S(1)} %get-tuple-element.121), channel_id=1, source_target_pairs={{0,4},{4,8},{8,12},{12,0},{1,5},{5,9},{9,13},{13,1},{2,6},{6,10},{... | collective-permute-start | bytes 393224 | tf_op jit(solution)/shard_map/ppermute | solution.py:303
  151.3 9.4 %collective-permute-start.26 = (bf16[2,4,64,128]{3,2,1,0:T(8,128)(2,1)S(1)}, bf16[2,4,64,128]{3,2,1,0:T(8,128)(2,1)S(1)}, u32[]{:S(2)}, u32[]{:S(2)}) collective-permute-start(bf16[2,4,64,128]{3,2,1,0:T(8,128)(2,1)S(1)} %get-tuple-element.122), channel_id=1, source_target_pairs={{0,8},{4,12},{8,0},{12,4},{1,9},{5,13},{9,1},{13,5},{2,10},{6,14},... | collective-permute-start | bytes 393224 | tf_op jit(solution)/shard_map/ppermute | solution.py:303
  151.9 8.9 %collective-permute-start.27 = (bf16[2,4,64,128]{3,2,1,0:T(8,128)(2,1)S(1)}, bf16[2,4,64,128]{3,2,1,0:T(8,128)(2,1)S(1)}, u32[]{:S(2)}, u32[]{:S(2)}) collective-permute-start(bf16[2,4,64,128]{3,2,1,0:T(8,128)(2,1)S(1)} %get-tuple-element.123), channel_id=1, source_target_pairs={{0,12},{4,0},{8,4},{12,8},{1,13},{5,1},{9,5},{13,9},{2,14},{6,2},{... | collective-permute-start | bytes 393224 | tf_op jit(solution)/shard_map/ppermute | solution.py:303
  (9 other events, 75.5 us)
